TPU v7x, 512 devices: a whole 4x8x8 slice. The times are simulated.
512 devices in a mesh: req: 64 (over y, z_lo, core), head: 8 (over z_hi, x).
Axes of the slice: x: 4, y: 8, z: 8 (z_hi: 2, z_lo: 4; z = z_hi * 4 + z_lo), core: 2. Of those that a mesh axis runs over, the one named last changes fastest.
Arguments:
- queries: bfloat16 [256, 8192], P('req', 'head'), may hold values from -200 to 200
- new_kv: bfloat16 [2, 256, 1024], P(None, 'req', 'head'), may hold values from -6 to 6
- own_kv: bfloat16 [2, 2048, 64, 1024], P(None, 'req', None, 'head'), may hold values from -6 to 6
- man_kv: bfloat16 [2, 128, 64, 1024], P(None, 'req', None, 'head'), may hold values from -6 to 6
- pages: int32 [256, 8], P('req'), may hold values from 0 to 31
- own_len: int32 [256], P('req'), may hold values from 1 to 8, as said below
- resid: bfloat16 [256, 8192], P(None, 'req'), may hold values from -3 to 3
- w_out: bfloat16 [8192, 8192], P('head', 'req'), may hold values from -0.8984375 to 0.8984375
- w_gate: bfloat16 [8192, 14336], P('req', 'head'), may hold values from -0.0625 to 0.0625
- w_up: bfloat16 [8192, 14336], P('req', 'head'), may hold values from -0.0625 to 0.0625
Outputs:
- resid_out: bfloat16 [256, 8192], P(None, 'req')
- hidden: bfloat16 [256, 14336], P('req', 'head')
Inputs may be any that keep to these rules, and one draw needn't show every extreme that they name: `pages`: entries at and past a request's length are padding. `own_len`: among the 4 requests of each index of req one has 8 pages.
All inputs are finite; a program needn't handle non-finite values.
Results may differ from a plain program's by a relative error of at most 0.03.
Values may be sent and summed in bfloat16 or wider, within the bound.
No kernel may reach another device: no remote copies, remote signals or barrier semaphores. Data moves between devices by JAX's collectives and lax.ppermute only.
A program may use at most 64 MiB of HBM per device.

v0:
```python
import jax
import jax.numpy as jnp
from jax import lax
from jax.sharding import PartitionSpec as P

HD = 128
PAGE = 64
MAXP = 8
GROUP = 8


def block_scores(query_matrix, keys):
    return jnp.einsum(
        "bkgd,tkd->bkgt", query_matrix, keys, preferred_element_type=jnp.float32
    ) * HD ** (-0.5)


def fold_block(carry, scores, values):
    top, total, acc = carry
    new_top = jnp.maximum(top, scores.max(-1))
    factor = jnp.exp(top - new_top)
    weights = jnp.exp(scores - new_top[..., None])
    total = total * factor + weights.sum(-1)
    acc = acc * factor[..., None] + jnp.einsum(
        "bkgt,tkd->bkgd", weights.astype(jnp.bfloat16), values, preferred_element_type=jnp.float32
    )
    return (new_top, total, acc)


def on_device(queries, new_kv, own_kv, man_kv, pages, own_len, resid, w_out, w_gate, w_up):
    rows = queries.shape[0]
    kv_dev = new_kv.shape[2] // HD
    query_matrix = queries.reshape(rows, kv_dev, GROUP, HD)
    picked = own_kv[:, pages].reshape(2, rows, MAXP * PAGE, kv_dev, HD)
    valid = jnp.repeat(jnp.arange(MAXP, dtype=jnp.int32)[None, :] < own_len[:, None], PAGE, axis=1)
    s_own = jnp.einsum(
        "bkgd,btkd->bkgt", query_matrix, picked[0], preferred_element_type=jnp.float32
    ) * HD ** (-0.5)
    s_own = jnp.where(valid[:, None, None, :], s_own, -jnp.inf)
    newest_token = new_kv.reshape(2, rows, kv_dev, HD)
    s_new = jnp.einsum(
        "slea,sla->sle", query_matrix, newest_token[0], preferred_element_type=jnp.float32
    ) * HD ** (-0.5)
    top = jnp.maximum(s_own.max(-1), s_new)
    w_own = jnp.exp(s_own - top[..., None])
    newest_weight = jnp.exp(s_new - top)
    total = w_own.sum(-1) + newest_weight
    acc = jnp.einsum(
        "bkgt,btkd->bkgd", w_own.astype(jnp.bfloat16), picked[1], preferred_element_type=jnp.float32
    )
    acc = acc + jnp.einsum(
        "acy,acx->acyx",
        newest_weight.astype(jnp.bfloat16),
        newest_token[1],
        preferred_element_type=jnp.float32,
    )
    carry = (top, total, acc)
    piece = lax.all_gather(man_kv, "req", axis=1, tiled=True)
    keys = piece[0].reshape(-1, kv_dev, HD)
    values = piece[1].reshape(-1, kv_dev, HD)
    top, total, acc = fold_block(carry, block_scores(query_matrix, keys), values)
    attn = (acc / total[..., None]).astype(jnp.bfloat16).reshape(rows, kv_dev * GROUP * HD)
    partial_out = jnp.dot(
        lax.all_gather(attn, "req", axis=0, tiled=True), w_out, preferred_element_type=jnp.float32
    )
    summed = lax.psum(partial_out.astype(jnp.bfloat16), "head").astype(jnp.float32)
    resid_out = (resid.astype(jnp.float32) + summed).astype(jnp.bfloat16)
    gate_part = jnp.dot(resid_out, w_gate, preferred_element_type=jnp.float32)
    up_projection_piece = jnp.dot(resid_out, w_up, preferred_element_type=jnp.float32)
    joined = lax.psum_scatter(
        jnp.concatenate([gate_part, up_projection_piece], axis=1),
        "req",
        scatter_dimension=0,
        tiled=True,
    )
    width = w_gate.shape[1]
    hidden = (jax.nn.silu(joined[:, :width]) * joined[:, width:]).astype(jnp.bfloat16)
    return (resid_out, hidden)


def solution(mesh):
    in_specs = (
        P("req", "head"),
        P(None, "req", "head"),
        P(None, "req", None, "head"),
        P(None, "req", None, "head"),
        P("req", None),
        P("req"),
        P(None, "req"),
        P("head", "req"),
        P("req", "head"),
        P("req", "head"),
    )
    out_specs = (P(None, "req"), P("req", "head"))
    return jax.shard_map(
        on_device, mesh=mesh, in_specs=in_specs, out_specs=out_specs, check_vma=False
    )
```

profile of v0, /device:TPU:1, one launch (start us, length us, event | category | flops | bytes accessed | tf_op | source)
XLA Modules:
  0.0 886.8 jit_solution(1648127448730967259)
XLA Ops:
  7.2 0.0 all-gather.3.cloned.1.call-start
  7.2 0.7 all-gather.3.cloned.1.call-update
  7.9 0.0 all-reduce.4.cloned.1.call-start
  8.0 0.7 compare_select_fusion
  8.6 0.1 reshape.129
  8.7 0.7 iota_compare_fusion
  9.5 0.1 broadcast_in_dim.26
  9.5 0.1 broadcast_in_dim.27
  9.7 0.7 gather_fusion
  10.4 0.1 copy.36
  10.5 0.1 fusion.20
  10.7 0.1 fusion.28
  10.7 0.3 fusion.29
  11.1 0.2 fusion.13
  11.3 125.6 %all-gather.3.cloned.1.call-done = bf16[2,128,64,128]{3,2,1,0:T(8,128)(2,1)} async-done(((bf16[2,2,64,128]{3,2,1,0:T(8,128)(2,1)}), bf16[2,128,64,128]{3,2,1,0:T(8,128)(2,1)}) %all-gather.3.cloned.1.call-update) | async-done | bytes 4194320 | tf_op jit(solution)/shard_map/all_gather | solution.py:58
  136.8 3.2 fusion.27
  140.0 0.9 fusion.30
  140.9 0.3 fusion.8
  141.3 0.2 fusion.6
  141.5 0.5 fusion.7
  142.0 79.0 %all-gather = bf16[64,4,1024]{2,1,0:T(4,128)(2,1)S(1)} all-gather(bf16[1,4,1024]{2,1,0:T(4,128)(2,1)S(1)} %reshape.137), channel_id=1, replica_groups=mesh['req'=64,'head'=8] {'req'}, dimensions={0}, use_global_device_ids=true | all-gather | bytes 532480 | tf_op jit(solution)/shard_map/all_gather | solution.py:64
  221.1 0.1 reshape.138
  221.2 0.9 convolution_convert_fusion
  222.2 0.0 all-reduce.6.cloned.1.call-start
  222.2 101.3 %all-reduce.4.cloned.1.call-done = bf16[256,128]{1,0:T(8,128)(2,1)} async-done(((bf16[256,128]{1,0:T(8,128)(2,1)}), bf16[256,128]{1,0:T(8,128)(2,1)}) %all-reduce.4.cloned.1.call-update) | async-done | bytes 65552 | tf_op jit(solution)/shard_map/psum | solution.py:66
  323.5 0.9 add_convert_fusion
  324.4 0.4 fusion.32
  324.8 0.4 fusion.31
  325.2 2.3 pad_maximum_fusion
  327.5 1.3 dynamic-slice
  329.4 549.4 %all-reduce.6.cloned.1.call-done = f32[256,3584]{1,0:T(8,128)} async-done(((f32[256,3584]{1,0:T(8,128)}), f32[256,3584]{1,0:T(8,128)}) %all-reduce.6.cloned.1.call-update) | async-done | bytes 3670032
  878.8 1.5 fusion.18
  (24 shorter events, 0.1 us)
Async XLA Ops:
  7.2 2.5 copy-start
  7.2 129.7 %all-gather.3.cloned.1.call-start = ((), (), s32[]{:S(2)}) async-start(), calls=%async_computation | async-start | bytes 4259840 | tf_op jit(solution)/shard_map/all_gather | solution.py:58
  7.9 315.6 %all-reduce.4.cloned.1.call-start = ((), (), s32[]{:S(2)}) async-start(), calls=%async_computation.1 | async-start | bytes 131072 | tf_op jit(solution)/shard_map/psum | solution.py:66
  9.6 0.9 copy-start.7
  9.7 0.9 copy-start.6
  141.5 79.7 %copy-start.4 = (bf16[1024,128]{1,0:T(8,128)(2,1)S(1)}, bf16[1024,128]{1,0:T(8,128)(2,1)}, u32[]{:S(2)}) copy-start(bf16[1024,128]{1,0:T(8,128)(2,1)} %param.17) | copy-start | bytes 786436
  141.5 182.0 %copy-start.5 = (bf16[256,128]{1,0:T(8,128)(2,1)S(1)}, bf16[256,128]{1,0:T(8,128)(2,1)}, u32[]{:S(2)}) copy-start(bf16[256,128]{1,0:T(8,128)(2,1)} %param.16) | copy-start | bytes 196612
  142.0 182.3 %copy-start.2 = (bf16[128,1792]{1,0:T(8,128)(2,1)S(1)}, bf16[128,1792]{1,0:T(8,128)(2,1)}, u32[]{:S(2)}) copy-start(bf16[128,1792]{1,0:T(8,128)(2,1)} %param.19) | copy-start | bytes 1376260
  221.1 103.7 %copy-start.3 = (bf16[128,1792]{1,0:T(8,128)(2,1)S(1)}, bf16[128,1792]{1,0:T(8,128)(2,1)}, u32[]{:S(2)}) copy-start(bf16[128,1792]{1,0:T(8,128)(2,1)} %param.18) | copy-start | bytes 1376260
  222.2 656.6 %all-reduce.6.cloned.1.call-start = ((), (), s32[]{:S(2)}) async-start(), calls=%async_computation.2 | async-start | bytes 7340032
  324.4 0.8 copy-start.1
Sparse Core Ops, SparseCore 0:
  10.2 126.6 all-gather.2
  222.3 101.1 all-reduce.3
  327.6 551.1 all-reduce.5
where the time goes:
time: 887 us
  waiting for transfers between devices  777 us (88%)
  blocking collectives  79 us (9%)
  between operations  14.6 us (2%)
    unnamed x4, waiting for transfers between devices  550 us
    all_gather x1, waiting for transfers between devices, on_device(): piece = lax.all_gather(man_kv, 'req', axis=1, tiled=True)  126 us
    psum x1, waiting for transfers between devices, on_device(): lax.psum(partial_out.astype(jnp.bfloat16), 'head').astype(jnp.float32)  101 us
    all_gather x1, blocking collectives, on_device(): lax.all_gather(attn, 'req', axis=0, tiled=True)  79 us
  transfers between devices with their start and end apart: 3, of which 3 were waited for; matrix products, arithmetic and copies ran while one was open for 1% of the time, Pallas kernels for 0%

commit v1 on v0

v1 whole, which is shorter than its diff:
```python
import jax
import jax.numpy as jnp
from jax import lax
from jax.experimental import pallas as pl
from jax.experimental.pallas import tpu as pltpu
from jax.sharding import Mesh, PartitionSpec as P

HD = 128
PAGE = 64
MAXP = 8
GROUP = 8
ROWS = 4
QROWS = ROWS * GROUP
POOL = 32
CHIPS = 32
STATS = 8
SCALE = HD**-0.5
PLANE = ("y", "zl")
HEAD = ("zh", "x")
REQ = ("y", "zl", "c")
BF = jnp.bfloat16
F32 = jnp.float32


def dot(a, b, ca, cb):
    return lax.dot_general(a, b, (((ca,), (cb,)), ((), ())), preferred_element_type=F32)


def own_kernel(pages_ref, len_ref, q_ref, new_ref, own_ref, acc_ref, top_ref, total_ref):
    tokens = POOL * PAGE
    scores = dot(q_ref[...], own_ref[0], 1, 1) * SCALE
    page_of = lax.broadcasted_iota(jnp.int32, (GROUP, tokens), 1) // PAGE
    weights, tops, totals, news = [], [], [], []
    for b in range(ROWS):
        count = jnp.zeros((GROUP, tokens), F32)
        for i in range(MAXP):
            page = jnp.where(i < len_ref[b], pages_ref[b, i], -1)
            count = count + jnp.where(page_of == page, 1.0, 0.0)
        s = jnp.where(count > 0.0, scores[b * GROUP : (b + 1) * GROUP], -jnp.inf)
        q = q_ref[b * GROUP : (b + 1) * GROUP].astype(F32)
        s_new = jnp.sum(q * new_ref[0, b : b + 1].astype(F32), axis=1, keepdims=True) * SCALE
        top = jnp.maximum(jnp.max(s, axis=1, keepdims=True), s_new)
        w = jnp.exp(s - top) * count
        w_new = jnp.exp(s_new - top)
        weights.append(w.astype(BF))
        tops.append(top)
        totals.append(jnp.sum(w, axis=1, keepdims=True) + w_new)
        news.append(w_new.astype(BF).astype(F32) * new_ref[1, b : b + 1].astype(F32))
    acc = dot(jnp.concatenate(weights, axis=0), own_ref[1], 1, 0)
    acc_ref[...] = acc + jnp.concatenate(news, axis=0)
    top_ref[...] = jnp.broadcast_to(jnp.concatenate(tops, axis=0), (QROWS, HD))
    total_ref[...] = jnp.broadcast_to(jnp.concatenate(totals, axis=0), (QROWS, HD))


def own_part(pages, own_len, q, new_kv, own_kv):
    smem = pl.BlockSpec(memory_space=pltpu.SMEM)
    vmem = pl.BlockSpec(memory_space=pltpu.VMEM)
    return pl.pallas_call(
        own_kernel,
        out_shape=[jax.ShapeDtypeStruct((QROWS, HD), F32)] * 3,
        in_specs=[smem, smem, vmem, vmem, vmem],
        out_specs=[vmem] * 3,
        compiler_params=pltpu.CompilerParams(vmem_limit_bytes=32 << 20),
        name="own_attention",
    )(pages, own_len, q, new_kv, own_kv)


def man_kernel(q_ref, kv_ref, out_ref):
    keys = jnp.concatenate([kv_ref[0, 0], kv_ref[1, 0]], axis=0)
    values = jnp.concatenate([kv_ref[0, 1], kv_ref[1, 1]], axis=0)
    row = lax.broadcasted_iota(jnp.int32, (STATS, HD), 0)
    for chunk in range(CHIPS * QROWS // HD):
        s = dot(keys, q_ref[chunk * HD : (chunk + 1) * HD], 1, 1) * SCALE
        top = jnp.max(s, axis=0, keepdims=True).astype(BF).astype(F32)
        w = jnp.exp(s - top)
        total = jnp.sum(w, axis=0, keepdims=True)
        high = total.astype(BF).astype(F32)
        acc = dot(w.astype(BF), values, 0, 0).astype(BF)
        stats = jnp.where(row == 0, top, jnp.where(row == 1, high, jnp.where(row == 2, total - high, 0.0)))
        stats = stats.astype(BF)
        for j in range(HD // QROWS):
            to = chunk * (HD // QROWS) + j
            out_ref[to, 0:QROWS] = acc[j * QROWS : (j + 1) * QROWS]
            out_ref[to, QROWS : QROWS + STATS] = stats


def man_part(q_all, kv):
    vmem = pl.BlockSpec(memory_space=pltpu.VMEM)
    return pl.pallas_call(
        man_kernel,
        out_shape=jax.ShapeDtypeStruct((CHIPS, QROWS + STATS, HD), BF),
        in_specs=[vmem, vmem],
        out_specs=vmem,
        compiler_params=pltpu.CompilerParams(vmem_limit_bytes=32 << 20),
        name="manifest_attention",
    )(q_all, kv)


def join_kernel(place_ref, parts_ref, acc_ref, top_ref, total_ref, out_ref, rows_ref):
    stats = parts_ref[:, QROWS : QROWS + STATS, :].reshape(CHIPS * STATS, HD)
    lane = lax.broadcasted_iota(jnp.int32, (QROWS, HD), 1)
    row = lax.broadcasted_iota(jnp.int32, (QROWS, HD), 0)
    pick = jnp.where(lane == row + place_ref[0] * QROWS, 1.0, 0.0).astype(BF)
    s = dot(pick, stats, 1, 1)
    n = CHIPS * STATS
    kind = lax.broadcasted_iota(jnp.int32, (QROWS, n), 1) % STATS
    totals = pltpu.roll(s, n - 1, 1) + pltpu.roll(s, n - 2, 1)
    own_top = top_ref[:, 0:1]
    top = jnp.maximum(jnp.max(jnp.where(kind == 0, s, -jnp.inf), axis=1, keepdims=True), own_top)
    factor = jnp.where(kind == 0, jnp.exp(jnp.minimum(s - top, 0.0)), 0.0)
    own_factor = jnp.exp(own_top - top)
    total = jnp.sum(factor * totals, axis=1, keepdims=True) + own_factor * total_ref[:, 0:1]
    acc = own_factor * acc_ref[...]
    for i in range(CHIPS):
        acc = acc + factor[:, i * STATS : i * STATS + 1] * parts_ref[i, 0:QROWS].astype(F32)
    rows_ref[...] = acc / total
    for h in range(GROUP):
        out_ref[:, h * HD : (h + 1) * HD] = rows_ref[pl.ds(h, ROWS, stride=GROUP), :].astype(BF)


def join_part(place, parts, acc, top, total):
    smem = pl.BlockSpec(memory_space=pltpu.SMEM)
    vmem = pl.BlockSpec(memory_space=pltpu.VMEM)
    return pl.pallas_call(
        join_kernel,
        out_shape=jax.ShapeDtypeStruct((ROWS, GROUP * HD), BF),
        in_specs=[smem, vmem, vmem, vmem, vmem],
        out_specs=vmem,
        scratch_shapes=[pltpu.VMEM((QROWS, HD), F32)],
        compiler_params=pltpu.CompilerParams(vmem_limit_bytes=32 << 20),
        name="join_attention",
    )(place, parts, acc, top, total)


def swap(x):
    return lax.ppermute(x, "c", [(0, 1), (1, 0)])


def spread(x, axes, n):
    return lax.all_to_all(jnp.broadcast_to(x[None], (n, *x.shape)), axes, 0, 0, tiled=True)


def on_device(queries, new_kv, own_kv, man_kv, pages, own_len, resid, w_out, w_gate, w_up):
    core = lax.axis_index("c")
    width = w_gate.shape[1]
    q = queries.reshape(QROWS, HD)
    kv = lax.all_gather(man_kv.reshape(2, 2 * PAGE, HD), "c", axis=0)
    w_out2 = jnp.concatenate([w_out, swap(w_out)], axis=1)
    w_gate2 = jnp.concatenate([w_gate, swap(w_gate)], axis=0)
    w_up2 = jnp.concatenate([w_up, swap(w_up)], axis=0)
    res = resid.reshape(CHIPS, 2, ROWS, HD)
    mine = jnp.where(core == 0, res[:, 0], res[:, 1])
    theirs = swap(jnp.where(core == 0, res[:, 1], res[:, 0]))
    res2 = jnp.concatenate([mine, theirs], axis=-1).reshape(CHIPS * ROWS, 2 * HD)

    acc, top, total = own_part(pages, own_len, q, new_kv, own_kv.reshape(2, POOL * PAGE, HD))
    q_all = spread(q, PLANE, CHIPS).reshape(CHIPS * QROWS, HD)
    parts = lax.all_to_all(man_part(q_all, kv), PLANE, 0, 0, tiled=True)
    place = lax.axis_index("zl").astype(jnp.int32).reshape(1)
    attn = join_part(place, parts, acc, top, total)
    attn_all = spread(attn, PLANE, CHIPS).reshape(CHIPS * ROWS, GROUP * HD)

    partial_out = jnp.dot(attn_all, w_out2, preferred_element_type=F32).astype(BF)
    summed = spread(partial_out, HEAD, 8).astype(F32).sum(0)
    out2 = (res2.astype(F32) + summed).astype(BF)

    gate_part = jnp.dot(out2, w_gate2, preferred_element_type=F32).astype(BF)
    up_part = jnp.dot(out2, w_up2, preferred_element_type=F32).astype(BF)
    both = jnp.concatenate(
        [gate_part.reshape(CHIPS, ROWS, width), up_part.reshape(CHIPS, ROWS, width)], axis=1
    )
    joined = lax.all_to_all(both, PLANE, 0, 0, tiled=True).astype(F32).sum(0)
    hidden = (jax.nn.silu(joined[:ROWS]) * joined[ROWS:]).astype(BF)

    kept = out2[:, :HD].reshape(CHIPS, 1, ROWS, HD)
    given = swap(out2[:, HD:]).reshape(CHIPS, 1, ROWS, HD)
    first = jnp.where(core == 0, kept, given)
    second = jnp.where(core == 0, given, kept)
    resid_out = jnp.concatenate([first, second], axis=1).reshape(CHIPS * 2 * ROWS, HD)
    return (resid_out, hidden)


def solution(mesh):
    fine = Mesh(mesh.devices.reshape(8, 4, 2, 2, 4), ("y", "zl", "c", "zh", "x"))
    in_specs = (
        P(REQ, HEAD),
        P(None, REQ, HEAD),
        P(None, REQ, None, HEAD),
        P(None, REQ, None, HEAD),
        P(REQ, None),
        P(REQ),
        P(None, REQ),
        P(HEAD, REQ),
        P(REQ, HEAD),
        P(REQ, HEAD),
    )
    out_specs = (P(None, REQ), P(REQ, HEAD))
    return jax.shard_map(
        on_device, mesh=fine, in_specs=in_specs, out_specs=out_specs, check_vma=False
    )
```

time: 887 us -> 126 us (0.14)
  the two profiles are of different devices: /device:TPU:1 before, /device:TPU:16 now
where the time goes in v1:
time: 126 us; the launch traced here: 125 us
  waiting for transfers between devices  59.7 us (47%)
  starting transfers between devices  51.3 us (41%)
  local copies, waits for them, and re-layouts  4.08 us (3%)
  Pallas kernels  3.53 us (3%)
  other arithmetic  2.36 us (2%)
  blocking collectives  2.11 us (2%)
    all_to_all x3, starting transfers between devices, spread(): lax.all_to_all(jnp.broadcast_to(x[None], (n, *x.shape)), axes, 0, 0, tile...  28.2 us
    all_to_all x3, waiting for transfers between devices, spread(): lax.all_to_all(jnp.broadcast_to(x[None], (n, *x.shape)), axes, 0, 0, tile...  27.5 us
    all_to_all x1, waiting for transfers between devices, on_device(): joined = lax.all_to_all(both, PLANE, 0, 0, tiled=True).astype(F32).sum(0)  19.5 us
    all_to_all x1, waiting for transfers between devices, on_device(): parts = lax.all_to_all(man_part(q_all, kv), PLANE, 0, 0, tiled=True)  11.5 us
    ppermute x5, starting transfers between devices, swap(): return lax.ppermute(x, 'c', [(0, 1), (1, 0)])  10.1 us
    all_to_all x1, starting transfers between devices, on_device(): joined = lax.all_to_all(both, PLANE, 0, 0, tiled=True).astype(F32).sum(0)  7.89 us
    all_to_all x1, starting transfers between devices, on_device(): parts = lax.all_to_all(man_part(q_all, kv), PLANE, 0, 0, tiled=True)  5.11 us
    broadcast_in_dim x4, local copies, waits for them, and re-layouts, spread(): jnp.broadcast_to(x[None], (n, *x.shape))  3.05 us
  transfers between devices with their start and end apart: 10, of which 6 were waited for; matrix products, arithmetic and copies ran while one was open for 1% of the time, Pallas kernels for 1%

profile of v1, /device:TPU:16, one launch (start us, length us, event | category | flops | bytes accessed | tf_op | source)
XLA Modules:
  0.0 124.9 jit_solution(12701903488808391214)
XLA Ops:
  0.6 0.7 broadcast_in_dim.8.q_ref
  1.3 0.7 broadcast_in_dim.9
  2.1 13.2 %all-to-all-start = ((bf16[32,32,128]{2,1,0:T(8,128)(2,1)}), bf16[32,32,128]{2,1,0:T(8,128)(2,1)S(1)}, u32[]{:S(2)}, u32[]{:S(2)}) async-start(bf16[32,32,128]{2,1,0:T(8,128)(2,1)} %broadcast_in_dim.9), calls=%async_computation | async-start | bytes 524288 | tf_op jit(solution)/shard_map/all_to_all | solution.py:140
  15.3 2.1 %all_gather.3.kv_ref = bf16[2,2,128,128]{3,2,1,0:T(8,128)(2,1)S(1)} all-gather(bf16[1,2,128,128]{3,2,1,0:T(8,128)(2,1)} %bitcast.31), channel_id=1, replica_groups=mesh['y'=8,'zl'=4,'c'=2,'zh'=2,'x'=4] {'c'}, dimensions={0}, use_global_device_ids=true | all-gather | bytes 196608 | tf_op jit(solution)/shard_map/all_gather | solution.py:147
  17.4 9.9 %all-to-all-done = bf16[32,32,128]{2,1,0:T(8,128)(2,1)S(1)} async-done(((bf16[32,32,128]{2,1,0:T(8,128)(2,1)}), bf16[32,32,128]{2,1,0:T(8,128)(2,1)S(1)}, u32[]{:S(2)}, u32[]{:S(2)}) %all-to-all-start) | async-done | bytes 262176 | tf_op jit(solution)/shard_map/all_to_all | solution.py:140
  27.2 1.6 %manifest_attention.1 = bf16[32,40,128]{2,1,0:T(8,128)(2,1)} custom-call(bf16[1024,128]{1,0:T(8,128)(2,1)S(1)} %bitcast.28, bf16[2,2,128,128]{3,2,1,0:T(8,128)(2,1)S(1)} %all_gather.3.kv_ref), custom_call_target="tpu_custom_call" | custom-call | tf_op jit(solution)/shard_map/manifest_attention/pallas_call | solution.py:89
  28.9 5.1 %all-to-all-start.1 = ((bf16[32,40,128]{2,1,0:T(8,128)(2,1)}), bf16[32,40,128]{2,1,0:T(8,128)(2,1)S(1)}, u32[]{:S(2)}, u32[]{:S(2)}) async-start(bf16[32,40,128]{2,1,0:T(8,128)(2,1)} %manifest_attention.1), calls=%async_computation.1 | async-start | bytes 655360 | tf_op jit(solution)/shard_map/all_to_all | solution.py:158
  34.0 1.2 own_attention.1
  35.3 11.5 %all-to-all-done.1.parts_ref = bf16[32,40,128]{2,1,0:T(8,128)(2,1)S(1)} async-done(((bf16[32,40,128]{2,1,0:T(8,128)(2,1)}), bf16[32,40,128]{2,1,0:T(8,128)(2,1)S(1)}, u32[]{:S(2)}, u32[]{:S(2)}) %all-to-all-start.1) | async-done | bytes 327712 | tf_op jit(solution)/shard_map/all_to_all | solution.py:158
  46.8 0.7 join_attention.1
  47.5 0.8 broadcast_in_dim.10
  48.3 5.0 %all-to-all-start.2 = ((bf16[32,4,1024]{2,1,0:T(4,128)(2,1)}), bf16[32,4,1024]{2,1,0:T(4,128)(2,1)S(1)}, u32[]{:S(2)}, u32[]{:S(2)}) async-start(bf16[32,4,1024]{2,1,0:T(4,128)(2,1)} %broadcast_in_dim.10), calls=%async_computation.2 | async-start | bytes 524288 | tf_op jit(solution)/shard_map/all_to_all | solution.py:140
  53.3 1.9 %collective-permute-start.1 = (bf16[1024,128]{1,0:T(8,128)(2,1)S(1)}, bf16[1024,128]{1,0:T(8,128)(2,1)S(1)}, u32[]{:S(2)}, u32[]{:S(2)}) collective-permute-start(bf16[1024,128]{1,0:T(8,128)(2,1)S(1)} %copy-done.7), channel_id=1, source_target_pairs={{0,8},{8,0},{1,9},{9,1},{2,10},{10,2},{3,11},{11,3},{4,12},{12,4},... | collective-permute-start | bytes 786440 | tf_op jit(solution)/shard_map/ppermute | solution.py:136
  55.2 9.6 %all-to-all-done.2 = bf16[32,4,1024]{2,1,0:T(4,128)(2,1)S(1)} async-done(((bf16[32,4,1024]{2,1,0:T(4,128)(2,1)}), bf16[32,4,1024]{2,1,0:T(4,128)(2,1)S(1)}, u32[]{:S(2)}, u32[]{:S(2)}) %all-to-all-start.2) | async-done | bytes 262176 | tf_op jit(solution)/shard_map/all_to_all | solution.py:140
  64.9 0.2 convolution_convert_fusion.2
  65.2 0.8 broadcast_in_dim.22
  66.0 10.0 %all-to-all-start.3 = ((bf16[8,128,256]{2,1,0:T(8,128)(2,1)}), bf16[8,128,256]{2,1,0:T(8,128)(2,1)S(1)}, u32[]{:S(2)}, u32[]{:S(2)}) async-start(bf16[8,128,256]{2,1,0:T(8,128)(2,1)} %broadcast_in_dim.22), calls=%async_computation.3 | async-start | bytes 1048576 | tf_op jit(solution)/shard_map/all_to_all | solution.py:140
  76.1 1.9 %collective-permute-start = (bf16[32,4,128]{2,1,0:T(4,128)(2,1)S(1)}, bf16[32,4,128]{2,1,0:T(4,128)(2,1)S(1)}, u32[]{:S(2)}, u32[]{:S(2)}) collective-permute-start(bf16[32,4,128]{2,1,0:T(4,128)(2,1)S(1)} %get-tuple-element.11), channel_id=1, source_target_pairs={{0,8},{8,0},{1,9},{9,1},{2,10},{10,2},{3,11},{11,3},{4,12},{12,4},... | collective-permute-start | bytes 98312 | tf_op jit(solution)/shard_map/ppermute | solution.py:136
  78.1 2.4 %collective-permute-start.3 = (bf16[128,1792]{1,0:T(8,128)(2,1)S(1)}, bf16[128,1792]{1,0:T(8,128)(2,1)S(1)}, u32[]{:S(2)}, u32[]{:S(2)}) collective-permute-start(bf16[128,1792]{1,0:T(8,128)(2,1)S(1)} %copy-done.5), channel_id=1, source_target_pairs={{0,8},{8,0},{1,9},{9,1},{2,10},{10,2},{3,11},{11,3},{4,12},{12,4},... | collective-permute-start | bytes 1376264 | tf_op jit(solution)/shard_map/ppermute | solution.py:136
  80.5 1.9 %collective-permute-start.4 = (bf16[128,1792]{1,0:T(8,128)(2,1)S(1)}, bf16[128,1792]{1,0:T(8,128)(2,1)S(1)}, u32[]{:S(2)}, u32[]{:S(2)}) collective-permute-start(bf16[128,1792]{1,0:T(8,128)(2,1)S(1)} %copy-done.6), channel_id=1, source_target_pairs={{0,8},{8,0},{1,9},{9,1},{2,10},{10,2},{3,11},{11,3},{4,12},{12,4},... | collective-permute-start | bytes 1376264 | tf_op jit(solution)/shard_map/ppermute | solution.py:136
  82.5 8.0 %all-to-all-done.3 = bf16[8,128,256]{2,1,0:T(8,128)(2,1)S(1)} async-done(((bf16[8,128,256]{2,1,0:T(8,128)(2,1)}), bf16[8,128,256]{2,1,0:T(8,128)(2,1)S(1)}, u32[]{:S(2)}, u32[]{:S(2)}) %all-to-all-start.3) | async-done | bytes 524320 | tf_op jit(solution)/shard_map/all_to_all | solution.py:140
  90.6 0.3 convolution_convert_fusion.1
  90.9 0.1 reshape.91
  91.1 0.3 convolution_convert_fusion
  91.5 1.4 %pad_maximum_fusion = bf16[32,8,1792]{2,1,0:T(8,128)(2,1)} fusion(bf16[32,4,1792]{2,1,0:T(4,128)(2,1)S(1)} %reshape.92, bf16[32,4,1792]{2,1,0:T(4,128)(2,1)S(1)} %reshape.91), kind=kLoop, calls=%fused_computation.11 | loop fusion | flops 1835008 | bytes 1835008 | tf_op jit(solution)/shard_map/concatenate | solution.py:169
  92.9 7.9 %all-to-all-start.4 = ((bf16[32,8,1792]{2,1,0:T(8,128)(2,1)}), bf16[32,8,1792]{2,1,0:T(8,128)(2,1)S(1)}, u32[]{:S(2)}, u32[]{:S(2)}) async-start(bf16[32,8,1792]{2,1,0:T(8,128)(2,1)} %pad_maximum_fusion), calls=%async_computation.4 | async-start | bytes 1835008 | tf_op jit(solution)/shard_map/all_to_all | solution.py:172
  100.8 1.9 %collective-permute-start.2 = (bf16[128,128]{1,0:T(8,128)(2,1)S(1)}, bf16[128,128]{1,0:T(8,128)(2,1)S(1)}, u32[]{:S(2)}, u32[]{:S(2)}) collective-permute-start(bf16[128,128]{1,0:T(8,128)(2,1)S(1)} %slice.29), channel_id=1, source_target_pairs={{0,8},{8,0},{1,9},{9,1},{2,10},{10,2},{3,11},{11,3},{4,12},{12,4},... | collective-permute-start | bytes 98312 | tf_op jit(solution)/shard_map/ppermute | solution.py:136
  102.7 1.2 collective-permute-done.2
  104.0 0.7 copy.22
  104.6 19.5 %all-to-all-done.4 = bf16[32,8,1792]{2,1,0:T(8,128)(2,1)S(1)} async-done(((bf16[32,8,1792]{2,1,0:T(8,128)(2,1)}), bf16[32,8,1792]{2,1,0:T(8,128)(2,1)S(1)}, u32[]{:S(2)}, u32[]{:S(2)}) %all-to-all-start.4) | async-done | bytes 917536 | tf_op jit(solution)/shard_map/all_to_all | solution.py:172
  124.1 0.1 convert_reduce_fusion
  124.2 0.6 fusion.10
  (30 shorter events, 0.5 us)
Async XLA Ops:
  2.1 31.9 %copy-start = (bf16[2,32,64,128]{3,2,1,0:T(8,128)(2,1)S(1)}, bf16[2,32,64,128]{3,2,1,0:T(8,128)(2,1)}, u32[]{:S(2)}) copy-start(bf16[2,32,64,128]{3,2,1,0:T(8,128)(2,1)} %param.12) | copy-start | bytes 3145732
  2.1 31.9 %copy-start.1 = (s32[4,8]{1,0:T(4,128)S(1)}, s32[4,8]{1,0:T(4,128)}, u32[]{:S(2)}) copy-start(s32[4,8]{1,0:T(4,128)} %pages_ref.1) | copy-start | bytes 388
  2.1 31.9 %copy-start.2 = (bf16[2,4,128]{2,1,0:T(4,128)(2,1)S(1)}, bf16[2,4,128]{2,1,0:T(4,128)(2,1)}, u32[]{:S(2)}) copy-start(bf16[2,4,128]{2,1,0:T(4,128)(2,1)} %new_ref.1) | copy-start | bytes 6148
  2.1 31.9 %copy-start.3 = (s32[4]{0:T(128)S(1)}, s32[4]{0:T(128)}, u32[]{:S(2)}) copy-start(s32[4]{0:T(128)} %len_ref.1) | copy-start | bytes 52
  2.1 25.1 %all-to-all-start = ((bf16[32,32,128]{2,1,0:T(8,128)(2,1)}), bf16[32,32,128]{2,1,0:T(8,128)(2,1)S(1)}, u32[]{:S(2)}, u32[]{:S(2)}) async-start(bf16[32,32,128]{2,1,0:T(8,128)(2,1)} %broadcast_in_dim.9), calls=%async_computation | async-start | bytes 524288 | tf_op jit(solution)/shard_map/all_to_all | solution.py:140
  28.9 17.9 %all-to-all-start.1 = ((bf16[32,40,128]{2,1,0:T(8,128)(2,1)}), bf16[32,40,128]{2,1,0:T(8,128)(2,1)S(1)}, u32[]{:S(2)}, u32[]{:S(2)}) async-start(bf16[32,40,128]{2,1,0:T(8,128)(2,1)} %manifest_attention.1), calls=%async_computation.1 | async-start | bytes 655360 | tf_op jit(solution)/shard_map/all_to_all | solution.py:158
  34.0 19.3 %copy-start.7 = (bf16[1024,128]{1,0:T(8,128)(2,1)S(1)}, bf16[1024,128]{1,0:T(8,128)(2,1)}, u32[]{:S(2)}) copy-start(bf16[1024,128]{1,0:T(8,128)(2,1)} %param.17) | copy-start | bytes 786436
  48.3 16.6 %all-to-all-start.2 = ((bf16[32,4,1024]{2,1,0:T(4,128)(2,1)}), bf16[32,4,1024]{2,1,0:T(4,128)(2,1)S(1)}, u32[]{:S(2)}, u32[]{:S(2)}) async-start(bf16[32,4,1024]{2,1,0:T(4,128)(2,1)} %broadcast_in_dim.10), calls=%async_computation.2 | async-start | bytes 524288 | tf_op jit(solution)/shard_map/all_to_all | solution.py:140
  53.3 11.6 %collective-permute-start.1 = (bf16[1024,128]{1,0:T(8,128)(2,1)S(1)}, bf16[1024,128]{1,0:T(8,128)(2,1)S(1)}, u32[]{:S(2)}, u32[]{:S(2)}) collective-permute-start(bf16[1024,128]{1,0:T(8,128)(2,1)S(1)} %copy-done.7), channel_id=1, source_target_pairs={{0,8},{8,0},{1,9},{9,1},{2,10},{10,2},{3,11},{11,3},{4,12},{12,4},... | collective-permute-start | bytes 786440 | tf_op jit(solution)/shard_map/ppermute | solution.py:136
  65.2 10.9 %copy-start.4 = (bf16[256,128]{1,0:T(8,128)(2,1)S(1)}, bf16[256,128]{1,0:T(8,128)(2,1)}, u32[]{:S(2)}) copy-start(bf16[256,128]{1,0:T(8,128)(2,1)} %param.16) | copy-start | bytes 196612
  65.2 12.9 %copy-start.5 = (bf16[128,1792]{1,0:T(8,128)(2,1)S(1)}, bf16[128,1792]{1,0:T(8,128)(2,1)}, u32[]{:S(2)}) copy-start(bf16[128,1792]{1,0:T(8,128)(2,1)} %param.18) | copy-start | bytes 1376260
  65.2 15.3 %copy-start.6 = (bf16[128,1792]{1,0:T(8,128)(2,1)S(1)}, bf16[128,1792]{1,0:T(8,128)(2,1)}, u32[]{:S(2)}) copy-start(bf16[128,1792]{1,0:T(8,128)(2,1)} %param.19) | copy-start | bytes 1376260
  66.0 24.5 %all-to-all-start.3 = ((bf16[8,128,256]{2,1,0:T(8,128)(2,1)}), bf16[8,128,256]{2,1,0:T(8,128)(2,1)S(1)}, u32[]{:S(2)}, u32[]{:S(2)}) async-start(bf16[8,128,256]{2,1,0:T(8,128)(2,1)} %broadcast_in_dim.22), calls=%async_computation.3 | async-start | bytes 1048576 | tf_op jit(solution)/shard_map/all_to_all | solution.py:140
  76.1 6.3 %collective-permute-start = (bf16[32,4,128]{2,1,0:T(4,128)(2,1)S(1)}, bf16[32,4,128]{2,1,0:T(4,128)(2,1)S(1)}, u32[]{:S(2)}, u32[]{:S(2)}) collective-permute-start(bf16[32,4,128]{2,1,0:T(4,128)(2,1)S(1)} %get-tuple-element.11), channel_id=1, source_target_pairs={{0,8},{8,0},{1,9},{9,1},{2,10},{10,2},{3,11},{11,3},{4,12},{12,4},... | collective-permute-start | bytes 98312 | tf_op jit(solution)/shard_map/ppermute | solution.py:136
  78.1 12.6 %collective-permute-start.3 = (bf16[128,1792]{1,0:T(8,128)(2,1)S(1)}, bf16[128,1792]{1,0:T(8,128)(2,1)S(1)}, u32[]{:S(2)}, u32[]{:S(2)}) collective-permute-start(bf16[128,1792]{1,0:T(8,128)(2,1)S(1)} %copy-done.5), channel_id=1, source_target_pairs={{0,8},{8,0},{1,9},{9,1},{2,10},{10,2},{3,11},{11,3},{4,12},{12,4},... | collective-permute-start | bytes 1376264 | tf_op jit(solution)/shard_map/ppermute | solution.py:136
  80.5 10.6 %collective-permute-start.4 = (bf16[128,1792]{1,0:T(8,128)(2,1)S(1)}, bf16[128,1792]{1,0:T(8,128)(2,1)S(1)}, u32[]{:S(2)}, u32[]{:S(2)}) collective-permute-start(bf16[128,1792]{1,0:T(8,128)(2,1)S(1)} %copy-done.6), channel_id=1, source_target_pairs={{0,8},{8,0},{1,9},{9,1},{2,10},{10,2},{3,11},{11,3},{4,12},{12,4},... | collective-permute-start | bytes 1376264 | tf_op jit(solution)/shard_map/ppermute | solution.py:136
  92.9 31.2 %all-to-all-start.4 = ((bf16[32,8,1792]{2,1,0:T(8,128)(2,1)}), bf16[32,8,1792]{2,1,0:T(8,128)(2,1)S(1)}, u32[]{:S(2)}, u32[]{:S(2)}) async-start(bf16[32,8,1792]{2,1,0:T(8,128)(2,1)} %pad_maximum_fusion), calls=%async_computation.4 | async-start | bytes 1835008 | tf_op jit(solution)/shard_map/all_to_all | solution.py:172
  100.8 3.1 %collective-permute-start.2 = (bf16[128,128]{1,0:T(8,128)(2,1)S(1)}, bf16[128,128]{1,0:T(8,128)(2,1)S(1)}, u32[]{:S(2)}, u32[]{:S(2)}) collective-permute-start(bf16[128,128]{1,0:T(8,128)(2,1)S(1)} %slice.29), channel_id=1, source_target_pairs={{0,8},{8,0},{1,9},{9,1},{2,10},{10,2},{3,11},{11,3},{4,12},{12,4},... | collective-permute-start | bytes 98312 | tf_op jit(solution)/shard_map/ppermute | solution.py:136

commit v2 on v0

v2 whole, which is shorter than its diff:
```python
import jax
import jax.numpy as jnp
from jax import lax
from jax.experimental import pallas as pl
from jax.experimental.pallas import tpu as pltpu
from jax.sharding import Mesh, PartitionSpec as P

HD = 128
PAGE = 64
MAXP = 8
GROUP = 8
ROWS = 4
QROWS = ROWS * GROUP
POOL = 32
NY = 8
NZ = 4
CHIPS = NY * NZ
SCALE = HD**-0.5
PLANE = ("y", "zl")
SIDE = ("zl", "zh", "x")
HEAD = ("zh", "x")
REQ = ("y", "zl", "c")
BF = jnp.bfloat16
F32 = jnp.float32
VMEM = pl.BlockSpec(memory_space=pltpu.VMEM)
SMEM = pl.BlockSpec(memory_space=pltpu.SMEM)


def dot(a, b, ca, cb):
    return lax.dot_general(a, b, (((ca,), (cb,)), ((), ())), preferred_element_type=F32)


def call(kernel, name, out_shape, *args, specs=None, scratch=()):
    return pl.pallas_call(
        kernel,
        out_shape=out_shape,
        in_specs=specs or [VMEM] * len(args),
        out_specs=jax.tree.map(lambda _: VMEM, out_shape),
        scratch_shapes=scratch,
        compiler_params=pltpu.CompilerParams(vmem_limit_bytes=40 << 20),
        name=name,
    )(*args)


def query_kernel(q_ref, out_ref, rows_ref):
    for h in range(GROUP):
        first = (h // 2) * 8 + h % 2
        rows_ref[pl.ds(first, ROWS, stride=2), :] = q_ref[:, h * HD : (h + 1) * HD].astype(F32)
    for z in range(NZ):
        block = rows_ref[z * 8 : z * 8 + 8].astype(BF)
        for y in range(NY):
            out_ref[y * NZ + z] = block


def own_kernel(pages_ref, len_ref, q_ref, new_ref, own_ref, out_ref):
    tokens = POOL * PAGE
    q = q_ref[0:NZ].reshape(QROWS, HD)
    scores = dot(q, own_ref[0], 1, 1) * SCALE
    page_of = lax.broadcasted_iota(jnp.int32, (8, tokens), 1) // PAGE
    req = lax.broadcasted_iota(jnp.int32, (8, HD), 0) // 2

    def by_request(values):
        return jnp.where(req == 0, values[0], jnp.where(req == 1, values[1], jnp.where(req == 2, values[2], values[3])))

    count = jnp.zeros((8, tokens), F32)
    for i in range(MAXP):
        page = by_request([jnp.where(i < len_ref[b], pages_ref[b, i], -1) for b in range(ROWS)])
        count = count + jnp.where(page_of == page[:, 0:1], 1.0, 0.0)
    new_k = by_request([new_ref[0, b : b + 1].astype(F32) for b in range(ROWS)])
    new_v = by_request([new_ref[1, b : b + 1].astype(F32) for b in range(ROWS)])
    lane = lax.broadcasted_iota(jnp.int32, (8, HD), 1)
    weights, news, stats = [], [], []
    for z in range(NZ):
        s = jnp.where(count > 0.0, scores[z * 8 : z * 8 + 8], -jnp.inf)
        s_new = jnp.sum(q_ref[z].astype(F32) * new_k, axis=1, keepdims=True) * SCALE
        top = jnp.maximum(jnp.max(s, axis=1, keepdims=True), s_new).astype(BF).astype(F32)
        w = jnp.exp(s - top) * count
        w_new = jnp.exp(s_new - top)
        total = jnp.sum(w, axis=1, keepdims=True) + w_new
        high = total.astype(BF).astype(F32)
        weights.append(w.astype(BF))
        news.append(w_new.astype(BF).astype(F32) * new_v)
        stats.append(jnp.where(lane == 0, top, jnp.where(lane == 1, high, jnp.where(lane == 2, total - high, 0.0))))
    acc = dot(jnp.concatenate(weights, axis=0), own_ref[1], 1, 0)
    for z in range(NZ):
        block = jnp.concatenate([acc[z * 8 : z * 8 + 8] + news[z], stats[z]], axis=0).astype(BF)
        for y in range(NY):
            out_ref[y * NZ + z] = block


def man_kernel(q_ref, kv_ref, out_ref):
    n = 2 * NZ
    keys = jnp.concatenate([kv_ref[i, 0] for i in range(n)], axis=0)
    values = jnp.concatenate([kv_ref[i, 1] for i in range(n)], axis=0)
    row = lax.broadcasted_iota(jnp.int32, (8, HD), 0)
    stats = jnp.zeros((8, HD), F32)
    accs = []
    for half in range(2):
        q = q_ref[half * 16 : half * 16 + 16].reshape(HD, HD)
        s = dot(keys, q, 1, 1) * SCALE
        top = jnp.max(s, axis=0, keepdims=True).astype(BF).astype(F32)
        w = jnp.exp(s - top)
        total = jnp.sum(w, axis=0, keepdims=True)
        high = total.astype(BF).astype(F32)
        accs.append(dot(w.astype(BF), values, 0, 0))
        for k, value in enumerate((top, high, total - high)):
            stats = jnp.where(row == 3 * half + k, value, stats)
    block = jnp.concatenate(accs + [stats], axis=0).astype(BF)
    for y in range(NY):
        out_ref[y] = block


def join_kernel(parts_ref, own_ref, w0_ref, w1_ref, out_ref, rows_ref):
    rows = 2 * HD
    stats = parts_ref[:, rows : rows + 8, :].reshape(NY * 8, HD)
    eye = lax.broadcasted_iota(jnp.int32, (HD, HD), 0) == lax.broadcasted_iota(jnp.int32, (HD, HD), 1)
    s = dot(jnp.where(eye, 1.0, 0.0).astype(BF), stats, 1, 1)
    n = NY * 8
    kind = lax.broadcasted_iota(jnp.int32, (HD, n), 1) % 8
    for half in range(2):
        base = 3 * half
        own = own_ref[half * 16 : half * 16 + 16].astype(F32)
        own_acc = own[:, 0:8].reshape(HD, HD)
        own_stats = own[:, 8:16].reshape(HD, HD)
        own_top = own_stats[:, 0:1]
        here = kind == base
        top = jnp.maximum(jnp.max(jnp.where(here, s, -jnp.inf), axis=1, keepdims=True), own_top)
        factor = jnp.where(here, jnp.exp(jnp.minimum(s - top, 0.0)), 0.0)
        totals = jnp.concatenate([s[:, 1:], s[:, :1]], axis=1) + jnp.concatenate([s[:, 2:], s[:, :2]], axis=1)
        own_factor = jnp.exp(own_top - top)
        total = jnp.sum(factor * totals, axis=1, keepdims=True) + own_factor * (own_stats[:, 1:2] + own_stats[:, 2:3])
        acc = own_factor * own_acc
        for y in range(NY):
            lane = y * 8 + base
            acc = acc + factor[:, lane : lane + 1] * parts_ref[y, half * HD : (half + 1) * HD].astype(F32)
        rows_ref[half * HD : (half + 1) * HD] = acc / total
    x = jnp.concatenate([rows_ref[pl.ds(h, HD, stride=2), :].astype(BF) for h in range(2)], axis=1)
    for k, w_ref in enumerate((w0_ref, w1_ref)):
        w = jnp.concatenate([w_ref[z] for z in range(NZ)], axis=1)
        y = dot(x, w, 1, 0).astype(BF)
        for b in range(16):
            out_ref[b * 2 + k] = y[b * 8 : b * 8 + 8]


def sum_kernel(parts_ref, res_ref, out_ref):
    total = parts_ref[0].astype(F32)
    for i in range(1, 32):
        total = total + parts_ref[i].astype(F32)
    res = jnp.concatenate([res_ref[z] for z in range(NZ)], axis=1).astype(F32)
    block = (res + total).astype(BF)
    for i in range(32):
        out_ref[i] = block


def mlp_kernel(r_ref, w0_ref, w1_ref, out_ref):
    z = dot(r_ref[:, 0].reshape(HD, 4 * HD), w0_ref[...], 1, 0)
    z = z + dot(r_ref[:, 1].reshape(HD, 4 * HD), w1_ref[...], 1, 0)
    out_ref[...] = z.astype(BF)


def swap(x):
    return lax.ppermute(x, "c", [(0, 1), (1, 0)])


def exchange(x, axes):
    return lax.all_to_all(x, axes, 0, 0, tiled=True)


def on_device(queries, new_kv, own_kv, man_kv, pages, own_len, resid, w_out, w_gate, w_up):
    shape = jax.ShapeDtypeStruct
    core, zl, zh, x = (lax.axis_index(a) for a in ("c", "zl", "zh", "x"))
    half = w_gate.shape[1] // 2

    q_out = call(query_kernel, "queries", shape((CHIPS, 8, HD), BF), queries, scratch=[pltpu.VMEM((QROWS, HD), F32)])
    q_all = exchange(q_out, PLANE)
    kv = exchange(jnp.broadcast_to(man_kv.reshape(1, 2, 2 * PAGE, HD), (NZ, 2, 2 * PAGE, HD)), "zl")
    kv = lax.all_gather(kv, "c", axis=0, tiled=True)

    own = call(
        own_kernel, "own_attention", shape((CHIPS, 16, HD), BF),
        pages, own_len, q_out, new_kv, own_kv.reshape(2, POOL * PAGE, HD),
        specs=[SMEM, SMEM, VMEM, VMEM, VMEM],
    )
    own_all = exchange(own, PLANE)

    w_a = exchange(w_out.reshape(NZ, 2 * HD, HD), "zl")
    w_b = swap(w_a)
    cut = jnp.stack([w_gate[:, :half], w_gate[:, half:], w_up[:, :half], w_up[:, half:]])
    v_a = exchange(cut, "zl")
    v_b = swap(v_a)

    res = resid.reshape(NZ, 4, 2, 2, ROWS, HD)
    res = lax.dynamic_index_in_dim(res, zh * 2 + x // 2, 1, keepdims=False)
    res = exchange(res.transpose(0, 2, 1, 3, 4).reshape(2 * NZ, 8, HD), ("zl", "c"))
    res = lax.dynamic_index_in_dim(res.reshape(NZ, 2, 8, HD), (core + x) % 2, 1, keepdims=False)

    parts = exchange(call(man_kernel, "manifest_attention", shape((NY, 2 * HD + 8, HD), BF), q_all, kv), "y")
    projected = call(
        join_kernel, "join_project", shape((32, 8, 4 * HD), BF), parts, own_all, w_a, w_b,
        scratch=[pltpu.VMEM((2 * HD, HD), F32)],
    )
    summed = call(sum_kernel, "head_sum", shape((32, 8, 4 * HD), BF), exchange(projected, SIDE), res)
    rows = exchange(summed, SIDE).reshape(16, 2, 8, 4 * HD)
    z = call(
        mlp_kernel, "gate_up", shape((CHIPS * ROWS, half), BF),
        rows, v_a.reshape(4 * HD, half), v_b.reshape(4 * HD, half),
    )
    joined = exchange(z.reshape(CHIPS, ROWS, half), PLANE).reshape(NY, NZ, ROWS, half)
    joined = joined.astype(F32).sum(0)
    gate = jnp.concatenate([joined[0], joined[1]], axis=1)
    up = jnp.concatenate([joined[2], joined[3]], axis=1)
    hidden = (jax.nn.silu(gate) * up).astype(BF)

    chip = lax.dynamic_slice_in_dim(rows, zl * HD, HD, 3)
    kept = chip[:, 0].reshape(CHIPS, 1, ROWS, HD)
    given = swap(chip[:, 1]).reshape(CHIPS, 1, ROWS, HD)
    first = jnp.where(core == 0, kept, given)
    second = jnp.where(core == 0, given, kept)
    resid_out = jnp.concatenate([first, second], axis=1).reshape(CHIPS * 2 * ROWS, HD)
    return (resid_out, hidden)


def solution(mesh):
    fine = Mesh(mesh.devices.reshape(8, 4, 2, 2, 4), ("y", "zl", "c", "zh", "x"))
    in_specs = (
        P(REQ, HEAD),
        P(None, REQ, HEAD),
        P(None, REQ, None, HEAD),
        P(None, REQ, None, HEAD),
        P(REQ, None),
        P(REQ),
        P(None, REQ),
        P(HEAD, REQ),
        P(REQ, HEAD),
        P(REQ, HEAD),
    )
    out_specs = (P(None, REQ), P(REQ, HEAD))
    return jax.shard_map(
        on_device, mesh=fine, in_specs=in_specs, out_specs=out_specs, check_vma=False
    )
```

time: 887 us -> 171 us (0.19)
  the two profiles are of different devices: /device:TPU:1 before, /device:TPU:8 now
where the time goes in v2:
time: 171 us; the launch traced here: 170 us
  waiting for transfers between devices  72.9 us (43%)
  starting transfers between devices  56.5 us (33%)
  blocking collectives  25.9 us (15%)
  Pallas kernels  7.49 us (4%)
  local copies, waits for them, and re-layouts  4.87 us (3%)
  other arithmetic  1.88 us (1%)
    all_to_all x8, waiting for transfers between devices, exchange(): return lax.all_to_all(x, axes, 0, 0, tiled=True)  70.3 us
    all_to_all x8, starting transfers between devices, exchange(): return lax.all_to_all(x, axes, 0, 0, tiled=True)  50.7 us
    all_to_all x2, blocking collectives, exchange(): return lax.all_to_all(x, axes, 0, 0, tiled=True)  23.7 us
    pallas_call x6, Pallas kernels, call(): pl.pallas_call(kernel, out_shape=out_shape, in_specs=specs or [VMEM] * le...  7.49 us
    ppermute x3, starting transfers between devices, swap(): return lax.ppermute(x, 'c', [(0, 1), (1, 0)])  5.75 us
  transfers between devices with their start and end apart: 11, of which 10 were waited for; matrix products, arithmetic and copies ran while one was open for 1% of the time, Pallas kernels for 4%

profile of v2, /device:TPU:8, one launch (start us, length us, event | category | flops | bytes accessed | tf_op | source)
XLA Modules:
  0.0 170.4 jit_solution(12071666059077156622)
XLA Ops:
  0.7 0.8 copy-done
  2.1 7.4 %all-to-all-start.6 = ((bf16[8,8,128]{2,1,0:T(8,128)(2,1)}), bf16[8,8,128]{2,1,0:T(8,128)(2,1)S(1)}, u32[]{:S(2)}, u32[]{:S(2)}) async-start(bf16[8,8,128]{2,1,0:T(8,128)(2,1)} %bitcast.6), calls=%async_computation.6 | async-start | bytes 32768 | tf_op jit(solution)/shard_map/all_to_all | solution.py:166
  10.1 5.0 %all-to-all-done.6 = bf16[8,8,128]{2,1,0:T(8,128)(2,1)S(1)} async-done(((bf16[8,8,128]{2,1,0:T(8,128)(2,1)}), bf16[8,8,128]{2,1,0:T(8,128)(2,1)S(1)}, u32[]{:S(2)}, u32[]{:S(2)}) %all-to-all-start.6) | async-done | bytes 16416 | tf_op jit(solution)/shard_map/all_to_all | solution.py:166
  15.1 7.9 %all-to-all-start = ((bf16[32,8,128]{2,1,0:T(8,128)(2,1)}), bf16[32,8,128]{2,1,0:T(8,128)(2,1)S(1)}, u32[]{:S(2)}, u32[]{:S(2)}) async-start(bf16[32,8,128]{2,1,0:T(8,128)(2,1)} %queries.1.q_ref), calls=%async_computation | async-start | bytes 131072 | tf_op jit(solution)/shard_map/all_to_all | solution.py:166
  23.7 1.2 copy-done.1
  24.9 1.4 own_attention.1
  26.4 6.1 %all-to-all-done.q_ref = bf16[32,8,128]{2,1,0:T(8,128)(2,1)S(1)} async-done(((bf16[32,8,128]{2,1,0:T(8,128)(2,1)}), bf16[32,8,128]{2,1,0:T(8,128)(2,1)S(1)}, u32[]{:S(2)}, u32[]{:S(2)}) %all-to-all-start) | async-done | bytes 65568 | tf_op jit(solution)/shard_map/all_to_all | solution.py:166
  32.5 14.2 %all_to_all.50.own_ref = bf16[32,16,128]{2,1,0:T(8,128)(2,1)S(1)} all-to-all(bf16[32,16,128]{2,1,0:T(8,128)(2,1)S(1)} %own_attention.1), channel_id=1, replica_groups=mesh['y'=8,'zl'=4,'c'=2,'zh'=2,'x'=4] {'y','zl'}, dimensions={0} | all-to-all | bytes 262144 | tf_op jit(solution)/shard_map/all_to_all | solution.py:166
  46.7 9.5 %all_to_all.51 = bf16[4,2,128,128]{3,2,1,0:T(8,128)(2,1)S(1)} all-to-all(bf16[4,2,128,128]{3,2,1,0:T(8,128)(2,1)S(1)} %broadcast_in_dim.8), channel_id=1, replica_groups=mesh['y'=8,'zl'=4,'c'=2,'zh'=2,'x'=4] {'zl'}, dimensions={0} | all-to-all | bytes 524288 | tf_op jit(solution)/shard_map/all_to_all | solution.py:166
  56.2 3.4 %all-to-all-start.4 = ((bf16[4,256,128]{2,1,0:T(8,128)(2,1)}), bf16[4,256,128]{2,1,0:T(8,128)(2,1)S(1)}, u32[]{:S(2)}, u32[]{:S(2)}) async-start(bf16[4,256,128]{2,1,0:T(8,128)(2,1)} %bitcast.2), calls=%async_computation.4 | async-start | bytes 524288 | tf_op jit(solution)/shard_map/all_to_all | solution.py:166
  59.6 2.2 %all_gather.3.kv_ref = bf16[8,2,128,128]{3,2,1,0:T(8,128)(2,1)S(1)} all-gather(bf16[4,2,128,128]{3,2,1,0:T(8,128)(2,1)S(1)} %all_to_all.51), channel_id=1, replica_groups=mesh['y'=8,'zl'=4,'c'=2,'zh'=2,'x'=4] {'c'}, dimensions={0}, use_global_device_ids=true | all-gather | bytes 786432 | tf_op jit(solution)/shard_map/all_gather | solution.py:177
  61.8 1.9 %manifest_attention.1 = bf16[8,264,128]{2,1,0:T(8,128)(2,1)} custom-call(bf16[32,8,128]{2,1,0:T(8,128)(2,1)S(1)} %all-to-all-done.q_ref, bf16[8,2,128,128]{3,2,1,0:T(8,128)(2,1)S(1)} %all_gather.3.kv_ref), custom_call_target="tpu_custom_call" | custom-call | tf_op jit(solution)/shard_map/manifest_attention/pallas_call | solution.py:34
  63.7 2.7 %all-to-all-done.4.w0_ref = bf16[4,256,128]{2,1,0:T(8,128)(2,1)S(1)} async-done(((bf16[4,256,128]{2,1,0:T(8,128)(2,1)}), bf16[4,256,128]{2,1,0:T(8,128)(2,1)S(1)}, u32[]{:S(2)}, u32[]{:S(2)}) %all-to-all-start.4) | async-done | bytes 262176 | tf_op jit(solution)/shard_map/all_to_all | solution.py:166
  66.4 4.7 %all-to-all-start.2 = ((bf16[8,264,128]{2,1,0:T(8,128)(2,1)}), bf16[8,264,128]{2,1,0:T(8,128)(2,1)S(1)}, u32[]{:S(2)}, u32[]{:S(2)}) async-start(bf16[8,264,128]{2,1,0:T(8,128)(2,1)} %manifest_attention.1), calls=%async_computation.2 | async-start | bytes 1081344 | tf_op jit(solution)/shard_map/all_to_all | solution.py:166
  71.2 1.1 pad_maximum_fusion
  72.3 13.3 %all-to-all-done.2.parts_ref = bf16[8,264,128]{2,1,0:T(8,128)(2,1)S(1)} async-done(((bf16[8,264,128]{2,1,0:T(8,128)(2,1)}), bf16[8,264,128]{2,1,0:T(8,128)(2,1)S(1)}, u32[]{:S(2)}, u32[]{:S(2)}) %all-to-all-start.2) | async-done | bytes 540704 | tf_op jit(solution)/shard_map/all_to_all | solution.py:166
  85.6 5.0 %all-to-all-start.8 = ((bf16[4,128,896]{2,1,0:T(8,128)(2,1)}), bf16[4,128,896]{2,1,0:T(8,128)(2,1)S(1)}, u32[]{:S(2)}, u32[]{:S(2)}) async-start(bf16[4,128,896]{2,1,0:T(8,128)(2,1)} %pad_maximum_fusion), calls=%async_computation.8 | async-start | bytes 1835008 | tf_op jit(solution)/shard_map/all_to_all | solution.py:166
  90.6 1.9 %collective-permute-start = (bf16[4,256,128]{2,1,0:T(8,128)(2,1)S(1)}, bf16[4,256,128]{2,1,0:T(8,128)(2,1)S(1)}, u32[]{:S(2)}, u32[]{:S(2)}) collective-permute-start(bf16[4,256,128]{2,1,0:T(8,128)(2,1)S(1)} %all-to-all-done.4.w0_ref), channel_id=1, source_target_pairs={{0,8},{8,0},{1,9},{9,1},{2,10},{10,2},{3,11},{11,3},{4,12},{12,4},... | collective-permute-start | bytes 786440 | tf_op jit(solution)/shard_map/ppermute | solution.py:162
  92.5 1.5 collective-permute-done.w1_ref
  94.0 2.3 %join_project.1 = bf16[32,8,512]{2,1,0:T(8,128)(2,1)} custom-call(bf16[8,264,128]{2,1,0:T(8,128)(2,1)S(1)} %all-to-all-done.2.parts_ref, bf16[32,16,128]{2,1,0:T(8,128)(2,1)S(1)} %all_to_all.50.own_ref, bf16[4,256,128]{2,1,0:T(8,128)(2,1)S(1)} %all-to-all-done.4.w0_ref, bf16[4,256,128]{2,1,0:T(8,128)(2,1)S(1)} %collective-permute-done.w1_ref), custom_call_target="tpu_custom_call" | custom-call | tf_op jit(solution)/shard_map/join_project/pallas_call | solution.py:34
  96.3 14.2 %all-to-all-done.8 = bf16[4,128,896]{2,1,0:T(8,128)(2,1)S(1)} async-done(((bf16[4,128,896]{2,1,0:T(8,128)(2,1)}), bf16[4,128,896]{2,1,0:T(8,128)(2,1)S(1)}, u32[]{:S(2)}, u32[]{:S(2)}) %all-to-all-start.8) | async-done | bytes 917536 | tf_op jit(solution)/shard_map/all_to_all | solution.py:166
  110.6 10.4 %all-to-all-start.5 = ((bf16[32,8,512]{2,1,0:T(8,128)(2,1)}), bf16[32,8,512]{2,1,0:T(8,128)(2,1)S(1)}, u32[]{:S(2)}, u32[]{:S(2)}) async-start(bf16[32,8,512]{2,1,0:T(8,128)(2,1)} %join_project.1), calls=%async_computation.5 | async-start | bytes 524288 | tf_op jit(solution)/shard_map/all_to_all | solution.py:166
  121.0 1.9 %collective-permute-start.2 = (bf16[4,128,896]{2,1,0:T(8,128)(2,1)S(1)}, bf16[4,128,896]{2,1,0:T(8,128)(2,1)S(1)}, u32[]{:S(2)}, u32[]{:S(2)}) collective-permute-start(bf16[4,128,896]{2,1,0:T(8,128)(2,1)S(1)} %all-to-all-done.8), channel_id=1, source_target_pairs={{0,8},{8,0},{1,9},{9,1},{2,10},{10,2},{3,11},{11,3},{4,12},{12,4},... | collective-permute-start | bytes 2752520 | tf_op jit(solution)/shard_map/ppermute | solution.py:162
  122.9 10.0 %all-to-all-done.5.parts_ref = bf16[32,8,512]{2,1,0:T(8,128)(2,1)S(1)} async-done(((bf16[32,8,512]{2,1,0:T(8,128)(2,1)}), bf16[32,8,512]{2,1,0:T(8,128)(2,1)S(1)}, u32[]{:S(2)}, u32[]{:S(2)}) %all-to-all-start.5) | async-done | bytes 262176 | tf_op jit(solution)/shard_map/all_to_all | solution.py:166
  133.0 0.8 head_sum.1
  133.7 3.9 %all-to-all-start.7 = ((bf16[32,8,512]{2,1,0:T(8,128)(2,1)}), bf16[32,8,512]{2,1,0:T(8,128)(2,1)S(1)}, u32[]{:S(2)}, u32[]{:S(2)}) async-start(bf16[32,8,512]{2,1,0:T(8,128)(2,1)} %head_sum.1), calls=%async_computation.7 | async-start | bytes 524288 | tf_op jit(solution)/shard_map/all_to_all | solution.py:166
  137.6 11.7 %all-to-all-done.7 = bf16[32,8,512]{2,1,0:T(8,128)(2,1)S(1)} async-done(((bf16[32,8,512]{2,1,0:T(8,128)(2,1)}), bf16[32,8,512]{2,1,0:T(8,128)(2,1)S(1)}, u32[]{:S(2)}, u32[]{:S(2)}) %all-to-all-start.7) | async-done | bytes 262176 | tf_op jit(solution)/shard_map/all_to_all | solution.py:166
  149.8 0.7 reshape.92
  150.6 8.0 %all-to-all-start.9 = ((bf16[32,4,896]{2,1,0:T(4,128)(2,1)}), bf16[32,4,896]{2,1,0:T(4,128)(2,1)S(1)}, u32[]{:S(2)}, u32[]{:S(2)}) async-start(bf16[32,4,896]{2,1,0:T(4,128)(2,1)} %reshape.92), calls=%async_computation.9 | async-start | bytes 458752 | tf_op jit(solution)/shard_map/all_to_all | solution.py:166
  158.7 1.9 %collective-permute-start.1 = (bf16[16,8,128]{2,1,0:T(8,128)(2,1)S(1)}, bf16[16,8,128]{2,1,0:T(8,128)(2,1)S(1)}, u32[]{:S(2)}, u32[]{:S(2)}) collective-permute-start(bf16[16,8,128]{2,1,0:T(8,128)(2,1)S(1)} %get-tuple-element.7), channel_id=1, source_target_pairs={{0,8},{8,0},{1,9},{9,1},{2,10},{10,2},{3,11},{11,3},{4,12},{12,4},... | collective-permute-start | bytes 98312 | tf_op jit(solution)/shard_map/ppermute | solution.py:162
  160.6 1.2 collective-permute-done.1
  162.5 7.1 %all-to-all-done.9 = bf16[32,4,896]{2,1,0:T(4,128)(2,1)S(1)} async-done(((bf16[32,4,896]{2,1,0:T(4,128)(2,1)}), bf16[32,4,896]{2,1,0:T(4,128)(2,1)S(1)}, u32[]{:S(2)}, u32[]{:S(2)}) %all-to-all-start.9) | async-done | bytes 229408 | tf_op jit(solution)/shard_map/all_to_all | solution.py:166
  (31 shorter events, 4.0 us)
Async XLA Ops:
  0.6 0.8 copy-start
  2.1 7.4 %copy-start.2 = (bf16[4,1024]{1,0:T(4,128)(2,1)S(1)}, bf16[4,1024]{1,0:T(4,128)(2,1)}, u32[]{:S(2)}) copy-start(bf16[4,1024]{1,0:T(4,128)(2,1)} %q_ref.1) | copy-start | bytes 24580
  2.1 13.1 %all-to-all-start.6 = ((bf16[8,8,128]{2,1,0:T(8,128)(2,1)}), bf16[8,8,128]{2,1,0:T(8,128)(2,1)S(1)}, u32[]{:S(2)}, u32[]{:S(2)}) async-start(bf16[8,8,128]{2,1,0:T(8,128)(2,1)} %bitcast.6), calls=%async_computation.6 | async-start | bytes 32768 | tf_op jit(solution)/shard_map/all_to_all | solution.py:166
  15.1 7.9 %copy-start.3 = (s32[4,8]{1,0:T(4,128)S(1)}, s32[4,8]{1,0:T(4,128)}, u32[]{:S(2)}) copy-start(s32[4,8]{1,0:T(4,128)} %pages_ref.1) | copy-start | bytes 388
  15.1 7.9 %copy-start.4 = (bf16[2,4,128]{2,1,0:T(4,128)(2,1)S(1)}, bf16[2,4,128]{2,1,0:T(4,128)(2,1)}, u32[]{:S(2)}) copy-start(bf16[2,4,128]{2,1,0:T(4,128)(2,1)} %new_ref.1) | copy-start | bytes 6148
  15.1 17.4 %all-to-all-start = ((bf16[32,8,128]{2,1,0:T(8,128)(2,1)}), bf16[32,8,128]{2,1,0:T(8,128)(2,1)S(1)}, u32[]{:S(2)}, u32[]{:S(2)}) async-start(bf16[32,8,128]{2,1,0:T(8,128)(2,1)} %queries.1.q_ref), calls=%async_computation | async-start | bytes 131072 | tf_op jit(solution)/shard_map/all_to_all | solution.py:166
  23.0 0.7 copy-start.5
  23.7 1.2 copy-start.1
  26.4 20.3 %copy-start.8 = (bf16[2,2,64,128]{3,2,1,0:T(8,128)(2,1)S(1)}, bf16[2,2,64,128]{3,2,1,0:T(8,128)(2,1)}, u32[]{:S(2)}) copy-start(bf16[2,2,64,128]{3,2,1,0:T(8,128)(2,1)} %param.13) | copy-start | bytes 196612
  56.2 10.2 %all-to-all-start.4 = ((bf16[4,256,128]{2,1,0:T(8,128)(2,1)}), bf16[4,256,128]{2,1,0:T(8,128)(2,1)S(1)}, u32[]{:S(2)}, u32[]{:S(2)}) async-start(bf16[4,256,128]{2,1,0:T(8,128)(2,1)} %bitcast.2), calls=%async_computation.4 | async-start | bytes 524288 | tf_op jit(solution)/shard_map/all_to_all | solution.py:166
  63.7 7.4 %copy-start.6 = (bf16[128,1792]{1,0:T(8,128)(2,1)S(1)}, bf16[128,1792]{1,0:T(8,128)(2,1)}, u32[]{:S(2)}) copy-start(bf16[128,1792]{1,0:T(8,128)(2,1)} %param.19) | copy-start | bytes 1376260
  63.7 7.4 %copy-start.7 = (bf16[128,1792]{1,0:T(8,128)(2,1)S(1)}, bf16[128,1792]{1,0:T(8,128)(2,1)}, u32[]{:S(2)}) copy-start(bf16[128,1792]{1,0:T(8,128)(2,1)} %param.18) | copy-start | bytes 1376260
  66.4 19.2 %all-to-all-start.2 = ((bf16[8,264,128]{2,1,0:T(8,128)(2,1)}), bf16[8,264,128]{2,1,0:T(8,128)(2,1)S(1)}, u32[]{:S(2)}, u32[]{:S(2)}) async-start(bf16[8,264,128]{2,1,0:T(8,128)(2,1)} %manifest_attention.1), calls=%async_computation.2 | async-start | bytes 1081344 | tf_op jit(solution)/shard_map/all_to_all | solution.py:166
  85.6 25.0 %all-to-all-start.8 = ((bf16[4,128,896]{2,1,0:T(8,128)(2,1)}), bf16[4,128,896]{2,1,0:T(8,128)(2,1)S(1)}, u32[]{:S(2)}, u32[]{:S(2)}) async-start(bf16[4,128,896]{2,1,0:T(8,128)(2,1)} %pad_maximum_fusion), calls=%async_computation.8 | async-start | bytes 1835008 | tf_op jit(solution)/shard_map/all_to_all | solution.py:166
  90.6 3.4 %collective-permute-start = (bf16[4,256,128]{2,1,0:T(8,128)(2,1)S(1)}, bf16[4,256,128]{2,1,0:T(8,128)(2,1)S(1)}, u32[]{:S(2)}, u32[]{:S(2)}) collective-permute-start(bf16[4,256,128]{2,1,0:T(8,128)(2,1)S(1)} %all-to-all-done.4.w0_ref), channel_id=1, source_target_pairs={{0,8},{8,0},{1,9},{9,1},{2,10},{10,2},{3,11},{11,3},{4,12},{12,4},... | collective-permute-start | bytes 786440 | tf_op jit(solution)/shard_map/ppermute | solution.py:162
  110.6 22.4 %all-to-all-start.5 = ((bf16[32,8,512]{2,1,0:T(8,128)(2,1)}), bf16[32,8,512]{2,1,0:T(8,128)(2,1)S(1)}, u32[]{:S(2)}, u32[]{:S(2)}) async-start(bf16[32,8,512]{2,1,0:T(8,128)(2,1)} %join_project.1), calls=%async_computation.5 | async-start | bytes 524288 | tf_op jit(solution)/shard_map/all_to_all | solution.py:166
  121.0 16.7 %collective-permute-start.2 = (bf16[4,128,896]{2,1,0:T(8,128)(2,1)S(1)}, bf16[4,128,896]{2,1,0:T(8,128)(2,1)S(1)}, u32[]{:S(2)}, u32[]{:S(2)}) collective-permute-start(bf16[4,128,896]{2,1,0:T(8,128)(2,1)S(1)} %all-to-all-done.8), channel_id=1, source_target_pairs={{0,8},{8,0},{1,9},{9,1},{2,10},{10,2},{3,11},{11,3},{4,12},{12,4},... | collective-permute-start | bytes 2752520 | tf_op jit(solution)/shard_map/ppermute | solution.py:162
  133.7 15.6 %all-to-all-start.7 = ((bf16[32,8,512]{2,1,0:T(8,128)(2,1)}), bf16[32,8,512]{2,1,0:T(8,128)(2,1)S(1)}, u32[]{:S(2)}, u32[]{:S(2)}) async-start(bf16[32,8,512]{2,1,0:T(8,128)(2,1)} %head_sum.1), calls=%async_computation.7 | async-start | bytes 524288 | tf_op jit(solution)/shard_map/all_to_all | solution.py:166
  150.6 19.0 %all-to-all-start.9 = ((bf16[32,4,896]{2,1,0:T(4,128)(2,1)}), bf16[32,4,896]{2,1,0:T(4,128)(2,1)S(1)}, u32[]{:S(2)}, u32[]{:S(2)}) async-start(bf16[32,4,896]{2,1,0:T(4,128)(2,1)} %reshape.92), calls=%async_computation.9 | async-start | bytes 458752 | tf_op jit(solution)/shard_map/all_to_all | solution.py:166
  158.7 3.1 %collective-permute-start.1 = (bf16[16,8,128]{2,1,0:T(8,128)(2,1)S(1)}, bf16[16,8,128]{2,1,0:T(8,128)(2,1)S(1)}, u32[]{:S(2)}, u32[]{:S(2)}) collective-permute-start(bf16[16,8,128]{2,1,0:T(8,128)(2,1)S(1)} %get-tuple-element.7), channel_id=1, source_target_pairs={{0,8},{8,0},{1,9},{9,1},{2,10},{10,2},{3,11},{11,3},{4,12},{12,4},... | collective-permute-start | bytes 98312 | tf_op jit(solution)/shard_map/ppermute | solution.py:162

commit v3 on v2

--- a/solution.py
+++ b/solution.py
@@ -52,7 +52,8 @@
             out_ref[y * NZ + z] = block
 
 
-def own_kernel(pages_ref, len_ref, q_ref, new_ref, own_ref, out_ref):
+def own_kernel(zl_ref, pages_ref, len_ref, q_ref, new_ref, own_ref, man_ref, *refs):
+    outs, (acc_ref, stats_ref) = refs[:NZ], refs[NZ:]
     tokens = POOL * PAGE
     q = q_ref[0:NZ].reshape(QROWS, HD)
     scores = dot(q, own_ref[0], 1, 1) * SCALE
@@ -68,8 +69,8 @@
         count = count + jnp.where(page_of == page[:, 0:1], 1.0, 0.0)
     new_k = by_request([new_ref[0, b : b + 1].astype(F32) for b in range(ROWS)])
     new_v = by_request([new_ref[1, b : b + 1].astype(F32) for b in range(ROWS)])
-    lane = lax.broadcasted_iota(jnp.int32, (8, HD), 1)
-    weights, news, stats = [], [], []
+    lane = lax.broadcasted_iota(jnp.int32, (8, HD), 1) % 32
+    weights, news = [], []
     for z in range(NZ):
         s = jnp.where(count > 0.0, scores[z * 8 : z * 8 + 8], -jnp.inf)
         s_new = jnp.sum(q_ref[z].astype(F32) * new_k, axis=1, keepdims=True) * SCALE
@@ -80,20 +81,30 @@
         high = total.astype(BF).astype(F32)
         weights.append(w.astype(BF))
         news.append(w_new.astype(BF).astype(F32) * new_v)
-        stats.append(jnp.where(lane == 0, top, jnp.where(lane == 1, high, jnp.where(lane == 2, total - high, 0.0))))
+        stats_ref[z * 8 : z * 8 + 8] = jnp.where(
+            lane == 0, top, jnp.where(lane == 1, high, jnp.where(lane == 2, total - high, 0.0))
+        )
     acc = dot(jnp.concatenate(weights, axis=0), own_ref[1], 1, 0)
-    for z in range(NZ):
-        block = jnp.concatenate([acc[z * 8 : z * 8 + 8] + news[z], stats[z]], axis=0).astype(BF)
-        for y in range(NY):
-            out_ref[y * NZ + z] = block
-
-
-def man_kernel(q_ref, kv_ref, out_ref):
+    acc_ref[...] = acc + jnp.concatenate(news, axis=0)
+    for s in range(NZ):
+        to = pl.ds(pl.multiple_of((zl_ref[0] + s) % NZ * 8, 8), 8)
+        outs[s][0 : 4 * PAGE] = man_ref[...]
+        outs[s][4 * PAGE :] = jnp.concatenate([acc_ref[to, :], stats_ref[to, :]], axis=0).astype(BF)
+
+
+def man_kernel(zl_ref, q_ref, kv_ref, p0_ref, p1_ref, p2_ref, p3_ref, out_ref, own_ref):
     n = 2 * NZ
     keys = jnp.concatenate([kv_ref[i, 0] for i in range(n)], axis=0)
     values = jnp.concatenate([kv_ref[i, 1] for i in range(n)], axis=0)
     row = lax.broadcasted_iota(jnp.int32, (8, HD), 0)
+    lane = lax.broadcasted_iota(jnp.int32, (8, HD), 1) // 32
     stats = jnp.zeros((8, HD), F32)
+    own_stats = jnp.zeros((8, HD), F32)
+    for s, p_ref in enumerate((p0_ref, p1_ref, p2_ref, p3_ref)):
+        source = (zl_ref[0] + NZ - s) % NZ
+        block = p_ref[4 * PAGE :].astype(F32)
+        own_ref[pl.ds(pl.multiple_of(source * 8, 8), 8), :] = block[0:8]
+        own_stats = jnp.where(lane == source, block[8:16], own_stats)
     accs = []
     for half in range(2):
         q = q_ref[half * 16 : half * 16 + 16].reshape(HD, HD)
@@ -105,12 +116,12 @@
         accs.append(dot(w.astype(BF), values, 0, 0))
         for k, value in enumerate((top, high, total - high)):
             stats = jnp.where(row == 3 * half + k, value, stats)
-    block = jnp.concatenate(accs + [stats], axis=0).astype(BF)
+    block = jnp.concatenate(accs + [stats, own_ref[...], own_stats], axis=0).astype(BF)
     for y in range(NY):
         out_ref[y] = block
 
 
-def join_kernel(parts_ref, own_ref, w0_ref, w1_ref, out_ref, rows_ref):
+def join_kernel(zl_ref, parts_ref, w0_ref, w1_ref, out_ref, rows_ref):
     rows = 2 * HD
     stats = parts_ref[:, rows : rows + 8, :].reshape(NY * 8, HD)
     eye = lax.broadcasted_iota(jnp.int32, (HD, HD), 0) == lax.broadcasted_iota(jnp.int32, (HD, HD), 1)
@@ -119,9 +130,13 @@
     kind = lax.broadcasted_iota(jnp.int32, (HD, n), 1) % 8
     for half in range(2):
         base = 3 * half
-        own = own_ref[half * 16 : half * 16 + 16].astype(F32)
-        own_acc = own[:, 0:8].reshape(HD, HD)
-        own_stats = own[:, 8:16].reshape(HD, HD)
+        own_acc, own_stats = [], []
+        for y in range(half * 4, half * 4 + 4):
+            own = parts_ref[y, rows + 8 : rows + 48].astype(F32)
+            own_acc.append(own[0:32])
+            own_stats += [own[32:40, z * 32 : z * 32 + 3] for z in range(NZ)]
+        own_acc = jnp.concatenate(own_acc, axis=0)
+        own_stats = jnp.concatenate(own_stats, axis=0)
         own_top = own_stats[:, 0:1]
         here = kind == base
         top = jnp.maximum(jnp.max(jnp.where(here, s, -jnp.inf), axis=1, keepdims=True), own_top)
@@ -136,26 +151,35 @@
         rows_ref[half * HD : (half + 1) * HD] = acc / total
     x = jnp.concatenate([rows_ref[pl.ds(h, HD, stride=2), :].astype(BF) for h in range(2)], axis=1)
     for k, w_ref in enumerate((w0_ref, w1_ref)):
-        w = jnp.concatenate([w_ref[z] for z in range(NZ)], axis=1)
+        w = jnp.concatenate([w_ref[(zl_ref[0] + NZ - z) % NZ, 0 : 2 * HD] for z in range(NZ)], axis=1)
         y = dot(x, w, 1, 0).astype(BF)
         for b in range(16):
             out_ref[b * 2 + k] = y[b * 8 : b * 8 + 8]
 
 
-def sum_kernel(parts_ref, res_ref, out_ref):
+def sum_kernel(place_ref, parts_ref, res0_ref, res1_ref, out_ref):
     total = parts_ref[0].astype(F32)
     for i in range(1, 32):
         total = total + parts_ref[i].astype(F32)
-    res = jnp.concatenate([res_ref[z] for z in range(NZ)], axis=1).astype(F32)
-    block = (res + total).astype(BF)
+    at = [(place_ref[0] + NZ - z) % NZ for z in range(NZ)]
+    res0 = jnp.concatenate([res0_ref[i, 2 * HD :] for i in at], axis=1).astype(F32)
+    res1 = jnp.concatenate([res1_ref[i, 2 * HD :] for i in at], axis=1).astype(F32)
+    block = (jnp.where(place_ref[1] == 0, res0, res1) + total).astype(BF)
     for i in range(32):
         out_ref[i] = block
 
 
-def mlp_kernel(r_ref, w0_ref, w1_ref, out_ref):
-    z = dot(r_ref[:, 0].reshape(HD, 4 * HD), w0_ref[...], 1, 0)
-    z = z + dot(r_ref[:, 1].reshape(HD, 4 * HD), w1_ref[...], 1, 0)
+def mlp_kernel(zl_ref, r_ref, w0_ref, w1_ref, out_ref):
+    at = [(zl_ref[0] + NZ - z) % NZ for z in range(NZ)]
+    z = dot(r_ref[:, 0].reshape(HD, 4 * HD), jnp.concatenate([w0_ref[i] for i in at], axis=0), 1, 0)
+    z = z + dot(r_ref[:, 1].reshape(HD, 4 * HD), jnp.concatenate([w1_ref[i] for i in at], axis=0), 1, 0)
     out_ref[...] = z.astype(BF)
+
+
+def shifted(pieces):
+    return [pieces[0]] + [
+        lax.ppermute(pieces[s], "zl", [(i, (i + s) % NZ) for i in range(NZ)]) for s in range(1, NZ)
+    ]
 
 
 def swap(x):
@@ -170,40 +194,47 @@
     shape = jax.ShapeDtypeStruct
     core, zl, zh, x = (lax.axis_index(a) for a in ("c", "zl", "zh", "x"))
     half = w_gate.shape[1] // 2
+    place = jnp.stack([zl, x % 2]).astype(jnp.int32)
 
     q_out = call(query_kernel, "queries", shape((CHIPS, 8, HD), BF), queries, scratch=[pltpu.VMEM((QROWS, HD), F32)])
     q_all = exchange(q_out, PLANE)
-    kv = exchange(jnp.broadcast_to(man_kv.reshape(1, 2, 2 * PAGE, HD), (NZ, 2, 2 * PAGE, HD)), "zl")
+    pieces = call(
+        own_kernel, "own_attention", [shape((4 * PAGE + 16, HD), BF)] * NZ,
+        place, pages, own_len, q_out, new_kv, own_kv.reshape(2, POOL * PAGE, HD), man_kv.reshape(4 * PAGE, HD),
+        specs=[SMEM, SMEM, SMEM, VMEM, VMEM, VMEM, VMEM], scratch=[pltpu.VMEM((QROWS, HD), F32)] * 2,
+    )
+    pieces = shifted(pieces)
+    kv = jnp.stack([p[: 4 * PAGE].reshape(2, 2 * PAGE, HD) for p in pieces])
     kv = lax.all_gather(kv, "c", axis=0, tiled=True)
-
-    own = call(
-        own_kernel, "own_attention", shape((CHIPS, 16, HD), BF),
-        pages, own_len, q_out, new_kv, own_kv.reshape(2, POOL * PAGE, HD),
-        specs=[SMEM, SMEM, VMEM, VMEM, VMEM],
-    )
-    own_all = exchange(own, PLANE)
-
-    w_a = exchange(w_out.reshape(NZ, 2 * HD, HD), "zl")
-    w_b = swap(w_a)
-    cut = jnp.stack([w_gate[:, :half], w_gate[:, half:], w_up[:, :half], w_up[:, half:]])
-    v_a = exchange(cut, "zl")
-    v_b = swap(v_a)
 
     res = resid.reshape(NZ, 4, 2, 2, ROWS, HD)
     res = lax.dynamic_index_in_dim(res, zh * 2 + x // 2, 1, keepdims=False)
-    res = exchange(res.transpose(0, 2, 1, 3, 4).reshape(2 * NZ, 8, HD), ("zl", "c"))
-    res = lax.dynamic_index_in_dim(res.reshape(NZ, 2, 8, HD), (core + x) % 2, 1, keepdims=False)
-
-    parts = exchange(call(man_kernel, "manifest_attention", shape((NY, 2 * HD + 8, HD), BF), q_all, kv), "y")
+    res = lax.dynamic_index_in_dim(res, (core + x) % 2, 2, keepdims=False).reshape(NZ, 8, HD)
+    w_cut = jnp.concatenate([w_out.reshape(NZ, 2 * HD, HD), res], axis=1)
+    w_cut, q_all = lax.optimization_barrier((w_cut, q_all))
+    at = [(zl + s) % NZ for s in range(NZ)]
+    w_a = jnp.stack(shifted([lax.dynamic_index_in_dim(w_cut, i, 0, keepdims=False) for i in at]))
+    w_b = swap(w_a)
+    (w_gate, w_up), kv = lax.optimization_barrier(((w_gate, w_up), kv))
+    v_cut = jnp.stack([w_gate[:, :half], w_gate[:, half:], w_up[:, :half], w_up[:, half:]])
+    v_a = jnp.stack(shifted([lax.dynamic_index_in_dim(v_cut, i, 0, keepdims=False) for i in at]))
+    v_b = swap(v_a)
+
+    man = call(
+        man_kernel, "manifest_attention", shape((NY, 2 * HD + 48, HD), BF), place, q_all, kv, *pieces,
+        specs=[SMEM] + [VMEM] * 6, scratch=[pltpu.VMEM((QROWS, HD), F32)],
+    )
     projected = call(
-        join_kernel, "join_project", shape((32, 8, 4 * HD), BF), parts, own_all, w_a, w_b,
-        scratch=[pltpu.VMEM((2 * HD, HD), F32)],
-    )
-    summed = call(sum_kernel, "head_sum", shape((32, 8, 4 * HD), BF), exchange(projected, SIDE), res)
+        join_kernel, "join_project", shape((32, 8, 4 * HD), BF), place, exchange(man, "y"), w_a, w_b,
+        specs=[SMEM] + [VMEM] * 3, scratch=[pltpu.VMEM((2 * HD, HD), F32)],
+    )
+    summed = call(
+        sum_kernel, "head_sum", shape((32, 8, 4 * HD), BF), place, exchange(projected, SIDE), w_a, w_b,
+        specs=[SMEM] + [VMEM] * 3,
+    )
     rows = exchange(summed, SIDE).reshape(16, 2, 8, 4 * HD)
     z = call(
-        mlp_kernel, "gate_up", shape((CHIPS * ROWS, half), BF),
-        rows, v_a.reshape(4 * HD, half), v_b.reshape(4 * HD, half),
+        mlp_kernel, "gate_up", shape((CHIPS * ROWS, half), BF), place, rows, v_a, v_b, specs=[SMEM] + [VMEM] * 3
     )
     joined = exchange(z.reshape(CHIPS, ROWS, half), PLANE).reshape(NY, NZ, ROWS, half)
     joined = joined.astype(F32).sum(0)

time: 171 us -> 141 us (0.82)
  waiting for transfers between devices: 72.9 us -> 41.4 us
  blocking collectives: 25.9 us -> 2.31 us
  starting transfers between devices: 56.5 us -> 78.1 us
  Pallas kernels: 7.49 us -> 9.79 us
    all_to_all x8 -> x5, waiting for transfers between devices: 70.3 us -> 31.7 us  [exchange(): return lax.all_to_all(x, axes, 0, 0, tiled=True)]
    ppermute x0 -> x9, starting transfers between devices: none -> 29.4 us  [shifted(): lax.ppermute(pieces[s], 'zl', [(i, (i + s) % NZ) for i in range(NZ)])]
    all_to_all x2 -> x0, blocking collectives: 23.7 us -> none  [exchange(): return lax.all_to_all(x, axes, 0, 0, tiled=True)]
    ppermute x0 -> x9, waiting for transfers between devices: none -> 8.51 us  [shifted(): lax.ppermute(pieces[s], 'zl', [(i, (i + s) % NZ) for i in range(NZ)])]
    all_to_all x8 -> x5, starting transfers between devices: 50.7 us -> 42.9 us  [exchange(): return lax.all_to_all(x, axes, 0, 0, tiled=True)]
    pallas_call x6, Pallas kernels: 7.49 us -> 9.79 us  [call(): pl.pallas_call(kernel, out_shape=out_shape, in_specs=specs or [VMEM] * le...]
    unnamed x18 -> x28, local copies, waits for them, and re-layouts: 2.7 us -> 3.91 us
  transfers between devices with their start and end apart: 11 -> 17, of which waited for: 10 -> 8; matrix products, arithmetic and copies ran while one was open for 1% -> 1% of each run, Pallas kernels for 4% -> 4%
where the time goes in v3:
time: 141 us; the launch traced here: 140 us
  starting transfers between devices  78.1 us (55%)
  waiting for transfers between devices  41.4 us (29%)
  Pallas kernels  9.79 us (7%)
  local copies, waits for them, and re-layouts  6.4 us (5%)
  blocking collectives  2.31 us (2%)
    all_to_all x5, starting transfers between devices, exchange(): return lax.all_to_all(x, axes, 0, 0, tiled=True)  42.9 us
    all_to_all x5, waiting for transfers between devices, exchange(): return lax.all_to_all(x, axes, 0, 0, tiled=True)  31.7 us
    ppermute x9, starting transfers between devices, shifted(): lax.ppermute(pieces[s], 'zl', [(i, (i + s) % NZ) for i in range(NZ)])  29.4 us
    pallas_call x6, Pallas kernels, call(): pl.pallas_call(kernel, out_shape=out_shape, in_specs=specs or [VMEM] * le...  9.79 us
    ppermute x9, waiting for transfers between devices, shifted(): lax.ppermute(pieces[s], 'zl', [(i, (i + s) % NZ) for i in range(NZ)])  8.51 us
    ppermute x3, starting transfers between devices, swap(): return lax.ppermute(x, 'c', [(0, 1), (1, 0)])  5.76 us
    unnamed x28, local copies, waits for them, and re-layouts  3.91 us
  transfers between devices with their start and end apart: 17, of which 8 were waited for; matrix products, arithmetic and copies ran while one was open for 1% of the time, Pallas kernels for 4%

profile of v3, /device:TPU:8, one launch (start us, length us, event | category | flops | bytes accessed | tf_op | source)
XLA Modules:
  0.0 140.3 jit_solution(11882497350736650090)
XLA Ops:
  2.0 13.3 %all-to-all-start = ((bf16[32,8,128]{2,1,0:T(8,128)(2,1)}), bf16[32,8,128]{2,1,0:T(8,128)(2,1)S(1)}, u32[]{:S(2)}, u32[]{:S(2)}) async-start(bf16[32,8,128]{2,1,0:T(8,128)(2,1)} %queries.1.q_ref), calls=%async_computation | async-start | bytes 131072 | tf_op jit(solution)/shard_map/all_to_all | solution.py:190
  16.1 1.2 copy-done.1
  17.3 1.5 %own_attention.1 = (bf16[272,128]{1,0:T(8,128)(2,1)S(1)}, bf16[272,128]{1,0:T(8,128)(2,1)S(1)}, bf16[272,128]{1,0:T(8,128)(2,1)S(1)}, bf16[272,128]{1,0:T(8,128)(2,1)S(1)}) custom-call(s32[2]{0:T(128)S(1)} %pad_add_fusion.zl_ref.place_ref, s32[4,8]{1,0:T(4,128)S(1)} %copy-done.8, s32[4]{0:T(128)S(1)} %copy-done.10, bf16[32,8,128]{2,1,0:T(8,128)(2,1)} %queries.1.q_ref, ...), custom_call_target="tpu_custom_call" | custom-call | tf_op jit(solution)/shard_map/own_attention/pallas_call | solution.py:34
  18.8 3.4 %collective-permute-start = (bf16[272,128]{1,0:T(8,128)(2,1)S(1)}, bf16[272,128]{1,0:T(8,128)(2,1)S(1)}, u32[]{:S(2)}, u32[]{:S(2)}) collective-permute-start(bf16[272,128]{1,0:T(8,128)(2,1)S(1)} %get-tuple-element.13), channel_id=1, source_target_pairs={{0,16},{16,32},{32,48},{48,0},{1,17},{17,33},{33,49},{49,1},{2,18}... | collective-permute-start | bytes 208904 | tf_op jit(solution)/shard_map/ppermute | solution.py:181
  22.2 4.3 %collective-permute-start.1 = (bf16[272,128]{1,0:T(8,128)(2,1)S(1)}, bf16[272,128]{1,0:T(8,128)(2,1)S(1)}, u32[]{:S(2)}, u32[]{:S(2)}) collective-permute-start(bf16[272,128]{1,0:T(8,128)(2,1)S(1)} %get-tuple-element.14), channel_id=1, source_target_pairs={{0,32},{16,48},{32,0},{48,16},{1,33},{17,49},{33,1},{49,17},{2,34}... | collective-permute-start | bytes 208904 | tf_op jit(solution)/shard_map/ppermute | solution.py:181
  26.4 3.4 %collective-permute-start.2 = (bf16[272,128]{1,0:T(8,128)(2,1)S(1)}, bf16[272,128]{1,0:T(8,128)(2,1)S(1)}, u32[]{:S(2)}, u32[]{:S(2)}) collective-permute-start(bf16[272,128]{1,0:T(8,128)(2,1)S(1)} %get-tuple-element.15), channel_id=1, source_target_pairs={{0,48},{16,0},{32,16},{48,32},{1,49},{17,1},{33,17},{49,33},{2,50}... | collective-permute-start | bytes 208904 | tf_op jit(solution)/shard_map/ppermute | solution.py:181
  31.2 1.4 %collective-permute-done.2.p3_ref = bf16[272,128]{1,0:T(8,128)(2,1)S(1)} collective-permute-done((bf16[272,128]{1,0:T(8,128)(2,1)S(1)}, bf16[272,128]{1,0:T(8,128)(2,1)S(1)}, u32[]{:S(2)}, u32[]{:S(2)}) %collective-permute-start.2) | collective-permute-done | bytes 69664 | tf_op jit(solution)/shard_map/ppermute | solution.py:181
  33.5 2.3 %all_gather.3.kv_ref = bf16[8,2,128,128]{3,2,1,0:T(8,128)(2,1)S(1)} all-gather(bf16[4,2,128,128]{3,2,1,0:T(8,128)(2,1)S(1)} %pad_maximum_fusion.4), channel_id=1, replica_groups=mesh['y'=8,'zl'=4,'c'=2,'zh'=2,'x'=4] {'c'}, dimensions={0}, use_global_device_ids=true | all-gather | bytes 786432 | tf_op jit(solution)/shard_map/all_gather | solution.py:208
  35.9 2.5 %manifest_attention.1 = bf16[8,304,128]{2,1,0:T(8,128)(2,1)} custom-call(s32[2]{0:T(128)S(1)} %pad_add_fusion.zl_ref.place_ref, bf16[32,8,128]{2,1,0:T(8,128)(2,1)S(1)} %all-to-all-done.q_ref, bf16[8,2,128,128]{3,2,1,0:T(8,128)(2,1)S(1)} %all_gather.3.kv_ref, bf16[272,128]{1,0:T(8,128)(2,1)S(1)} %get-tuple-element.12.p0_ref, bf16[272,128]{1,0:T(8,128)(2,1)S(1)} %copy-done.3, ...), custom_call_target="tpu_custom_call" | custom-call | tf_op jit(solution)/shard_map/manifest_attention/pallas_call | solution.py:34
  38.3 7.3 %all-to-all-start.1 = ((bf16[8,304,128]{2,1,0:T(8,128)(2,1)}), bf16[8,304,128]{2,1,0:T(8,128)(2,1)S(1)}, u32[]{:S(2)}, u32[]{:S(2)}) async-start(bf16[8,304,128]{2,1,0:T(8,128)(2,1)} %manifest_attention.1), calls=%async_computation.1 | async-start | bytes 1245184 | tf_op jit(solution)/shard_map/all_to_all | solution.py:190
  45.8 5.2 %collective-permute-start.5 = (bf16[264,128]{1,0:T(8,128)(2,1)S(1)}, bf16[264,128]{1,0:T(8,128)(2,1)S(1)}, u32[]{:S(2)}, u32[]{:S(2)}) collective-permute-start(bf16[264,128]{1,0:T(8,128)(2,1)S(1)} %get-tuple-element.29), channel_id=1, source_target_pairs={{0,48},{16,0},{32,16},{48,32},{1,49},{17,1},{33,17},{49,33},{2,50}... | collective-permute-start | bytes 202760 | tf_op jit(solution)/shard_map/ppermute | solution.py:181
  51.0 1.9 %collective-permute-start.4 = (bf16[264,128]{1,0:T(8,128)(2,1)S(1)}, bf16[264,128]{1,0:T(8,128)(2,1)S(1)}, u32[]{:S(2)}, u32[]{:S(2)}) collective-permute-start(bf16[264,128]{1,0:T(8,128)(2,1)S(1)} %get-tuple-element.30), channel_id=1, source_target_pairs={{0,32},{16,48},{32,0},{48,16},{1,33},{17,49},{33,1},{49,17},{2,34}... | collective-permute-start | bytes 202760 | tf_op jit(solution)/shard_map/ppermute | solution.py:181
  52.9 2.5 %collective-permute-start.3 = (bf16[264,128]{1,0:T(8,128)(2,1)S(1)}, bf16[264,128]{1,0:T(8,128)(2,1)S(1)}, u32[]{:S(2)}, u32[]{:S(2)}) collective-permute-start(bf16[264,128]{1,0:T(8,128)(2,1)S(1)} %get-tuple-element.31), channel_id=1, source_target_pairs={{0,16},{16,32},{32,48},{48,0},{1,17},{17,33},{33,49},{49,1},{2,18}... | collective-permute-start | bytes 202760 | tf_op jit(solution)/shard_map/ppermute | solution.py:181
  55.6 2.5 %collective-permute-done.4 = bf16[264,128]{1,0:T(8,128)(2,1)S(1)} collective-permute-done((bf16[264,128]{1,0:T(8,128)(2,1)S(1)}, bf16[264,128]{1,0:T(8,128)(2,1)S(1)}, u32[]{:S(2)}, u32[]{:S(2)}) %collective-permute-start.4) | collective-permute-done | bytes 67616 | tf_op jit(solution)/shard_map/ppermute | solution.py:181
  58.1 2.8 %collective-permute-done.3 = bf16[264,128]{1,0:T(8,128)(2,1)S(1)} collective-permute-done((bf16[264,128]{1,0:T(8,128)(2,1)S(1)}, bf16[264,128]{1,0:T(8,128)(2,1)S(1)}, u32[]{:S(2)}, u32[]{:S(2)}) %collective-permute-start.3) | collective-permute-done | bytes 67616 | tf_op jit(solution)/shard_map/ppermute | solution.py:181
  60.9 1.9 %collective-permute-start.6 = (bf16[4,264,128]{2,1,0:T(8,128)(2,1)S(1)}, bf16[4,264,128]{2,1,0:T(8,128)(2,1)S(1)}, u32[]{:S(2)}, u32[]{:S(2)}) collective-permute-start(bf16[4,264,128]{2,1,0:T(8,128)(2,1)S(1)} %pad_maximum_fusion.3.w0_ref.res0_ref), channel_id=1, source_target_pairs={{0,8},{8,0},{1,9},{9,1},{2,10},{10,2},{3,11},{11,3},{4,12},{12,4},... | collective-permute-start | bytes 811016 | tf_op jit(solution)/shard_map/ppermute | solution.py:186
  63.0 2.5 %collective-permute-start.10 = (bf16[128,896]{1,0:T(8,128)(2,1)S(1)}, bf16[128,896]{1,0:T(8,128)(2,1)S(1)}, u32[]{:S(2)}, u32[]{:S(2)}) collective-permute-start(bf16[128,896]{1,0:T(8,128)(2,1)S(1)} %get-tuple-element.21), channel_id=1, source_target_pairs={{0,48},{16,0},{32,16},{48,32},{1,49},{17,1},{33,17},{49,33},{2,50}... | collective-permute-start | bytes 688136 | tf_op jit(solution)/shard_map/ppermute | solution.py:181
  65.4 2.5 %collective-permute-start.9 = (bf16[128,896]{1,0:T(8,128)(2,1)S(1)}, bf16[128,896]{1,0:T(8,128)(2,1)S(1)}, u32[]{:S(2)}, u32[]{:S(2)}) collective-permute-start(bf16[128,896]{1,0:T(8,128)(2,1)S(1)} %get-tuple-element.22), channel_id=1, source_target_pairs={{0,32},{16,48},{32,0},{48,16},{1,33},{17,49},{33,1},{49,17},{2,34}... | collective-permute-start | bytes 688136 | tf_op jit(solution)/shard_map/ppermute | solution.py:181
  67.9 3.9 %collective-permute-start.8 = (bf16[128,896]{1,0:T(8,128)(2,1)S(1)}, bf16[128,896]{1,0:T(8,128)(2,1)S(1)}, u32[]{:S(2)}, u32[]{:S(2)}) collective-permute-start(bf16[128,896]{1,0:T(8,128)(2,1)S(1)} %get-tuple-element.23), channel_id=1, source_target_pairs={{0,16},{16,32},{32,48},{48,0},{1,17},{17,33},{33,49},{49,1},{2,18}... | collective-permute-start | bytes 688136 | tf_op jit(solution)/shard_map/ppermute | solution.py:181
  71.9 2.9 %join_project.1 = bf16[32,8,512]{2,1,0:T(8,128)(2,1)} custom-call(s32[2]{0:T(128)S(1)} %pad_add_fusion.zl_ref.place_ref, bf16[8,304,128]{2,1,0:T(8,128)(2,1)S(1)} %all-to-all-done.1.parts_ref, bf16[4,264,128]{2,1,0:T(8,128)(2,1)S(1)} %pad_maximum_fusion.3.w0_ref.res0_ref, bf16[4,264,128]{2,1,0:T(8,128)(2,1)S(1)} %collective-permute-done.6.w1_ref.res1_ref), custom_call_target="tpu_custom_call" | custom-call | tf_op jit(solution)/shard_map/join_project/pallas_call | solution.py:34
  74.8 10.4 %all-to-all-start.2 = ((bf16[32,8,512]{2,1,0:T(8,128)(2,1)}), bf16[32,8,512]{2,1,0:T(8,128)(2,1)S(1)}, u32[]{:S(2)}, u32[]{:S(2)}) async-start(bf16[32,8,512]{2,1,0:T(8,128)(2,1)} %join_project.1), calls=%async_computation.2 | async-start | bytes 524288 | tf_op jit(solution)/shard_map/all_to_all | solution.py:190
  85.2 1.7 %collective-permute-done.9 = bf16[128,896]{1,0:T(8,128)(2,1)S(1)} collective-permute-done((bf16[128,896]{1,0:T(8,128)(2,1)S(1)}, bf16[128,896]{1,0:T(8,128)(2,1)S(1)}, u32[]{:S(2)}, u32[]{:S(2)}) %collective-permute-start.9) | collective-permute-done | bytes 229408 | tf_op jit(solution)/shard_map/ppermute | solution.py:181
  87.1 1.9 %collective-permute-start.11 = (bf16[4,128,896]{2,1,0:T(8,128)(2,1)S(1)}, bf16[4,128,896]{2,1,0:T(8,128)(2,1)S(1)}, u32[]{:S(2)}, u32[]{:S(2)}) collective-permute-start(bf16[4,128,896]{2,1,0:T(8,128)(2,1)S(1)} %pad_maximum_fusion.1.w0_ref), channel_id=1, source_target_pairs={{0,8},{8,0},{1,9},{9,1},{2,10},{10,2},{3,11},{11,3},{4,12},{12,4},... | collective-permute-start | bytes 2752520 | tf_op jit(solution)/shard_map/ppermute | solution.py:186
  89.1 11.1 %all-to-all-done.2.parts_ref = bf16[32,8,512]{2,1,0:T(8,128)(2,1)S(1)} async-done(((bf16[32,8,512]{2,1,0:T(8,128)(2,1)}), bf16[32,8,512]{2,1,0:T(8,128)(2,1)S(1)}, u32[]{:S(2)}, u32[]{:S(2)}) %all-to-all-start.2) | async-done | bytes 262176 | tf_op jit(solution)/shard_map/all_to_all | solution.py:190
  100.1 1.3 head_sum.1
  101.4 3.9 %all-to-all-start.3 = ((bf16[32,8,512]{2,1,0:T(8,128)(2,1)}), bf16[32,8,512]{2,1,0:T(8,128)(2,1)S(1)}, u32[]{:S(2)}, u32[]{:S(2)}) async-start(bf16[32,8,512]{2,1,0:T(8,128)(2,1)} %head_sum.1), calls=%async_computation.3 | async-start | bytes 524288 | tf_op jit(solution)/shard_map/all_to_all | solution.py:190
  105.3 13.6 %all-to-all-done.3 = bf16[32,8,512]{2,1,0:T(8,128)(2,1)S(1)} async-done(((bf16[32,8,512]{2,1,0:T(8,128)(2,1)}), bf16[32,8,512]{2,1,0:T(8,128)(2,1)S(1)}, u32[]{:S(2)}, u32[]{:S(2)}) %all-to-all-start.3) | async-done | bytes 262176 | tf_op jit(solution)/shard_map/all_to_all | solution.py:190
  118.9 1.0 gate_up.1
  120.7 8.0 %all-to-all-start.4 = ((bf16[32,4,896]{2,1,0:T(4,128)(2,1)}), bf16[32,4,896]{2,1,0:T(4,128)(2,1)S(1)}, u32[]{:S(2)}, u32[]{:S(2)}) async-start(bf16[32,4,896]{2,1,0:T(4,128)(2,1)} %reshape.85), calls=%async_computation.4 | async-start | bytes 458752 | tf_op jit(solution)/shard_map/all_to_all | solution.py:190
  128.7 1.9 %collective-permute-start.7 = (bf16[16,8,128]{2,1,0:T(8,128)(2,1)S(1)}, bf16[16,8,128]{2,1,0:T(8,128)(2,1)S(1)}, u32[]{:S(2)}, u32[]{:S(2)}) collective-permute-start(bf16[16,8,128]{2,1,0:T(8,128)(2,1)S(1)} %get-tuple-element.33), channel_id=1, source_target_pairs={{0,8},{8,0},{1,9},{9,1},{2,10},{10,2},{3,11},{11,3},{4,12},{12,4},... | collective-permute-start | bytes 98312 | tf_op jit(solution)/shard_map/ppermute | solution.py:186
  130.6 1.2 collective-permute-done.7
  132.5 7.1 %all-to-all-done.4 = bf16[32,4,896]{2,1,0:T(4,128)(2,1)S(1)} async-done(((bf16[32,4,896]{2,1,0:T(4,128)(2,1)}), bf16[32,4,896]{2,1,0:T(4,128)(2,1)S(1)}, u32[]{:S(2)}, u32[]{:S(2)}) %all-to-all-start.4) | async-done | bytes 229408 | tf_op jit(solution)/shard_map/all_to_all | solution.py:190
  (61 shorter events, 7.1 us)
Async XLA Ops:
  0.6 29.2 %copy-start = (bf16[256,128]{1,0:T(8,128)(2,1)S(1)}, bf16[256,128]{1,0:T(8,128)(2,1)}, u32[]{:S(2)}) copy-start(bf16[256,128]{1,0:T(8,128)(2,1)} %param.16) | copy-start | bytes 196612
  0.6 0.7 copy-start.7
  2.0 13.4 %copy-start.6 = (bf16[2,2,64,128]{3,2,1,0:T(8,128)(2,1)S(1)}, bf16[2,2,64,128]{3,2,1,0:T(8,128)(2,1)}, u32[]{:S(2)}) copy-start(bf16[2,2,64,128]{3,2,1,0:T(8,128)(2,1)} %param.13) | copy-start | bytes 196612
  2.0 33.8 %all-to-all-start = ((bf16[32,8,128]{2,1,0:T(8,128)(2,1)}), bf16[32,8,128]{2,1,0:T(8,128)(2,1)S(1)}, u32[]{:S(2)}, u32[]{:S(2)}) async-start(bf16[32,8,128]{2,1,0:T(8,128)(2,1)} %queries.1.q_ref), calls=%async_computation | async-start | bytes 131072 | tf_op jit(solution)/shard_map/all_to_all | solution.py:190
  15.3 0.7 copy-start.9
  15.4 0.7 copy-start.8
  15.4 0.7 copy-start.10
  16.1 1.2 copy-start.1
  17.3 12.6 %copy-start.13 = (bf16[1024,128]{1,0:T(8,128)(2,1)S(1)}, bf16[1024,128]{1,0:T(8,128)(2,1)}, u32[]{:S(2)}) copy-start(bf16[1024,128]{1,0:T(8,128)(2,1)} %param.17) | copy-start | bytes 786436
  18.8 11.2 %collective-permute-start = (bf16[272,128]{1,0:T(8,128)(2,1)S(1)}, bf16[272,128]{1,0:T(8,128)(2,1)S(1)}, u32[]{:S(2)}, u32[]{:S(2)}) collective-permute-start(bf16[272,128]{1,0:T(8,128)(2,1)S(1)} %get-tuple-element.13), channel_id=1, source_target_pairs={{0,16},{16,32},{32,48},{48,0},{1,17},{17,33},{33,49},{49,1},{2,18}... | collective-permute-start | bytes 208904 | tf_op jit(solution)/shard_map/ppermute | solution.py:181
  22.2 8.4 %collective-permute-start.1 = (bf16[272,128]{1,0:T(8,128)(2,1)S(1)}, bf16[272,128]{1,0:T(8,128)(2,1)S(1)}, u32[]{:S(2)}, u32[]{:S(2)}) collective-permute-start(bf16[272,128]{1,0:T(8,128)(2,1)S(1)} %get-tuple-element.14), channel_id=1, source_target_pairs={{0,32},{16,48},{32,0},{48,16},{1,33},{17,49},{33,1},{49,17},{2,34}... | collective-permute-start | bytes 208904 | tf_op jit(solution)/shard_map/ppermute | solution.py:181
  26.4 6.2 %collective-permute-start.2 = (bf16[272,128]{1,0:T(8,128)(2,1)S(1)}, bf16[272,128]{1,0:T(8,128)(2,1)S(1)}, u32[]{:S(2)}, u32[]{:S(2)}) collective-permute-start(bf16[272,128]{1,0:T(8,128)(2,1)S(1)} %get-tuple-element.15), channel_id=1, source_target_pairs={{0,48},{16,0},{32,16},{48,32},{1,49},{17,1},{33,17},{49,33},{2,50}... | collective-permute-start | bytes 208904 | tf_op jit(solution)/shard_map/ppermute | solution.py:181
  30.0 0.6 copy-start.2
  31.2 1.4 %slice-start = ((bf16[272,128]{1,0:T(8,128)(2,1)}), bf16[256,128]{1,0:T(8,128)(2,1)S(1)}, s32[]{:S(2)}) async-start(bf16[272,128]{1,0:T(8,128)(2,1)} %copy-done.2), calls=%async_computation.5 | async-start | bytes 131072 | tf_op jit(solution)/shard_map/slice | solution.py:207
  32.6 0.8 slice-start.1
  33.5 2.3 %copy-start.3 = (bf16[272,128]{1,0:T(8,128)(2,1)S(1)}, bf16[272,128]{1,0:T(8,128)(2,1)}, u32[]{:S(2)}) copy-start(bf16[272,128]{1,0:T(8,128)(2,1)} %copy-done.2) | copy-start | bytes 208900
  33.5 2.3 %copy-start.5 = (bf16[272,128]{1,0:T(8,128)(2,1)S(1)}, bf16[272,128]{1,0:T(8,128)(2,1)}, u32[]{:S(2)}) copy-start(bf16[272,128]{1,0:T(8,128)(2,1)} %copy-done.4) | copy-start | bytes 208900
  38.3 7.4 %copy-start.11 = (bf16[128,1792]{1,0:T(8,128)(2,1)S(1)}, bf16[128,1792]{1,0:T(8,128)(2,1)}, u32[]{:S(2)}) copy-start(bf16[128,1792]{1,0:T(8,128)(2,1)} %param.19) | copy-start | bytes 1376260
  38.3 7.4 %copy-start.12 = (bf16[128,1792]{1,0:T(8,128)(2,1)S(1)}, bf16[128,1792]{1,0:T(8,128)(2,1)}, u32[]{:S(2)}) copy-start(bf16[128,1792]{1,0:T(8,128)(2,1)} %param.18) | copy-start | bytes 1376260
  38.3 33.5 %all-to-all-start.1 = ((bf16[8,304,128]{2,1,0:T(8,128)(2,1)}), bf16[8,304,128]{2,1,0:T(8,128)(2,1)S(1)}, u32[]{:S(2)}, u32[]{:S(2)}) async-start(bf16[8,304,128]{2,1,0:T(8,128)(2,1)} %manifest_attention.1), calls=%async_computation.1 | async-start | bytes 1245184 | tf_op jit(solution)/shard_map/all_to_all | solution.py:190
  45.8 9.7 %collective-permute-start.5 = (bf16[264,128]{1,0:T(8,128)(2,1)S(1)}, bf16[264,128]{1,0:T(8,128)(2,1)S(1)}, u32[]{:S(2)}, u32[]{:S(2)}) collective-permute-start(bf16[264,128]{1,0:T(8,128)(2,1)S(1)} %get-tuple-element.29), channel_id=1, source_target_pairs={{0,48},{16,0},{32,16},{48,32},{1,49},{17,1},{33,17},{49,33},{2,50}... | collective-permute-start | bytes 202760 | tf_op jit(solution)/shard_map/ppermute | solution.py:181
  51.0 7.1 %collective-permute-start.4 = (bf16[264,128]{1,0:T(8,128)(2,1)S(1)}, bf16[264,128]{1,0:T(8,128)(2,1)S(1)}, u32[]{:S(2)}, u32[]{:S(2)}) collective-permute-start(bf16[264,128]{1,0:T(8,128)(2,1)S(1)} %get-tuple-element.30), channel_id=1, source_target_pairs={{0,32},{16,48},{32,0},{48,16},{1,33},{17,49},{33,1},{49,17},{2,34}... | collective-permute-start | bytes 202760 | tf_op jit(solution)/shard_map/ppermute | solution.py:181
  52.9 8.0 %collective-permute-start.3 = (bf16[264,128]{1,0:T(8,128)(2,1)S(1)}, bf16[264,128]{1,0:T(8,128)(2,1)S(1)}, u32[]{:S(2)}, u32[]{:S(2)}) collective-permute-start(bf16[264,128]{1,0:T(8,128)(2,1)S(1)} %get-tuple-element.31), channel_id=1, source_target_pairs={{0,16},{16,32},{32,48},{48,0},{1,17},{17,33},{33,49},{49,1},{2,18}... | collective-permute-start | bytes 202760 | tf_op jit(solution)/shard_map/ppermute | solution.py:181
  60.9 10.9 %collective-permute-start.6 = (bf16[4,264,128]{2,1,0:T(8,128)(2,1)S(1)}, bf16[4,264,128]{2,1,0:T(8,128)(2,1)S(1)}, u32[]{:S(2)}, u32[]{:S(2)}) collective-permute-start(bf16[4,264,128]{2,1,0:T(8,128)(2,1)S(1)} %pad_maximum_fusion.3.w0_ref.res0_ref), channel_id=1, source_target_pairs={{0,8},{8,0},{1,9},{9,1},{2,10},{10,2},{3,11},{11,3},{4,12},{12,4},... | collective-permute-start | bytes 811016 | tf_op jit(solution)/shard_map/ppermute | solution.py:186
  63.0 22.3 %collective-permute-start.10 = (bf16[128,896]{1,0:T(8,128)(2,1)S(1)}, bf16[128,896]{1,0:T(8,128)(2,1)S(1)}, u32[]{:S(2)}, u32[]{:S(2)}) collective-permute-start(bf16[128,896]{1,0:T(8,128)(2,1)S(1)} %get-tuple-element.21), channel_id=1, source_target_pairs={{0,48},{16,0},{32,16},{48,32},{1,49},{17,1},{33,17},{49,33},{2,50}... | collective-permute-start | bytes 688136 | tf_op jit(solution)/shard_map/ppermute | solution.py:181
  65.4 21.5 %collective-permute-start.9 = (bf16[128,896]{1,0:T(8,128)(2,1)S(1)}, bf16[128,896]{1,0:T(8,128)(2,1)S(1)}, u32[]{:S(2)}, u32[]{:S(2)}) collective-permute-start(bf16[128,896]{1,0:T(8,128)(2,1)S(1)} %get-tuple-element.22), channel_id=1, source_target_pairs={{0,32},{16,48},{32,0},{48,16},{1,33},{17,49},{33,1},{49,17},{2,34}... | collective-permute-start | bytes 688136 | tf_op jit(solution)/shard_map/ppermute | solution.py:181
  67.9 19.1 %collective-permute-start.8 = (bf16[128,896]{1,0:T(8,128)(2,1)S(1)}, bf16[128,896]{1,0:T(8,128)(2,1)S(1)}, u32[]{:S(2)}, u32[]{:S(2)}) collective-permute-start(bf16[128,896]{1,0:T(8,128)(2,1)S(1)} %get-tuple-element.23), channel_id=1, source_target_pairs={{0,16},{16,32},{32,48},{48,0},{1,17},{17,33},{33,49},{49,1},{2,18}... | collective-permute-start | bytes 688136 | tf_op jit(solution)/shard_map/ppermute | solution.py:181
  74.8 25.3 %all-to-all-start.2 = ((bf16[32,8,512]{2,1,0:T(8,128)(2,1)}), bf16[32,8,512]{2,1,0:T(8,128)(2,1)S(1)}, u32[]{:S(2)}, u32[]{:S(2)}) async-start(bf16[32,8,512]{2,1,0:T(8,128)(2,1)} %join_project.1), calls=%async_computation.2 | async-start | bytes 524288 | tf_op jit(solution)/shard_map/all_to_all | solution.py:190
  87.1 18.1 %collective-permute-start.11 = (bf16[4,128,896]{2,1,0:T(8,128)(2,1)S(1)}, bf16[4,128,896]{2,1,0:T(8,128)(2,1)S(1)}, u32[]{:S(2)}, u32[]{:S(2)}) collective-permute-start(bf16[4,128,896]{2,1,0:T(8,128)(2,1)S(1)} %pad_maximum_fusion.1.w0_ref), channel_id=1, source_target_pairs={{0,8},{8,0},{1,9},{9,1},{2,10},{10,2},{3,11},{11,3},{4,12},{12,4},... | collective-permute-start | bytes 2752520 | tf_op jit(solution)/shard_map/ppermute | solution.py:186
  101.4 17.5 %all-to-all-start.3 = ((bf16[32,8,512]{2,1,0:T(8,128)(2,1)}), bf16[32,8,512]{2,1,0:T(8,128)(2,1)S(1)}, u32[]{:S(2)}, u32[]{:S(2)}) async-start(bf16[32,8,512]{2,1,0:T(8,128)(2,1)} %head_sum.1), calls=%async_computation.3 | async-start | bytes 524288 | tf_op jit(solution)/shard_map/all_to_all | solution.py:190
  120.7 18.9 %all-to-all-start.4 = ((bf16[32,4,896]{2,1,0:T(4,128)(2,1)}), bf16[32,4,896]{2,1,0:T(4,128)(2,1)S(1)}, u32[]{:S(2)}, u32[]{:S(2)}) async-start(bf16[32,4,896]{2,1,0:T(4,128)(2,1)} %reshape.85), calls=%async_computation.4 | async-start | bytes 458752 | tf_op jit(solution)/shard_map/all_to_all | solution.py:190
  128.7 3.1 %collective-permute-start.7 = (bf16[16,8,128]{2,1,0:T(8,128)(2,1)S(1)}, bf16[16,8,128]{2,1,0:T(8,128)(2,1)S(1)}, u32[]{:S(2)}, u32[]{:S(2)}) collective-permute-start(bf16[16,8,128]{2,1,0:T(8,128)(2,1)S(1)} %get-tuple-element.33), channel_id=1, source_target_pairs={{0,8},{8,0},{1,9},{9,1},{2,10},{10,2},{3,11},{11,3},{4,12},{12,4},... | collective-permute-start | bytes 98312 | tf_op jit(solution)/shard_map/ppermute | solution.py:186
  (1 other events, 0.6 us)

commit v4 on v1

--- a/solution.py
+++ b/solution.py
@@ -13,11 +13,13 @@
 QROWS = ROWS * GROUP
 POOL = 32
 CHIPS = 32
+PEERS = 16
 STATS = 8
 SCALE = HD**-0.5
-PLANE = ("y", "zl")
+PLANE = ("y", "zq", "p")
+SPARSE = ("y", "zq")
 HEAD = ("zh", "x")
-REQ = ("y", "zl", "c")
+REQ = ("y", "zq", "p", "c")
 BF = jnp.bfloat16
 F32 = jnp.float32
 
@@ -66,10 +68,10 @@
 
 
 def man_kernel(q_ref, kv_ref, out_ref):
-    keys = jnp.concatenate([kv_ref[0, 0], kv_ref[1, 0]], axis=0)
-    values = jnp.concatenate([kv_ref[0, 1], kv_ref[1, 1]], axis=0)
+    keys = jnp.concatenate([kv_ref[i, 0] for i in range(4)], axis=0)
+    values = jnp.concatenate([kv_ref[i, 1] for i in range(4)], axis=0)
     row = lax.broadcasted_iota(jnp.int32, (STATS, HD), 0)
-    for chunk in range(CHIPS * QROWS // HD):
+    for chunk in range(PEERS * QROWS // HD):
         s = dot(keys, q_ref[chunk * HD : (chunk + 1) * HD], 1, 1) * SCALE
         top = jnp.max(s, axis=0, keepdims=True).astype(BF).astype(F32)
         w = jnp.exp(s - top)
@@ -88,7 +90,7 @@
     vmem = pl.BlockSpec(memory_space=pltpu.VMEM)
     return pl.pallas_call(
         man_kernel,
-        out_shape=jax.ShapeDtypeStruct((CHIPS, QROWS + STATS, HD), BF),
+        out_shape=jax.ShapeDtypeStruct((PEERS, QROWS + STATS, HD), BF),
         in_specs=[vmem, vmem],
         out_specs=vmem,
         compiler_params=pltpu.CompilerParams(vmem_limit_bytes=32 << 20),
@@ -97,12 +99,12 @@
 
 
 def join_kernel(place_ref, parts_ref, acc_ref, top_ref, total_ref, out_ref, rows_ref):
-    stats = parts_ref[:, QROWS : QROWS + STATS, :].reshape(CHIPS * STATS, HD)
+    stats = parts_ref[:, QROWS : QROWS + STATS, :].reshape(PEERS * STATS, HD)
     lane = lax.broadcasted_iota(jnp.int32, (QROWS, HD), 1)
     row = lax.broadcasted_iota(jnp.int32, (QROWS, HD), 0)
     pick = jnp.where(lane == row + place_ref[0] * QROWS, 1.0, 0.0).astype(BF)
     s = dot(pick, stats, 1, 1)
-    n = CHIPS * STATS
+    n = PEERS * STATS
     kind = lax.broadcasted_iota(jnp.int32, (QROWS, n), 1) % STATS
     totals = pltpu.roll(s, n - 1, 1) + pltpu.roll(s, n - 2, 1)
     own_top = top_ref[:, 0:1]
@@ -111,11 +113,13 @@
     own_factor = jnp.exp(own_top - top)
     total = jnp.sum(factor * totals, axis=1, keepdims=True) + own_factor * total_ref[:, 0:1]
     acc = own_factor * acc_ref[...]
-    for i in range(CHIPS):
+    for i in range(PEERS):
         acc = acc + factor[:, i * STATS : i * STATS + 1] * parts_ref[i, 0:QROWS].astype(F32)
     rows_ref[...] = acc / total
     for h in range(GROUP):
-        out_ref[:, h * HD : (h + 1) * HD] = rows_ref[pl.ds(h, ROWS, stride=GROUP), :].astype(BF)
+        rows = rows_ref[pl.ds(h, ROWS, stride=GROUP), :].astype(BF)
+        for i in range(CHIPS):
+            out_ref[i, :, h * HD : (h + 1) * HD] = rows
 
 
 def join_part(place, parts, acc, top, total):
@@ -123,7 +127,7 @@
     vmem = pl.BlockSpec(memory_space=pltpu.VMEM)
     return pl.pallas_call(
         join_kernel,
-        out_shape=jax.ShapeDtypeStruct((ROWS, GROUP * HD), BF),
+        out_shape=jax.ShapeDtypeStruct((CHIPS, ROWS, GROUP * HD), BF),
         in_specs=[smem, vmem, vmem, vmem, vmem],
         out_specs=vmem,
         scratch_shapes=[pltpu.VMEM((QROWS, HD), F32)],
@@ -136,41 +140,46 @@
     return lax.ppermute(x, "c", [(0, 1), (1, 0)])
 
 
-def spread(x, axes, n):
-    return lax.all_to_all(jnp.broadcast_to(x[None], (n, *x.shape)), axes, 0, 0, tiled=True)
+def pair(x):
+    return lax.ppermute(x, "p", [(0, 1), (1, 0)])
+
+
+def exchange(x, axes):
+    return lax.all_to_all(x, axes, 0, 0, tiled=True)
 
 
 def on_device(queries, new_kv, own_kv, man_kv, pages, own_len, resid, w_out, w_gate, w_up):
-    core = lax.axis_index("c")
+    core, side = lax.axis_index("c"), lax.axis_index("p")
     width = w_gate.shape[1]
     q = queries.reshape(QROWS, HD)
-    kv = lax.all_gather(man_kv.reshape(2, 2 * PAGE, HD), "c", axis=0)
+    kv = man_kv.reshape(2, 2 * PAGE, HD)
+    kv = lax.all_gather(jnp.stack([kv, pair(kv)]), "c", axis=0, tiled=True)
     w_out2 = jnp.concatenate([w_out, swap(w_out)], axis=1)
-    w_gate2 = jnp.concatenate([w_gate, swap(w_gate)], axis=0)
-    w_up2 = jnp.concatenate([w_up, swap(w_up)], axis=0)
+    w_keep = jnp.where(side == 0, w_gate, w_up)
+    w_pair = pair(jnp.where(side == 0, w_up, w_gate))
+    w_keep2 = jnp.concatenate([w_keep, swap(w_keep)], axis=0)
     res = resid.reshape(CHIPS, 2, ROWS, HD)
     mine = jnp.where(core == 0, res[:, 0], res[:, 1])
     theirs = swap(jnp.where(core == 0, res[:, 1], res[:, 0]))
     res2 = jnp.concatenate([mine, theirs], axis=-1).reshape(CHIPS * ROWS, 2 * HD)
 
     acc, top, total = own_part(pages, own_len, q, new_kv, own_kv.reshape(2, POOL * PAGE, HD))
-    q_all = spread(q, PLANE, CHIPS).reshape(CHIPS * QROWS, HD)
-    parts = lax.all_to_all(man_part(q_all, kv), PLANE, 0, 0, tiled=True)
-    place = lax.axis_index("zl").astype(jnp.int32).reshape(1)
-    attn = join_part(place, parts, acc, top, total)
-    attn_all = spread(attn, PLANE, CHIPS).reshape(CHIPS * ROWS, GROUP * HD)
-
-    partial_out = jnp.dot(attn_all, w_out2, preferred_element_type=F32).astype(BF)
-    summed = spread(partial_out, HEAD, 8).astype(F32).sum(0)
-    out2 = (res2.astype(F32) + summed).astype(BF)
-
-    gate_part = jnp.dot(out2, w_gate2, preferred_element_type=F32).astype(BF)
-    up_part = jnp.dot(out2, w_up2, preferred_element_type=F32).astype(BF)
-    both = jnp.concatenate(
-        [gate_part.reshape(CHIPS, ROWS, width), up_part.reshape(CHIPS, ROWS, width)], axis=1
-    )
-    joined = lax.all_to_all(both, PLANE, 0, 0, tiled=True).astype(F32).sum(0)
-    hidden = (jax.nn.silu(joined[:ROWS]) * joined[ROWS:]).astype(BF)
+    q_all = exchange(jnp.broadcast_to(q[None], (PEERS, QROWS, HD)), SPARSE).reshape(PEERS * QROWS, HD)
+    parts = exchange(man_part(q_all, kv), SPARSE)
+    place = (lax.axis_index(SPARSE) % 4).astype(jnp.int32).reshape(1)
+    attn = exchange(join_part(place, parts, acc, top, total), PLANE).reshape(CHIPS * ROWS, GROUP * HD)
+    attn, w_pair = lax.optimization_barrier((attn, w_pair))
+    w_pair2 = jnp.concatenate([w_pair, swap(w_pair)], axis=0)
+
+    partial_out = jnp.dot(attn, w_out2, preferred_element_type=F32).astype(BF)
+    heads = exchange(jnp.broadcast_to(partial_out[None], (8, *partial_out.shape)), HEAD)
+    out2 = (res2.astype(F32) + heads.astype(F32).sum(0)).astype(BF)
+
+    z = jnp.dot(out2, w_keep2, preferred_element_type=F32)
+    z = (z + jnp.dot(pair(out2), w_pair2, preferred_element_type=F32)).astype(BF)
+    joined = exchange(z.reshape(CHIPS, ROWS, width), PLANE).reshape(PEERS, 2, ROWS, width)
+    joined = joined.astype(F32).sum(0)
+    hidden = (jax.nn.silu(joined[0]) * joined[1]).astype(BF)
 
     kept = out2[:, :HD].reshape(CHIPS, 1, ROWS, HD)
     given = swap(out2[:, HD:]).reshape(CHIPS, 1, ROWS, HD)
@@ -181,7 +190,7 @@
 
 
 def solution(mesh):
-    fine = Mesh(mesh.devices.reshape(8, 4, 2, 2, 4), ("y", "zl", "c", "zh", "x"))
+    fine = Mesh(mesh.devices.reshape(8, 2, 2, 2, 2, 4), ("y", "zq", "p", "c", "zh", "x"))
     in_specs = (
         P(REQ, HEAD),
         P(None, REQ, HEAD),

time: 126 us -> 124 us (0.984)
  the two profiles are of different devices: /device:TPU:16 before, /device:TPU:8 now
where the time goes in v4:
time: 124 us; the launch traced here: 123 us
  starting transfers between devices  62.8 us (51%)
  waiting for transfers between devices  46.6 us (38%)
  Pallas kernels  4.25 us (3%)
  local copies, waits for them, and re-layouts  3.9 us (3%)
  blocking collectives  1.99 us (2%)
  other arithmetic  1.95 us (2%)
    all_to_all x5, starting transfers between devices, exchange(): return lax.all_to_all(x, axes, 0, 0, tiled=True)  40.7 us
    all_to_all x5, waiting for transfers between devices, exchange(): return lax.all_to_all(x, axes, 0, 0, tiled=True)  39.7 us
    ppermute x3, starting transfers between devices, pair(): return lax.ppermute(x, 'p', [(0, 1), (1, 0)])  12 us
    ppermute x5, starting transfers between devices, swap(): return lax.ppermute(x, 'c', [(0, 1), (1, 0)])  10.1 us
    ppermute x3, waiting for transfers between devices, pair(): return lax.ppermute(x, 'p', [(0, 1), (1, 0)])  5.75 us
  transfers between devices with their start and end apart: 13, of which 8 were waited for; matrix products, arithmetic and copies ran while one was open for 3% of the time, Pallas kernels for 1%

profile of v4, /device:TPU:8, one launch (start us, length us, event | category | flops | bytes accessed | tf_op | source)
XLA Modules:
  0.0 123.3 jit_solution(11996045413535579387)
XLA Ops:
  0.7 4.4 %collective-permute-start.1 = (bf16[2,128,128]{2,1,0:T(8,128)(2,1)}, bf16[2,128,128]{2,1,0:T(8,128)(2,1)S(1)}, u32[]{:S(2)}, u32[]{:S(2)}) collective-permute-start(bf16[2,128,128]{2,1,0:T(8,128)(2,1)} %bitcast.50), channel_id=1, source_target_pairs={{0,16},{16,0},{1,17},{17,1},{2,18},{18,2},{3,19},{19,3},{4,20},{20... | collective-permute-start | bytes 196616 | tf_op jit(solution)/shard_map/ppermute | solution.py:144
  5.1 0.7 broadcast_in_dim.6.q_ref
  5.8 0.7 broadcast_in_dim.14
  6.5 11.2 %all-to-all-start = ((bf16[16,32,128]{2,1,0:T(8,128)(2,1)}), bf16[16,32,128]{2,1,0:T(8,128)(2,1)S(1)}, u32[]{:S(2)}, u32[]{:S(2)}) async-start(bf16[16,32,128]{2,1,0:T(8,128)(2,1)} %broadcast_in_dim.14), calls=%async_computation | async-start | bytes 262144 | tf_op jit(solution)/shard_map/all_to_all | solution.py:148
  17.6 0.9 pad_maximum_fusion
  18.5 2.0 %all_gather.3.kv_ref = bf16[4,2,128,128]{3,2,1,0:T(8,128)(2,1)S(1)} all-gather(bf16[2,2,128,128]{3,2,1,0:T(8,128)(2,1)S(1)} %pad_maximum_fusion), channel_id=1, replica_groups=mesh['y'=8,'zq'=2,'p'=2,'c'=2,'zh'=2,'x'=4] {'c'}, dimensions={0}, use_global_device_ids=true | all-gather | bytes 393216 | tf_op jit(solution)/shard_map/all_gather | solution.py:156
  20.5 6.1 %all-to-all-done = bf16[16,32,128]{2,1,0:T(8,128)(2,1)S(1)} async-done(((bf16[16,32,128]{2,1,0:T(8,128)(2,1)}), bf16[16,32,128]{2,1,0:T(8,128)(2,1)S(1)}, u32[]{:S(2)}, u32[]{:S(2)}) %all-to-all-start) | async-done | bytes 131104 | tf_op jit(solution)/shard_map/all_to_all | solution.py:148
  26.6 1.6 %manifest_attention.1 = bf16[16,40,128]{2,1,0:T(8,128)(2,1)} custom-call(bf16[512,128]{1,0:T(8,128)(2,1)S(1)} %bitcast.44, bf16[4,2,128,128]{3,2,1,0:T(8,128)(2,1)S(1)} %all_gather.3.kv_ref), custom_call_target="tpu_custom_call" | custom-call | tf_op jit(solution)/shard_map/manifest_attention/pallas_call | solution.py:91
  28.3 4.9 %all-to-all-start.1 = ((bf16[16,40,128]{2,1,0:T(8,128)(2,1)}), bf16[16,40,128]{2,1,0:T(8,128)(2,1)S(1)}, u32[]{:S(2)}, u32[]{:S(2)}) async-start(bf16[16,40,128]{2,1,0:T(8,128)(2,1)} %manifest_attention.1), calls=%async_computation.1 | async-start | bytes 327680 | tf_op jit(solution)/shard_map/all_to_all | solution.py:148
  33.3 1.2 own_attention.1
  34.5 8.2 %all-to-all-done.1.parts_ref = bf16[16,40,128]{2,1,0:T(8,128)(2,1)S(1)} async-done(((bf16[16,40,128]{2,1,0:T(8,128)(2,1)}), bf16[16,40,128]{2,1,0:T(8,128)(2,1)S(1)}, u32[]{:S(2)}, u32[]{:S(2)}) %all-to-all-start.1) | async-done | bytes 163872 | tf_op jit(solution)/shard_map/all_to_all | solution.py:148
  42.7 1.4 %join_attention.1 = bf16[32,4,1024]{2,1,0:T(4,128)(2,1)} custom-call(s32[1]{0:T(128)} %bitcast.3.place_ref, bf16[16,40,128]{2,1,0:T(8,128)(2,1)S(1)} %all-to-all-done.1.parts_ref, f32[32,128]{1,0:T(8,128)S(1)} %get-tuple-element.7.acc_ref, f32[32,128]{1,0:T(8,128)S(1)} %get-tuple-element.8.top_ref, f32[32,128]{1,0:T(8,128)S(1)} %get-tuple-element.9.total_ref), custom_call_target="tpu_custom_call" | custom-call | tf_op jit(solution)/shard_map/join_attention/pallas_call | solution.py:128
  44.1 5.1 %all-to-all-start.2 = ((bf16[32,4,1024]{2,1,0:T(4,128)(2,1)}), bf16[32,4,1024]{2,1,0:T(4,128)(2,1)S(1)}, u32[]{:S(2)}, u32[]{:S(2)}) async-start(bf16[32,4,1024]{2,1,0:T(4,128)(2,1)} %join_attention.1), calls=%async_computation.2 | async-start | bytes 524288 | tf_op jit(solution)/shard_map/all_to_all | solution.py:148
  49.3 3.4 %collective-permute-start.2 = (bf16[128,1792]{1,0:T(8,128)(2,1)S(1)}, bf16[128,1792]{1,0:T(8,128)(2,1)S(1)}, u32[]{:S(2)}, u32[]{:S(2)}) collective-permute-start(bf16[128,1792]{1,0:T(8,128)(2,1)S(1)} %get-tuple-element.13), channel_id=1, source_target_pairs={{0,16},{16,0},{1,17},{17,1},{2,18},{18,2},{3,19},{19,3},{4,20},{20... | collective-permute-start | bytes 1376264 | tf_op jit(solution)/shard_map/ppermute | solution.py:144
  52.7 1.9 %collective-permute-start.3 = (bf16[1024,128]{1,0:T(8,128)(2,1)S(1)}, bf16[1024,128]{1,0:T(8,128)(2,1)S(1)}, u32[]{:S(2)}, u32[]{:S(2)}) collective-permute-start(bf16[1024,128]{1,0:T(8,128)(2,1)S(1)} %copy-done.7), channel_id=1, source_target_pairs={{0,8},{8,0},{1,9},{9,1},{2,10},{10,2},{3,11},{11,3},{4,12},{12,4},... | collective-permute-start | bytes 786440 | tf_op jit(solution)/shard_map/ppermute | solution.py:140
  54.6 5.8 %all-to-all-done.2 = bf16[32,4,1024]{2,1,0:T(4,128)(2,1)S(1)} async-done(((bf16[32,4,1024]{2,1,0:T(4,128)(2,1)}), bf16[32,4,1024]{2,1,0:T(4,128)(2,1)S(1)}, u32[]{:S(2)}, u32[]{:S(2)}) %all-to-all-start.2) | async-done | bytes 262176 | tf_op jit(solution)/shard_map/all_to_all | solution.py:148
  60.5 3.5 %collective-permute-done.2 = bf16[128,1792]{1,0:T(8,128)(2,1)S(1)} collective-permute-done((bf16[128,1792]{1,0:T(8,128)(2,1)S(1)}, bf16[128,1792]{1,0:T(8,128)(2,1)S(1)}, u32[]{:S(2)}, u32[]{:S(2)}) %collective-permute-start.2) | collective-permute-done | bytes 458784 | tf_op jit(solution)/shard_map/ppermute | solution.py:144
  64.3 0.8 broadcast_in_dim.15
  65.1 10.1 %all-to-all-start.3 = ((bf16[8,128,256]{2,1,0:T(8,128)(2,1)}), bf16[8,128,256]{2,1,0:T(8,128)(2,1)S(1)}, u32[]{:S(2)}, u32[]{:S(2)}) async-start(bf16[8,128,256]{2,1,0:T(8,128)(2,1)} %broadcast_in_dim.15), calls=%async_computation.3 | async-start | bytes 1048576 | tf_op jit(solution)/shard_map/all_to_all | solution.py:148
  75.3 1.9 %collective-permute-start = (bf16[32,4,128]{2,1,0:T(4,128)(2,1)S(1)}, bf16[32,4,128]{2,1,0:T(4,128)(2,1)S(1)}, u32[]{:S(2)}, u32[]{:S(2)}) collective-permute-start(bf16[32,4,128]{2,1,0:T(4,128)(2,1)S(1)} %get-tuple-element.17), channel_id=1, source_target_pairs={{0,8},{8,0},{1,9},{9,1},{2,10},{10,2},{3,11},{11,3},{4,12},{12,4},... | collective-permute-start | bytes 98312 | tf_op jit(solution)/shard_map/ppermute | solution.py:140
  77.2 2.4 %collective-permute-start.5 = (bf16[128,1792]{1,0:T(8,128)(2,1)S(1)}, bf16[128,1792]{1,0:T(8,128)(2,1)S(1)}, u32[]{:S(2)}, u32[]{:S(2)}) collective-permute-start(bf16[128,1792]{1,0:T(8,128)(2,1)S(1)} %get-tuple-element.12), channel_id=1, source_target_pairs={{0,8},{8,0},{1,9},{9,1},{2,10},{10,2},{3,11},{11,3},{4,12},{12,4},... | collective-permute-start | bytes 1376264 | tf_op jit(solution)/shard_map/ppermute | solution.py:140
  79.6 1.9 %collective-permute-start.7 = (bf16[128,1792]{1,0:T(8,128)(2,1)S(1)}, bf16[128,1792]{1,0:T(8,128)(2,1)S(1)}, u32[]{:S(2)}, u32[]{:S(2)}) collective-permute-start(bf16[128,1792]{1,0:T(8,128)(2,1)S(1)} %collective-permute-done.2), channel_id=1, source_target_pairs={{0,8},{8,0},{1,9},{9,1},{2,10},{10,2},{3,11},{11,3},{4,12},{12,4},... | collective-permute-start | bytes 1376264 | tf_op jit(solution)/shard_map/ppermute | solution.py:140
  81.7 9.2 %all-to-all-done.3 = bf16[8,128,256]{2,1,0:T(8,128)(2,1)S(1)} async-done(((bf16[8,128,256]{2,1,0:T(8,128)(2,1)}), bf16[8,128,256]{2,1,0:T(8,128)(2,1)S(1)}, u32[]{:S(2)}, u32[]{:S(2)}) %all-to-all-start.3) | async-done | bytes 524320 | tf_op jit(solution)/shard_map/all_to_all | solution.py:148
  91.0 4.2 %collective-permute-start.6 = (bf16[128,256]{1,0:T(8,128)(2,1)S(1)}, bf16[128,256]{1,0:T(8,128)(2,1)S(1)}, u32[]{:S(2)}, u32[]{:S(2)}) collective-permute-start(bf16[128,256]{1,0:T(8,128)(2,1)S(1)} %add_convert_fusion), channel_id=1, source_target_pairs={{0,16},{16,0},{1,17},{17,1},{2,18},{18,2},{3,19},{19,3},{4,20},{20... | collective-permute-start | bytes 196616 | tf_op jit(solution)/shard_map/ppermute | solution.py:144
  95.2 2.2 %collective-permute-done.6 = bf16[128,256]{1,0:T(8,128)(2,1)S(1)} collective-permute-done((bf16[128,256]{1,0:T(8,128)(2,1)S(1)}, bf16[128,256]{1,0:T(8,128)(2,1)S(1)}, u32[]{:S(2)}, u32[]{:S(2)}) %collective-permute-start.6) | collective-permute-done | bytes 65568 | tf_op jit(solution)/shard_map/ppermute | solution.py:144
  98.1 0.9 reshape.94
  98.9 9.4 %all-to-all-start.4 = ((bf16[32,4,1792]{2,1,0:T(4,128)(2,1)}), bf16[32,4,1792]{2,1,0:T(4,128)(2,1)S(1)}, u32[]{:S(2)}, u32[]{:S(2)}) async-start(bf16[32,4,1792]{2,1,0:T(4,128)(2,1)} %reshape.94), calls=%async_computation.4 | async-start | bytes 917504 | tf_op jit(solution)/shard_map/all_to_all | solution.py:148
  108.4 1.9 %collective-permute-start.4 = (bf16[128,128]{1,0:T(8,128)(2,1)S(1)}, bf16[128,128]{1,0:T(8,128)(2,1)S(1)}, u32[]{:S(2)}, u32[]{:S(2)}) collective-permute-start(bf16[128,128]{1,0:T(8,128)(2,1)S(1)} %slice.29), channel_id=1, source_target_pairs={{0,8},{8,0},{1,9},{9,1},{2,10},{10,2},{3,11},{11,3},{4,12},{12,4},... | collective-permute-start | bytes 98312 | tf_op jit(solution)/shard_map/ppermute | solution.py:140
  110.3 1.2 collective-permute-done.4
  111.5 0.7 copy.22
  112.2 10.3 %all-to-all-done.4 = bf16[32,4,1792]{2,1,0:T(4,128)(2,1)S(1)} async-done(((bf16[32,4,1792]{2,1,0:T(4,128)(2,1)}), bf16[32,4,1792]{2,1,0:T(4,128)(2,1)S(1)}, u32[]{:S(2)}, u32[]{:S(2)}) %all-to-all-start.4) | async-done | bytes 458784 | tf_op jit(solution)/shard_map/all_to_all | solution.py:148
  122.7 0.6 fusion.12
  (35 shorter events, 1.5 us)
Async XLA Ops:
  0.6 32.6 %copy-start = (bf16[2,32,64,128]{3,2,1,0:T(8,128)(2,1)S(1)}, bf16[2,32,64,128]{3,2,1,0:T(8,128)(2,1)}, u32[]{:S(2)}) copy-start(bf16[2,32,64,128]{3,2,1,0:T(8,128)(2,1)} %param.12) | copy-start | bytes 3145732
  0.6 32.6 %copy-start.2 = (bf16[2,4,128]{2,1,0:T(4,128)(2,1)S(1)}, bf16[2,4,128]{2,1,0:T(4,128)(2,1)}, u32[]{:S(2)}) copy-start(bf16[2,4,128]{2,1,0:T(4,128)(2,1)} %new_ref.1) | copy-start | bytes 6148
  0.7 32.6 %copy-start.1 = (s32[4,8]{1,0:T(4,128)S(1)}, s32[4,8]{1,0:T(4,128)}, u32[]{:S(2)}) copy-start(s32[4,8]{1,0:T(4,128)} %pages_ref.1) | copy-start | bytes 388
  0.7 32.6 %copy-start.3 = (s32[4]{0:T(128)S(1)}, s32[4]{0:T(128)}, u32[]{:S(2)}) copy-start(s32[4]{0:T(128)} %len_ref.1) | copy-start | bytes 52
  0.7 17.0 %collective-permute-start.1 = (bf16[2,128,128]{2,1,0:T(8,128)(2,1)}, bf16[2,128,128]{2,1,0:T(8,128)(2,1)S(1)}, u32[]{:S(2)}, u32[]{:S(2)}) collective-permute-start(bf16[2,128,128]{2,1,0:T(8,128)(2,1)} %bitcast.50), channel_id=1, source_target_pairs={{0,16},{16,0},{1,17},{17,1},{2,18},{18,2},{3,19},{19,3},{4,20},{20... | collective-permute-start | bytes 196616 | tf_op jit(solution)/shard_map/ppermute | solution.py:144
  6.5 20.2 %all-to-all-start = ((bf16[16,32,128]{2,1,0:T(8,128)(2,1)}), bf16[16,32,128]{2,1,0:T(8,128)(2,1)S(1)}, u32[]{:S(2)}, u32[]{:S(2)}) async-start(bf16[16,32,128]{2,1,0:T(8,128)(2,1)} %broadcast_in_dim.14), calls=%async_computation | async-start | bytes 262144 | tf_op jit(solution)/shard_map/all_to_all | solution.py:148
  28.3 14.4 %all-to-all-start.1 = ((bf16[16,40,128]{2,1,0:T(8,128)(2,1)}), bf16[16,40,128]{2,1,0:T(8,128)(2,1)S(1)}, u32[]{:S(2)}, u32[]{:S(2)}) async-start(bf16[16,40,128]{2,1,0:T(8,128)(2,1)} %manifest_attention.1), calls=%async_computation.1 | async-start | bytes 327680 | tf_op jit(solution)/shard_map/all_to_all | solution.py:148
  33.2 16.0 %copy-start.4 = (bf16[128,1792]{1,0:T(8,128)(2,1)S(1)}, bf16[128,1792]{1,0:T(8,128)(2,1)}, u32[]{:S(2)}) copy-start(bf16[128,1792]{1,0:T(8,128)(2,1)} %param.18) | copy-start | bytes 1376260
  33.2 16.0 %copy-start.5 = (bf16[128,1792]{1,0:T(8,128)(2,1)S(1)}, bf16[128,1792]{1,0:T(8,128)(2,1)}, u32[]{:S(2)}) copy-start(bf16[128,1792]{1,0:T(8,128)(2,1)} %param.19) | copy-start | bytes 1376260
  44.1 16.3 %all-to-all-start.2 = ((bf16[32,4,1024]{2,1,0:T(4,128)(2,1)}), bf16[32,4,1024]{2,1,0:T(4,128)(2,1)S(1)}, u32[]{:S(2)}, u32[]{:S(2)}) async-start(bf16[32,4,1024]{2,1,0:T(4,128)(2,1)} %join_attention.1), calls=%async_computation.2 | async-start | bytes 524288 | tf_op jit(solution)/shard_map/all_to_all | solution.py:148
  49.2 3.5 %copy-start.7 = (bf16[1024,128]{1,0:T(8,128)(2,1)S(1)}, bf16[1024,128]{1,0:T(8,128)(2,1)}, u32[]{:S(2)}) copy-start(bf16[1024,128]{1,0:T(8,128)(2,1)} %param.17) | copy-start | bytes 786436
  49.3 14.7 %collective-permute-start.2 = (bf16[128,1792]{1,0:T(8,128)(2,1)S(1)}, bf16[128,1792]{1,0:T(8,128)(2,1)S(1)}, u32[]{:S(2)}, u32[]{:S(2)}) collective-permute-start(bf16[128,1792]{1,0:T(8,128)(2,1)S(1)} %get-tuple-element.13), channel_id=1, source_target_pairs={{0,16},{16,0},{1,17},{17,1},{2,18},{18,2},{3,19},{19,3},{4,20},{20... | collective-permute-start | bytes 1376264 | tf_op jit(solution)/shard_map/ppermute | solution.py:144
  52.7 11.3 %collective-permute-start.3 = (bf16[1024,128]{1,0:T(8,128)(2,1)S(1)}, bf16[1024,128]{1,0:T(8,128)(2,1)S(1)}, u32[]{:S(2)}, u32[]{:S(2)}) collective-permute-start(bf16[1024,128]{1,0:T(8,128)(2,1)S(1)} %copy-done.7), channel_id=1, source_target_pairs={{0,8},{8,0},{1,9},{9,1},{2,10},{10,2},{3,11},{11,3},{4,12},{12,4},... | collective-permute-start | bytes 786440 | tf_op jit(solution)/shard_map/ppermute | solution.py:140
  64.3 11.0 %copy-start.6 = (bf16[256,128]{1,0:T(8,128)(2,1)S(1)}, bf16[256,128]{1,0:T(8,128)(2,1)}, u32[]{:S(2)}) copy-start(bf16[256,128]{1,0:T(8,128)(2,1)} %param.16) | copy-start | bytes 196612
  65.1 25.8 %all-to-all-start.3 = ((bf16[8,128,256]{2,1,0:T(8,128)(2,1)}), bf16[8,128,256]{2,1,0:T(8,128)(2,1)S(1)}, u32[]{:S(2)}, u32[]{:S(2)}) async-start(bf16[8,128,256]{2,1,0:T(8,128)(2,1)} %broadcast_in_dim.15), calls=%async_computation.3 | async-start | bytes 1048576 | tf_op jit(solution)/shard_map/all_to_all | solution.py:148
  75.3 6.3 %collective-permute-start = (bf16[32,4,128]{2,1,0:T(4,128)(2,1)S(1)}, bf16[32,4,128]{2,1,0:T(4,128)(2,1)S(1)}, u32[]{:S(2)}, u32[]{:S(2)}) collective-permute-start(bf16[32,4,128]{2,1,0:T(4,128)(2,1)S(1)} %get-tuple-element.17), channel_id=1, source_target_pairs={{0,8},{8,0},{1,9},{9,1},{2,10},{10,2},{3,11},{11,3},{4,12},{12,4},... | collective-permute-start | bytes 98312 | tf_op jit(solution)/shard_map/ppermute | solution.py:140
  77.2 20.5 %collective-permute-start.5 = (bf16[128,1792]{1,0:T(8,128)(2,1)S(1)}, bf16[128,1792]{1,0:T(8,128)(2,1)S(1)}, u32[]{:S(2)}, u32[]{:S(2)}) collective-permute-start(bf16[128,1792]{1,0:T(8,128)(2,1)S(1)} %get-tuple-element.12), channel_id=1, source_target_pairs={{0,8},{8,0},{1,9},{9,1},{2,10},{10,2},{3,11},{11,3},{4,12},{12,4},... | collective-permute-start | bytes 1376264 | tf_op jit(solution)/shard_map/ppermute | solution.py:140
  79.6 15.6 %collective-permute-start.7 = (bf16[128,1792]{1,0:T(8,128)(2,1)S(1)}, bf16[128,1792]{1,0:T(8,128)(2,1)S(1)}, u32[]{:S(2)}, u32[]{:S(2)}) collective-permute-start(bf16[128,1792]{1,0:T(8,128)(2,1)S(1)} %collective-permute-done.2), channel_id=1, source_target_pairs={{0,8},{8,0},{1,9},{9,1},{2,10},{10,2},{3,11},{11,3},{4,12},{12,4},... | collective-permute-start | bytes 1376264 | tf_op jit(solution)/shard_map/ppermute | solution.py:140
  91.0 6.4 %collective-permute-start.6 = (bf16[128,256]{1,0:T(8,128)(2,1)S(1)}, bf16[128,256]{1,0:T(8,128)(2,1)S(1)}, u32[]{:S(2)}, u32[]{:S(2)}) collective-permute-start(bf16[128,256]{1,0:T(8,128)(2,1)S(1)} %add_convert_fusion), channel_id=1, source_target_pairs={{0,16},{16,0},{1,17},{17,1},{2,18},{18,2},{3,19},{19,3},{4,20},{20... | collective-permute-start | bytes 196616 | tf_op jit(solution)/shard_map/ppermute | solution.py:144
  98.9 23.5 %all-to-all-start.4 = ((bf16[32,4,1792]{2,1,0:T(4,128)(2,1)}), bf16[32,4,1792]{2,1,0:T(4,128)(2,1)S(1)}, u32[]{:S(2)}, u32[]{:S(2)}) async-start(bf16[32,4,1792]{2,1,0:T(4,128)(2,1)} %reshape.94), calls=%async_computation.4 | async-start | bytes 917504 | tf_op jit(solution)/shard_map/all_to_all | solution.py:148
  108.4 3.1 %collective-permute-start.4 = (bf16[128,128]{1,0:T(8,128)(2,1)S(1)}, bf16[128,128]{1,0:T(8,128)(2,1)S(1)}, u32[]{:S(2)}, u32[]{:S(2)}) collective-permute-start(bf16[128,128]{1,0:T(8,128)(2,1)S(1)} %slice.29), channel_id=1, source_target_pairs={{0,8},{8,0},{1,9},{9,1},{2,10},{10,2},{3,11},{11,3},{4,12},{12,4},... | collective-permute-start | bytes 98312 | tf_op jit(solution)/shard_map/ppermute | solution.py:140

commit v5 on v4

--- a/solution.py
+++ b/solution.py
@@ -12,11 +12,9 @@
 ROWS = 4
 QROWS = ROWS * GROUP
 POOL = 32
-CHIPS = 32
 PEERS = 16
 STATS = 8
 SCALE = HD**-0.5
-PLANE = ("y", "zq", "p")
 SPARSE = ("y", "zq")
 HEAD = ("zh", "x")
 REQ = ("y", "zq", "p", "c")
@@ -118,7 +116,7 @@
     rows_ref[...] = acc / total
     for h in range(GROUP):
         rows = rows_ref[pl.ds(h, ROWS, stride=GROUP), :].astype(BF)
-        for i in range(CHIPS):
+        for i in range(PEERS):
             out_ref[i, :, h * HD : (h + 1) * HD] = rows
 
 
@@ -127,7 +125,7 @@
     vmem = pl.BlockSpec(memory_space=pltpu.VMEM)
     return pl.pallas_call(
         join_kernel,
-        out_shape=jax.ShapeDtypeStruct((CHIPS, ROWS, GROUP * HD), BF),
+        out_shape=jax.ShapeDtypeStruct((PEERS, ROWS, GROUP * HD), BF),
         in_specs=[smem, vmem, vmem, vmem, vmem],
         out_specs=vmem,
         scratch_shapes=[pltpu.VMEM((QROWS, HD), F32)],
@@ -136,6 +134,38 @@
     )(place, parts, acc, top, total)
 
 
+def project_kernel(x_ref, w0_ref, w1_ref, w2_ref, w3_ref, out_ref):
+    for k, w_ref in enumerate((w0_ref, w1_ref, w2_ref, w3_ref)):
+        y = dot(x_ref[...], w_ref[...], 1, 0).astype(BF)
+        for i in range(8):
+            out_ref[i, :, k * HD : (k + 1) * HD] = y
+
+
+def mlp_kernel(x_ref, g0_ref, g1_ref, g2_ref, g3_ref, u0_ref, u1_ref, u2_ref, u3_ref, out_ref):
+    def product(*w_refs):
+        w = [w_ref[...] for w_ref in w_refs]
+        low = dot(x_ref[:, 0 : 2 * HD], jnp.concatenate(w[:2], axis=0), 1, 0)
+        return low + dot(x_ref[:, 2 * HD :], jnp.concatenate(w[2:], axis=0), 1, 0)
+
+    gate = product(g0_ref, g1_ref, g2_ref, g3_ref)
+    up = product(u0_ref, u1_ref, u2_ref, u3_ref)
+    for j in range(PEERS):
+        at = slice(j * ROWS, (j + 1) * ROWS)
+        out_ref[j] = jnp.concatenate([gate[at], up[at]], axis=0).astype(BF)
+
+
+def dense(kernel, name, out_shape, *args):
+    vmem = pl.BlockSpec(memory_space=pltpu.VMEM)
+    return pl.pallas_call(
+        kernel,
+        out_shape=jax.ShapeDtypeStruct(out_shape, BF),
+        in_specs=[vmem] * len(args),
+        out_specs=vmem,
+        compiler_params=pltpu.CompilerParams(vmem_limit_bytes=40 << 20),
+        name=name,
+    )(*args)
+
+
 def swap(x):
     return lax.ppermute(x, "c", [(0, 1), (1, 0)])
 
@@ -148,45 +178,48 @@
     return lax.all_to_all(x, axes, 0, 0, tiled=True)
 
 
+def pick(x, index, axis):
+    return jnp.where(index == 0, lax.index_in_dim(x, 0, axis, False), lax.index_in_dim(x, 1, axis, False))
+
+
+def ordered(own, other, index, axis):
+    return jnp.where(index == 0, jnp.stack([own, other], axis), jnp.stack([other, own], axis))
+
+
 def on_device(queries, new_kv, own_kv, man_kv, pages, own_len, resid, w_out, w_gate, w_up):
     core, side = lax.axis_index("c"), lax.axis_index("p")
+    tie = lax.optimization_barrier
     width = w_gate.shape[1]
+    rows = PEERS * ROWS
     q = queries.reshape(QROWS, HD)
+    q_all = exchange(jnp.broadcast_to(q[None], (PEERS, QROWS, HD)), SPARSE).reshape(PEERS * QROWS, HD)
     kv = man_kv.reshape(2, 2 * PAGE, HD)
     kv = lax.all_gather(jnp.stack([kv, pair(kv)]), "c", axis=0, tiled=True)
-    w_out2 = jnp.concatenate([w_out, swap(w_out)], axis=1)
-    w_keep = jnp.where(side == 0, w_gate, w_up)
-    w_pair = pair(jnp.where(side == 0, w_up, w_gate))
-    w_keep2 = jnp.concatenate([w_keep, swap(w_keep)], axis=0)
-    res = resid.reshape(CHIPS, 2, ROWS, HD)
-    mine = jnp.where(core == 0, res[:, 0], res[:, 1])
-    theirs = swap(jnp.where(core == 0, res[:, 1], res[:, 0]))
-    res2 = jnp.concatenate([mine, theirs], axis=-1).reshape(CHIPS * ROWS, 2 * HD)
-
-    acc, top, total = own_part(pages, own_len, q, new_kv, own_kv.reshape(2, POOL * PAGE, HD))
-    q_all = exchange(jnp.broadcast_to(q[None], (PEERS, QROWS, HD)), SPARSE).reshape(PEERS * QROWS, HD)
+    own = own_part(pages, own_len, q, new_kv, own_kv.reshape(2, POOL * PAGE, HD))
+    q_all, kv, own = tie((q_all, kv, own))
     parts = exchange(man_part(q_all, kv), SPARSE)
+    w_out_p = pair(w_out)
+    parts, w_out_p, w_out_c, w_out_pc = tie((parts, w_out_p, swap(w_out), swap(w_out_p)))
     place = (lax.axis_index(SPARSE) % 4).astype(jnp.int32).reshape(1)
-    attn = exchange(join_part(place, parts, acc, top, total), PLANE).reshape(CHIPS * ROWS, GROUP * HD)
-    attn, w_pair = lax.optimization_barrier((attn, w_pair))
-    w_pair2 = jnp.concatenate([w_pair, swap(w_pair)], axis=0)
-
-    partial_out = jnp.dot(attn, w_out2, preferred_element_type=F32).astype(BF)
-    heads = exchange(jnp.broadcast_to(partial_out[None], (8, *partial_out.shape)), HEAD)
-    out2 = (res2.astype(F32) + heads.astype(F32).sum(0)).astype(BF)
-
-    z = jnp.dot(out2, w_keep2, preferred_element_type=F32)
-    z = (z + jnp.dot(pair(out2), w_pair2, preferred_element_type=F32)).astype(BF)
-    joined = exchange(z.reshape(CHIPS, ROWS, width), PLANE).reshape(PEERS, 2, ROWS, width)
-    joined = joined.astype(F32).sum(0)
-    hidden = (jax.nn.silu(joined[0]) * joined[1]).astype(BF)
-
-    kept = out2[:, :HD].reshape(CHIPS, 1, ROWS, HD)
-    given = swap(out2[:, HD:]).reshape(CHIPS, 1, ROWS, HD)
-    first = jnp.where(core == 0, kept, given)
-    second = jnp.where(core == 0, given, kept)
-    resid_out = jnp.concatenate([first, second], axis=1).reshape(CHIPS * 2 * ROWS, HD)
-    return (resid_out, hidden)
+    attn = exchange(join_part(place, parts, *own), SPARSE).reshape(rows, GROUP * HD)
+    res = resid.reshape(PEERS, 2, 2, ROWS, HD)
+    res = jnp.stack([pick(res, core, 2), swap(pick(res, 1 - core, 2))], axis=3)
+    attn, w_gate_p, w_up_p, res = tie((attn, pair(w_gate), pair(w_up), res))
+    res = jnp.stack([pick(res, side, 1), pair(pick(res, 1 - side, 1))], axis=2).reshape(rows, 4 * HD)
+
+    heads = exchange(dense(project_kernel, "project", (8, rows, 4 * HD), attn, w_out, w_out_c, w_out_p, w_out_pc), HEAD)
+    out4 = (res.astype(F32) + heads.astype(F32).sum(0)).astype(BF)
+    both = dense(
+        mlp_kernel, "gate_up", (PEERS, 2 * ROWS, width), out4,
+        w_gate, swap(w_gate), w_gate_p, swap(w_gate_p), w_up, swap(w_up), w_up_p, swap(w_up_p),
+    )
+    joined = exchange(both, SPARSE).astype(F32).sum(0)
+    hidden = (jax.nn.silu(joined[:ROWS]) * joined[ROWS:]).astype(BF)
+
+    out = out4.reshape(PEERS, ROWS, 2, 2, HD)
+    out = ordered(out[:, :, 0], pair(out[:, :, 1]), side, 1)
+    out = ordered(out[:, :, :, 0], swap(out[:, :, :, 1]), core, 2)
+    return (out.reshape(PEERS * 4 * ROWS, HD), hidden)
 
 
 def solution(mesh):

time: 124 us -> 125 us (level)
  the two profiles are of different devices: /device:TPU:8 before, /device:TPU:2 now
where the time goes in v5:
time: 125 us; the launch traced here: 124 us
  starting transfers between devices  80.7 us (65%)
  waiting for transfers between devices  25.9 us (21%)
  Pallas kernels  7.99 us (6%)
  local copies, waits for them, and re-layouts  3.67 us (3%)
  other arithmetic  2.18 us (2%)
  blocking collectives  2.13 us (2%)
    all_to_all x5, starting transfers between devices, exchange(): return lax.all_to_all(x, axes, 0, 0, tiled=True)  45.7 us
    all_to_all x5, waiting for transfers between devices, exchange(): return lax.all_to_all(x, axes, 0, 0, tiled=True)  19.1 us
    ppermute x6, starting transfers between devices, pair(): return lax.ppermute(x, 'p', [(0, 1), (1, 0)])  18.1 us
    ppermute x8, starting transfers between devices, swap(): return lax.ppermute(x, 'c', [(0, 1), (1, 0)])  16.8 us
    ppermute x6, waiting for transfers between devices, pair(): return lax.ppermute(x, 'p', [(0, 1), (1, 0)])  4.47 us
    pallas_call x2, Pallas kernels, dense(): pl.pallas_call(kernel, out_shape=jax.ShapeDtypeStruct(out_shape, BF), in_...  3.83 us
  transfers between devices with their start and end apart: 19, of which 8 were waited for; matrix products, arithmetic and copies ran while one was open for 3% of the time, Pallas kernels for 3%

profile of v5, /device:TPU:2, one launch (start us, length us, event | category | flops | bytes accessed | tf_op | source)
XLA Modules:
  0.0 123.6 jit_solution(13696393620139238169)
XLA Ops:
  0.6 4.4 %collective-permute-start = (bf16[2,128,128]{2,1,0:T(8,128)(2,1)}, bf16[2,128,128]{2,1,0:T(8,128)(2,1)S(1)}, u32[]{:S(2)}, u32[]{:S(2)}) collective-permute-start(bf16[2,128,128]{2,1,0:T(8,128)(2,1)} %bitcast.42), channel_id=1, source_target_pairs={{0,16},{16,0},{1,17},{17,1},{2,18},{18,2},{3,19},{19,3},{4,20},{20... | collective-permute-start | bytes 196616 | tf_op jit(solution)/shard_map/ppermute | solution.py:174
  6.4 11.0 %all-to-all-start = ((bf16[16,32,128]{2,1,0:T(8,128)(2,1)}), bf16[16,32,128]{2,1,0:T(8,128)(2,1)S(1)}, u32[]{:S(2)}, u32[]{:S(2)}) async-start(bf16[16,32,128]{2,1,0:T(8,128)(2,1)} %broadcast_in_dim.8), calls=%async_computation | async-start | bytes 262144 | tf_op jit(solution)/shard_map/all_to_all | solution.py:178
  17.4 1.9 %collective-permute-start.1 = (bf16[1024,128]{1,0:T(8,128)(2,1)S(1)}, bf16[1024,128]{1,0:T(8,128)(2,1)S(1)}, u32[]{:S(2)}, u32[]{:S(2)}) collective-permute-start(bf16[1024,128]{1,0:T(8,128)(2,1)S(1)} %copy-done.3), channel_id=1, source_target_pairs={{0,16},{16,0},{1,17},{17,1},{2,18},{18,2},{3,19},{19,3},{4,20},{20... | collective-permute-start | bytes 786440 | tf_op jit(solution)/shard_map/ppermute | solution.py:174
  19.4 1.2 copy-done
  20.6 1.2 own_attention.1
  21.9 2.1 %all_gather.3.kv_ref = bf16[4,2,128,128]{3,2,1,0:T(8,128)(2,1)S(1)} all-gather(bf16[2,2,128,128]{3,2,1,0:T(8,128)(2,1)S(1)} %pad_maximum_fusion), channel_id=1, replica_groups=mesh['y'=8,'zq'=2,'p'=2,'c'=2,'zh'=2,'x'=4] {'c'}, dimensions={0}, use_global_device_ids=true | all-gather | bytes 393216 | tf_op jit(solution)/shard_map/all_gather | solution.py:197
  24.0 4.0 %all-to-all-done = bf16[16,32,128]{2,1,0:T(8,128)(2,1)S(1)} async-done(((bf16[16,32,128]{2,1,0:T(8,128)(2,1)}), bf16[16,32,128]{2,1,0:T(8,128)(2,1)S(1)}, u32[]{:S(2)}, u32[]{:S(2)}) %all-to-all-start) | async-done | bytes 131104 | tf_op jit(solution)/shard_map/all_to_all | solution.py:178
  28.0 1.7 %manifest_attention.1 = bf16[16,40,128]{2,1,0:T(8,128)(2,1)} custom-call(bf16[512,128]{1,0:T(8,128)(2,1)S(1)} %bitcast.37, bf16[4,2,128,128]{3,2,1,0:T(8,128)(2,1)S(1)} %all_gather.3.kv_ref), custom_call_target="tpu_custom_call" | custom-call | tf_op jit(solution)/shard_map/manifest_attention/pallas_call | solution.py:89
  29.7 5.0 %all-to-all-start.1 = ((bf16[16,40,128]{2,1,0:T(8,128)(2,1)}), bf16[16,40,128]{2,1,0:T(8,128)(2,1)S(1)}, u32[]{:S(2)}, u32[]{:S(2)}) async-start(bf16[16,40,128]{2,1,0:T(8,128)(2,1)} %manifest_attention.1), calls=%async_computation.1 | async-start | bytes 327680 | tf_op jit(solution)/shard_map/all_to_all | solution.py:178
  34.7 1.9 %collective-permute-start.2 = (bf16[1024,128]{1,0:T(8,128)(2,1)S(1)}, bf16[1024,128]{1,0:T(8,128)(2,1)S(1)}, u32[]{:S(2)}, u32[]{:S(2)}) collective-permute-start(bf16[1024,128]{1,0:T(8,128)(2,1)S(1)} %copy-done.3), channel_id=1, source_target_pairs={{0,8},{8,0},{1,9},{9,1},{2,10},{10,2},{3,11},{11,3},{4,12},{12,4},... | collective-permute-start | bytes 786440 | tf_op jit(solution)/shard_map/ppermute | solution.py:170
  36.6 2.4 %collective-permute-start.3 = (bf16[1024,128]{1,0:T(8,128)(2,1)S(1)}, bf16[1024,128]{1,0:T(8,128)(2,1)S(1)}, u32[]{:S(2)}, u32[]{:S(2)}) collective-permute-start(bf16[1024,128]{1,0:T(8,128)(2,1)S(1)} %collective-permute-done.1.w2_ref), channel_id=1, source_target_pairs={{0,8},{8,0},{1,9},{9,1},{2,10},{10,2},{3,11},{11,3},{4,12},{12,4},... | collective-permute-start | bytes 786440 | tf_op jit(solution)/shard_map/ppermute | solution.py:170
  39.1 3.9 %collective-permute-start.4 = (bf16[128,1792]{1,0:T(8,128)(2,1)S(1)}, bf16[128,1792]{1,0:T(8,128)(2,1)S(1)}, u32[]{:S(2)}, u32[]{:S(2)}) collective-permute-start(bf16[128,1792]{1,0:T(8,128)(2,1)S(1)} %copy-done.1), channel_id=1, source_target_pairs={{0,16},{16,0},{1,17},{17,1},{2,18},{18,2},{3,19},{19,3},{4,20},{20... | collective-permute-start | bytes 1376264 | tf_op jit(solution)/shard_map/ppermute | solution.py:174
  43.0 1.9 %collective-permute-start.5 = (bf16[128,1792]{1,0:T(8,128)(2,1)S(1)}, bf16[128,1792]{1,0:T(8,128)(2,1)S(1)}, u32[]{:S(2)}, u32[]{:S(2)}) collective-permute-start(bf16[128,1792]{1,0:T(8,128)(2,1)S(1)} %copy-done.2), channel_id=1, source_target_pairs={{0,16},{16,0},{1,17},{17,1},{2,18},{18,2},{3,19},{19,3},{4,20},{20... | collective-permute-start | bytes 1376264 | tf_op jit(solution)/shard_map/ppermute | solution.py:174
  45.0 1.2 all-to-all-done.1.parts_ref
  46.2 1.3 %join_attention.1 = bf16[16,4,1024]{2,1,0:T(4,128)(2,1)} custom-call(s32[1]{0:T(128)} %bitcast.place_ref, bf16[16,40,128]{2,1,0:T(8,128)(2,1)S(1)} %all-to-all-done.1.parts_ref, f32[32,128]{1,0:T(8,128)S(1)} %get-tuple-element.24.acc_ref, f32[32,128]{1,0:T(8,128)S(1)} %get-tuple-element.25.top_ref, f32[32,128]{1,0:T(8,128)S(1)} %get-tuple-element.26.total_ref), custom_call_target="tpu_custom_call" | custom-call | tf_op jit(solution)/shard_map/join_attention/pallas_call | solution.py:126
  47.5 7.9 %all-to-all-start.2 = ((bf16[16,4,1024]{2,1,0:T(4,128)(2,1)}), bf16[16,4,1024]{2,1,0:T(4,128)(2,1)S(1)}, u32[]{:S(2)}, u32[]{:S(2)}) async-start(bf16[16,4,1024]{2,1,0:T(4,128)(2,1)} %join_attention.1), calls=%async_computation.2 | async-start | bytes 262144 | tf_op jit(solution)/shard_map/all_to_all | solution.py:178
  55.5 1.9 %collective-permute-start.6 = (bf16[16,2,4,128]{3,2,1,0:T(4,128)(2,1)S(1)}, bf16[16,2,4,128]{3,2,1,0:T(4,128)(2,1)S(1)}, u32[]{:S(2)}, u32[]{:S(2)}) collective-permute-start(bf16[16,2,4,128]{3,2,1,0:T(4,128)(2,1)S(1)} %get-tuple-element.39), channel_id=1, source_target_pairs={{0,8},{8,0},{1,9},{9,1},{2,10},{10,2},{3,11},{11,3},{4,12},{12,4},... | collective-permute-start | bytes 98312 | tf_op jit(solution)/shard_map/ppermute | solution.py:170
  57.4 1.2 collective-permute-done.6
  58.6 7.3 %all-to-all-done.2 = bf16[16,4,1024]{2,1,0:T(4,128)(2,1)S(1)} async-done(((bf16[16,4,1024]{2,1,0:T(4,128)(2,1)}), bf16[16,4,1024]{2,1,0:T(4,128)(2,1)S(1)}, u32[]{:S(2)}, u32[]{:S(2)}) %all-to-all-start.2) | async-done | bytes 131104 | tf_op jit(solution)/shard_map/all_to_all | solution.py:178
  67.1 11.2 %all-to-all-start.3 = ((bf16[8,64,512]{2,1,0:T(8,128)(2,1)}), bf16[8,64,512]{2,1,0:T(8,128)(2,1)}, u32[]{:S(2)}, u32[]{:S(2)}) async-start(bf16[8,64,512]{2,1,0:T(8,128)(2,1)} %project.1), calls=%async_computation.3 | async-start | bytes 1048576 | tf_op jit(solution)/shard_map/all_to_all | solution.py:178
  78.3 1.9 %collective-permute-start.10 = (bf16[128,1792]{1,0:T(8,128)(2,1)S(1)}, bf16[128,1792]{1,0:T(8,128)(2,1)S(1)}, u32[]{:S(2)}, u32[]{:S(2)}) collective-permute-start(bf16[128,1792]{1,0:T(8,128)(2,1)S(1)} %copy-done.1), channel_id=1, source_target_pairs={{0,8},{8,0},{1,9},{9,1},{2,10},{10,2},{3,11},{11,3},{4,12},{12,4},... | collective-permute-start | bytes 1376264 | tf_op jit(solution)/shard_map/ppermute | solution.py:170
  80.2 2.4 %collective-permute-start.12 = (bf16[128,1792]{1,0:T(8,128)(2,1)S(1)}, bf16[128,1792]{1,0:T(8,128)(2,1)S(1)}, u32[]{:S(2)}, u32[]{:S(2)}) collective-permute-start(bf16[128,1792]{1,0:T(8,128)(2,1)S(1)} %copy-done.2), channel_id=1, source_target_pairs={{0,8},{8,0},{1,9},{9,1},{2,10},{10,2},{3,11},{11,3},{4,12},{12,4},... | collective-permute-start | bytes 1376264 | tf_op jit(solution)/shard_map/ppermute | solution.py:170
  82.7 3.5 %collective-permute-start.7 = (bf16[16,4,2,128]{3,1,0,2:T(4,128)(2,1)S(1)}, bf16[16,4,2,128]{3,1,0,2:T(4,128)(2,1)S(1)}, u32[]{:S(2)}, u32[]{:S(2)}) collective-permute-start(bf16[16,4,2,128]{3,1,0,2:T(4,128)(2,1)S(1)} %fusion.1), channel_id=1, source_target_pairs={{0,16},{16,0},{1,17},{17,1},{2,18},{18,2},{3,19},{19,3},{4,20},{20... | collective-permute-start | bytes 98312 | tf_op jit(solution)/shard_map/ppermute | solution.py:174
  86.2 1.9 %collective-permute-start.11 = (bf16[128,1792]{1,0:T(8,128)(2,1)S(1)}, bf16[128,1792]{1,0:T(8,128)(2,1)}, u32[]{:S(2)}, u32[]{:S(2)}) collective-permute-start(bf16[128,1792]{1,0:T(8,128)(2,1)S(1)} %collective-permute-done.4.g2_ref), channel_id=1, source_target_pairs={{0,8},{8,0},{1,9},{9,1},{2,10},{10,2},{3,11},{11,3},{4,12},{12,4},... | collective-permute-start | bytes 1376264 | tf_op jit(solution)/shard_map/ppermute | solution.py:170
  88.1 2.4 %collective-permute-start.13 = (bf16[128,1792]{1,0:T(8,128)(2,1)S(1)}, bf16[128,1792]{1,0:T(8,128)(2,1)}, u32[]{:S(2)}, u32[]{:S(2)}) collective-permute-start(bf16[128,1792]{1,0:T(8,128)(2,1)S(1)} %collective-permute-done.5.u2_ref), channel_id=1, source_target_pairs={{0,8},{8,0},{1,9},{9,1},{2,10},{10,2},{3,11},{11,3},{4,12},{12,4},... | collective-permute-start | bytes 1376264 | tf_op jit(solution)/shard_map/ppermute | solution.py:170
  92.9 2.7 %gate_up.1 = bf16[16,8,1792]{2,1,0:T(8,128)(2,1)} custom-call(bf16[64,512]{1,0:T(8,128)(2,1)S(1)} %add_convert_fusion.x_ref, bf16[128,1792]{1,0:T(8,128)(2,1)S(1)} %copy-done.1, bf16[128,1792]{1,0:T(8,128)(2,1)S(1)} %collective-permute-done.10.g1_ref, bf16[128,1792]{1,0:T(8,128)(2,1)S(1)} %collective-permute-done.4.g2_ref, ...), custom_call_target="tpu_custom_call" | custom-call | tf_op jit(solution)/shard_map/gate_up/pallas_call | solution.py:159
  95.6 10.7 %all-to-all-start.4 = ((bf16[16,8,1792]{2,1,0:T(8,128)(2,1)}), bf16[16,8,1792]{2,1,0:T(8,128)(2,1)S(1)}, u32[]{:S(2)}, u32[]{:S(2)}) async-start(bf16[16,8,1792]{2,1,0:T(8,128)(2,1)} %gate_up.1), calls=%async_computation.4 | async-start | bytes 917504 | tf_op jit(solution)/shard_map/all_to_all | solution.py:178
  106.4 2.5 %collective-permute-start.8 = (bf16[16,4,2,128]{3,1,0,2:T(4,128)(2,1)S(1)}, bf16[16,4,2,128]{3,1,0,2:T(4,128)(2,1)S(1)}, u32[]{:S(2)}, u32[]{:S(2)}) collective-permute-start(bf16[16,4,2,128]{3,1,0,2:T(4,128)(2,1)S(1)} %get-tuple-element.37), channel_id=1, source_target_pairs={{0,16},{16,0},{1,17},{17,1},{2,18},{18,2},{3,19},{19,3},{4,20},{20... | collective-permute-start | bytes 98312 | tf_op jit(solution)/shard_map/ppermute | solution.py:174
  108.9 3.6 %collective-permute-done.8 = bf16[16,4,2,128]{3,1,0,2:T(4,128)(2,1)S(1)} collective-permute-done((bf16[16,4,2,128]{3,1,0,2:T(4,128)(2,1)S(1)}, bf16[16,4,2,128]{3,1,0,2:T(4,128)(2,1)S(1)}, u32[]{:S(2)}, u32[]{:S(2)}) %collective-permute-start.8) | collective-permute-done | bytes 32800 | tf_op jit(solution)/shard_map/ppermute | solution.py:174
  112.6 1.9 %collective-permute-start.9 = (bf16[16,2,4,128]{3,2,0,1:T(4,128)(2,1)S(1)}, bf16[16,2,4,128]{3,2,0,1:T(4,128)(2,1)S(1)}, u32[]{:S(2)}, u32[]{:S(2)}) collective-permute-start(bf16[16,2,4,128]{3,2,0,1:T(4,128)(2,1)S(1)} %get-tuple-element.35), channel_id=1, source_target_pairs={{0,8},{8,0},{1,9},{9,1},{2,10},{10,2},{3,11},{11,3},{4,12},{12,4},... | collective-permute-start | bytes 98312 | tf_op jit(solution)/shard_map/ppermute | solution.py:170
  114.5 1.2 collective-permute-done.9
  116.4 6.5 %all-to-all-done.4 = bf16[16,8,1792]{2,1,0:T(8,128)(2,1)S(1)} async-done(((bf16[16,8,1792]{2,1,0:T(8,128)(2,1)}), bf16[16,8,1792]{2,1,0:T(8,128)(2,1)S(1)}, u32[]{:S(2)}, u32[]{:S(2)}) %all-to-all-start.4) | async-done | bytes 458784 | tf_op jit(solution)/shard_map/all_to_all | solution.py:178
  (52 shorter events, 6.6 us)
Async XLA Ops:
  0.6 16.8 %copy-start.3 = (bf16[1024,128]{1,0:T(8,128)(2,1)S(1)}, bf16[1024,128]{1,0:T(8,128)(2,1)}, u32[]{:S(2)}) copy-start(bf16[1024,128]{1,0:T(8,128)(2,1)} %w0_ref.1) | copy-start | bytes 786436
  0.6 21.2 %collective-permute-start = (bf16[2,128,128]{2,1,0:T(8,128)(2,1)}, bf16[2,128,128]{2,1,0:T(8,128)(2,1)S(1)}, u32[]{:S(2)}, u32[]{:S(2)}) collective-permute-start(bf16[2,128,128]{2,1,0:T(8,128)(2,1)} %bitcast.42), channel_id=1, source_target_pairs={{0,16},{16,0},{1,17},{17,1},{2,18},{18,2},{3,19},{19,3},{4,20},{20... | collective-permute-start | bytes 196616 | tf_op jit(solution)/shard_map/ppermute | solution.py:174
  6.4 12.9 %copy-start.4 = (s32[4,8]{1,0:T(4,128)S(1)}, s32[4,8]{1,0:T(4,128)}, u32[]{:S(2)}) copy-start(s32[4,8]{1,0:T(4,128)} %pages_ref.1) | copy-start | bytes 388
  6.4 12.9 %copy-start.5 = (bf16[2,4,128]{2,1,0:T(4,128)(2,1)S(1)}, bf16[2,4,128]{2,1,0:T(4,128)(2,1)}, u32[]{:S(2)}) copy-start(bf16[2,4,128]{2,1,0:T(4,128)(2,1)} %new_ref.1) | copy-start | bytes 6148
  6.4 21.6 %all-to-all-start = ((bf16[16,32,128]{2,1,0:T(8,128)(2,1)}), bf16[16,32,128]{2,1,0:T(8,128)(2,1)S(1)}, u32[]{:S(2)}, u32[]{:S(2)}) async-start(bf16[16,32,128]{2,1,0:T(8,128)(2,1)} %broadcast_in_dim.8), calls=%async_computation | async-start | bytes 262144 | tf_op jit(solution)/shard_map/all_to_all | solution.py:178
  17.4 2.0 %copy-start.6 = (s32[4]{0:T(128)S(1)}, s32[4]{0:T(128)}, u32[]{:S(2)}) copy-start(s32[4]{0:T(128)} %len_ref.1) | copy-start | bytes 52
  17.4 19.2 %collective-permute-start.1 = (bf16[1024,128]{1,0:T(8,128)(2,1)S(1)}, bf16[1024,128]{1,0:T(8,128)(2,1)S(1)}, u32[]{:S(2)}, u32[]{:S(2)}) collective-permute-start(bf16[1024,128]{1,0:T(8,128)(2,1)S(1)} %copy-done.3), channel_id=1, source_target_pairs={{0,16},{16,0},{1,17},{17,1},{2,18},{18,2},{3,19},{19,3},{4,20},{20... | collective-permute-start | bytes 786440 | tf_op jit(solution)/shard_map/ppermute | solution.py:174
  19.4 1.2 copy-start
  20.6 1.2 copy-start.8
  21.9 21.1 %copy-start.2 = (bf16[128,1792]{1,0:T(8,128)(2,1)S(1)}, bf16[128,1792]{1,0:T(8,128)(2,1)}, u32[]{:S(2)}) copy-start(bf16[128,1792]{1,0:T(8,128)(2,1)} %u0_ref.1) | copy-start | bytes 1376260
  24.0 15.0 %copy-start.1 = (bf16[128,1792]{1,0:T(8,128)(2,1)S(1)}, bf16[128,1792]{1,0:T(8,128)(2,1)}, u32[]{:S(2)}) copy-start(bf16[128,1792]{1,0:T(8,128)(2,1)} %g0_ref.1) | copy-start | bytes 1376260
  29.7 16.5 %all-to-all-start.1 = ((bf16[16,40,128]{2,1,0:T(8,128)(2,1)}), bf16[16,40,128]{2,1,0:T(8,128)(2,1)S(1)}, u32[]{:S(2)}, u32[]{:S(2)}) async-start(bf16[16,40,128]{2,1,0:T(8,128)(2,1)} %manifest_attention.1), calls=%async_computation.1 | async-start | bytes 327680 | tf_op jit(solution)/shard_map/all_to_all | solution.py:178
  34.7 10.3 %collective-permute-start.2 = (bf16[1024,128]{1,0:T(8,128)(2,1)S(1)}, bf16[1024,128]{1,0:T(8,128)(2,1)S(1)}, u32[]{:S(2)}, u32[]{:S(2)}) collective-permute-start(bf16[1024,128]{1,0:T(8,128)(2,1)S(1)} %copy-done.3), channel_id=1, source_target_pairs={{0,8},{8,0},{1,9},{9,1},{2,10},{10,2},{3,11},{11,3},{4,12},{12,4},... | collective-permute-start | bytes 786440 | tf_op jit(solution)/shard_map/ppermute | solution.py:170
  36.6 8.3 %collective-permute-start.3 = (bf16[1024,128]{1,0:T(8,128)(2,1)S(1)}, bf16[1024,128]{1,0:T(8,128)(2,1)S(1)}, u32[]{:S(2)}, u32[]{:S(2)}) collective-permute-start(bf16[1024,128]{1,0:T(8,128)(2,1)S(1)} %collective-permute-done.1.w2_ref), channel_id=1, source_target_pairs={{0,8},{8,0},{1,9},{9,1},{2,10},{10,2},{3,11},{11,3},{4,12},{12,4},... | collective-permute-start | bytes 786440 | tf_op jit(solution)/shard_map/ppermute | solution.py:170
  39.1 26.9 %collective-permute-start.4 = (bf16[128,1792]{1,0:T(8,128)(2,1)S(1)}, bf16[128,1792]{1,0:T(8,128)(2,1)S(1)}, u32[]{:S(2)}, u32[]{:S(2)}) collective-permute-start(bf16[128,1792]{1,0:T(8,128)(2,1)S(1)} %copy-done.1), channel_id=1, source_target_pairs={{0,16},{16,0},{1,17},{17,1},{2,18},{18,2},{3,19},{19,3},{4,20},{20... | collective-permute-start | bytes 1376264 | tf_op jit(solution)/shard_map/ppermute | solution.py:174
  43.0 23.0 %collective-permute-start.5 = (bf16[128,1792]{1,0:T(8,128)(2,1)S(1)}, bf16[128,1792]{1,0:T(8,128)(2,1)S(1)}, u32[]{:S(2)}, u32[]{:S(2)}) collective-permute-start(bf16[128,1792]{1,0:T(8,128)(2,1)S(1)} %copy-done.2), channel_id=1, source_target_pairs={{0,16},{16,0},{1,17},{17,1},{2,18},{18,2},{3,19},{19,3},{4,20},{20... | collective-permute-start | bytes 1376264 | tf_op jit(solution)/shard_map/ppermute | solution.py:174
  47.5 7.9 %copy-start.7 = (bf16[256,128]{1,0:T(8,128)(2,1)S(1)}, bf16[256,128]{1,0:T(8,128)(2,1)}, u32[]{:S(2)}) copy-start(bf16[256,128]{1,0:T(8,128)(2,1)} %param.16) | copy-start | bytes 196612
  47.5 18.4 %all-to-all-start.2 = ((bf16[16,4,1024]{2,1,0:T(4,128)(2,1)}), bf16[16,4,1024]{2,1,0:T(4,128)(2,1)S(1)}, u32[]{:S(2)}, u32[]{:S(2)}) async-start(bf16[16,4,1024]{2,1,0:T(4,128)(2,1)} %join_attention.1), calls=%async_computation.2 | async-start | bytes 262144 | tf_op jit(solution)/shard_map/all_to_all | solution.py:178
  55.5 3.1 %collective-permute-start.6 = (bf16[16,2,4,128]{3,2,1,0:T(4,128)(2,1)S(1)}, bf16[16,2,4,128]{3,2,1,0:T(4,128)(2,1)S(1)}, u32[]{:S(2)}, u32[]{:S(2)}) collective-permute-start(bf16[16,2,4,128]{3,2,1,0:T(4,128)(2,1)S(1)} %get-tuple-element.39), channel_id=1, source_target_pairs={{0,8},{8,0},{1,9},{9,1},{2,10},{10,2},{3,11},{11,3},{4,12},{12,4},... | collective-permute-start | bytes 98312 | tf_op jit(solution)/shard_map/ppermute | solution.py:170
  67.1 24.5 %all-to-all-start.3 = ((bf16[8,64,512]{2,1,0:T(8,128)(2,1)}), bf16[8,64,512]{2,1,0:T(8,128)(2,1)}, u32[]{:S(2)}, u32[]{:S(2)}) async-start(bf16[8,64,512]{2,1,0:T(8,128)(2,1)} %project.1), calls=%async_computation.3 | async-start | bytes 1048576 | tf_op jit(solution)/shard_map/all_to_all | solution.py:178
  78.3 14.6 %collective-permute-start.10 = (bf16[128,1792]{1,0:T(8,128)(2,1)S(1)}, bf16[128,1792]{1,0:T(8,128)(2,1)S(1)}, u32[]{:S(2)}, u32[]{:S(2)}) collective-permute-start(bf16[128,1792]{1,0:T(8,128)(2,1)S(1)} %copy-done.1), channel_id=1, source_target_pairs={{0,8},{8,0},{1,9},{9,1},{2,10},{10,2},{3,11},{11,3},{4,12},{12,4},... | collective-permute-start | bytes 1376264 | tf_op jit(solution)/shard_map/ppermute | solution.py:170
  80.2 12.7 %collective-permute-start.12 = (bf16[128,1792]{1,0:T(8,128)(2,1)S(1)}, bf16[128,1792]{1,0:T(8,128)(2,1)S(1)}, u32[]{:S(2)}, u32[]{:S(2)}) collective-permute-start(bf16[128,1792]{1,0:T(8,128)(2,1)S(1)} %copy-done.2), channel_id=1, source_target_pairs={{0,8},{8,0},{1,9},{9,1},{2,10},{10,2},{3,11},{11,3},{4,12},{12,4},... | collective-permute-start | bytes 1376264 | tf_op jit(solution)/shard_map/ppermute | solution.py:170
  82.7 8.7 %collective-permute-start.7 = (bf16[16,4,2,128]{3,1,0,2:T(4,128)(2,1)S(1)}, bf16[16,4,2,128]{3,1,0,2:T(4,128)(2,1)S(1)}, u32[]{:S(2)}, u32[]{:S(2)}) collective-permute-start(bf16[16,4,2,128]{3,1,0,2:T(4,128)(2,1)S(1)} %fusion.1), channel_id=1, source_target_pairs={{0,16},{16,0},{1,17},{17,1},{2,18},{18,2},{3,19},{19,3},{4,20},{20... | collective-permute-start | bytes 98312 | tf_op jit(solution)/shard_map/ppermute | solution.py:174
  86.2 6.7 %collective-permute-start.11 = (bf16[128,1792]{1,0:T(8,128)(2,1)S(1)}, bf16[128,1792]{1,0:T(8,128)(2,1)}, u32[]{:S(2)}, u32[]{:S(2)}) collective-permute-start(bf16[128,1792]{1,0:T(8,128)(2,1)S(1)} %collective-permute-done.4.g2_ref), channel_id=1, source_target_pairs={{0,8},{8,0},{1,9},{9,1},{2,10},{10,2},{3,11},{11,3},{4,12},{12,4},... | collective-permute-start | bytes 1376264 | tf_op jit(solution)/shard_map/ppermute | solution.py:170
  88.1 4.8 %collective-permute-start.13 = (bf16[128,1792]{1,0:T(8,128)(2,1)S(1)}, bf16[128,1792]{1,0:T(8,128)(2,1)}, u32[]{:S(2)}, u32[]{:S(2)}) collective-permute-start(bf16[128,1792]{1,0:T(8,128)(2,1)S(1)} %collective-permute-done.5.u2_ref), channel_id=1, source_target_pairs={{0,8},{8,0},{1,9},{9,1},{2,10},{10,2},{3,11},{11,3},{4,12},{12,4},... | collective-permute-start | bytes 1376264 | tf_op jit(solution)/shard_map/ppermute | solution.py:170
  95.6 27.3 %all-to-all-start.4 = ((bf16[16,8,1792]{2,1,0:T(8,128)(2,1)}), bf16[16,8,1792]{2,1,0:T(8,128)(2,1)S(1)}, u32[]{:S(2)}, u32[]{:S(2)}) async-start(bf16[16,8,1792]{2,1,0:T(8,128)(2,1)} %gate_up.1), calls=%async_computation.4 | async-start | bytes 917504 | tf_op jit(solution)/shard_map/all_to_all | solution.py:178
  106.4 6.1 %collective-permute-start.8 = (bf16[16,4,2,128]{3,1,0,2:T(4,128)(2,1)S(1)}, bf16[16,4,2,128]{3,1,0,2:T(4,128)(2,1)S(1)}, u32[]{:S(2)}, u32[]{:S(2)}) collective-permute-start(bf16[16,4,2,128]{3,1,0,2:T(4,128)(2,1)S(1)} %get-tuple-element.37), channel_id=1, source_target_pairs={{0,16},{16,0},{1,17},{17,1},{2,18},{18,2},{3,19},{19,3},{4,20},{20... | collective-permute-start | bytes 98312 | tf_op jit(solution)/shard_map/ppermute | solution.py:174
  112.6 3.1 %collective-permute-start.9 = (bf16[16,2,4,128]{3,2,0,1:T(4,128)(2,1)S(1)}, bf16[16,2,4,128]{3,2,0,1:T(4,128)(2,1)S(1)}, u32[]{:S(2)}, u32[]{:S(2)}) collective-permute-start(bf16[16,2,4,128]{3,2,0,1:T(4,128)(2,1)S(1)} %get-tuple-element.35), channel_id=1, source_target_pairs={{0,8},{8,0},{1,9},{9,1},{2,10},{10,2},{3,11},{11,3},{4,12},{12,4},... | collective-permute-start | bytes 98312 | tf_op jit(solution)/shard_map/ppermute | solution.py:170

commit v6 on v4

--- a/solution.py
+++ b/solution.py
@@ -136,50 +136,66 @@
     )(place, parts, acc, top, total)
 
 
+def project_kernel(x_ref, w0_ref, w1_ref, out_ref):
+    w = jnp.concatenate([w0_ref[...], w1_ref[...]], axis=1)
+    y = dot(x_ref[...], w, 1, 0).astype(BF)
+    for i in range(8):
+        out_ref[i] = y
+
+
+def mlp_kernel(x_ref, g0_ref, g1_ref, u0_ref, u1_ref, out_ref):
+    x = x_ref[...]
+    gate = dot(x, jnp.concatenate([g0_ref[...], g1_ref[...]], axis=0), 1, 0)
+    up = dot(x, jnp.concatenate([u0_ref[...], u1_ref[...]], axis=0), 1, 0)
+    for j in range(CHIPS):
+        at = slice(j * ROWS, (j + 1) * ROWS)
+        out_ref[j] = jnp.concatenate([gate[at], up[at]], axis=0).astype(BF)
+
+
+def dense(kernel, name, out_shape, *args):
+    vmem = pl.BlockSpec(memory_space=pltpu.VMEM)
+    return pl.pallas_call(
+        kernel,
+        out_shape=jax.ShapeDtypeStruct(out_shape, BF),
+        in_specs=[vmem] * len(args),
+        out_specs=vmem,
+        compiler_params=pltpu.CompilerParams(vmem_limit_bytes=40 << 20),
+        name=name,
+    )(*args)
+
+
 def swap(x):
     return lax.ppermute(x, "c", [(0, 1), (1, 0)])
 
 
-def pair(x):
-    return lax.ppermute(x, "p", [(0, 1), (1, 0)])
-
-
 def exchange(x, axes):
     return lax.all_to_all(x, axes, 0, 0, tiled=True)
 
 
 def on_device(queries, new_kv, own_kv, man_kv, pages, own_len, resid, w_out, w_gate, w_up):
-    core, side = lax.axis_index("c"), lax.axis_index("p")
+    core = lax.axis_index("c")
+    tie = lax.optimization_barrier
     width = w_gate.shape[1]
+    rows = CHIPS * ROWS
     q = queries.reshape(QROWS, HD)
-    kv = man_kv.reshape(2, 2 * PAGE, HD)
-    kv = lax.all_gather(jnp.stack([kv, pair(kv)]), "c", axis=0, tiled=True)
-    w_out2 = jnp.concatenate([w_out, swap(w_out)], axis=1)
-    w_keep = jnp.where(side == 0, w_gate, w_up)
-    w_pair = pair(jnp.where(side == 0, w_up, w_gate))
-    w_keep2 = jnp.concatenate([w_keep, swap(w_keep)], axis=0)
+    q_all = exchange(jnp.broadcast_to(q[None], (PEERS, QROWS, HD)), SPARSE).reshape(PEERS * QROWS, HD)
+    kv = lax.all_gather(man_kv.reshape(1, 2, 2 * PAGE, HD), ("p", "c"), axis=0, tiled=True)
+    parts = exchange(man_part(q_all, kv), SPARSE)
+    own = own_part(pages, own_len, q, new_kv, own_kv.reshape(2, POOL * PAGE, HD))
+    parts, own, w_out_c = tie((parts, own, swap(w_out)))
+    place = (lax.axis_index(SPARSE) % 4).astype(jnp.int32).reshape(1)
+    attn = exchange(join_part(place, parts, *own), PLANE).reshape(rows, GROUP * HD)
     res = resid.reshape(CHIPS, 2, ROWS, HD)
     mine = jnp.where(core == 0, res[:, 0], res[:, 1])
     theirs = swap(jnp.where(core == 0, res[:, 1], res[:, 0]))
-    res2 = jnp.concatenate([mine, theirs], axis=-1).reshape(CHIPS * ROWS, 2 * HD)
-
-    acc, top, total = own_part(pages, own_len, q, new_kv, own_kv.reshape(2, POOL * PAGE, HD))
-    q_all = exchange(jnp.broadcast_to(q[None], (PEERS, QROWS, HD)), SPARSE).reshape(PEERS * QROWS, HD)
-    parts = exchange(man_part(q_all, kv), SPARSE)
-    place = (lax.axis_index(SPARSE) % 4).astype(jnp.int32).reshape(1)
-    attn = exchange(join_part(place, parts, acc, top, total), PLANE).reshape(CHIPS * ROWS, GROUP * HD)
-    attn, w_pair = lax.optimization_barrier((attn, w_pair))
-    w_pair2 = jnp.concatenate([w_pair, swap(w_pair)], axis=0)
-
-    partial_out = jnp.dot(attn, w_out2, preferred_element_type=F32).astype(BF)
-    heads = exchange(jnp.broadcast_to(partial_out[None], (8, *partial_out.shape)), HEAD)
-    out2 = (res2.astype(F32) + heads.astype(F32).sum(0)).astype(BF)
-
-    z = jnp.dot(out2, w_keep2, preferred_element_type=F32)
-    z = (z + jnp.dot(pair(out2), w_pair2, preferred_element_type=F32)).astype(BF)
-    joined = exchange(z.reshape(CHIPS, ROWS, width), PLANE).reshape(PEERS, 2, ROWS, width)
-    joined = joined.astype(F32).sum(0)
-    hidden = (jax.nn.silu(joined[0]) * joined[1]).astype(BF)
+    res = jnp.concatenate([mine, theirs], axis=-1).reshape(rows, 2 * HD).astype(F32)
+    attn, w_gate_c, w_up_c, res = tie((attn, swap(w_gate), swap(w_up), res))
+
+    heads = exchange(dense(project_kernel, "project", (8, rows, 2 * HD), attn, w_out, w_out_c), HEAD)
+    out2 = (res + heads.astype(F32).sum(0)).astype(BF)
+    both = dense(mlp_kernel, "gate_up", (CHIPS, 2 * ROWS, width), out2, w_gate, w_gate_c, w_up, w_up_c)
+    joined = exchange(both, PLANE).astype(F32).sum(0)
+    hidden = (jax.nn.silu(joined[:ROWS]) * joined[ROWS:]).astype(BF)
 
     kept = out2[:, :HD].reshape(CHIPS, 1, ROWS, HD)
     given = swap(out2[:, HD:]).reshape(CHIPS, 1, ROWS, HD)

time: 124 us -> 123 us (level)
  the two profiles are of different devices: /device:TPU:8 before, /device:TPU:16 now
where the time goes in v6:
time: 123 us
  starting transfers between devices  45.5 us (37%)
  waiting for transfers between devices  35.6 us (29%)
  blocking collectives  31.5 us (26%)
  Pallas kernels  5.87 us (5%)
  local copies, waits for them, and re-layouts  2.3 us (2%)
    all_to_all x4, starting transfers between devices, exchange(): return lax.all_to_all(x, axes, 0, 0, tiled=True)  35.4 us
    all_to_all x4, waiting for transfers between devices, exchange(): return lax.all_to_all(x, axes, 0, 0, tiled=True)  33.1 us
    all_to_all x1, blocking collectives, exchange(): return lax.all_to_all(x, axes, 0, 0, tiled=True)  24.4 us
    ppermute x5, starting transfers between devices, swap(): return lax.ppermute(x, 'c', [(0, 1), (1, 0)])  10.1 us
    all_gather x1, blocking collectives, on_device(): lax.all_gather(man_kv.reshape(1, 2, 2 * PAGE, HD), ('p', 'c'), axis=0, ti...  7.1 us
    ppermute x5, waiting for transfers between devices, swap(): return lax.ppermute(x, 'c', [(0, 1), (1, 0)])  2.56 us
  transfers between devices with their start and end apart: 9, of which 7 were waited for; matrix products, arithmetic and copies ran while one was open for 1% of the time, Pallas kernels for 1%

profile of v6, /device:TPU:16, one launch (start us, length us, event | category | flops | bytes accessed | tf_op | source)
XLA Modules:
  0.0 122.6 jit_solution(6599418695779065698)
XLA Ops:
  0.7 0.8 broadcast_in_dim.7.q_ref
  1.5 0.7 broadcast_in_dim.8
  2.2 11.1 %all-to-all-start = ((bf16[16,32,128]{2,1,0:T(8,128)(2,1)}), bf16[16,32,128]{2,1,0:T(8,128)(2,1)S(1)}, u32[]{:S(2)}, u32[]{:S(2)}) async-start(bf16[16,32,128]{2,1,0:T(8,128)(2,1)} %broadcast_in_dim.8), calls=%async_computation | async-start | bytes 262144 | tf_op jit(solution)/shard_map/all_to_all | solution.py:172
  13.2 7.1 %all_gather.3.kv_ref = bf16[4,2,128,128]{3,2,1,0:T(8,128)(2,1)S(1)} all-gather(bf16[1,2,128,128]{3,2,1,0:T(8,128)(2,1)} %bitcast.28), channel_id=1, replica_groups=mesh['y'=8,'zq'=2,'p'=2,'c'=2,'zh'=2,'x'=4] {'p','c'}, dimensions={0}, use_global_device_ids=true | all-gather | bytes 327680 | tf_op jit(solution)/shard_map/all_gather | solution.py:182
  20.3 1.2 %all-to-all-done = bf16[16,32,128]{2,1,0:T(8,128)(2,1)S(1)} async-done(((bf16[16,32,128]{2,1,0:T(8,128)(2,1)}), bf16[16,32,128]{2,1,0:T(8,128)(2,1)S(1)}, u32[]{:S(2)}, u32[]{:S(2)}) %all-to-all-start) | async-done | bytes 131104 | tf_op jit(solution)/shard_map/all_to_all | solution.py:172
  21.6 1.7 %manifest_attention.1 = bf16[16,40,128]{2,1,0:T(8,128)(2,1)} custom-call(bf16[512,128]{1,0:T(8,128)(2,1)S(1)} %bitcast.25, bf16[4,2,128,128]{3,2,1,0:T(8,128)(2,1)S(1)} %all_gather.3.kv_ref), custom_call_target="tpu_custom_call" | custom-call | tf_op jit(solution)/shard_map/manifest_attention/pallas_call | solution.py:91
  23.2 8.1 %all-to-all-start.1 = ((bf16[16,40,128]{2,1,0:T(8,128)(2,1)}), bf16[16,40,128]{2,1,0:T(8,128)(2,1)S(1)}, u32[]{:S(2)}, u32[]{:S(2)}) async-start(bf16[16,40,128]{2,1,0:T(8,128)(2,1)} %manifest_attention.1), calls=%async_computation.1 | async-start | bytes 327680 | tf_op jit(solution)/shard_map/all_to_all | solution.py:172
  31.4 1.9 %collective-permute-start = (bf16[1024,128]{1,0:T(8,128)(2,1)S(1)}, bf16[1024,128]{1,0:T(8,128)(2,1)S(1)}, u32[]{:S(2)}, u32[]{:S(2)}) collective-permute-start(bf16[1024,128]{1,0:T(8,128)(2,1)S(1)} %copy-done.3), channel_id=1, source_target_pairs={{0,8},{8,0},{1,9},{9,1},{2,10},{10,2},{3,11},{11,3},{4,12},{12,4},... | collective-permute-start | bytes 786440 | tf_op jit(solution)/shard_map/ppermute | solution.py:168
  33.3 0.0 copy-start.1
  33.3 0.0 copy-start.2
  33.4 1.2 own_attention.1
  34.6 0.2 collective-permute-done.w1_ref
  34.8 6.3 %all-to-all-done.1.parts_ref = bf16[16,40,128]{2,1,0:T(8,128)(2,1)S(1)} async-done(((bf16[16,40,128]{2,1,0:T(8,128)(2,1)}), bf16[16,40,128]{2,1,0:T(8,128)(2,1)S(1)}, u32[]{:S(2)}, u32[]{:S(2)}) %all-to-all-start.1) | async-done | bytes 163872 | tf_op jit(solution)/shard_map/all_to_all | solution.py:172
  41.0 1.4 %join_attention.1 = bf16[32,4,1024]{2,1,0:T(4,128)(2,1)} custom-call(s32[1]{0:T(128)} %bitcast.place_ref, bf16[16,40,128]{2,1,0:T(8,128)(2,1)S(1)} %all-to-all-done.1.parts_ref, f32[32,128]{1,0:T(8,128)S(1)} %get-tuple-element.18.acc_ref, f32[32,128]{1,0:T(8,128)S(1)} %get-tuple-element.19.top_ref, f32[32,128]{1,0:T(8,128)S(1)} %get-tuple-element.20.total_ref), custom_call_target="tpu_custom_call" | custom-call | tf_op jit(solution)/shard_map/join_attention/pallas_call | solution.py:128
  42.4 5.5 %all-to-all-start.2 = ((bf16[32,4,1024]{2,1,0:T(4,128)(2,1)}), bf16[32,4,1024]{2,1,0:T(4,128)(2,1)S(1)}, u32[]{:S(2)}, u32[]{:S(2)}) async-start(bf16[32,4,1024]{2,1,0:T(4,128)(2,1)} %join_attention.1), calls=%async_computation.2 | async-start | bytes 524288 | tf_op jit(solution)/shard_map/all_to_all | solution.py:172
  48.0 1.9 %collective-permute-start.1 = (bf16[128,1792]{1,0:T(8,128)(2,1)S(1)}, bf16[128,1792]{1,0:T(8,128)(2,1)S(1)}, u32[]{:S(2)}, u32[]{:S(2)}) collective-permute-start(bf16[128,1792]{1,0:T(8,128)(2,1)S(1)} %copy-done.1), channel_id=1, source_target_pairs={{0,8},{8,0},{1,9},{9,1},{2,10},{10,2},{3,11},{11,3},{4,12},{12,4},... | collective-permute-start | bytes 1376264 | tf_op jit(solution)/shard_map/ppermute | solution.py:168
  49.9 2.4 %collective-permute-start.2 = (bf16[128,1792]{1,0:T(8,128)(2,1)S(1)}, bf16[128,1792]{1,0:T(8,128)(2,1)S(1)}, u32[]{:S(2)}, u32[]{:S(2)}) collective-permute-start(bf16[128,1792]{1,0:T(8,128)(2,1)S(1)} %copy-done.2), channel_id=1, source_target_pairs={{0,8},{8,0},{1,9},{9,1},{2,10},{10,2},{3,11},{11,3},{4,12},{12,4},... | collective-permute-start | bytes 1376264 | tf_op jit(solution)/shard_map/ppermute | solution.py:168
  52.4 1.9 %collective-permute-start.3 = (bf16[32,4,128]{2,1,0:T(4,128)(2,1)S(1)}, bf16[32,4,128]{2,1,0:T(4,128)(2,1)S(1)}, u32[]{:S(2)}, u32[]{:S(2)}) collective-permute-start(bf16[32,4,128]{2,1,0:T(4,128)(2,1)S(1)} %get-tuple-element.29), channel_id=1, source_target_pairs={{0,8},{8,0},{1,9},{9,1},{2,10},{10,2},{3,11},{11,3},{4,12},{12,4},... | collective-permute-start | bytes 98312 | tf_op jit(solution)/shard_map/ppermute | solution.py:168
  54.3 1.2 collective-permute-done.3
  55.6 3.5 %all-to-all-done.2 = bf16[32,4,1024]{2,1,0:T(4,128)(2,1)S(1)} async-done(((bf16[32,4,1024]{2,1,0:T(4,128)(2,1)}), bf16[32,4,1024]{2,1,0:T(4,128)(2,1)S(1)}, u32[]{:S(2)}, u32[]{:S(2)}) %all-to-all-start.2) | async-done | bytes 262176 | tf_op jit(solution)/shard_map/all_to_all | solution.py:172
  59.1 0.1 reshape.84.x_ref
  59.2 0.2 project.1
  59.5 24.4 %all_to_all.25 = bf16[8,128,256]{2,1,0:T(8,128)(2,1)S(1)} all-to-all(bf16[8,128,256]{2,1,0:T(8,128)(2,1)S(1)} %project.1), channel_id=1, replica_groups=mesh['y'=8,'zq'=2,'p'=2,'c'=2,'zh'=2,'x'=4] {'zh','x'}, dimensions={0} | all-to-all | bytes 1048576 | tf_op jit(solution)/shard_map/all_to_all | solution.py:172
  83.9 0.1 convert_reduce_fusion.1
  83.9 1.4 %gate_up.1 = bf16[32,8,1792]{2,1,0:T(8,128)(2,1)} custom-call(bf16[128,256]{1,0:T(8,128)(2,1)S(1)} %add_convert_fusion.x_ref, bf16[128,1792]{1,0:T(8,128)(2,1)S(1)} %copy-done.1, bf16[128,1792]{1,0:T(8,128)(2,1)S(1)} %collective-permute-done.1.g1_ref, bf16[128,1792]{1,0:T(8,128)(2,1)S(1)} %copy-done.2, bf16[128,1792]{1,0:T(8,128)(2,1)S(1)} %collective-permute-done.2.u1_ref), custom_call_target="tpu_custom_call" | custom-call | tf_op jit(solution)/shard_map/gate_up/pallas_call | solution.py:157
  85.3 10.7 %all-to-all-start.4 = ((bf16[32,8,1792]{2,1,0:T(8,128)(2,1)}), bf16[32,8,1792]{2,1,0:T(8,128)(2,1)S(1)}, u32[]{:S(2)}, u32[]{:S(2)}) async-start(bf16[32,8,1792]{2,1,0:T(8,128)(2,1)} %gate_up.1), calls=%async_computation.4 | async-start | bytes 1835008 | tf_op jit(solution)/shard_map/all_to_all | solution.py:172
  96.0 1.9 %collective-permute-start.4 = (bf16[128,128]{1,0:T(8,128)(2,1)S(1)}, bf16[128,128]{1,0:T(8,128)(2,1)S(1)}, u32[]{:S(2)}, u32[]{:S(2)}) collective-permute-start(bf16[128,128]{1,0:T(8,128)(2,1)S(1)} %slice.29), channel_id=1, source_target_pairs={{0,8},{8,0},{1,9},{9,1},{2,10},{10,2},{3,11},{11,3},{4,12},{12,4},... | collective-permute-start | bytes 98312 | tf_op jit(solution)/shard_map/ppermute | solution.py:168
  98.0 1.2 collective-permute-done.4
  99.2 0.7 copy.17
  99.9 22.0 %all-to-all-done.4 = bf16[32,8,1792]{2,1,0:T(8,128)(2,1)S(1)} async-done(((bf16[32,8,1792]{2,1,0:T(8,128)(2,1)}), bf16[32,8,1792]{2,1,0:T(8,128)(2,1)S(1)}, u32[]{:S(2)}, u32[]{:S(2)}) %all-to-all-start.4) | async-done | bytes 917536 | tf_op jit(solution)/shard_map/all_to_all | solution.py:172
  121.9 0.1 convert_reduce_fusion
  122.0 0.6 fusion.1
  (23 shorter events, 0.2 us)
Async XLA Ops:
  0.6 30.7 %copy-start.3 = (bf16[1024,128]{1,0:T(8,128)(2,1)S(1)}, bf16[1024,128]{1,0:T(8,128)(2,1)}, u32[]{:S(2)}) copy-start(bf16[1024,128]{1,0:T(8,128)(2,1)} %w0_ref.1) | copy-start | bytes 786436
  0.6 32.7 %copy-start.6 = (s32[4]{0:T(128)S(1)}, s32[4]{0:T(128)}, u32[]{:S(2)}) copy-start(s32[4]{0:T(128)} %len_ref.1) | copy-start | bytes 52
  0.7 32.7 %copy-start.4 = (s32[4,8]{1,0:T(4,128)S(1)}, s32[4,8]{1,0:T(4,128)}, u32[]{:S(2)}) copy-start(s32[4,8]{1,0:T(4,128)} %pages_ref.1) | copy-start | bytes 388
  0.7 32.7 %copy-start = (bf16[2,32,64,128]{3,2,1,0:T(8,128)(2,1)S(1)}, bf16[2,32,64,128]{3,2,1,0:T(8,128)(2,1)}, u32[]{:S(2)}) copy-start(bf16[2,32,64,128]{3,2,1,0:T(8,128)(2,1)} %param.12) | copy-start | bytes 3145732
  0.7 32.7 %copy-start.5 = (bf16[2,4,128]{2,1,0:T(4,128)(2,1)S(1)}, bf16[2,4,128]{2,1,0:T(4,128)(2,1)}, u32[]{:S(2)}) copy-start(bf16[2,4,128]{2,1,0:T(4,128)(2,1)} %new_ref.1) | copy-start | bytes 6148
  2.2 19.4 %all-to-all-start = ((bf16[16,32,128]{2,1,0:T(8,128)(2,1)}), bf16[16,32,128]{2,1,0:T(8,128)(2,1)S(1)}, u32[]{:S(2)}, u32[]{:S(2)}) async-start(bf16[16,32,128]{2,1,0:T(8,128)(2,1)} %broadcast_in_dim.8), calls=%async_computation | async-start | bytes 262144 | tf_op jit(solution)/shard_map/all_to_all | solution.py:172
  23.2 17.8 %all-to-all-start.1 = ((bf16[16,40,128]{2,1,0:T(8,128)(2,1)}), bf16[16,40,128]{2,1,0:T(8,128)(2,1)S(1)}, u32[]{:S(2)}, u32[]{:S(2)}) async-start(bf16[16,40,128]{2,1,0:T(8,128)(2,1)} %manifest_attention.1), calls=%async_computation.1 | async-start | bytes 327680 | tf_op jit(solution)/shard_map/all_to_all | solution.py:172
  31.4 3.4 %collective-permute-start = (bf16[1024,128]{1,0:T(8,128)(2,1)S(1)}, bf16[1024,128]{1,0:T(8,128)(2,1)S(1)}, u32[]{:S(2)}, u32[]{:S(2)}) collective-permute-start(bf16[1024,128]{1,0:T(8,128)(2,1)S(1)} %copy-done.3), channel_id=1, source_target_pairs={{0,8},{8,0},{1,9},{9,1},{2,10},{10,2},{3,11},{11,3},{4,12},{12,4},... | collective-permute-start | bytes 786440 | tf_op jit(solution)/shard_map/ppermute | solution.py:168
  33.3 14.7 %copy-start.1 = (bf16[128,1792]{1,0:T(8,128)(2,1)S(1)}, bf16[128,1792]{1,0:T(8,128)(2,1)}, u32[]{:S(2)}) copy-start(bf16[128,1792]{1,0:T(8,128)(2,1)} %g0_ref.1) | copy-start | bytes 1376260
  33.3 16.6 %copy-start.2 = (bf16[128,1792]{1,0:T(8,128)(2,1)S(1)}, bf16[128,1792]{1,0:T(8,128)(2,1)}, u32[]{:S(2)}) copy-start(bf16[128,1792]{1,0:T(8,128)(2,1)} %u0_ref.1) | copy-start | bytes 1376260
  33.3 19.0 %copy-start.7 = (bf16[256,128]{1,0:T(8,128)(2,1)S(1)}, bf16[256,128]{1,0:T(8,128)(2,1)}, u32[]{:S(2)}) copy-start(bf16[256,128]{1,0:T(8,128)(2,1)} %param.16) | copy-start | bytes 196612
  42.4 16.7 %all-to-all-start.2 = ((bf16[32,4,1024]{2,1,0:T(4,128)(2,1)}), bf16[32,4,1024]{2,1,0:T(4,128)(2,1)S(1)}, u32[]{:S(2)}, u32[]{:S(2)}) async-start(bf16[32,4,1024]{2,1,0:T(4,128)(2,1)} %join_attention.1), calls=%async_computation.2 | async-start | bytes 524288 | tf_op jit(solution)/shard_map/all_to_all | solution.py:172
  48.0 11.2 %collective-permute-start.1 = (bf16[128,1792]{1,0:T(8,128)(2,1)S(1)}, bf16[128,1792]{1,0:T(8,128)(2,1)S(1)}, u32[]{:S(2)}, u32[]{:S(2)}) collective-permute-start(bf16[128,1792]{1,0:T(8,128)(2,1)S(1)} %copy-done.1), channel_id=1, source_target_pairs={{0,8},{8,0},{1,9},{9,1},{2,10},{10,2},{3,11},{11,3},{4,12},{12,4},... | collective-permute-start | bytes 1376264 | tf_op jit(solution)/shard_map/ppermute | solution.py:168
  49.9 9.3 %collective-permute-start.2 = (bf16[128,1792]{1,0:T(8,128)(2,1)S(1)}, bf16[128,1792]{1,0:T(8,128)(2,1)S(1)}, u32[]{:S(2)}, u32[]{:S(2)}) collective-permute-start(bf16[128,1792]{1,0:T(8,128)(2,1)S(1)} %copy-done.2), channel_id=1, source_target_pairs={{0,8},{8,0},{1,9},{9,1},{2,10},{10,2},{3,11},{11,3},{4,12},{12,4},... | collective-permute-start | bytes 1376264 | tf_op jit(solution)/shard_map/ppermute | solution.py:168
  52.4 3.1 %collective-permute-start.3 = (bf16[32,4,128]{2,1,0:T(4,128)(2,1)S(1)}, bf16[32,4,128]{2,1,0:T(4,128)(2,1)S(1)}, u32[]{:S(2)}, u32[]{:S(2)}) collective-permute-start(bf16[32,4,128]{2,1,0:T(4,128)(2,1)S(1)} %get-tuple-element.29), channel_id=1, source_target_pairs={{0,8},{8,0},{1,9},{9,1},{2,10},{10,2},{3,11},{11,3},{4,12},{12,4},... | collective-permute-start | bytes 98312 | tf_op jit(solution)/shard_map/ppermute | solution.py:168
  85.3 36.6 %all-to-all-start.4 = ((bf16[32,8,1792]{2,1,0:T(8,128)(2,1)}), bf16[32,8,1792]{2,1,0:T(8,128)(2,1)S(1)}, u32[]{:S(2)}, u32[]{:S(2)}) async-start(bf16[32,8,1792]{2,1,0:T(8,128)(2,1)} %gate_up.1), calls=%async_computation.4 | async-start | bytes 1835008 | tf_op jit(solution)/shard_map/all_to_all | solution.py:172
  96.0 3.1 %collective-permute-start.4 = (bf16[128,128]{1,0:T(8,128)(2,1)S(1)}, bf16[128,128]{1,0:T(8,128)(2,1)S(1)}, u32[]{:S(2)}, u32[]{:S(2)}) collective-permute-start(bf16[128,128]{1,0:T(8,128)(2,1)S(1)} %slice.29), channel_id=1, source_target_pairs={{0,8},{8,0},{1,9},{9,1},{2,10},{10,2},{3,11},{11,3},{4,12},{12,4},... | collective-permute-start | bytes 98312 | tf_op jit(solution)/shard_map/ppermute | solution.py:168

commit v7 on v6

--- a/solution.py
+++ b/solution.py
@@ -138,9 +138,13 @@
 
 def project_kernel(x_ref, w0_ref, w1_ref, out_ref):
     w = jnp.concatenate([w0_ref[...], w1_ref[...]], axis=1)
-    y = dot(x_ref[...], w, 1, 0).astype(BF)
-    for i in range(8):
-        out_ref[i] = y
+    out_ref[...] = dot(x_ref[...], w, 1, 0).astype(BF)
+
+
+def add_kernel(a_ref, b_ref, out_ref):
+    block = (a_ref[...].astype(F32) + b_ref[...].astype(F32)).astype(BF)
+    for i in range(4):
+        out_ref[i] = block
 
 
 def mlp_kernel(x_ref, g0_ref, g1_ref, u0_ref, u1_ref, out_ref):
@@ -191,7 +195,9 @@
     res = jnp.concatenate([mine, theirs], axis=-1).reshape(rows, 2 * HD).astype(F32)
     attn, w_gate_c, w_up_c, res = tie((attn, swap(w_gate), swap(w_up), res))
 
-    heads = exchange(dense(project_kernel, "project", (8, rows, 2 * HD), attn, w_out, w_out_c), HEAD)
+    share = dense(project_kernel, "project", (rows, 2 * HD), attn, w_out, w_out_c)
+    share2 = lax.ppermute(share, "zh", [(0, 1), (1, 0)])
+    heads = exchange(dense(add_kernel, "add_shares", (4, rows, 2 * HD), share, share2), "x")
     out2 = (res + heads.astype(F32).sum(0)).astype(BF)
     both = dense(mlp_kernel, "gate_up", (CHIPS, 2 * ROWS, width), out2, w_gate, w_gate_c, w_up, w_up_c)
     joined = exchange(both, PLANE).astype(F32).sum(0)

time: 123 us -> 116 us (0.943)
  blocking collectives: 31.5 us -> 17.9 us
  starting transfers between devices: 45.5 us -> 50.5 us
    all_to_all x1, blocking collectives: 24.4 us -> 10.8 us  [exchange(): return lax.all_to_all(x, axes, 0, 0, tiled=True)]
    ppermute x0 -> x1, starting transfers between devices: none -> 8.22 us  [on_device(): share2 = lax.ppermute(share, 'zh', [(0, 1), (1, 0)])]
    all_to_all x4, starting transfers between devices: 35.4 us -> 32.2 us  [exchange(): return lax.all_to_all(x, axes, 0, 0, tiled=True)]
    ppermute x0 -> x1, waiting for transfers between devices: none -> 2.23 us  [on_device(): share2 = lax.ppermute(share, 'zh', [(0, 1), (1, 0)])]
    all_to_all x4, waiting for transfers between devices: 33.1 us -> 31.8 us  [exchange(): return lax.all_to_all(x, axes, 0, 0, tiled=True)]
  transfers between devices with their start and end apart: 9 -> 10, of which waited for: 7 -> 8; matrix products, arithmetic and copies ran while one was open for 1% -> 1% of each run, Pallas kernels for 1% -> 1%
where the time goes in v7:
time: 116 us; the launch traced here: 115 us
  starting transfers between devices  50.5 us (44%)
  waiting for transfers between devices  36.6 us (32%)
  blocking collectives  17.9 us (15%)
  Pallas kernels  5.84 us (5%)
  local copies, waits for them, and re-layouts  2.28 us (2%)
    all_to_all x4, starting transfers between devices, exchange(): return lax.all_to_all(x, axes, 0, 0, tiled=True)  32.2 us
    all_to_all x4, waiting for transfers between devices, exchange(): return lax.all_to_all(x, axes, 0, 0, tiled=True)  31.8 us
    all_to_all x1, blocking collectives, exchange(): return lax.all_to_all(x, axes, 0, 0, tiled=True)  10.8 us
    ppermute x5, starting transfers between devices, swap(): return lax.ppermute(x, 'c', [(0, 1), (1, 0)])  10.1 us
    ppermute x1, starting transfers between devices, on_device(): share2 = lax.ppermute(share, 'zh', [(0, 1), (1, 0)])  8.22 us
    all_gather x1, blocking collectives, on_device(): lax.all_gather(man_kv.reshape(1, 2, 2 * PAGE, HD), ('p', 'c'), axis=0, ti...  7.1 us
    ppermute x5, waiting for transfers between devices, swap(): return lax.ppermute(x, 'c', [(0, 1), (1, 0)])  2.56 us
  transfers between devices with their start and end apart: 10, of which 8 were waited for; matrix products, arithmetic and copies ran while one was open for 1% of the time, Pallas kernels for 1%

profile of v7, /device:TPU:16, one launch (start us, length us, event | category | flops | bytes accessed | tf_op | source)
XLA Modules:
  0.0 115.0 jit_solution(2858576404633365391)
XLA Ops:
  0.7 0.8 broadcast_in_dim.7.q_ref
  1.5 0.7 broadcast_in_dim.8
  2.2 11.1 %all-to-all-start = ((bf16[16,32,128]{2,1,0:T(8,128)(2,1)}), bf16[16,32,128]{2,1,0:T(8,128)(2,1)S(1)}, u32[]{:S(2)}, u32[]{:S(2)}) async-start(bf16[16,32,128]{2,1,0:T(8,128)(2,1)} %broadcast_in_dim.8), calls=%async_computation | async-start | bytes 262144 | tf_op jit(solution)/shard_map/all_to_all | solution.py:176
  13.2 7.1 %all_gather.3.kv_ref = bf16[4,2,128,128]{3,2,1,0:T(8,128)(2,1)S(1)} all-gather(bf16[1,2,128,128]{3,2,1,0:T(8,128)(2,1)} %bitcast.28), channel_id=1, replica_groups=mesh['y'=8,'zq'=2,'p'=2,'c'=2,'zh'=2,'x'=4] {'p','c'}, dimensions={0}, use_global_device_ids=true | all-gather | bytes 327680 | tf_op jit(solution)/shard_map/all_gather | solution.py:186
  20.3 1.2 %all-to-all-done = bf16[16,32,128]{2,1,0:T(8,128)(2,1)S(1)} async-done(((bf16[16,32,128]{2,1,0:T(8,128)(2,1)}), bf16[16,32,128]{2,1,0:T(8,128)(2,1)S(1)}, u32[]{:S(2)}, u32[]{:S(2)}) %all-to-all-start) | async-done | bytes 131104 | tf_op jit(solution)/shard_map/all_to_all | solution.py:176
  21.6 1.6 %manifest_attention.1 = bf16[16,40,128]{2,1,0:T(8,128)(2,1)} custom-call(bf16[512,128]{1,0:T(8,128)(2,1)S(1)} %bitcast.25, bf16[4,2,128,128]{3,2,1,0:T(8,128)(2,1)S(1)} %all_gather.3.kv_ref), custom_call_target="tpu_custom_call" | custom-call | tf_op jit(solution)/shard_map/manifest_attention/pallas_call | solution.py:91
  23.2 8.1 %all-to-all-start.1 = ((bf16[16,40,128]{2,1,0:T(8,128)(2,1)}), bf16[16,40,128]{2,1,0:T(8,128)(2,1)S(1)}, u32[]{:S(2)}, u32[]{:S(2)}) async-start(bf16[16,40,128]{2,1,0:T(8,128)(2,1)} %manifest_attention.1), calls=%async_computation.1 | async-start | bytes 327680 | tf_op jit(solution)/shard_map/all_to_all | solution.py:176
  31.3 1.9 %collective-permute-start = (bf16[1024,128]{1,0:T(8,128)(2,1)S(1)}, bf16[1024,128]{1,0:T(8,128)(2,1)S(1)}, u32[]{:S(2)}, u32[]{:S(2)}) collective-permute-start(bf16[1024,128]{1,0:T(8,128)(2,1)S(1)} %copy-done.3), channel_id=1, source_target_pairs={{0,8},{8,0},{1,9},{9,1},{2,10},{10,2},{3,11},{11,3},{4,12},{12,4},... | collective-permute-start | bytes 786440 | tf_op jit(solution)/shard_map/ppermute | solution.py:172
  33.3 0.0 copy-start.1
  33.3 1.2 %own_attention.1 = (f32[32,128]{1,0:T(8,128)S(1)}, f32[32,128]{1,0:T(8,128)S(1)}, f32[32,128]{1,0:T(8,128)S(1)}) custom-call(s32[4,8]{1,0:T(4,128)S(1)} %copy-done.4, s32[4]{0:T(128)S(1)} %copy-done.6, bf16[32,128]{1,0:T(8,128)(2,1)S(1)} %broadcast_in_dim.7.q_ref, bf16[2,4,128]{2,1,0:T(4,128)(2,1)S(1)} %copy-done.5, bf16[2,2048,128]{2,1,0:T(8,128)(2,1)S(1)} %bitcast.24), custom_call_target="tpu_custom_call" | custom-call | tf_op jit(solution)/shard_map/own_attention/pallas_call | solution.py:60
  34.5 0.2 collective-permute-done.w1_ref
  34.8 6.3 %all-to-all-done.1.parts_ref = bf16[16,40,128]{2,1,0:T(8,128)(2,1)S(1)} async-done(((bf16[16,40,128]{2,1,0:T(8,128)(2,1)}), bf16[16,40,128]{2,1,0:T(8,128)(2,1)S(1)}, u32[]{:S(2)}, u32[]{:S(2)}) %all-to-all-start.1) | async-done | bytes 163872 | tf_op jit(solution)/shard_map/all_to_all | solution.py:176
  41.0 1.4 %join_attention.1 = bf16[32,4,1024]{2,1,0:T(4,128)(2,1)} custom-call(s32[1]{0:T(128)} %bitcast.place_ref, bf16[16,40,128]{2,1,0:T(8,128)(2,1)S(1)} %all-to-all-done.1.parts_ref, f32[32,128]{1,0:T(8,128)S(1)} %get-tuple-element.18.acc_ref, f32[32,128]{1,0:T(8,128)S(1)} %get-tuple-element.19.top_ref, f32[32,128]{1,0:T(8,128)S(1)} %get-tuple-element.20.total_ref), custom_call_target="tpu_custom_call" | custom-call | tf_op jit(solution)/shard_map/join_attention/pallas_call | solution.py:128
  42.4 5.5 %all-to-all-start.2 = ((bf16[32,4,1024]{2,1,0:T(4,128)(2,1)}), bf16[32,4,1024]{2,1,0:T(4,128)(2,1)S(1)}, u32[]{:S(2)}, u32[]{:S(2)}) async-start(bf16[32,4,1024]{2,1,0:T(4,128)(2,1)} %join_attention.1), calls=%async_computation.2 | async-start | bytes 524288 | tf_op jit(solution)/shard_map/all_to_all | solution.py:176
  48.0 1.9 %collective-permute-start.1 = (bf16[128,1792]{1,0:T(8,128)(2,1)S(1)}, bf16[128,1792]{1,0:T(8,128)(2,1)S(1)}, u32[]{:S(2)}, u32[]{:S(2)}) collective-permute-start(bf16[128,1792]{1,0:T(8,128)(2,1)S(1)} %copy-done.1), channel_id=1, source_target_pairs={{0,8},{8,0},{1,9},{9,1},{2,10},{10,2},{3,11},{11,3},{4,12},{12,4},... | collective-permute-start | bytes 1376264 | tf_op jit(solution)/shard_map/ppermute | solution.py:172
  49.9 2.4 %collective-permute-start.2 = (bf16[128,1792]{1,0:T(8,128)(2,1)S(1)}, bf16[128,1792]{1,0:T(8,128)(2,1)S(1)}, u32[]{:S(2)}, u32[]{:S(2)}) collective-permute-start(bf16[128,1792]{1,0:T(8,128)(2,1)S(1)} %copy-done.2), channel_id=1, source_target_pairs={{0,8},{8,0},{1,9},{9,1},{2,10},{10,2},{3,11},{11,3},{4,12},{12,4},... | collective-permute-start | bytes 1376264 | tf_op jit(solution)/shard_map/ppermute | solution.py:172
  52.4 1.9 %collective-permute-start.3 = (bf16[32,4,128]{2,1,0:T(4,128)(2,1)S(1)}, bf16[32,4,128]{2,1,0:T(4,128)(2,1)S(1)}, u32[]{:S(2)}, u32[]{:S(2)}) collective-permute-start(bf16[32,4,128]{2,1,0:T(4,128)(2,1)S(1)} %get-tuple-element.29), channel_id=1, source_target_pairs={{0,8},{8,0},{1,9},{9,1},{2,10},{10,2},{3,11},{11,3},{4,12},{12,4},... | collective-permute-start | bytes 98312 | tf_op jit(solution)/shard_map/ppermute | solution.py:172
  54.3 1.2 %collective-permute-done.3 = bf16[32,4,128]{2,1,0:T(4,128)(2,1)S(1)} collective-permute-done((bf16[32,4,128]{2,1,0:T(4,128)(2,1)S(1)}, bf16[32,4,128]{2,1,0:T(4,128)(2,1)S(1)}, u32[]{:S(2)}, u32[]{:S(2)}) %collective-permute-start.3) | collective-permute-done | bytes 32800 | tf_op jit(solution)/shard_map/ppermute | solution.py:172
  55.5 3.5 %all-to-all-done.2 = bf16[32,4,1024]{2,1,0:T(4,128)(2,1)S(1)} async-done(((bf16[32,4,1024]{2,1,0:T(4,128)(2,1)}), bf16[32,4,1024]{2,1,0:T(4,128)(2,1)S(1)}, u32[]{:S(2)}, u32[]{:S(2)}) %all-to-all-start.2) | async-done | bytes 262176 | tf_op jit(solution)/shard_map/all_to_all | solution.py:176
  59.1 0.1 reshape.84.x_ref
  59.2 0.2 project.1.a_ref
  59.4 8.2 %collective-permute-start.4 = (bf16[128,256]{1,0:T(8,128)(2,1)S(1)}, bf16[128,256]{1,0:T(8,128)(2,1)S(1)}, u32[]{:S(2)}, u32[]{:S(2)}) collective-permute-start(bf16[128,256]{1,0:T(8,128)(2,1)S(1)} %project.1.a_ref), channel_id=1, source_target_pairs={{0,4},{4,0},{1,5},{5,1},{2,6},{6,2},{3,7},{7,3},{8,12},{12,8},{9,1... | collective-permute-start | bytes 196616 | tf_op jit(solution)/shard_map/ppermute | solution.py:199
  67.6 2.2 %collective-permute-done.4.b_ref = bf16[128,256]{1,0:T(8,128)(2,1)S(1)} collective-permute-done((bf16[128,256]{1,0:T(8,128)(2,1)S(1)}, bf16[128,256]{1,0:T(8,128)(2,1)S(1)}, u32[]{:S(2)}, u32[]{:S(2)}) %collective-permute-start.4) | collective-permute-done | bytes 65568 | tf_op jit(solution)/shard_map/ppermute | solution.py:199
  69.9 10.8 %all_to_all.25 = bf16[4,128,256]{2,1,0:T(8,128)(2,1)S(1)} all-to-all(bf16[4,128,256]{2,1,0:T(8,128)(2,1)S(1)} %add_shares.1), channel_id=1, replica_groups=mesh['y'=8,'zq'=2,'p'=2,'c'=2,'zh'=2,'x'=4] {'x'}, dimensions={0} | all-to-all | bytes 524288 | tf_op jit(solution)/shard_map/all_to_all | solution.py:176
  80.7 1.4 %gate_up.1 = bf16[32,8,1792]{2,1,0:T(8,128)(2,1)} custom-call(bf16[128,256]{1,0:T(8,128)(2,1)S(1)} %add_convert_fusion.x_ref, bf16[128,1792]{1,0:T(8,128)(2,1)S(1)} %copy-done.1, bf16[128,1792]{1,0:T(8,128)(2,1)S(1)} %collective-permute-done.1.g1_ref, bf16[128,1792]{1,0:T(8,128)(2,1)S(1)} %copy-done.2, bf16[128,1792]{1,0:T(8,128)(2,1)S(1)} %collective-permute-done.2.u1_ref), custom_call_target="tpu_custom_call" | custom-call | tf_op jit(solution)/shard_map/gate_up/pallas_call | solution.py:161
  82.1 7.5 %all-to-all-start.4 = ((bf16[32,8,1792]{2,1,0:T(8,128)(2,1)}), bf16[32,8,1792]{2,1,0:T(8,128)(2,1)S(1)}, u32[]{:S(2)}, u32[]{:S(2)}) async-start(bf16[32,8,1792]{2,1,0:T(8,128)(2,1)} %gate_up.1), calls=%async_computation.4 | async-start | bytes 1835008 | tf_op jit(solution)/shard_map/all_to_all | solution.py:176
  89.6 1.9 %collective-permute-start.5 = (bf16[128,128]{1,0:T(8,128)(2,1)S(1)}, bf16[128,128]{1,0:T(8,128)(2,1)S(1)}, u32[]{:S(2)}, u32[]{:S(2)}) collective-permute-start(bf16[128,128]{1,0:T(8,128)(2,1)S(1)} %slice.29), channel_id=1, source_target_pairs={{0,8},{8,0},{1,9},{9,1},{2,10},{10,2},{3,11},{11,3},{4,12},{12,4},... | collective-permute-start | bytes 98312 | tf_op jit(solution)/shard_map/ppermute | solution.py:172
  91.5 1.2 %collective-permute-done.5 = bf16[128,128]{1,0:T(8,128)(2,1)S(1)} collective-permute-done((bf16[128,128]{1,0:T(8,128)(2,1)S(1)}, bf16[128,128]{1,0:T(8,128)(2,1)S(1)}, u32[]{:S(2)}, u32[]{:S(2)}) %collective-permute-start.5) | collective-permute-done | bytes 32800 | tf_op jit(solution)/shard_map/ppermute | solution.py:172
  92.8 0.7 copy.17
  93.4 20.8 %all-to-all-done.4 = bf16[32,8,1792]{2,1,0:T(8,128)(2,1)S(1)} async-done(((bf16[32,8,1792]{2,1,0:T(8,128)(2,1)}), bf16[32,8,1792]{2,1,0:T(8,128)(2,1)S(1)}, u32[]{:S(2)}, u32[]{:S(2)}) %all-to-all-start.4) | async-done | bytes 917536 | tf_op jit(solution)/shard_map/all_to_all | solution.py:176
  114.2 0.1 convert_reduce_fusion
  114.4 0.6 fusion.1
  (26 shorter events, 0.3 us)
Async XLA Ops:
  0.6 30.7 %copy-start.3 = (bf16[1024,128]{1,0:T(8,128)(2,1)S(1)}, bf16[1024,128]{1,0:T(8,128)(2,1)}, u32[]{:S(2)}) copy-start(bf16[1024,128]{1,0:T(8,128)(2,1)} %w0_ref.1) | copy-start | bytes 786436
  0.6 32.7 %copy-start.6 = (s32[4]{0:T(128)S(1)}, s32[4]{0:T(128)}, u32[]{:S(2)}) copy-start(s32[4]{0:T(128)} %len_ref.1) | copy-start | bytes 52
  0.7 32.7 %copy-start.4 = (s32[4,8]{1,0:T(4,128)S(1)}, s32[4,8]{1,0:T(4,128)}, u32[]{:S(2)}) copy-start(s32[4,8]{1,0:T(4,128)} %pages_ref.1) | copy-start | bytes 388
  0.7 32.7 %copy-start = (bf16[2,32,64,128]{3,2,1,0:T(8,128)(2,1)S(1)}, bf16[2,32,64,128]{3,2,1,0:T(8,128)(2,1)}, u32[]{:S(2)}) copy-start(bf16[2,32,64,128]{3,2,1,0:T(8,128)(2,1)} %param.12) | copy-start | bytes 3145732
  0.7 32.7 %copy-start.5 = (bf16[2,4,128]{2,1,0:T(4,128)(2,1)S(1)}, bf16[2,4,128]{2,1,0:T(4,128)(2,1)}, u32[]{:S(2)}) copy-start(bf16[2,4,128]{2,1,0:T(4,128)(2,1)} %new_ref.1) | copy-start | bytes 6148
  2.2 19.4 %all-to-all-start = ((bf16[16,32,128]{2,1,0:T(8,128)(2,1)}), bf16[16,32,128]{2,1,0:T(8,128)(2,1)S(1)}, u32[]{:S(2)}, u32[]{:S(2)}) async-start(bf16[16,32,128]{2,1,0:T(8,128)(2,1)} %broadcast_in_dim.8), calls=%async_computation | async-start | bytes 262144 | tf_op jit(solution)/shard_map/all_to_all | solution.py:176
  23.2 17.8 %all-to-all-start.1 = ((bf16[16,40,128]{2,1,0:T(8,128)(2,1)}), bf16[16,40,128]{2,1,0:T(8,128)(2,1)S(1)}, u32[]{:S(2)}, u32[]{:S(2)}) async-start(bf16[16,40,128]{2,1,0:T(8,128)(2,1)} %manifest_attention.1), calls=%async_computation.1 | async-start | bytes 327680 | tf_op jit(solution)/shard_map/all_to_all | solution.py:176
  31.3 3.4 %collective-permute-start = (bf16[1024,128]{1,0:T(8,128)(2,1)S(1)}, bf16[1024,128]{1,0:T(8,128)(2,1)S(1)}, u32[]{:S(2)}, u32[]{:S(2)}) collective-permute-start(bf16[1024,128]{1,0:T(8,128)(2,1)S(1)} %copy-done.3), channel_id=1, source_target_pairs={{0,8},{8,0},{1,9},{9,1},{2,10},{10,2},{3,11},{11,3},{4,12},{12,4},... | collective-permute-start | bytes 786440 | tf_op jit(solution)/shard_map/ppermute | solution.py:172
  33.3 14.7 %copy-start.1 = (bf16[128,1792]{1,0:T(8,128)(2,1)S(1)}, bf16[128,1792]{1,0:T(8,128)(2,1)}, u32[]{:S(2)}) copy-start(bf16[128,1792]{1,0:T(8,128)(2,1)} %g0_ref.1) | copy-start | bytes 1376260
  33.3 16.6 %copy-start.2 = (bf16[128,1792]{1,0:T(8,128)(2,1)S(1)}, bf16[128,1792]{1,0:T(8,128)(2,1)}, u32[]{:S(2)}) copy-start(bf16[128,1792]{1,0:T(8,128)(2,1)} %u0_ref.1) | copy-start | bytes 1376260
  33.3 19.0 %copy-start.7 = (bf16[256,128]{1,0:T(8,128)(2,1)S(1)}, bf16[256,128]{1,0:T(8,128)(2,1)}, u32[]{:S(2)}) copy-start(bf16[256,128]{1,0:T(8,128)(2,1)} %param.16) | copy-start | bytes 196612
  42.4 16.7 %all-to-all-start.2 = ((bf16[32,4,1024]{2,1,0:T(4,128)(2,1)}), bf16[32,4,1024]{2,1,0:T(4,128)(2,1)S(1)}, u32[]{:S(2)}, u32[]{:S(2)}) async-start(bf16[32,4,1024]{2,1,0:T(4,128)(2,1)} %join_attention.1), calls=%async_computation.2 | async-start | bytes 524288 | tf_op jit(solution)/shard_map/all_to_all | solution.py:176
  48.0 11.2 %collective-permute-start.1 = (bf16[128,1792]{1,0:T(8,128)(2,1)S(1)}, bf16[128,1792]{1,0:T(8,128)(2,1)S(1)}, u32[]{:S(2)}, u32[]{:S(2)}) collective-permute-start(bf16[128,1792]{1,0:T(8,128)(2,1)S(1)} %copy-done.1), channel_id=1, source_target_pairs={{0,8},{8,0},{1,9},{9,1},{2,10},{10,2},{3,11},{11,3},{4,12},{12,4},... | collective-permute-start | bytes 1376264 | tf_op jit(solution)/shard_map/ppermute | solution.py:172
  49.9 9.3 %collective-permute-start.2 = (bf16[128,1792]{1,0:T(8,128)(2,1)S(1)}, bf16[128,1792]{1,0:T(8,128)(2,1)S(1)}, u32[]{:S(2)}, u32[]{:S(2)}) collective-permute-start(bf16[128,1792]{1,0:T(8,128)(2,1)S(1)} %copy-done.2), channel_id=1, source_target_pairs={{0,8},{8,0},{1,9},{9,1},{2,10},{10,2},{3,11},{11,3},{4,12},{12,4},... | collective-permute-start | bytes 1376264 | tf_op jit(solution)/shard_map/ppermute | solution.py:172
  52.4 3.1 %collective-permute-start.3 = (bf16[32,4,128]{2,1,0:T(4,128)(2,1)S(1)}, bf16[32,4,128]{2,1,0:T(4,128)(2,1)S(1)}, u32[]{:S(2)}, u32[]{:S(2)}) collective-permute-start(bf16[32,4,128]{2,1,0:T(4,128)(2,1)S(1)} %get-tuple-element.29), channel_id=1, source_target_pairs={{0,8},{8,0},{1,9},{9,1},{2,10},{10,2},{3,11},{11,3},{4,12},{12,4},... | collective-permute-start | bytes 98312 | tf_op jit(solution)/shard_map/ppermute | solution.py:172
  59.4 10.5 %collective-permute-start.4 = (bf16[128,256]{1,0:T(8,128)(2,1)S(1)}, bf16[128,256]{1,0:T(8,128)(2,1)S(1)}, u32[]{:S(2)}, u32[]{:S(2)}) collective-permute-start(bf16[128,256]{1,0:T(8,128)(2,1)S(1)} %project.1.a_ref), channel_id=1, source_target_pairs={{0,4},{4,0},{1,5},{5,1},{2,6},{6,2},{3,7},{7,3},{8,12},{12,8},{9,1... | collective-permute-start | bytes 196616 | tf_op jit(solution)/shard_map/ppermute | solution.py:199
  82.1 32.1 %all-to-all-start.4 = ((bf16[32,8,1792]{2,1,0:T(8,128)(2,1)}), bf16[32,8,1792]{2,1,0:T(8,128)(2,1)S(1)}, u32[]{:S(2)}, u32[]{:S(2)}) async-start(bf16[32,8,1792]{2,1,0:T(8,128)(2,1)} %gate_up.1), calls=%async_computation.4 | async-start | bytes 1835008 | tf_op jit(solution)/shard_map/all_to_all | solution.py:176
  89.6 3.1 %collective-permute-start.5 = (bf16[128,128]{1,0:T(8,128)(2,1)S(1)}, bf16[128,128]{1,0:T(8,128)(2,1)S(1)}, u32[]{:S(2)}, u32[]{:S(2)}) collective-permute-start(bf16[128,128]{1,0:T(8,128)(2,1)S(1)} %slice.29), channel_id=1, source_target_pairs={{0,8},{8,0},{1,9},{9,1},{2,10},{10,2},{3,11},{11,3},{4,12},{12,4},... | collective-permute-start | bytes 98312 | tf_op jit(solution)/shard_map/ppermute | solution.py:172

commit v8 on v5

--- a/solution.py
+++ b/solution.py
@@ -135,20 +135,26 @@
 
 
 def project_kernel(x_ref, w0_ref, w1_ref, w2_ref, w3_ref, out_ref):
-    for k, w_ref in enumerate((w0_ref, w1_ref, w2_ref, w3_ref)):
-        y = dot(x_ref[...], w_ref[...], 1, 0).astype(BF)
-        for i in range(8):
-            out_ref[i, :, k * HD : (k + 1) * HD] = y
-
-
-def mlp_kernel(x_ref, g0_ref, g1_ref, g2_ref, g3_ref, u0_ref, u1_ref, u2_ref, u3_ref, out_ref):
-    def product(*w_refs):
-        w = [w_ref[...] for w_ref in w_refs]
-        low = dot(x_ref[:, 0 : 2 * HD], jnp.concatenate(w[:2], axis=0), 1, 0)
-        return low + dot(x_ref[:, 2 * HD :], jnp.concatenate(w[2:], axis=0), 1, 0)
-
-    gate = product(g0_ref, g1_ref, g2_ref, g3_ref)
-    up = product(u0_ref, u1_ref, u2_ref, u3_ref)
+    x = x_ref[...]
+    for k in range(2):
+        w = [w_ref[0 : GROUP * HD] for w_ref in ((w0_ref, w1_ref), (w2_ref, w3_ref))[k]]
+        out_ref[:, 2 * k * HD : 2 * (k + 1) * HD] = dot(x, jnp.concatenate(w, axis=1), 1, 0).astype(BF)
+
+
+def add_kernel(a_ref, b_ref, out_ref):
+    block = (a_ref[...].astype(F32) + b_ref[...].astype(F32)).astype(BF)
+    for i in range(4):
+        out_ref[i] = block
+
+
+def mlp_kernel(x_ref, w0_ref, w1_ref, w2_ref, w3_ref, out_ref):
+    low, high = x_ref[:, 0 : 2 * HD], x_ref[:, 2 * HD :]
+
+    def product(k):
+        w = [w_ref[k * HD : (k + 1) * HD] for w_ref in (w0_ref, w1_ref, w2_ref, w3_ref)]
+        return dot(low, jnp.concatenate(w[:2], axis=0), 1, 0) + dot(high, jnp.concatenate(w[2:], axis=0), 1, 0)
+
+    gate, up = product(0), product(1)
     for j in range(PEERS):
         at = slice(j * ROWS, (j + 1) * ROWS)
         out_ref[j] = jnp.concatenate([gate[at], up[at]], axis=0).astype(BF)
@@ -193,25 +199,26 @@
     rows = PEERS * ROWS
     q = queries.reshape(QROWS, HD)
     q_all = exchange(jnp.broadcast_to(q[None], (PEERS, QROWS, HD)), SPARSE).reshape(PEERS * QROWS, HD)
-    kv = man_kv.reshape(2, 2 * PAGE, HD)
-    kv = lax.all_gather(jnp.stack([kv, pair(kv)]), "c", axis=0, tiled=True)
+    kv = lax.all_gather(man_kv.reshape(1, 2, 2 * PAGE, HD), ("p", "c"), axis=0, tiled=True)
+    parts = exchange(man_part(q_all, kv), SPARSE)
     own = own_part(pages, own_len, q, new_kv, own_kv.reshape(2, POOL * PAGE, HD))
-    q_all, kv, own = tie((q_all, kv, own))
-    parts = exchange(man_part(q_all, kv), SPARSE)
-    w_out_p = pair(w_out)
-    parts, w_out_p, w_out_c, w_out_pc = tie((parts, w_out_p, swap(w_out), swap(w_out_p)))
+    out_w = jnp.concatenate([w_out, resid], axis=0)
+    parts, own, out_w_c, out_w_p = tie((parts, own, swap(out_w), pair(out_w)))
     place = (lax.axis_index(SPARSE) % 4).astype(jnp.int32).reshape(1)
     attn = exchange(join_part(place, parts, *own), SPARSE).reshape(rows, GROUP * HD)
-    res = resid.reshape(PEERS, 2, 2, ROWS, HD)
-    res = jnp.stack([pick(res, core, 2), swap(pick(res, 1 - core, 2))], axis=3)
-    attn, w_gate_p, w_up_p, res = tie((attn, pair(w_gate), pair(w_up), res))
-    res = jnp.stack([pick(res, side, 1), pair(pick(res, 1 - side, 1))], axis=2).reshape(rows, 4 * HD)
-
-    heads = exchange(dense(project_kernel, "project", (8, rows, 4 * HD), attn, w_out, w_out_c, w_out_p, w_out_pc), HEAD)
-    out4 = (res.astype(F32) + heads.astype(F32).sum(0)).astype(BF)
+    mlp_w = jnp.concatenate([w_gate, w_up], axis=0)
+    mlp_w_p = pair(mlp_w)
+    attn, out_w_pc, mlp_w_p = tie((attn, swap(out_w_p), mlp_w_p))
+    out_ws = (out_w, out_w_c, out_w_p, out_w_pc)
+    res = [pick(pick(w[GROUP * HD :].reshape(PEERS, 2, 2, ROWS, HD), side, 1), core, 1) for w in out_ws]
+    res = jnp.concatenate(res, axis=-1).reshape(rows, 4 * HD).astype(F32)
+
+    share = dense(project_kernel, "project", (rows, 4 * HD), attn, *out_ws)
+    share2 = lax.ppermute(share, "zh", [(0, 1), (1, 0)])
+    heads = exchange(dense(add_kernel, "add_shares", (4, rows, 4 * HD), share, share2), "x")
+    out4 = (res + heads.astype(F32).sum(0)).astype(BF)
     both = dense(
-        mlp_kernel, "gate_up", (PEERS, 2 * ROWS, width), out4,
-        w_gate, swap(w_gate), w_gate_p, swap(w_gate_p), w_up, swap(w_up), w_up_p, swap(w_up_p),
+        mlp_kernel, "gate_up", (PEERS, 2 * ROWS, width), out4, mlp_w, swap(mlp_w), mlp_w_p, swap(mlp_w_p)
     )
     joined = exchange(both, SPARSE).astype(F32).sum(0)
     hidden = (jax.nn.silu(joined[:ROWS]) * joined[ROWS:]).astype(BF)

time: 125 us -> 115 us (0.920)
  starting transfers between devices: 80.7 us -> 59 us
  waiting for transfers between devices: 25.9 us -> 31.7 us
  blocking collectives: 2.13 us -> 5.88 us
  local copies, waits for them, and re-layouts: 3.67 us -> 6.04 us
  other arithmetic: 2.18 us -> 0.89 us
    all_to_all x5, starting transfers between devices: 45.7 us -> 31.7 us  [exchange(): return lax.all_to_all(x, axes, 0, 0, tiled=True)]
    ppermute x6 -> x3, starting transfers between devices: 18.1 us -> 8.99 us  [pair(): return lax.ppermute(x, 'p', [(0, 1), (1, 0)])]
    ppermute x0 -> x1, starting transfers between devices: none -> 8.41 us  [on_device(): share2 = lax.ppermute(share, 'zh', [(0, 1), (1, 0)])]
    all_to_all x5, waiting for transfers between devices: 19.1 us -> 26.3 us  [exchange(): return lax.all_to_all(x, axes, 0, 0, tiled=True)]
    ppermute x8 -> x5, starting transfers between devices: 16.8 us -> 9.94 us  [swap(): return lax.ppermute(x, 'c', [(0, 1), (1, 0)])]
    all_gather x1, blocking collectives: 2.13 us -> 5.88 us  [on_device(): lax.all_gather(man_kv.reshape(1, 2, 2 * PAGE, HD), ('p', 'c'), axis=0, ti...]
    slice x0 -> x8, local copies, waits for them, and re-layouts: none -> 1.85 us  [the longest x3 1.7 us: on_device(): w[GROUP * HD:].reshape(PEERS, 2, 2, ROWS, HD)]
    pallas_call x2 -> x3, Pallas kernels: 3.83 us -> 4.82 us  [dense(): pl.pallas_call(kernel, out_shape=jax.ShapeDtypeStruct(out_shape, BF), in_...]
  transfers between devices with their start and end apart: 19 -> 14, of which waited for: 8 -> 8; matrix products, arithmetic and copies ran while one was open for 3% -> 4% of each run, Pallas kernels for 3% -> 6%
where the time goes in v8:
time: 115 us; the launch traced here: 114 us
  starting transfers between devices  59 us (51%)
  waiting for transfers between devices  31.7 us (28%)
  Pallas kernels  9.02 us (8%)
  local copies, waits for them, and re-layouts  6.04 us (5%)
  blocking collectives  5.88 us (5%)
    all_to_all x5, starting transfers between devices, exchange(): return lax.all_to_all(x, axes, 0, 0, tiled=True)  31.7 us
    all_to_all x5, waiting for transfers between devices, exchange(): return lax.all_to_all(x, axes, 0, 0, tiled=True)  26.3 us
    ppermute x5, starting transfers between devices, swap(): return lax.ppermute(x, 'c', [(0, 1), (1, 0)])  9.94 us
    ppermute x3, starting transfers between devices, pair(): return lax.ppermute(x, 'p', [(0, 1), (1, 0)])  8.99 us
    ppermute x1, starting transfers between devices, on_device(): share2 = lax.ppermute(share, 'zh', [(0, 1), (1, 0)])  8.41 us
    all_gather x1, blocking collectives, on_device(): lax.all_gather(man_kv.reshape(1, 2, 2 * PAGE, HD), ('p', 'c'), axis=0, ti...  5.88 us
    pallas_call x3, Pallas kernels, dense(): pl.pallas_call(kernel, out_shape=jax.ShapeDtypeStruct(out_shape, BF), in_...  4.82 us
    ppermute x3, waiting for transfers between devices, pair(): return lax.ppermute(x, 'p', [(0, 1), (1, 0)])  3.95 us
  transfers between devices with their start and end apart: 14, of which 8 were waited for; matrix products, arithmetic and copies ran while one was open for 4% of the time, Pallas kernels for 6%

profile of v8, /device:TPU:2, one launch (start us, length us, event | category | flops | bytes accessed | tf_op | source)
XLA Modules:
  0.0 113.6 jit_solution(10171947797919401795)
XLA Ops:
  0.6 1.0 constant_dynamic-update-slice_fusion.1
  1.7 2.1 %collective-permute-start = (bf16[1280,128]{1,0:T(8,128)(2,1)S(1)}, bf16[1280,128]{1,0:T(8,128)(2,1)}, u32[]{:S(2)}, u32[]{:S(2)}) collective-permute-start(bf16[1280,128]{1,0:T(8,128)(2,1)S(1)} %constant_dynamic-update-slice_fusion.w0_ref), channel_id=1, source_target_pairs={{0,8},{8,0},{1,9},{9,1},{2,10},{10,2},{3,11},{11,3},{4,12},{12,4},... | collective-permute-start | bytes 983048 | tf_op jit(solution)/shard_map/ppermute | solution.py:176
  3.8 4.3 %collective-permute-start.1 = (bf16[1280,128]{1,0:T(8,128)(2,1)S(1)}, bf16[1280,128]{1,0:T(8,128)(2,1)}, u32[]{:S(2)}, u32[]{:S(2)}) collective-permute-start(bf16[1280,128]{1,0:T(8,128)(2,1)S(1)} %constant_dynamic-update-slice_fusion.w0_ref), channel_id=1, source_target_pairs={{0,16},{16,0},{1,17},{17,1},{2,18},{18,2},{3,19},{19,3},{4,20},{20... | collective-permute-start | bytes 983048 | tf_op jit(solution)/shard_map/ppermute | solution.py:180
  8.7 11.0 %all-to-all-start = ((bf16[16,32,128]{2,1,0:T(8,128)(2,1)}), bf16[16,32,128]{2,1,0:T(8,128)(2,1)S(1)}, u32[]{:S(2)}, u32[]{:S(2)}) async-start(bf16[16,32,128]{2,1,0:T(8,128)(2,1)} %broadcast_in_dim.8), calls=%async_computation | async-start | bytes 262144 | tf_op jit(solution)/shard_map/all_to_all | solution.py:184
  19.7 5.9 %all_gather.3.kv_ref = bf16[4,2,128,128]{3,2,1,0:T(8,128)(2,1)S(1)} all-gather(bf16[1,2,128,128]{3,2,1,0:T(8,128)(2,1)S(1)} %bitcast.40), channel_id=1, replica_groups=mesh['y'=8,'zq'=2,'p'=2,'c'=2,'zh'=2,'x'=4] {'p','c'}, dimensions={0}, use_global_device_ids=true | all-gather | bytes 327680 | tf_op jit(solution)/shard_map/all_gather | solution.py:202
  25.6 5.0 %all-to-all-done = bf16[16,32,128]{2,1,0:T(8,128)(2,1)S(1)} async-done(((bf16[16,32,128]{2,1,0:T(8,128)(2,1)}), bf16[16,32,128]{2,1,0:T(8,128)(2,1)S(1)}, u32[]{:S(2)}, u32[]{:S(2)}) %all-to-all-start) | async-done | bytes 131104 | tf_op jit(solution)/shard_map/all_to_all | solution.py:184
  30.6 1.7 %manifest_attention.1 = bf16[16,40,128]{2,1,0:T(8,128)(2,1)} custom-call(bf16[512,128]{1,0:T(8,128)(2,1)S(1)} %bitcast.34, bf16[4,2,128,128]{3,2,1,0:T(8,128)(2,1)S(1)} %all_gather.3.kv_ref), custom_call_target="tpu_custom_call" | custom-call | tf_op jit(solution)/shard_map/manifest_attention/pallas_call | solution.py:89
  32.3 4.0 %all-to-all-start.1 = ((bf16[16,40,128]{2,1,0:T(8,128)(2,1)}), bf16[16,40,128]{2,1,0:T(8,128)(2,1)S(1)}, u32[]{:S(2)}, u32[]{:S(2)}) async-start(bf16[16,40,128]{2,1,0:T(8,128)(2,1)} %manifest_attention.1), calls=%async_computation.1 | async-start | bytes 327680 | tf_op jit(solution)/shard_map/all_to_all | solution.py:184
  36.3 1.1 constant_dynamic-update-slice_fusion.2.w0_ref
  37.3 2.6 %collective-permute-start.3 = (bf16[256,1792]{1,0:T(8,128)(2,1)S(1)}, bf16[256,1792]{1,0:T(8,128)(2,1)S(1)}, u32[]{:S(2)}, u32[]{:S(2)}) collective-permute-start(bf16[256,1792]{1,0:T(8,128)(2,1)S(1)} %constant_dynamic-update-slice_fusion.2.w0_ref), channel_id=1, source_target_pairs={{0,16},{16,0},{1,17},{17,1},{2,18},{18,2},{3,19},{19,3},{4,20},{20... | collective-permute-start | bytes 2752520 | tf_op jit(solution)/shard_map/ppermute | solution.py:180
  39.9 1.9 %collective-permute-start.7 = (bf16[256,1792]{1,0:T(8,128)(2,1)S(1)}, bf16[256,1792]{1,0:T(8,128)(2,1)}, u32[]{:S(2)}, u32[]{:S(2)}) collective-permute-start(bf16[256,1792]{1,0:T(8,128)(2,1)S(1)} %constant_dynamic-update-slice_fusion.2.w0_ref), channel_id=1, source_target_pairs={{0,8},{8,0},{1,9},{9,1},{2,10},{10,2},{3,11},{11,3},{4,12},{12,4},... | collective-permute-start | bytes 2752520 | tf_op jit(solution)/shard_map/ppermute | solution.py:176
  42.6 1.2 %own_attention.1 = (f32[32,128]{1,0:T(8,128)S(1)}, f32[32,128]{1,0:T(8,128)S(1)}, f32[32,128]{1,0:T(8,128)S(1)}) custom-call(s32[4,8]{1,0:T(4,128)S(1)} %copy-done.1, s32[4]{0:T(128)S(1)} %copy-done.3, bf16[32,128]{1,0:T(8,128)(2,1)S(1)} %broadcast_in_dim.7.q_ref, bf16[2,4,128]{2,1,0:T(4,128)(2,1)S(1)} %copy-done.2, bf16[2,2048,128]{2,1,0:T(8,128)(2,1)S(1)} %bitcast.33), custom_call_target="tpu_custom_call" | custom-call | tf_op jit(solution)/shard_map/own_attention/pallas_call | solution.py:58
  43.8 4.0 %all-to-all-done.1.parts_ref = bf16[16,40,128]{2,1,0:T(8,128)(2,1)S(1)} async-done(((bf16[16,40,128]{2,1,0:T(8,128)(2,1)}), bf16[16,40,128]{2,1,0:T(8,128)(2,1)S(1)}, u32[]{:S(2)}, u32[]{:S(2)}) %all-to-all-start.1) | async-done | bytes 163872 | tf_op jit(solution)/shard_map/all_to_all | solution.py:184
  47.8 1.3 %join_attention.1 = bf16[16,4,1024]{2,1,0:T(4,128)(2,1)} custom-call(s32[1]{0:T(128)} %bitcast.12.place_ref, bf16[16,40,128]{2,1,0:T(8,128)(2,1)S(1)} %all-to-all-done.1.parts_ref, f32[32,128]{1,0:T(8,128)S(1)} %get-tuple-element.20.acc_ref, f32[32,128]{1,0:T(8,128)S(1)} %get-tuple-element.21.top_ref, f32[32,128]{1,0:T(8,128)S(1)} %get-tuple-element.22.total_ref), custom_call_target="tpu_custom_call" | custom-call | tf_op jit(solution)/shard_map/join_attention/pallas_call | solution.py:126
  49.2 5.0 %all-to-all-start.2 = ((bf16[16,4,1024]{2,1,0:T(4,128)(2,1)}), bf16[16,4,1024]{2,1,0:T(4,128)(2,1)S(1)}, u32[]{:S(2)}, u32[]{:S(2)}) async-start(bf16[16,4,1024]{2,1,0:T(4,128)(2,1)} %join_attention.1), calls=%async_computation.2 | async-start | bytes 262144 | tf_op jit(solution)/shard_map/all_to_all | solution.py:184
  54.2 2.1 %collective-permute-start.2 = (bf16[1280,128]{1,0:T(8,128)(2,1)}, bf16[1280,128]{1,0:T(8,128)(2,1)S(1)}, u32[]{:S(2)}, u32[]{:S(2)}) collective-permute-start(bf16[1280,128]{1,0:T(8,128)(2,1)} %collective-permute-done.1.w2_ref), channel_id=1, source_target_pairs={{0,8},{8,0},{1,9},{9,1},{2,10},{10,2},{3,11},{11,3},{4,12},{12,4},... | collective-permute-start | bytes 983048 | tf_op jit(solution)/shard_map/ppermute | solution.py:176
  56.3 0.8 slice.79
  57.3 0.8 slice.84
  58.2 7.2 %all-to-all-done.2 = bf16[16,4,1024]{2,1,0:T(4,128)(2,1)S(1)} async-done(((bf16[16,4,1024]{2,1,0:T(4,128)(2,1)}), bf16[16,4,1024]{2,1,0:T(4,128)(2,1)S(1)}, u32[]{:S(2)}, u32[]{:S(2)}) %all-to-all-start.2) | async-done | bytes 131104 | tf_op jit(solution)/shard_map/all_to_all | solution.py:184
  65.4 1.4 %project.1.a_ref = bf16[64,512]{1,0:T(8,128)(2,1)S(1)} custom-call(bf16[64,1024]{1,0:T(8,128)(2,1)S(1)} %reshape.80.x_ref, bf16[1280,128]{1,0:T(8,128)(2,1)S(1)} %constant_dynamic-update-slice_fusion.w0_ref, bf16[1280,128]{1,0:T(8,128)(2,1)} %collective-permute-done.w1_ref, bf16[1280,128]{1,0:T(8,128)(2,1)} %collective-permute-done.1.w2_ref, ...), custom_call_target="tpu_custom_call" | custom-call | tf_op jit(solution)/shard_map/project/pallas_call | solution.py:165
  66.8 8.4 %collective-permute-start.4 = (bf16[64,512]{1,0:T(8,128)(2,1)S(1)}, bf16[64,512]{1,0:T(8,128)(2,1)S(1)}, u32[]{:S(2)}, u32[]{:S(2)}) collective-permute-start(bf16[64,512]{1,0:T(8,128)(2,1)S(1)} %project.1.a_ref), channel_id=1, source_target_pairs={{0,4},{4,0},{1,5},{5,1},{2,6},{6,2},{3,7},{7,3},{8,12},{12,8},{9,1... | collective-permute-start | bytes 196616 | tf_op jit(solution)/shard_map/ppermute | solution.py:217
  75.2 1.9 %collective-permute-start.8 = (bf16[256,1792]{1,0:T(8,128)(2,1)S(1)}, bf16[256,1792]{1,0:T(8,128)(2,1)S(1)}, u32[]{:S(2)}, u32[]{:S(2)}) collective-permute-start(bf16[256,1792]{1,0:T(8,128)(2,1)S(1)} %collective-permute-done.3.w2_ref), channel_id=1, source_target_pairs={{0,8},{8,0},{1,9},{9,1},{2,10},{10,2},{3,11},{11,3},{4,12},{12,4},... | collective-permute-start | bytes 2752520 | tf_op jit(solution)/shard_map/ppermute | solution.py:176
  77.5 0.7 add_shares.1
  78.2 4.8 %all-to-all-start.3 = ((bf16[4,64,512]{2,1,0:T(8,128)(2,1)}), bf16[4,64,512]{2,1,0:T(8,128)(2,1)S(1)}, u32[]{:S(2)}, u32[]{:S(2)}) async-start(bf16[4,64,512]{2,1,0:T(8,128)(2,1)} %add_shares.1), calls=%async_computation.3 | async-start | bytes 524288 | tf_op jit(solution)/shard_map/all_to_all | solution.py:184
  83.0 5.6 %all-to-all-done.3 = bf16[4,64,512]{2,1,0:T(8,128)(2,1)S(1)} async-done(((bf16[4,64,512]{2,1,0:T(8,128)(2,1)}), bf16[4,64,512]{2,1,0:T(8,128)(2,1)S(1)}, u32[]{:S(2)}, u32[]{:S(2)}) %all-to-all-start.3) | async-done | bytes 262176 | tf_op jit(solution)/shard_map/all_to_all | solution.py:184
  88.7 2.7 %gate_up.1 = bf16[16,8,1792]{2,1,0:T(8,128)(2,1)} custom-call(bf16[64,512]{1,0:T(8,128)(2,1)S(1)} %add_convert_fusion.x_ref, bf16[256,1792]{1,0:T(8,128)(2,1)S(1)} %constant_dynamic-update-slice_fusion.2.w0_ref, bf16[256,1792]{1,0:T(8,128)(2,1)} %collective-permute-done.7.w1_ref, bf16[256,1792]{1,0:T(8,128)(2,1)S(1)} %collective-permute-done.3.w2_ref, ...), custom_call_target="tpu_custom_call" | custom-call | tf_op jit(solution)/shard_map/gate_up/pallas_call | solution.py:165
  91.5 6.9 %all-to-all-start.4 = ((bf16[16,8,1792]{2,1,0:T(8,128)(2,1)}), bf16[16,8,1792]{2,1,0:T(8,128)(2,1)S(1)}, u32[]{:S(2)}, u32[]{:S(2)}) async-start(bf16[16,8,1792]{2,1,0:T(8,128)(2,1)} %gate_up.1), calls=%async_computation.4 | async-start | bytes 917504 | tf_op jit(solution)/shard_map/all_to_all | solution.py:184
  98.5 2.1 %collective-permute-start.5 = (bf16[16,4,2,128]{3,0,1,2:T(8,128)(2,1)S(1)}, bf16[16,4,2,128]{3,0,1,2:T(8,128)(2,1)S(1)}, u32[]{:S(2)}, u32[]{:S(2)}) collective-permute-start(bf16[16,4,2,128]{3,0,1,2:T(8,128)(2,1)S(1)} %bitcast.46), channel_id=1, source_target_pairs={{0,16},{16,0},{1,17},{17,1},{2,18},{18,2},{3,19},{19,3},{4,20},{20... | collective-permute-start | bytes 98312 | tf_op jit(solution)/shard_map/ppermute | solution.py:180
  100.6 3.9 %collective-permute-done.5 = bf16[16,4,2,128]{3,0,1,2:T(8,128)(2,1)S(1)} collective-permute-done((bf16[16,4,2,128]{3,0,1,2:T(8,128)(2,1)S(1)}, bf16[16,4,2,128]{3,0,1,2:T(8,128)(2,1)S(1)}, u32[]{:S(2)}, u32[]{:S(2)}) %collective-permute-start.5) | collective-permute-done | bytes 32800 | tf_op jit(solution)/shard_map/ppermute | solution.py:180
  104.6 1.9 %collective-permute-start.6 = (bf16[16,2,4,128]{3,0,2,1:T(8,128)(2,1)S(1)}, bf16[16,2,4,128]{3,0,2,1:T(8,128)(2,1)S(1)}, u32[]{:S(2)}, u32[]{:S(2)}) collective-permute-start(bf16[16,2,4,128]{3,0,2,1:T(8,128)(2,1)S(1)} %get-tuple-element.27), channel_id=1, source_target_pairs={{0,8},{8,0},{1,9},{9,1},{2,10},{10,2},{3,11},{11,3},{4,12},{12,4},... | collective-permute-start | bytes 98312 | tf_op jit(solution)/shard_map/ppermute | solution.py:176
  106.5 1.2 %collective-permute-done.6 = bf16[16,2,4,128]{3,0,2,1:T(8,128)(2,1)S(1)} collective-permute-done((bf16[16,2,4,128]{3,0,2,1:T(8,128)(2,1)S(1)}, bf16[16,2,4,128]{3,0,2,1:T(8,128)(2,1)S(1)}, u32[]{:S(2)}, u32[]{:S(2)}) %collective-permute-start.6) | collective-permute-done | bytes 32800 | tf_op jit(solution)/shard_map/ppermute | solution.py:176
  108.3 4.6 %all-to-all-done.4 = bf16[16,8,1792]{2,1,0:T(8,128)(2,1)S(1)} async-done(((bf16[16,8,1792]{2,1,0:T(8,128)(2,1)}), bf16[16,8,1792]{2,1,0:T(8,128)(2,1)S(1)}, u32[]{:S(2)}, u32[]{:S(2)}) %all-to-all-start.4) | async-done | bytes 458784 | tf_op jit(solution)/shard_map/all_to_all | solution.py:184
  (51 shorter events, 3.4 us)
Async XLA Ops:
  0.6 1.0 copy-start.5
  0.6 7.4 %copy-start.7 = (bf16[4,1024]{1,0:T(4,128)(2,1)S(1)}, bf16[4,1024]{1,0:T(4,128)(2,1)}, u32[]{:S(2)}) copy-start(bf16[4,1024]{1,0:T(4,128)(2,1)} %param.10) | copy-start | bytes 24580
  1.7 23.9 %copy-start.4 = (bf16[128,1792]{1,0:T(8,128)(2,1)S(1)}, bf16[128,1792]{1,0:T(8,128)(2,1)}, u32[]{:S(2)}) copy-start(bf16[128,1792]{1,0:T(8,128)(2,1)} %param.18) | copy-start | bytes 1376260
  1.7 42.1 %collective-permute-start = (bf16[1280,128]{1,0:T(8,128)(2,1)S(1)}, bf16[1280,128]{1,0:T(8,128)(2,1)}, u32[]{:S(2)}, u32[]{:S(2)}) collective-permute-start(bf16[1280,128]{1,0:T(8,128)(2,1)S(1)} %constant_dynamic-update-slice_fusion.w0_ref), channel_id=1, source_target_pairs={{0,8},{8,0},{1,9},{9,1},{2,10},{10,2},{3,11},{11,3},{4,12},{12,4},... | collective-permute-start | bytes 983048 | tf_op jit(solution)/shard_map/ppermute | solution.py:176
  3.8 40.1 %collective-permute-start.1 = (bf16[1280,128]{1,0:T(8,128)(2,1)S(1)}, bf16[1280,128]{1,0:T(8,128)(2,1)}, u32[]{:S(2)}, u32[]{:S(2)}) collective-permute-start(bf16[1280,128]{1,0:T(8,128)(2,1)S(1)} %constant_dynamic-update-slice_fusion.w0_ref), channel_id=1, source_target_pairs={{0,16},{16,0},{1,17},{17,1},{2,18},{18,2},{3,19},{19,3},{4,20},{20... | collective-permute-start | bytes 983048 | tf_op jit(solution)/shard_map/ppermute | solution.py:180
  8.7 11.0 %copy-start.6 = (bf16[2,2,64,128]{3,2,1,0:T(8,128)(2,1)S(1)}, bf16[2,2,64,128]{3,2,1,0:T(8,128)(2,1)}, u32[]{:S(2)}) copy-start(bf16[2,2,64,128]{3,2,1,0:T(8,128)(2,1)} %param.13) | copy-start | bytes 196612
  8.7 21.9 %all-to-all-start = ((bf16[16,32,128]{2,1,0:T(8,128)(2,1)}), bf16[16,32,128]{2,1,0:T(8,128)(2,1)S(1)}, u32[]{:S(2)}, u32[]{:S(2)}) async-start(bf16[16,32,128]{2,1,0:T(8,128)(2,1)} %broadcast_in_dim.8), calls=%async_computation | async-start | bytes 262144 | tf_op jit(solution)/shard_map/all_to_all | solution.py:184
  25.6 16.3 %copy-start = (bf16[2,32,64,128]{3,2,1,0:T(8,128)(2,1)S(1)}, bf16[2,32,64,128]{3,2,1,0:T(8,128)(2,1)}, u32[]{:S(2)}) copy-start(bf16[2,32,64,128]{3,2,1,0:T(8,128)(2,1)} %param.12) | copy-start | bytes 3145732
  32.3 15.6 %all-to-all-start.1 = ((bf16[16,40,128]{2,1,0:T(8,128)(2,1)}), bf16[16,40,128]{2,1,0:T(8,128)(2,1)S(1)}, u32[]{:S(2)}, u32[]{:S(2)}) async-start(bf16[16,40,128]{2,1,0:T(8,128)(2,1)} %manifest_attention.1), calls=%async_computation.1 | async-start | bytes 327680 | tf_op jit(solution)/shard_map/all_to_all | solution.py:184
  37.3 28.1 %collective-permute-start.3 = (bf16[256,1792]{1,0:T(8,128)(2,1)S(1)}, bf16[256,1792]{1,0:T(8,128)(2,1)S(1)}, u32[]{:S(2)}, u32[]{:S(2)}) collective-permute-start(bf16[256,1792]{1,0:T(8,128)(2,1)S(1)} %constant_dynamic-update-slice_fusion.2.w0_ref), channel_id=1, source_target_pairs={{0,16},{16,0},{1,17},{17,1},{2,18},{18,2},{3,19},{19,3},{4,20},{20... | collective-permute-start | bytes 2752520 | tf_op jit(solution)/shard_map/ppermute | solution.py:180
  39.9 48.8 %collective-permute-start.7 = (bf16[256,1792]{1,0:T(8,128)(2,1)S(1)}, bf16[256,1792]{1,0:T(8,128)(2,1)}, u32[]{:S(2)}, u32[]{:S(2)}) collective-permute-start(bf16[256,1792]{1,0:T(8,128)(2,1)S(1)} %constant_dynamic-update-slice_fusion.2.w0_ref), channel_id=1, source_target_pairs={{0,8},{8,0},{1,9},{9,1},{2,10},{10,2},{3,11},{11,3},{4,12},{12,4},... | collective-permute-start | bytes 2752520 | tf_op jit(solution)/shard_map/ppermute | solution.py:176
  41.9 0.7 copy-start.2
  41.9 0.7 copy-start.1
  41.9 0.7 copy-start.3
  49.2 16.2 %all-to-all-start.2 = ((bf16[16,4,1024]{2,1,0:T(4,128)(2,1)}), bf16[16,4,1024]{2,1,0:T(4,128)(2,1)S(1)}, u32[]{:S(2)}, u32[]{:S(2)}) async-start(bf16[16,4,1024]{2,1,0:T(4,128)(2,1)} %join_attention.1), calls=%async_computation.2 | async-start | bytes 262144 | tf_op jit(solution)/shard_map/all_to_all | solution.py:184
  54.2 11.2 %collective-permute-start.2 = (bf16[1280,128]{1,0:T(8,128)(2,1)}, bf16[1280,128]{1,0:T(8,128)(2,1)S(1)}, u32[]{:S(2)}, u32[]{:S(2)}) collective-permute-start(bf16[1280,128]{1,0:T(8,128)(2,1)} %collective-permute-done.1.w2_ref), channel_id=1, source_target_pairs={{0,8},{8,0},{1,9},{9,1},{2,10},{10,2},{3,11},{11,3},{4,12},{12,4},... | collective-permute-start | bytes 983048 | tf_op jit(solution)/shard_map/ppermute | solution.py:176
  66.8 10.6 %collective-permute-start.4 = (bf16[64,512]{1,0:T(8,128)(2,1)S(1)}, bf16[64,512]{1,0:T(8,128)(2,1)S(1)}, u32[]{:S(2)}, u32[]{:S(2)}) collective-permute-start(bf16[64,512]{1,0:T(8,128)(2,1)S(1)} %project.1.a_ref), channel_id=1, source_target_pairs={{0,4},{4,0},{1,5},{5,1},{2,6},{6,2},{3,7},{7,3},{8,12},{12,8},{9,1... | collective-permute-start | bytes 196616 | tf_op jit(solution)/shard_map/ppermute | solution.py:217
  75.2 13.5 %collective-permute-start.8 = (bf16[256,1792]{1,0:T(8,128)(2,1)S(1)}, bf16[256,1792]{1,0:T(8,128)(2,1)S(1)}, u32[]{:S(2)}, u32[]{:S(2)}) collective-permute-start(bf16[256,1792]{1,0:T(8,128)(2,1)S(1)} %collective-permute-done.3.w2_ref), channel_id=1, source_target_pairs={{0,8},{8,0},{1,9},{9,1},{2,10},{10,2},{3,11},{11,3},{4,12},{12,4},... | collective-permute-start | bytes 2752520 | tf_op jit(solution)/shard_map/ppermute | solution.py:176
  78.2 10.5 %all-to-all-start.3 = ((bf16[4,64,512]{2,1,0:T(8,128)(2,1)}), bf16[4,64,512]{2,1,0:T(8,128)(2,1)S(1)}, u32[]{:S(2)}, u32[]{:S(2)}) async-start(bf16[4,64,512]{2,1,0:T(8,128)(2,1)} %add_shares.1), calls=%async_computation.3 | async-start | bytes 524288 | tf_op jit(solution)/shard_map/all_to_all | solution.py:184
  91.5 21.5 %all-to-all-start.4 = ((bf16[16,8,1792]{2,1,0:T(8,128)(2,1)}), bf16[16,8,1792]{2,1,0:T(8,128)(2,1)S(1)}, u32[]{:S(2)}, u32[]{:S(2)}) async-start(bf16[16,8,1792]{2,1,0:T(8,128)(2,1)} %gate_up.1), calls=%async_computation.4 | async-start | bytes 917504 | tf_op jit(solution)/shard_map/all_to_all | solution.py:184
  98.5 6.1 %collective-permute-start.5 = (bf16[16,4,2,128]{3,0,1,2:T(8,128)(2,1)S(1)}, bf16[16,4,2,128]{3,0,1,2:T(8,128)(2,1)S(1)}, u32[]{:S(2)}, u32[]{:S(2)}) collective-permute-start(bf16[16,4,2,128]{3,0,1,2:T(8,128)(2,1)S(1)} %bitcast.46), channel_id=1, source_target_pairs={{0,16},{16,0},{1,17},{17,1},{2,18},{18,2},{3,19},{19,3},{4,20},{20... | collective-permute-start | bytes 98312 | tf_op jit(solution)/shard_map/ppermute | solution.py:180
  104.6 3.1 %collective-permute-start.6 = (bf16[16,2,4,128]{3,0,2,1:T(8,128)(2,1)S(1)}, bf16[16,2,4,128]{3,0,2,1:T(8,128)(2,1)S(1)}, u32[]{:S(2)}, u32[]{:S(2)}) collective-permute-start(bf16[16,2,4,128]{3,0,2,1:T(8,128)(2,1)S(1)} %get-tuple-element.27), channel_id=1, source_target_pairs={{0,8},{8,0},{1,9},{9,1},{2,10},{10,2},{3,11},{11,3},{4,12},{12,4},... | collective-permute-start | bytes 98312 | tf_op jit(solution)/shard_map/ppermute | solution.py:176

commit v9 on v8

--- a/solution.py
+++ b/solution.py
@@ -134,11 +134,11 @@
     )(place, parts, acc, top, total)
 
 
-def project_kernel(x_ref, w0_ref, w1_ref, w2_ref, w3_ref, out_ref):
+def project_kernel(x_ref, w0_ref, w1_ref, out_ref):
     x = x_ref[...]
     for k in range(2):
-        w = [w_ref[0 : GROUP * HD] for w_ref in ((w0_ref, w1_ref), (w2_ref, w3_ref))[k]]
-        out_ref[:, 2 * k * HD : 2 * (k + 1) * HD] = dot(x, jnp.concatenate(w, axis=1), 1, 0).astype(BF)
+        w = jnp.concatenate([w0_ref[k], w1_ref[k]], axis=1)
+        out_ref[:, 2 * k * HD : 2 * (k + 1) * HD] = dot(x, w, 1, 0).astype(BF)
 
 
 def add_kernel(a_ref, b_ref, out_ref):
@@ -200,21 +200,25 @@
     q = queries.reshape(QROWS, HD)
     q_all = exchange(jnp.broadcast_to(q[None], (PEERS, QROWS, HD)), SPARSE).reshape(PEERS * QROWS, HD)
     kv = lax.all_gather(man_kv.reshape(1, 2, 2 * PAGE, HD), ("p", "c"), axis=0, tiled=True)
+    kv, w_out = tie((kv, w_out))
     parts = exchange(man_part(q_all, kv), SPARSE)
     own = own_part(pages, own_len, q, new_kv, own_kv.reshape(2, POOL * PAGE, HD))
-    out_w = jnp.concatenate([w_out, resid], axis=0)
-    parts, own, out_w_c, out_w_p = tie((parts, own, swap(out_w), pair(out_w)))
+    out_w = w_out
+    out_w = jnp.stack([out_w, pair(out_w)])
+    parts, own = tie((parts, own))
     place = (lax.axis_index(SPARSE) % 4).astype(jnp.int32).reshape(1)
     attn = exchange(join_part(place, parts, *own), SPARSE).reshape(rows, GROUP * HD)
     mlp_w = jnp.concatenate([w_gate, w_up], axis=0)
     mlp_w_p = pair(mlp_w)
-    attn, out_w_pc, mlp_w_p = tie((attn, swap(out_w_p), mlp_w_p))
-    out_ws = (out_w, out_w_c, out_w_p, out_w_pc)
-    res = [pick(pick(w[GROUP * HD :].reshape(PEERS, 2, 2, ROWS, HD), side, 1), core, 1) for w in out_ws]
-    res = jnp.concatenate(res, axis=-1).reshape(rows, 4 * HD).astype(F32)
-
+    attn, out_w_c = tie((attn, swap(out_w)))
+    out_ws = (out_w, out_w_c)
     share = dense(project_kernel, "project", (rows, 4 * HD), attn, *out_ws)
     share2 = lax.ppermute(share, "zh", [(0, 1), (1, 0)])
+    share2, resid = tie((share2, resid))
+    res = resid.reshape(PEERS, 2, 2, ROWS, HD)
+    res = jnp.stack([pick(res, core, 2), swap(pick(res, 1 - core, 2))], axis=3)
+    res = jnp.stack([pick(res, side, 1), pair(pick(res, 1 - side, 1))], axis=2)
+    res = res.reshape(rows, 4 * HD).astype(F32)
     heads = exchange(dense(add_kernel, "add_shares", (4, rows, 4 * HD), share, share2), "x")
     out4 = (res + heads.astype(F32).sum(0)).astype(BF)
     both = dense(

time: 115 us -> 126 us (1.096)
  blocking collectives: 5.88 us -> 27.4 us
  waiting for transfers between devices: 31.7 us -> 21.2 us
  local copies, waits for them, and re-layouts: 6.04 us -> 3.78 us
  starting transfers between devices: 59 us -> 60.6 us
    all_to_all x0 -> x1, blocking collectives: none -> 20.2 us  [exchange(): return lax.all_to_all(x, axes, 0, 0, tiled=True)]
    all_to_all x5 -> x4, waiting for transfers between devices: 26.3 us -> 15.7 us  [exchange(): return lax.all_to_all(x, axes, 0, 0, tiled=True)]
    ppermute x3 -> x4, starting transfers between devices: 8.99 us -> 13.7 us  [pair(): return lax.ppermute(x, 'p', [(0, 1), (1, 0)])]
    all_to_all x5 -> x4, starting transfers between devices: 31.7 us -> 28.6 us  [exchange(): return lax.all_to_all(x, axes, 0, 0, tiled=True)]
    slice x8 -> x0, local copies, waits for them, and re-layouts: 1.85 us -> none  [the longest x3 1.7 us: on_device(): w[GROUP * HD:].reshape(PEERS, 2, 2, ROWS, HD)]
    all_gather x1, blocking collectives: 5.88 us -> 7.18 us  [on_device(): lax.all_gather(man_kv.reshape(1, 2, 2 * PAGE, HD), ('p', 'c'), axis=0, ti...]
    ppermute x3 -> x4, waiting for transfers between devices: 3.95 us -> 3.96 us  [pair(): return lax.ppermute(x, 'p', [(0, 1), (1, 0)])]
  transfers between devices with their start and end apart: 14 -> 14, of which waited for: 8 -> 6; matrix products, arithmetic and copies ran while one was open for 4% -> 2% of each run, Pallas kernels for 6% -> 5%
where the time goes in v9:
time: 126 us; the launch traced here: 125 us
  starting transfers between devices  60.6 us (48%)
  blocking collectives  27.4 us (22%)
  waiting for transfers between devices  21.2 us (17%)
  Pallas kernels  9.25 us (7%)
  local copies, waits for them, and re-layouts  3.78 us (3%)
  other arithmetic  2.15 us (2%)
    all_to_all x4, starting transfers between devices, exchange(): return lax.all_to_all(x, axes, 0, 0, tiled=True)  28.6 us
    all_to_all x1, blocking collectives, exchange(): return lax.all_to_all(x, axes, 0, 0, tiled=True)  20.2 us
    all_to_all x4, waiting for transfers between devices, exchange(): return lax.all_to_all(x, axes, 0, 0, tiled=True)  15.7 us
    ppermute x4, starting transfers between devices, pair(): return lax.ppermute(x, 'p', [(0, 1), (1, 0)])  13.7 us
    ppermute x5, starting transfers between devices, swap(): return lax.ppermute(x, 'c', [(0, 1), (1, 0)])  10.1 us
    ppermute x1, starting transfers between devices, on_device(): share2 = lax.ppermute(share, 'zh', [(0, 1), (1, 0)])  8.22 us
    all_gather x1, blocking collectives, on_device(): lax.all_gather(man_kv.reshape(1, 2, 2 * PAGE, HD), ('p', 'c'), axis=0, ti...  7.18 us
    pallas_call x3, Pallas kernels, dense(): pl.pallas_call(kernel, out_shape=jax.ShapeDtypeStruct(out_shape, BF), in_...  4.84 us
  transfers between devices with their start and end apart: 14, of which 6 were waited for; matrix products, arithmetic and copies ran while one was open for 2% of the time, Pallas kernels for 5%

profile of v9, /device:TPU:2, one launch (start us, length us, event | category | flops | bytes accessed | tf_op | source)
XLA Modules:
  0.0 125.4 jit_solution(15101607612318959170)
XLA Ops:
  0.6 0.8 broadcast_in_dim.7.q_ref
  1.4 0.7 broadcast_in_dim.8
  2.1 10.8 %all-to-all-start = ((bf16[16,32,128]{2,1,0:T(8,128)(2,1)}), bf16[16,32,128]{2,1,0:T(8,128)(2,1)S(1)}, u32[]{:S(2)}, u32[]{:S(2)}) async-start(bf16[16,32,128]{2,1,0:T(8,128)(2,1)} %broadcast_in_dim.8), calls=%async_computation | async-start | bytes 262144 | tf_op jit(solution)/shard_map/all_to_all | solution.py:184
  12.9 7.2 %all_gather.3.kv_ref = bf16[4,2,128,128]{3,2,1,0:T(8,128)(2,1)S(1)} all-gather(bf16[1,2,128,128]{3,2,1,0:T(8,128)(2,1)} %bitcast.42), channel_id=1, replica_groups=mesh['y'=8,'zq'=2,'p'=2,'c'=2,'zh'=2,'x'=4] {'p','c'}, dimensions={0}, use_global_device_ids=true | all-gather | bytes 327680 | tf_op jit(solution)/shard_map/all_gather | solution.py:202
  20.1 3.5 %collective-permute-start = (bf16[1024,128]{1,0:T(8,128)(2,1)}, bf16[1024,128]{1,0:T(8,128)(2,1)}, u32[]{:S(2)}, u32[]{:S(2)}) collective-permute-start(bf16[1024,128]{1,0:T(8,128)(2,1)} %param.17), channel_id=1, source_target_pairs={{0,16},{16,0},{1,17},{17,1},{2,18},{18,2},{3,19},{19,3},{4,20},{20... | collective-permute-start | bytes 786440 | tf_op jit(solution)/shard_map/ppermute | solution.py:180
  23.7 2.6 %collective-permute-start.8 = (bf16[256,1792]{1,0:T(8,128)(2,1)S(1)}, bf16[256,1792]{1,0:T(8,128)(2,1)S(1)}, u32[]{:S(2)}, u32[]{:S(2)}) collective-permute-start(bf16[256,1792]{1,0:T(8,128)(2,1)S(1)} %constant_dynamic-update-slice_fusion.w0_ref), channel_id=1, source_target_pairs={{0,16},{16,0},{1,17},{17,1},{2,18},{18,2},{3,19},{19,3},{4,20},{20... | collective-permute-start | bytes 2752520 | tf_op jit(solution)/shard_map/ppermute | solution.py:180
  26.3 1.6 %manifest_attention.1 = bf16[16,40,128]{2,1,0:T(8,128)(2,1)} custom-call(bf16[512,128]{1,0:T(8,128)(2,1)S(1)} %bitcast.37, bf16[4,2,128,128]{3,2,1,0:T(8,128)(2,1)S(1)} %all_gather.3.kv_ref), custom_call_target="tpu_custom_call" | custom-call | tf_op jit(solution)/shard_map/manifest_attention/pallas_call | solution.py:89
  28.0 9.3 %all-to-all-start.1 = ((bf16[16,40,128]{2,1,0:T(8,128)(2,1)}), bf16[16,40,128]{2,1,0:T(8,128)(2,1)}, u32[]{:S(2)}, u32[]{:S(2)}) async-start(bf16[16,40,128]{2,1,0:T(8,128)(2,1)} %manifest_attention.1), calls=%async_computation.1 | async-start | bytes 327680 | tf_op jit(solution)/shard_map/all_to_all | solution.py:184
  37.3 1.1 pad_maximum_fusion.w0_ref
  38.4 1.9 %collective-permute-start.1 = (bf16[2,1024,128]{2,1,0:T(8,128)(2,1)S(1)}, bf16[2,1024,128]{2,1,0:T(8,128)(2,1)}, u32[]{:S(2)}, u32[]{:S(2)}) collective-permute-start(bf16[2,1024,128]{2,1,0:T(8,128)(2,1)S(1)} %pad_maximum_fusion.w0_ref), channel_id=1, source_target_pairs={{0,8},{8,0},{1,9},{9,1},{2,10},{10,2},{3,11},{11,3},{4,12},{12,4},... | collective-permute-start | bytes 1572872 | tf_op jit(solution)/shard_map/ppermute | solution.py:176
  40.4 0.6 copy-done.2
  41.0 1.2 own_attention.1
  42.2 9.0 %all-to-all-done.1.parts_ref = bf16[16,40,128]{2,1,0:T(8,128)(2,1)} async-done(((bf16[16,40,128]{2,1,0:T(8,128)(2,1)}), bf16[16,40,128]{2,1,0:T(8,128)(2,1)}, u32[]{:S(2)}, u32[]{:S(2)}) %all-to-all-start.1) | async-done | bytes 163872 | tf_op jit(solution)/shard_map/all_to_all | solution.py:184
  51.3 1.6 %join_attention.1 = bf16[16,4,1024]{2,1,0:T(4,128)(2,1)S(1)} custom-call(s32[1]{0:T(128)} %bitcast.place_ref, bf16[16,40,128]{2,1,0:T(8,128)(2,1)} %all-to-all-done.1.parts_ref, f32[32,128]{1,0:T(8,128)S(1)} %get-tuple-element.20.acc_ref, f32[32,128]{1,0:T(8,128)S(1)} %get-tuple-element.21.top_ref, f32[32,128]{1,0:T(8,128)S(1)} %get-tuple-element.22.total_ref), custom_call_target="tpu_custom_call" | custom-call | tf_op jit(solution)/shard_map/join_attention/pallas_call | solution.py:126
  52.8 20.2 %all_to_all.25 = bf16[16,4,1024]{2,1,0:T(4,128)(2,1)S(1)} all-to-all(bf16[16,4,1024]{2,1,0:T(4,128)(2,1)S(1)} %join_attention.1), channel_id=1, replica_groups=mesh['y'=8,'zq'=2,'p'=2,'c'=2,'zh'=2,'x'=4] {'y','zq'}, dimensions={0} | all-to-all | bytes 262144 | tf_op jit(solution)/shard_map/all_to_all | solution.py:184
  73.1 1.4 %project.1.a_ref = bf16[64,512]{1,0:T(8,128)(2,1)S(1)} custom-call(bf16[64,1024]{1,0:T(8,128)(2,1)S(1)} %reshape.80.x_ref, bf16[2,1024,128]{2,1,0:T(8,128)(2,1)S(1)} %pad_maximum_fusion.w0_ref, bf16[2,1024,128]{2,1,0:T(8,128)(2,1)} %collective-permute-done.1.w1_ref), custom_call_target="tpu_custom_call" | custom-call | tf_op jit(solution)/shard_map/project/pallas_call | solution.py:165
  74.4 8.2 %collective-permute-start.2 = (bf16[64,512]{1,0:T(8,128)(2,1)S(1)}, bf16[64,512]{1,0:T(8,128)(2,1)S(1)}, u32[]{:S(2)}, u32[]{:S(2)}) collective-permute-start(bf16[64,512]{1,0:T(8,128)(2,1)S(1)} %project.1.a_ref), channel_id=1, source_target_pairs={{0,4},{4,0},{1,5},{5,1},{2,6},{6,2},{3,7},{7,3},{8,12},{12,8},{9,1... | collective-permute-start | bytes 196616 | tf_op jit(solution)/shard_map/ppermute | solution.py:216
  82.7 1.9 %collective-permute-start.7 = (bf16[256,1792]{1,0:T(8,128)(2,1)S(1)}, bf16[256,1792]{1,0:T(8,128)(2,1)S(1)}, u32[]{:S(2)}, u32[]{:S(2)}) collective-permute-start(bf16[256,1792]{1,0:T(8,128)(2,1)S(1)} %constant_dynamic-update-slice_fusion.w0_ref), channel_id=1, source_target_pairs={{0,8},{8,0},{1,9},{9,1},{2,10},{10,2},{3,11},{11,3},{4,12},{12,4},... | collective-permute-start | bytes 2752520 | tf_op jit(solution)/shard_map/ppermute | solution.py:176
  84.9 2.1 %collective-permute-start.9 = (bf16[256,1792]{1,0:T(8,128)(2,1)S(1)}, bf16[256,1792]{1,0:T(8,128)(2,1)}, u32[]{:S(2)}, u32[]{:S(2)}) collective-permute-start(bf16[256,1792]{1,0:T(8,128)(2,1)S(1)} %collective-permute-done.8.w2_ref), channel_id=1, source_target_pairs={{0,8},{8,0},{1,9},{9,1},{2,10},{10,2},{3,11},{11,3},{4,12},{12,4},... | collective-permute-start | bytes 2752520 | tf_op jit(solution)/shard_map/ppermute | solution.py:176
  87.1 2.2 %collective-permute-start.3 = (bf16[16,2,4,128]{3,2,1,0:T(4,128)(2,1)S(1)}, bf16[16,2,4,128]{3,2,1,0:T(4,128)(2,1)S(1)}, u32[]{:S(2)}, u32[]{:S(2)}) collective-permute-start(bf16[16,2,4,128]{3,2,1,0:T(4,128)(2,1)S(1)} %get-tuple-element.33), channel_id=1, source_target_pairs={{0,8},{8,0},{1,9},{9,1},{2,10},{10,2},{3,11},{11,3},{4,12},{12,4},... | collective-permute-start | bytes 98312 | tf_op jit(solution)/shard_map/ppermute | solution.py:176
  89.3 0.7 add_shares.1
  90.0 4.8 %all-to-all-start.3 = ((bf16[4,64,512]{2,1,0:T(8,128)(2,1)}), bf16[4,64,512]{2,1,0:T(8,128)(2,1)S(1)}, u32[]{:S(2)}, u32[]{:S(2)}) async-start(bf16[4,64,512]{2,1,0:T(8,128)(2,1)} %add_shares.1), calls=%async_computation.3 | async-start | bytes 524288 | tf_op jit(solution)/shard_map/all_to_all | solution.py:184
  94.9 3.8 %collective-permute-start.4 = (bf16[16,4,2,128]{3,1,0,2:T(4,128)(2,1)S(1)}, bf16[16,4,2,128]{3,1,0,2:T(4,128)(2,1)S(1)}, u32[]{:S(2)}, u32[]{:S(2)}) collective-permute-start(bf16[16,4,2,128]{3,1,0,2:T(4,128)(2,1)S(1)} %select_bitcast_fusion), channel_id=1, source_target_pairs={{0,16},{16,0},{1,17},{17,1},{2,18},{18,2},{3,19},{19,3},{4,20},{20... | collective-permute-start | bytes 98312 | tf_op jit(solution)/shard_map/ppermute | solution.py:180
  98.8 2.0 %collective-permute-done.4 = bf16[16,4,2,128]{3,1,0,2:T(4,128)(2,1)S(1)} collective-permute-done((bf16[16,4,2,128]{3,1,0,2:T(4,128)(2,1)S(1)}, bf16[16,4,2,128]{3,1,0,2:T(4,128)(2,1)S(1)}, u32[]{:S(2)}, u32[]{:S(2)}) %collective-permute-start.4) | collective-permute-done | bytes 32800 | tf_op jit(solution)/shard_map/ppermute | solution.py:180
  101.8 2.7 %gate_up.1 = bf16[16,8,1792]{2,1,0:T(8,128)(2,1)} custom-call(bf16[64,512]{1,0:T(8,128)(2,1)S(1)} %add_convert_fusion.x_ref, bf16[256,1792]{1,0:T(8,128)(2,1)S(1)} %constant_dynamic-update-slice_fusion.w0_ref, bf16[256,1792]{1,0:T(8,128)(2,1)S(1)} %collective-permute-done.7.w1_ref, bf16[256,1792]{1,0:T(8,128)(2,1)S(1)} %collective-permute-done.8.w2_ref, ...), custom_call_target="tpu_custom_call" | custom-call | tf_op jit(solution)/shard_map/gate_up/pallas_call | solution.py:165
  104.5 3.7 %all-to-all-start.4 = ((bf16[16,8,1792]{2,1,0:T(8,128)(2,1)}), bf16[16,8,1792]{2,1,0:T(8,128)(2,1)S(1)}, u32[]{:S(2)}, u32[]{:S(2)}) async-start(bf16[16,8,1792]{2,1,0:T(8,128)(2,1)} %gate_up.1), calls=%async_computation.4 | async-start | bytes 917504 | tf_op jit(solution)/shard_map/all_to_all | solution.py:184
  108.3 3.8 %collective-permute-start.5 = (bf16[16,4,2,128]{3,1,0,2:T(4,128)(2,1)S(1)}, bf16[16,4,2,128]{3,1,0,2:T(4,128)(2,1)S(1)}, u32[]{:S(2)}, u32[]{:S(2)}) collective-permute-start(bf16[16,4,2,128]{3,1,0,2:T(4,128)(2,1)S(1)} %get-tuple-element.31), channel_id=1, source_target_pairs={{0,16},{16,0},{1,17},{17,1},{2,18},{18,2},{3,19},{19,3},{4,20},{20... | collective-permute-start | bytes 98312 | tf_op jit(solution)/shard_map/ppermute | solution.py:180
  112.1 2.0 %collective-permute-done.5 = bf16[16,4,2,128]{3,1,0,2:T(4,128)(2,1)S(1)} collective-permute-done((bf16[16,4,2,128]{3,1,0,2:T(4,128)(2,1)S(1)}, bf16[16,4,2,128]{3,1,0,2:T(4,128)(2,1)S(1)}, u32[]{:S(2)}, u32[]{:S(2)}) %collective-permute-start.5) | collective-permute-done | bytes 32800 | tf_op jit(solution)/shard_map/ppermute | solution.py:180
  114.2 1.9 %collective-permute-start.6 = (bf16[16,2,4,128]{3,2,0,1:T(4,128)(2,1)S(1)}, bf16[16,2,4,128]{3,2,0,1:T(4,128)(2,1)S(1)}, u32[]{:S(2)}, u32[]{:S(2)}) collective-permute-start(bf16[16,2,4,128]{3,2,0,1:T(4,128)(2,1)S(1)} %get-tuple-element.29), channel_id=1, source_target_pairs={{0,8},{8,0},{1,9},{9,1},{2,10},{10,2},{3,11},{11,3},{4,12},{12,4},... | collective-permute-start | bytes 98312 | tf_op jit(solution)/shard_map/ppermute | solution.py:176
  116.1 1.2 collective-permute-done.6
  117.4 0.7 copy.39
  118.0 6.7 %all-to-all-done.4 = bf16[16,8,1792]{2,1,0:T(8,128)(2,1)S(1)} async-done(((bf16[16,8,1792]{2,1,0:T(8,128)(2,1)}), bf16[16,8,1792]{2,1,0:T(8,128)(2,1)S(1)}, u32[]{:S(2)}, u32[]{:S(2)}) %all-to-all-start.4) | async-done | bytes 458784 | tf_op jit(solution)/shard_map/all_to_all | solution.py:184
  (45 shorter events, 2.5 us)
Async XLA Ops:
  0.6 22.9 %copy-start.4 = (bf16[128,1792]{1,0:T(8,128)(2,1)S(1)}, bf16[128,1792]{1,0:T(8,128)(2,1)}, u32[]{:S(2)}) copy-start(bf16[128,1792]{1,0:T(8,128)(2,1)} %param.18) | copy-start | bytes 1376260
  2.1 24.2 %all-to-all-start = ((bf16[16,32,128]{2,1,0:T(8,128)(2,1)}), bf16[16,32,128]{2,1,0:T(8,128)(2,1)S(1)}, u32[]{:S(2)}, u32[]{:S(2)}) async-start(bf16[16,32,128]{2,1,0:T(8,128)(2,1)} %broadcast_in_dim.8), calls=%async_computation | async-start | bytes 262144 | tf_op jit(solution)/shard_map/all_to_all | solution.py:184
  20.1 3.5 %copy-start.5 = (bf16[128,1792]{1,0:T(8,128)(2,1)S(1)}, bf16[128,1792]{1,0:T(8,128)(2,1)}, u32[]{:S(2)}) copy-start(bf16[128,1792]{1,0:T(8,128)(2,1)} %param.19) | copy-start | bytes 1376260
  20.1 17.2 %collective-permute-start = (bf16[1024,128]{1,0:T(8,128)(2,1)}, bf16[1024,128]{1,0:T(8,128)(2,1)}, u32[]{:S(2)}, u32[]{:S(2)}) collective-permute-start(bf16[1024,128]{1,0:T(8,128)(2,1)} %param.17), channel_id=1, source_target_pairs={{0,16},{16,0},{1,17},{17,1},{2,18},{18,2},{3,19},{19,3},{4,20},{20... | collective-permute-start | bytes 786440 | tf_op jit(solution)/shard_map/ppermute | solution.py:180
  23.7 16.7 %copy-start = (bf16[2,32,64,128]{3,2,1,0:T(8,128)(2,1)S(1)}, bf16[2,32,64,128]{3,2,1,0:T(8,128)(2,1)}, u32[]{:S(2)}) copy-start(bf16[2,32,64,128]{3,2,1,0:T(8,128)(2,1)} %param.12) | copy-start | bytes 3145732
  23.7 61.2 %collective-permute-start.8 = (bf16[256,1792]{1,0:T(8,128)(2,1)S(1)}, bf16[256,1792]{1,0:T(8,128)(2,1)S(1)}, u32[]{:S(2)}, u32[]{:S(2)}) collective-permute-start(bf16[256,1792]{1,0:T(8,128)(2,1)S(1)} %constant_dynamic-update-slice_fusion.w0_ref), channel_id=1, source_target_pairs={{0,16},{16,0},{1,17},{17,1},{2,18},{18,2},{3,19},{19,3},{4,20},{20... | collective-permute-start | bytes 2752520 | tf_op jit(solution)/shard_map/ppermute | solution.py:180
  28.0 23.3 %all-to-all-start.1 = ((bf16[16,40,128]{2,1,0:T(8,128)(2,1)}), bf16[16,40,128]{2,1,0:T(8,128)(2,1)}, u32[]{:S(2)}, u32[]{:S(2)}) async-start(bf16[16,40,128]{2,1,0:T(8,128)(2,1)} %manifest_attention.1), calls=%async_computation.1 | async-start | bytes 327680 | tf_op jit(solution)/shard_map/all_to_all | solution.py:184
  38.4 34.7 %collective-permute-start.1 = (bf16[2,1024,128]{2,1,0:T(8,128)(2,1)S(1)}, bf16[2,1024,128]{2,1,0:T(8,128)(2,1)}, u32[]{:S(2)}, u32[]{:S(2)}) collective-permute-start(bf16[2,1024,128]{2,1,0:T(8,128)(2,1)S(1)} %pad_maximum_fusion.w0_ref), channel_id=1, source_target_pairs={{0,8},{8,0},{1,9},{9,1},{2,10},{10,2},{3,11},{11,3},{4,12},{12,4},... | collective-permute-start | bytes 1572872 | tf_op jit(solution)/shard_map/ppermute | solution.py:176
  40.3 0.7 copy-start.2
  40.3 0.7 copy-start.1
  40.3 0.7 copy-start.3
  73.0 14.0 %copy-start.8 = (bf16[256,128]{1,0:T(8,128)(2,1)S(1)}, bf16[256,128]{1,0:T(8,128)(2,1)}, u32[]{:S(2)}) copy-start(bf16[256,128]{1,0:T(8,128)(2,1)} %param.16) | copy-start | bytes 196612
  74.4 10.5 %collective-permute-start.2 = (bf16[64,512]{1,0:T(8,128)(2,1)S(1)}, bf16[64,512]{1,0:T(8,128)(2,1)S(1)}, u32[]{:S(2)}, u32[]{:S(2)}) collective-permute-start(bf16[64,512]{1,0:T(8,128)(2,1)S(1)} %project.1.a_ref), channel_id=1, source_target_pairs={{0,4},{4,0},{1,5},{5,1},{2,6},{6,2},{3,7},{7,3},{8,12},{12,8},{9,1... | collective-permute-start | bytes 196616 | tf_op jit(solution)/shard_map/ppermute | solution.py:216
  82.7 19.1 %collective-permute-start.7 = (bf16[256,1792]{1,0:T(8,128)(2,1)S(1)}, bf16[256,1792]{1,0:T(8,128)(2,1)S(1)}, u32[]{:S(2)}, u32[]{:S(2)}) collective-permute-start(bf16[256,1792]{1,0:T(8,128)(2,1)S(1)} %constant_dynamic-update-slice_fusion.w0_ref), channel_id=1, source_target_pairs={{0,8},{8,0},{1,9},{9,1},{2,10},{10,2},{3,11},{11,3},{4,12},{12,4},... | collective-permute-start | bytes 2752520 | tf_op jit(solution)/shard_map/ppermute | solution.py:176
  84.9 16.8 %collective-permute-start.9 = (bf16[256,1792]{1,0:T(8,128)(2,1)S(1)}, bf16[256,1792]{1,0:T(8,128)(2,1)}, u32[]{:S(2)}, u32[]{:S(2)}) collective-permute-start(bf16[256,1792]{1,0:T(8,128)(2,1)S(1)} %collective-permute-done.8.w2_ref), channel_id=1, source_target_pairs={{0,8},{8,0},{1,9},{9,1},{2,10},{10,2},{3,11},{11,3},{4,12},{12,4},... | collective-permute-start | bytes 2752520 | tf_op jit(solution)/shard_map/ppermute | solution.py:176
  87.1 7.8 %collective-permute-start.3 = (bf16[16,2,4,128]{3,2,1,0:T(4,128)(2,1)S(1)}, bf16[16,2,4,128]{3,2,1,0:T(4,128)(2,1)S(1)}, u32[]{:S(2)}, u32[]{:S(2)}) collective-permute-start(bf16[16,2,4,128]{3,2,1,0:T(4,128)(2,1)S(1)} %get-tuple-element.33), channel_id=1, source_target_pairs={{0,8},{8,0},{1,9},{9,1},{2,10},{10,2},{3,11},{11,3},{4,12},{12,4},... | collective-permute-start | bytes 98312 | tf_op jit(solution)/shard_map/ppermute | solution.py:176
  90.0 11.5 %all-to-all-start.3 = ((bf16[4,64,512]{2,1,0:T(8,128)(2,1)}), bf16[4,64,512]{2,1,0:T(8,128)(2,1)S(1)}, u32[]{:S(2)}, u32[]{:S(2)}) async-start(bf16[4,64,512]{2,1,0:T(8,128)(2,1)} %add_shares.1), calls=%async_computation.3 | async-start | bytes 524288 | tf_op jit(solution)/shard_map/all_to_all | solution.py:184
  94.9 5.8 %collective-permute-start.4 = (bf16[16,4,2,128]{3,1,0,2:T(4,128)(2,1)S(1)}, bf16[16,4,2,128]{3,1,0,2:T(4,128)(2,1)S(1)}, u32[]{:S(2)}, u32[]{:S(2)}) collective-permute-start(bf16[16,4,2,128]{3,1,0,2:T(4,128)(2,1)S(1)} %select_bitcast_fusion), channel_id=1, source_target_pairs={{0,16},{16,0},{1,17},{17,1},{2,18},{18,2},{3,19},{19,3},{4,20},{20... | collective-permute-start | bytes 98312 | tf_op jit(solution)/shard_map/ppermute | solution.py:180
  100.7 0.6 copy-start.6
  104.5 3.7 %copy-start.7 = (bf16[16,4,2,128]{3,1,0,2:T(4,128)(2,1)S(1)}, bf16[16,4,2,128]{3,1,0,2:T(4,128)(2,1)}, u32[]{:S(2)}) copy-start(bf16[16,4,2,128]{3,1,0,2:T(4,128)(2,1)} %copy-done.6) | copy-start | bytes 98308
  104.5 20.2 %all-to-all-start.4 = ((bf16[16,8,1792]{2,1,0:T(8,128)(2,1)}), bf16[16,8,1792]{2,1,0:T(8,128)(2,1)S(1)}, u32[]{:S(2)}, u32[]{:S(2)}) async-start(bf16[16,8,1792]{2,1,0:T(8,128)(2,1)} %gate_up.1), calls=%async_computation.4 | async-start | bytes 917504 | tf_op jit(solution)/shard_map/all_to_all | solution.py:184
  108.3 5.8 %collective-permute-start.5 = (bf16[16,4,2,128]{3,1,0,2:T(4,128)(2,1)S(1)}, bf16[16,4,2,128]{3,1,0,2:T(4,128)(2,1)S(1)}, u32[]{:S(2)}, u32[]{:S(2)}) collective-permute-start(bf16[16,4,2,128]{3,1,0,2:T(4,128)(2,1)S(1)} %get-tuple-element.31), channel_id=1, source_target_pairs={{0,16},{16,0},{1,17},{17,1},{2,18},{18,2},{3,19},{19,3},{4,20},{20... | collective-permute-start | bytes 98312 | tf_op jit(solution)/shard_map/ppermute | solution.py:180
  114.2 3.1 %collective-permute-start.6 = (bf16[16,2,4,128]{3,2,0,1:T(4,128)(2,1)S(1)}, bf16[16,2,4,128]{3,2,0,1:T(4,128)(2,1)S(1)}, u32[]{:S(2)}, u32[]{:S(2)}) collective-permute-start(bf16[16,2,4,128]{3,2,0,1:T(4,128)(2,1)S(1)} %get-tuple-element.29), channel_id=1, source_target_pairs={{0,8},{8,0},{1,9},{9,1},{2,10},{10,2},{3,11},{11,3},{4,12},{12,4},... | collective-permute-start | bytes 98312 | tf_op jit(solution)/shard_map/ppermute | solution.py:176

commit v10 on v7

--- a/solution.py
+++ b/solution.py
@@ -141,19 +141,23 @@
     out_ref[...] = dot(x_ref[...], w, 1, 0).astype(BF)
 
 
-def add_kernel(a_ref, b_ref, out_ref):
-    block = (a_ref[...].astype(F32) + b_ref[...].astype(F32)).astype(BF)
+def add_kernel(a_ref, out_ref):
+    block = (a_ref[0].astype(F32) + a_ref[1].astype(F32)).astype(BF)
     for i in range(4):
         out_ref[i] = block
 
 
 def mlp_kernel(x_ref, g0_ref, g1_ref, u0_ref, u1_ref, out_ref):
     x = x_ref[...]
+    turned = x.astype(F32).reshape(CHIPS // 2, 2 * ROWS, 2 * HD)
+    turned = jnp.concatenate([turned[:, ROWS:], turned[:, :ROWS]], axis=1).reshape(CHIPS * ROWS, 2 * HD).astype(BF)
     gate = dot(x, jnp.concatenate([g0_ref[...], g1_ref[...]], axis=0), 1, 0)
-    up = dot(x, jnp.concatenate([u0_ref[...], u1_ref[...]], axis=0), 1, 0)
-    for j in range(CHIPS):
-        at = slice(j * ROWS, (j + 1) * ROWS)
-        out_ref[j] = jnp.concatenate([gate[at], up[at]], axis=0).astype(BF)
+    up = dot(turned, jnp.concatenate([u0_ref[...], u1_ref[...]], axis=0), 1, 0)
+    low = lax.broadcasted_iota(jnp.int32, (2 * ROWS, gate.shape[1]), 0) < ROWS
+    for j in range(CHIPS // 2):
+        at = slice(2 * j * ROWS, 2 * (j + 1) * ROWS)
+        out_ref[2 * j] = jnp.where(low, gate[at], up[at]).astype(BF)
+        out_ref[2 * j + 1] = jnp.where(low, up[at], gate[at]).astype(BF)
 
 
 def dense(kernel, name, out_shape, *args):
@@ -189,19 +193,23 @@
     parts, own, w_out_c = tie((parts, own, swap(w_out)))
     place = (lax.axis_index(SPARSE) % 4).astype(jnp.int32).reshape(1)
     attn = exchange(join_part(place, parts, *own), PLANE).reshape(rows, GROUP * HD)
+    attn, w_gate_c, w_up_c = tie((attn, swap(w_gate), swap(w_up)))
+
+    share = dense(project_kernel, "project", (rows, 2 * HD), attn, w_out, w_out_c)
+    shares = lax.all_gather(share, "zh", axis=0)
+    shares, resid = tie((shares, resid))
+    heads = exchange(dense(add_kernel, "add_shares", (4, rows, 2 * HD), shares), "x")
     res = resid.reshape(CHIPS, 2, ROWS, HD)
     mine = jnp.where(core == 0, res[:, 0], res[:, 1])
     theirs = swap(jnp.where(core == 0, res[:, 1], res[:, 0]))
     res = jnp.concatenate([mine, theirs], axis=-1).reshape(rows, 2 * HD).astype(F32)
-    attn, w_gate_c, w_up_c, res = tie((attn, swap(w_gate), swap(w_up), res))
-
-    share = dense(project_kernel, "project", (rows, 2 * HD), attn, w_out, w_out_c)
-    share2 = lax.ppermute(share, "zh", [(0, 1), (1, 0)])
-    heads = exchange(dense(add_kernel, "add_shares", (4, rows, 2 * HD), share, share2), "x")
     out2 = (res + heads.astype(F32).sum(0)).astype(BF)
     both = dense(mlp_kernel, "gate_up", (CHIPS, 2 * ROWS, width), out2, w_gate, w_gate_c, w_up, w_up_c)
     joined = exchange(both, PLANE).astype(F32).sum(0)
-    hidden = (jax.nn.silu(joined[:ROWS]) * joined[ROWS:]).astype(BF)
+    odd = lax.axis_index("p") == 1
+    gate = jnp.where(odd, joined[ROWS:], joined[:ROWS])
+    up = jnp.where(odd, joined[:ROWS], joined[ROWS:])
+    hidden = (jax.nn.silu(gate) * up).astype(BF)
 
     kept = out2[:, :HD].reshape(CHIPS, 1, ROWS, HD)
     given = swap(out2[:, HD:]).reshape(CHIPS, 1, ROWS, HD)

time: 116 us -> 113 us (0.974)
  the two profiles are of different devices: /device:TPU:16 before, /device:TPU:2 now
where the time goes in v10:
time: 113 us; the launch traced here: 112 us
  waiting for transfers between devices  45.3 us (40%)
  starting transfers between devices  39.6 us (35%)
  blocking collectives  16.5 us (15%)
  Pallas kernels  6.54 us (6%)
  local copies, waits for them, and re-layouts  2.28 us (2%)
    all_to_all x5, waiting for transfers between devices, exchange(): return lax.all_to_all(x, axes, 0, 0, tiled=True)  42.8 us
    all_to_all x5, starting transfers between devices, exchange(): return lax.all_to_all(x, axes, 0, 0, tiled=True)  29.4 us
    ppermute x5, starting transfers between devices, swap(): return lax.ppermute(x, 'c', [(0, 1), (1, 0)])  10.1 us
    all_gather x1, blocking collectives, on_device(): shares = lax.all_gather(share, 'zh', axis=0)  9.34 us
    all_gather x1, blocking collectives, on_device(): lax.all_gather(man_kv.reshape(1, 2, 2 * PAGE, HD), ('p', 'c'), axis=0, ti...  7.18 us
    ppermute x5, waiting for transfers between devices, swap(): return lax.ppermute(x, 'c', [(0, 1), (1, 0)])  2.51 us
    pallas_call x3, Pallas kernels, dense(): pl.pallas_call(kernel, out_shape=jax.ShapeDtypeStruct(out_shape, BF), in_...  2.31 us
  transfers between devices with their start and end apart: 10, of which 8 were waited for; matrix products, arithmetic and copies ran while one was open for 1% of the time, Pallas kernels for 1%

profile of v10, /device:TPU:2, one launch (start us, length us, event | category | flops | bytes accessed | tf_op | source)
XLA Modules:
  0.0 112.1 jit_solution(4465461901870989783)
XLA Ops:
  0.7 0.8 broadcast_in_dim.7.q_ref
  1.5 0.7 broadcast_in_dim.8
  2.2 10.8 %all-to-all-start = ((bf16[16,32,128]{2,1,0:T(8,128)(2,1)}), bf16[16,32,128]{2,1,0:T(8,128)(2,1)S(1)}, u32[]{:S(2)}, u32[]{:S(2)}) async-start(bf16[16,32,128]{2,1,0:T(8,128)(2,1)} %broadcast_in_dim.8), calls=%async_computation | async-start | bytes 262144 | tf_op jit(solution)/shard_map/all_to_all | solution.py:180
  13.0 7.2 %all_gather.9.kv_ref = bf16[4,2,128,128]{3,2,1,0:T(8,128)(2,1)S(1)} all-gather(bf16[1,2,128,128]{3,2,1,0:T(8,128)(2,1)} %bitcast.30), channel_id=1, replica_groups=mesh['y'=8,'zq'=2,'p'=2,'c'=2,'zh'=2,'x'=4] {'p','c'}, dimensions={0}, use_global_device_ids=true | all-gather | bytes 327680 | tf_op jit(solution)/shard_map/all_gather | solution.py:190
  20.2 3.3 %all-to-all-done = bf16[16,32,128]{2,1,0:T(8,128)(2,1)S(1)} async-done(((bf16[16,32,128]{2,1,0:T(8,128)(2,1)}), bf16[16,32,128]{2,1,0:T(8,128)(2,1)S(1)}, u32[]{:S(2)}, u32[]{:S(2)}) %all-to-all-start) | async-done | bytes 131104 | tf_op jit(solution)/shard_map/all_to_all | solution.py:180
  23.5 1.6 %manifest_attention.1 = bf16[16,40,128]{2,1,0:T(8,128)(2,1)} custom-call(bf16[512,128]{1,0:T(8,128)(2,1)S(1)} %bitcast.26, bf16[4,2,128,128]{3,2,1,0:T(8,128)(2,1)S(1)} %all_gather.9.kv_ref), custom_call_target="tpu_custom_call" | custom-call | tf_op jit(solution)/shard_map/manifest_attention/pallas_call | solution.py:91
  25.1 5.9 %all-to-all-start.1 = ((bf16[16,40,128]{2,1,0:T(8,128)(2,1)}), bf16[16,40,128]{2,1,0:T(8,128)(2,1)S(1)}, u32[]{:S(2)}, u32[]{:S(2)}) async-start(bf16[16,40,128]{2,1,0:T(8,128)(2,1)} %manifest_attention.1), calls=%async_computation.1 | async-start | bytes 327680 | tf_op jit(solution)/shard_map/all_to_all | solution.py:180
  31.1 2.0 %collective-permute-start = (bf16[1024,128]{1,0:T(8,128)(2,1)S(1)}, bf16[1024,128]{1,0:T(8,128)(2,1)S(1)}, u32[]{:S(2)}, u32[]{:S(2)}) collective-permute-start(bf16[1024,128]{1,0:T(8,128)(2,1)S(1)} %copy-done.3), channel_id=1, source_target_pairs={{0,8},{8,0},{1,9},{9,1},{2,10},{10,2},{3,11},{11,3},{4,12},{12,4},... | collective-permute-start | bytes 786440 | tf_op jit(solution)/shard_map/ppermute | solution.py:176
  33.2 1.2 %own_attention.1 = (f32[32,128]{1,0:T(8,128)S(1)}, f32[32,128]{1,0:T(8,128)S(1)}, f32[32,128]{1,0:T(8,128)S(1)}) custom-call(s32[4,8]{1,0:T(4,128)S(1)} %copy-done.4, s32[4]{0:T(128)S(1)} %copy-done.6, bf16[32,128]{1,0:T(8,128)(2,1)S(1)} %broadcast_in_dim.7.q_ref, bf16[2,4,128]{2,1,0:T(4,128)(2,1)S(1)} %copy-done.5, bf16[2,2048,128]{2,1,0:T(8,128)(2,1)S(1)} %bitcast.25), custom_call_target="tpu_custom_call" | custom-call | tf_op jit(solution)/shard_map/own_attention/pallas_call | solution.py:60
  34.4 0.2 collective-permute-done.w1_ref
  34.5 8.1 %all-to-all-done.1.parts_ref = bf16[16,40,128]{2,1,0:T(8,128)(2,1)S(1)} async-done(((bf16[16,40,128]{2,1,0:T(8,128)(2,1)}), bf16[16,40,128]{2,1,0:T(8,128)(2,1)S(1)}, u32[]{:S(2)}, u32[]{:S(2)}) %all-to-all-start.1) | async-done | bytes 163872 | tf_op jit(solution)/shard_map/all_to_all | solution.py:180
  42.7 1.4 %join_attention.1 = bf16[32,4,1024]{2,1,0:T(4,128)(2,1)} custom-call(s32[1]{0:T(128)} %bitcast.place_ref, bf16[16,40,128]{2,1,0:T(8,128)(2,1)S(1)} %all-to-all-done.1.parts_ref, f32[32,128]{1,0:T(8,128)S(1)} %get-tuple-element.19.acc_ref, f32[32,128]{1,0:T(8,128)S(1)} %get-tuple-element.20.top_ref, f32[32,128]{1,0:T(8,128)S(1)} %get-tuple-element.21.total_ref), custom_call_target="tpu_custom_call" | custom-call | tf_op jit(solution)/shard_map/join_attention/pallas_call | solution.py:128
  44.0 3.9 %all-to-all-start.2 = ((bf16[32,4,1024]{2,1,0:T(4,128)(2,1)}), bf16[32,4,1024]{2,1,0:T(4,128)(2,1)S(1)}, u32[]{:S(2)}, u32[]{:S(2)}) async-start(bf16[32,4,1024]{2,1,0:T(4,128)(2,1)} %join_attention.1), calls=%async_computation.2 | async-start | bytes 524288 | tf_op jit(solution)/shard_map/all_to_all | solution.py:180
  47.9 1.9 %collective-permute-start.1 = (bf16[128,1792]{1,0:T(8,128)(2,1)S(1)}, bf16[128,1792]{1,0:T(8,128)(2,1)S(1)}, u32[]{:S(2)}, u32[]{:S(2)}) collective-permute-start(bf16[128,1792]{1,0:T(8,128)(2,1)S(1)} %copy-done.1), channel_id=1, source_target_pairs={{0,8},{8,0},{1,9},{9,1},{2,10},{10,2},{3,11},{11,3},{4,12},{12,4},... | collective-permute-start | bytes 1376264 | tf_op jit(solution)/shard_map/ppermute | solution.py:176
  49.9 2.4 %collective-permute-start.2 = (bf16[128,1792]{1,0:T(8,128)(2,1)S(1)}, bf16[128,1792]{1,0:T(8,128)(2,1)S(1)}, u32[]{:S(2)}, u32[]{:S(2)}) collective-permute-start(bf16[128,1792]{1,0:T(8,128)(2,1)S(1)} %copy-done.2), channel_id=1, source_target_pairs={{0,8},{8,0},{1,9},{9,1},{2,10},{10,2},{3,11},{11,3},{4,12},{12,4},... | collective-permute-start | bytes 1376264 | tf_op jit(solution)/shard_map/ppermute | solution.py:176
  52.3 8.5 %all-to-all-done.2 = bf16[32,4,1024]{2,1,0:T(4,128)(2,1)S(1)} async-done(((bf16[32,4,1024]{2,1,0:T(4,128)(2,1)}), bf16[32,4,1024]{2,1,0:T(4,128)(2,1)S(1)}, u32[]{:S(2)}, u32[]{:S(2)}) %all-to-all-start.2) | async-done | bytes 262176 | tf_op jit(solution)/shard_map/all_to_all | solution.py:180
  60.8 0.1 reshape.84.x_ref
  60.9 0.2 project.1
  61.1 9.3 %all-gather = bf16[256,256]{1,0:T(8,128)(2,1)S(1)} all-gather(bf16[128,256]{1,0:T(8,128)(2,1)S(1)} %project.1), channel_id=2, replica_groups=mesh['y'=8,'zq'=2,'p'=2,'c'=2,'zh'=2,'x'=4] {'zh'}, dimensions={0}, use_global_device_ids=true | all-gather | bytes 196608 | tf_op jit(solution)/shard_map/all_gather | solution.py:199
  70.4 0.7 add_shares.1
  71.2 4.8 %all-to-all-start.3 = ((bf16[4,128,256]{2,1,0:T(8,128)(2,1)}), bf16[4,128,256]{2,1,0:T(8,128)(2,1)S(1)}, u32[]{:S(2)}, u32[]{:S(2)}) async-start(bf16[4,128,256]{2,1,0:T(8,128)(2,1)} %add_shares.1), calls=%async_computation.3 | async-start | bytes 524288 | tf_op jit(solution)/shard_map/all_to_all | solution.py:180
  76.0 1.9 %collective-permute-start.3 = (bf16[32,4,128]{2,1,0:T(4,128)(2,1)S(1)}, bf16[32,4,128]{2,1,0:T(4,128)(2,1)S(1)}, u32[]{:S(2)}, u32[]{:S(2)}) collective-permute-start(bf16[32,4,128]{2,1,0:T(4,128)(2,1)S(1)} %get-tuple-element.31), channel_id=1, source_target_pairs={{0,8},{8,0},{1,9},{9,1},{2,10},{10,2},{3,11},{11,3},{4,12},{12,4},... | collective-permute-start | bytes 98312 | tf_op jit(solution)/shard_map/ppermute | solution.py:176
  78.0 1.2 %collective-permute-done.3 = bf16[32,4,128]{2,1,0:T(4,128)(2,1)S(1)} collective-permute-done((bf16[32,4,128]{2,1,0:T(4,128)(2,1)S(1)}, bf16[32,4,128]{2,1,0:T(4,128)(2,1)S(1)}, u32[]{:S(2)}, u32[]{:S(2)}) %collective-permute-start.3) | collective-permute-done | bytes 32800 | tf_op jit(solution)/shard_map/ppermute | solution.py:176
  79.2 2.0 %all-to-all-done.3 = bf16[4,128,256]{2,1,0:T(8,128)(2,1)S(1)} async-done(((bf16[4,128,256]{2,1,0:T(8,128)(2,1)}), bf16[4,128,256]{2,1,0:T(8,128)(2,1)S(1)}, u32[]{:S(2)}, u32[]{:S(2)}) %all-to-all-start.3) | async-done | bytes 262176 | tf_op jit(solution)/shard_map/all_to_all | solution.py:180
  81.3 1.4 %gate_up.1 = bf16[32,8,1792]{2,1,0:T(8,128)(2,1)} custom-call(bf16[128,256]{1,0:T(8,128)(2,1)S(1)} %add_convert_fusion.x_ref, bf16[128,1792]{1,0:T(8,128)(2,1)S(1)} %copy-done.1, bf16[128,1792]{1,0:T(8,128)(2,1)S(1)} %collective-permute-done.1.g1_ref, bf16[128,1792]{1,0:T(8,128)(2,1)S(1)} %copy-done.2, bf16[128,1792]{1,0:T(8,128)(2,1)S(1)} %collective-permute-done.2.u1_ref), custom_call_target="tpu_custom_call" | custom-call | tf_op jit(solution)/shard_map/gate_up/pallas_call | solution.py:165
  82.6 4.0 %all-to-all-start.4 = ((bf16[32,8,1792]{2,1,0:T(8,128)(2,1)}), bf16[32,8,1792]{2,1,0:T(8,128)(2,1)S(1)}, u32[]{:S(2)}, u32[]{:S(2)}) async-start(bf16[32,8,1792]{2,1,0:T(8,128)(2,1)} %gate_up.1), calls=%async_computation.4 | async-start | bytes 1835008 | tf_op jit(solution)/shard_map/all_to_all | solution.py:180
  86.6 1.9 %collective-permute-start.4 = (bf16[128,128]{1,0:T(8,128)(2,1)S(1)}, bf16[128,128]{1,0:T(8,128)(2,1)S(1)}, u32[]{:S(2)}, u32[]{:S(2)}) collective-permute-start(bf16[128,128]{1,0:T(8,128)(2,1)S(1)} %slice.31), channel_id=1, source_target_pairs={{0,8},{8,0},{1,9},{9,1},{2,10},{10,2},{3,11},{11,3},{4,12},{12,4},... | collective-permute-start | bytes 98312 | tf_op jit(solution)/shard_map/ppermute | solution.py:176
  88.5 1.2 %collective-permute-done.4 = bf16[128,128]{1,0:T(8,128)(2,1)S(1)} collective-permute-done((bf16[128,128]{1,0:T(8,128)(2,1)S(1)}, bf16[128,128]{1,0:T(8,128)(2,1)S(1)}, u32[]{:S(2)}, u32[]{:S(2)}) %collective-permute-start.4) | collective-permute-done | bytes 32800 | tf_op jit(solution)/shard_map/ppermute | solution.py:176
  89.8 0.7 copy.17
  90.4 20.8 %all-to-all-done.4 = bf16[32,8,1792]{2,1,0:T(8,128)(2,1)S(1)} async-done(((bf16[32,8,1792]{2,1,0:T(8,128)(2,1)}), bf16[32,8,1792]{2,1,0:T(8,128)(2,1)S(1)}, u32[]{:S(2)}, u32[]{:S(2)}) %all-to-all-start.4) | async-done | bytes 917536 | tf_op jit(solution)/shard_map/all_to_all | solution.py:180
  111.3 0.1 convert_reduce_fusion
  111.4 0.6 fusion.1
  (26 shorter events, 0.3 us)
Async XLA Ops:
  0.6 30.5 %copy-start.3 = (bf16[1024,128]{1,0:T(8,128)(2,1)S(1)}, bf16[1024,128]{1,0:T(8,128)(2,1)}, u32[]{:S(2)}) copy-start(bf16[1024,128]{1,0:T(8,128)(2,1)} %w0_ref.1) | copy-start | bytes 786436
  0.6 32.5 %copy-start.6 = (s32[4]{0:T(128)S(1)}, s32[4]{0:T(128)}, u32[]{:S(2)}) copy-start(s32[4]{0:T(128)} %len_ref.1) | copy-start | bytes 52
  0.7 32.5 %copy-start.4 = (s32[4,8]{1,0:T(4,128)S(1)}, s32[4,8]{1,0:T(4,128)}, u32[]{:S(2)}) copy-start(s32[4,8]{1,0:T(4,128)} %pages_ref.1) | copy-start | bytes 388
  0.7 32.5 %copy-start = (bf16[2,32,64,128]{3,2,1,0:T(8,128)(2,1)S(1)}, bf16[2,32,64,128]{3,2,1,0:T(8,128)(2,1)}, u32[]{:S(2)}) copy-start(bf16[2,32,64,128]{3,2,1,0:T(8,128)(2,1)} %param.12) | copy-start | bytes 3145732
  0.7 32.5 %copy-start.5 = (bf16[2,4,128]{2,1,0:T(4,128)(2,1)S(1)}, bf16[2,4,128]{2,1,0:T(4,128)(2,1)}, u32[]{:S(2)}) copy-start(bf16[2,4,128]{2,1,0:T(4,128)(2,1)} %new_ref.1) | copy-start | bytes 6148
  2.2 21.3 %all-to-all-start = ((bf16[16,32,128]{2,1,0:T(8,128)(2,1)}), bf16[16,32,128]{2,1,0:T(8,128)(2,1)S(1)}, u32[]{:S(2)}, u32[]{:S(2)}) async-start(bf16[16,32,128]{2,1,0:T(8,128)(2,1)} %broadcast_in_dim.8), calls=%async_computation | async-start | bytes 262144 | tf_op jit(solution)/shard_map/all_to_all | solution.py:180
  25.1 17.5 %all-to-all-start.1 = ((bf16[16,40,128]{2,1,0:T(8,128)(2,1)}), bf16[16,40,128]{2,1,0:T(8,128)(2,1)S(1)}, u32[]{:S(2)}, u32[]{:S(2)}) async-start(bf16[16,40,128]{2,1,0:T(8,128)(2,1)} %manifest_attention.1), calls=%async_computation.1 | async-start | bytes 327680 | tf_op jit(solution)/shard_map/all_to_all | solution.py:180
  31.1 3.4 %collective-permute-start = (bf16[1024,128]{1,0:T(8,128)(2,1)S(1)}, bf16[1024,128]{1,0:T(8,128)(2,1)S(1)}, u32[]{:S(2)}, u32[]{:S(2)}) collective-permute-start(bf16[1024,128]{1,0:T(8,128)(2,1)S(1)} %copy-done.3), channel_id=1, source_target_pairs={{0,8},{8,0},{1,9},{9,1},{2,10},{10,2},{3,11},{11,3},{4,12},{12,4},... | collective-permute-start | bytes 786440 | tf_op jit(solution)/shard_map/ppermute | solution.py:176
  33.1 14.8 %copy-start.1 = (bf16[128,1792]{1,0:T(8,128)(2,1)S(1)}, bf16[128,1792]{1,0:T(8,128)(2,1)}, u32[]{:S(2)}) copy-start(bf16[128,1792]{1,0:T(8,128)(2,1)} %g0_ref.1) | copy-start | bytes 1376260
  33.1 16.8 %copy-start.2 = (bf16[128,1792]{1,0:T(8,128)(2,1)S(1)}, bf16[128,1792]{1,0:T(8,128)(2,1)}, u32[]{:S(2)}) copy-start(bf16[128,1792]{1,0:T(8,128)(2,1)} %u0_ref.1) | copy-start | bytes 1376260
  44.0 16.7 %all-to-all-start.2 = ((bf16[32,4,1024]{2,1,0:T(4,128)(2,1)}), bf16[32,4,1024]{2,1,0:T(4,128)(2,1)S(1)}, u32[]{:S(2)}, u32[]{:S(2)}) async-start(bf16[32,4,1024]{2,1,0:T(4,128)(2,1)} %join_attention.1), calls=%async_computation.2 | async-start | bytes 524288 | tf_op jit(solution)/shard_map/all_to_all | solution.py:180
  47.9 12.9 %collective-permute-start.1 = (bf16[128,1792]{1,0:T(8,128)(2,1)S(1)}, bf16[128,1792]{1,0:T(8,128)(2,1)S(1)}, u32[]{:S(2)}, u32[]{:S(2)}) collective-permute-start(bf16[128,1792]{1,0:T(8,128)(2,1)S(1)} %copy-done.1), channel_id=1, source_target_pairs={{0,8},{8,0},{1,9},{9,1},{2,10},{10,2},{3,11},{11,3},{4,12},{12,4},... | collective-permute-start | bytes 1376264 | tf_op jit(solution)/shard_map/ppermute | solution.py:176
  49.9 11.0 %collective-permute-start.2 = (bf16[128,1792]{1,0:T(8,128)(2,1)S(1)}, bf16[128,1792]{1,0:T(8,128)(2,1)S(1)}, u32[]{:S(2)}, u32[]{:S(2)}) collective-permute-start(bf16[128,1792]{1,0:T(8,128)(2,1)S(1)} %copy-done.2), channel_id=1, source_target_pairs={{0,8},{8,0},{1,9},{9,1},{2,10},{10,2},{3,11},{11,3},{4,12},{12,4},... | collective-permute-start | bytes 1376264 | tf_op jit(solution)/shard_map/ppermute | solution.py:176
  60.8 15.2 %copy-start.7 = (bf16[256,128]{1,0:T(8,128)(2,1)S(1)}, bf16[256,128]{1,0:T(8,128)(2,1)}, u32[]{:S(2)}) copy-start(bf16[256,128]{1,0:T(8,128)(2,1)} %param.16) | copy-start | bytes 196612
  71.2 10.0 %all-to-all-start.3 = ((bf16[4,128,256]{2,1,0:T(8,128)(2,1)}), bf16[4,128,256]{2,1,0:T(8,128)(2,1)S(1)}, u32[]{:S(2)}, u32[]{:S(2)}) async-start(bf16[4,128,256]{2,1,0:T(8,128)(2,1)} %add_shares.1), calls=%async_computation.3 | async-start | bytes 524288 | tf_op jit(solution)/shard_map/all_to_all | solution.py:180
  76.0 3.1 %collective-permute-start.3 = (bf16[32,4,128]{2,1,0:T(4,128)(2,1)S(1)}, bf16[32,4,128]{2,1,0:T(4,128)(2,1)S(1)}, u32[]{:S(2)}, u32[]{:S(2)}) collective-permute-start(bf16[32,4,128]{2,1,0:T(4,128)(2,1)S(1)} %get-tuple-element.31), channel_id=1, source_target_pairs={{0,8},{8,0},{1,9},{9,1},{2,10},{10,2},{3,11},{11,3},{4,12},{12,4},... | collective-permute-start | bytes 98312 | tf_op jit(solution)/shard_map/ppermute | solution.py:176
  82.6 28.7 %all-to-all-start.4 = ((bf16[32,8,1792]{2,1,0:T(8,128)(2,1)}), bf16[32,8,1792]{2,1,0:T(8,128)(2,1)S(1)}, u32[]{:S(2)}, u32[]{:S(2)}) async-start(bf16[32,8,1792]{2,1,0:T(8,128)(2,1)} %gate_up.1), calls=%async_computation.4 | async-start | bytes 1835008 | tf_op jit(solution)/shard_map/all_to_all | solution.py:180
  86.6 3.1 %collective-permute-start.4 = (bf16[128,128]{1,0:T(8,128)(2,1)S(1)}, bf16[128,128]{1,0:T(8,128)(2,1)S(1)}, u32[]{:S(2)}, u32[]{:S(2)}) collective-permute-start(bf16[128,128]{1,0:T(8,128)(2,1)S(1)} %slice.31), channel_id=1, source_target_pairs={{0,8},{8,0},{1,9},{9,1},{2,10},{10,2},{3,11},{11,3},{4,12},{12,4},... | collective-permute-start | bytes 98312 | tf_op jit(solution)/shard_map/ppermute | solution.py:176

commit v11 on v10

--- a/solution.py
+++ b/solution.py
@@ -147,25 +147,34 @@
         out_ref[i] = block
 
 
-def mlp_kernel(x_ref, g0_ref, g1_ref, u0_ref, u1_ref, out_ref):
-    x = x_ref[...]
-    turned = x.astype(F32).reshape(CHIPS // 2, 2 * ROWS, 2 * HD)
-    turned = jnp.concatenate([turned[:, ROWS:], turned[:, :ROWS]], axis=1).reshape(CHIPS * ROWS, 2 * HD).astype(BF)
-    gate = dot(x, jnp.concatenate([g0_ref[...], g1_ref[...]], axis=0), 1, 0)
-    up = dot(turned, jnp.concatenate([u0_ref[...], u1_ref[...]], axis=0), 1, 0)
-    low = lax.broadcasted_iota(jnp.int32, (2 * ROWS, gate.shape[1]), 0) < ROWS
+def mlp_kernel(side_ref, x_ref, both_ref, w0_ref, w1_ref, w2_ref, w3_ref, out_ref):
+    def turn(x):
+        x = x.astype(F32).reshape(CHIPS // 2, 2 * ROWS, 2 * HD)
+        return jnp.concatenate([x[:, ROWS:], x[:, :ROWS]], axis=1).reshape(CHIPS * ROWS, 2 * HD).astype(BF)
+
+    x, other = x_ref[...], both_ref[1 - side_ref[0]]
+    half = w0_ref.shape[1] // 2
+
+    def product(a, b, at):
+        w = [w_ref[:, at] for w_ref in (w0_ref, w1_ref, w2_ref, w3_ref)]
+        return dot(a, jnp.concatenate(w[:2], axis=0), 1, 0) + dot(b, jnp.concatenate(w[2:], axis=0), 1, 0)
+
+    left = product(x, other, slice(0, half))
+    right = product(turn(x), turn(other), slice(half, 2 * half))
+    low = lax.broadcasted_iota(jnp.int32, (2 * ROWS, half), 0) < ROWS
     for j in range(CHIPS // 2):
         at = slice(2 * j * ROWS, 2 * (j + 1) * ROWS)
-        out_ref[2 * j] = jnp.where(low, gate[at], up[at]).astype(BF)
-        out_ref[2 * j + 1] = jnp.where(low, up[at], gate[at]).astype(BF)
-
-
-def dense(kernel, name, out_shape, *args):
-    vmem = pl.BlockSpec(memory_space=pltpu.VMEM)
+        out_ref[2 * j] = jnp.where(low, left[at], right[at]).astype(BF)
+        out_ref[2 * j + 1] = jnp.where(low, right[at], left[at]).astype(BF)
+
+
+def dense(kernel, name, out_shape, *args, scalars=0):
+    vmem = pl.BlockSpec(memory_space=pltpu.VMEM)
+    smem = pl.BlockSpec(memory_space=pltpu.SMEM)
     return pl.pallas_call(
         kernel,
         out_shape=jax.ShapeDtypeStruct(out_shape, BF),
-        in_specs=[vmem] * len(args),
+        in_specs=[smem] * scalars + [vmem] * (len(args) - scalars),
         out_specs=vmem,
         compiler_params=pltpu.CompilerParams(vmem_limit_bytes=40 << 20),
         name=name,
@@ -174,6 +183,10 @@
 
 def swap(x):
     return lax.ppermute(x, "c", [(0, 1), (1, 0)])
+
+
+def pair(x):
+    return lax.ppermute(x, "p", [(0, 1), (1, 0)])
 
 
 def exchange(x, axes):
@@ -193,23 +206,31 @@
     parts, own, w_out_c = tie((parts, own, swap(w_out)))
     place = (lax.axis_index(SPARSE) % 4).astype(jnp.int32).reshape(1)
     attn = exchange(join_part(place, parts, *own), PLANE).reshape(rows, GROUP * HD)
-    attn, w_gate_c, w_up_c = tie((attn, swap(w_gate), swap(w_up)))
+    side = lax.axis_index("p")
+    w_keep = jnp.where(side == 0, w_gate, w_up)
+    w_pair = pair(jnp.where(side == 0, w_up, w_gate))
+    attn, w_keep_c = tie((attn, swap(w_keep)))
 
     share = dense(project_kernel, "project", (rows, 2 * HD), attn, w_out, w_out_c)
     shares = lax.all_gather(share, "zh", axis=0)
-    shares, resid = tie((shares, resid))
+    shares, resid, w_pair = tie((shares, resid, w_pair))
     heads = exchange(dense(add_kernel, "add_shares", (4, rows, 2 * HD), shares), "x")
     res = resid.reshape(CHIPS, 2, ROWS, HD)
     mine = jnp.where(core == 0, res[:, 0], res[:, 1])
     theirs = swap(jnp.where(core == 0, res[:, 1], res[:, 0]))
     res = jnp.concatenate([mine, theirs], axis=-1).reshape(rows, 2 * HD).astype(F32)
     out2 = (res + heads.astype(F32).sum(0)).astype(BF)
-    both = dense(mlp_kernel, "gate_up", (CHIPS, 2 * ROWS, width), out2, w_gate, w_gate_c, w_up, w_up_c)
-    joined = exchange(both, PLANE).astype(F32).sum(0)
-    odd = lax.axis_index("p") == 1
-    gate = jnp.where(odd, joined[ROWS:], joined[:ROWS])
-    up = jnp.where(odd, joined[:ROWS], joined[ROWS:])
-    hidden = (jax.nn.silu(gate) * up).astype(BF)
+    place = side.astype(jnp.int32).reshape(1)
+    pairs = lax.all_gather(out2, "p", axis=0)
+    both = dense(
+        mlp_kernel, "gate_up", (CHIPS, 2 * ROWS, width // 2),
+        place, out2, pairs, w_keep, w_keep_c, w_pair, swap(w_pair), scalars=1,
+    )
+    joined = exchange(both, PLANE).reshape(PEERS, 2, 2 * ROWS, width // 2).astype(F32).sum(0)
+    first, second = joined[:, :ROWS], joined[:, ROWS:]
+    odd = side == 1
+    joined = jnp.concatenate([jnp.where(odd, second, first), jnp.where(odd, first, second)], axis=-1)
+    hidden = (jax.nn.silu(joined[0]) * joined[1]).astype(BF)
 
     kept = out2[:, :HD].reshape(CHIPS, 1, ROWS, HD)
     given = swap(out2[:, HD:]).reshape(CHIPS, 1, ROWS, HD)

time: 113 us -> 117 us (1.035)
  waiting for transfers between devices: 45.3 us -> 32.1 us
  blocking collectives: 16.5 us -> 25.1 us
  starting transfers between devices: 39.6 us -> 47.8 us
    all_to_all x5, waiting for transfers between devices: 42.8 us -> 30.9 us  [exchange(): return lax.all_to_all(x, axes, 0, 0, tiled=True)]
    all_gather x0 -> x1, blocking collectives: none -> 4.94 us  [on_device(): pairs = lax.all_gather(out2, 'p', axis=0)]
    all_to_all x5, starting transfers between devices: 29.4 us -> 34.1 us  [exchange(): return lax.all_to_all(x, axes, 0, 0, tiled=True)]
    all_gather x1, blocking collectives: 9.34 us -> 12.9 us  [on_device(): shares = lax.all_gather(share, 'zh', axis=0)]
    ppermute x0 -> x1, starting transfers between devices: none -> 3.59 us  [pair(): return lax.ppermute(x, 'p', [(0, 1), (1, 0)])]
    ppermute x5, waiting for transfers between devices: 2.51 us -> 1.18 us  [swap(): return lax.ppermute(x, 'c', [(0, 1), (1, 0)])]
  transfers between devices with their start and end apart: 10 -> 11, of which waited for: 8 -> 6; matrix products, arithmetic and copies ran while one was open for 1% -> 1% of each run, Pallas kernels for 1% -> 1%
where the time goes in v11:
time: 117 us; the launch traced here: 116 us
  starting transfers between devices  47.8 us (41%)
  waiting for transfers between devices  32.1 us (27%)
  blocking collectives  25.1 us (21%)
  Pallas kernels  6.4 us (5%)
  local copies, waits for them, and re-layouts  2.96 us (3%)
    all_to_all x5, starting transfers between devices, exchange(): return lax.all_to_all(x, axes, 0, 0, tiled=True)  34.1 us
    all_to_all x5, waiting for transfers between devices, exchange(): return lax.all_to_all(x, axes, 0, 0, tiled=True)  30.9 us
    all_gather x1, blocking collectives, on_device(): shares = lax.all_gather(share, 'zh', axis=0)  12.9 us
    ppermute x5, starting transfers between devices, swap(): return lax.ppermute(x, 'c', [(0, 1), (1, 0)])  10.1 us
    all_gather x1, blocking collectives, on_device(): lax.all_gather(man_kv.reshape(1, 2, 2 * PAGE, HD), ('p', 'c'), axis=0, ti...  7.18 us
    all_gather x1, blocking collectives, on_device(): pairs = lax.all_gather(out2, 'p', axis=0)  4.94 us
    ppermute x1, starting transfers between devices, pair(): return lax.ppermute(x, 'p', [(0, 1), (1, 0)])  3.59 us
  transfers between devices with their start and end apart: 11, of which 6 were waited for; matrix products, arithmetic and copies ran while one was open for 1% of the time, Pallas kernels for 1%

profile of v11, /device:TPU:2, one launch (start us, length us, event | category | flops | bytes accessed | tf_op | source)
XLA Modules:
  0.0 116.2 jit_solution(4153098925345422449)
XLA Ops:
  0.6 0.8 broadcast_in_dim.7.q_ref
  1.4 0.7 broadcast_in_dim.8
  2.1 10.8 %all-to-all-start = ((bf16[16,32,128]{2,1,0:T(8,128)(2,1)}), bf16[16,32,128]{2,1,0:T(8,128)(2,1)S(1)}, u32[]{:S(2)}, u32[]{:S(2)}) async-start(bf16[16,32,128]{2,1,0:T(8,128)(2,1)} %broadcast_in_dim.8), calls=%async_computation | async-start | bytes 262144 | tf_op jit(solution)/shard_map/all_to_all | solution.py:193
  12.9 7.2 %all_gather.13.kv_ref = bf16[4,2,128,128]{3,2,1,0:T(8,128)(2,1)S(1)} all-gather(bf16[1,2,128,128]{3,2,1,0:T(8,128)(2,1)} %bitcast.50), channel_id=1, replica_groups=mesh['y'=8,'zq'=2,'p'=2,'c'=2,'zh'=2,'x'=4] {'p','c'}, dimensions={0}, use_global_device_ids=true | all-gather | bytes 327680 | tf_op jit(solution)/shard_map/all_gather | solution.py:203
  20.1 3.3 %all-to-all-done = bf16[16,32,128]{2,1,0:T(8,128)(2,1)S(1)} async-done(((bf16[16,32,128]{2,1,0:T(8,128)(2,1)}), bf16[16,32,128]{2,1,0:T(8,128)(2,1)S(1)}, u32[]{:S(2)}, u32[]{:S(2)}) %all-to-all-start) | async-done | bytes 131104 | tf_op jit(solution)/shard_map/all_to_all | solution.py:193
  23.5 1.6 %manifest_attention.1 = bf16[16,40,128]{2,1,0:T(8,128)(2,1)} custom-call(bf16[512,128]{1,0:T(8,128)(2,1)S(1)} %bitcast.45, bf16[4,2,128,128]{3,2,1,0:T(8,128)(2,1)S(1)} %all_gather.13.kv_ref), custom_call_target="tpu_custom_call" | custom-call | tf_op jit(solution)/shard_map/manifest_attention/pallas_call | solution.py:91
  25.1 6.1 %all-to-all-start.1 = ((bf16[16,40,128]{2,1,0:T(8,128)(2,1)}), bf16[16,40,128]{2,1,0:T(8,128)(2,1)S(1)}, u32[]{:S(2)}, u32[]{:S(2)}) async-start(bf16[16,40,128]{2,1,0:T(8,128)(2,1)} %manifest_attention.1), calls=%async_computation.1 | async-start | bytes 327680 | tf_op jit(solution)/shard_map/all_to_all | solution.py:193
  31.2 2.0 %collective-permute-start = (bf16[1024,128]{1,0:T(8,128)(2,1)S(1)}, bf16[1024,128]{1,0:T(8,128)(2,1)S(1)}, u32[]{:S(2)}, u32[]{:S(2)}) collective-permute-start(bf16[1024,128]{1,0:T(8,128)(2,1)S(1)} %copy-done.1), channel_id=1, source_target_pairs={{0,8},{8,0},{1,9},{9,1},{2,10},{10,2},{3,11},{11,3},{4,12},{12,4},... | collective-permute-start | bytes 786440 | tf_op jit(solution)/shard_map/ppermute | solution.py:185
  33.2 0.6 copy-done.3
  33.9 1.2 %own_attention.1 = (f32[32,128]{1,0:T(8,128)S(1)}, f32[32,128]{1,0:T(8,128)S(1)}, f32[32,128]{1,0:T(8,128)S(1)}) custom-call(s32[4,8]{1,0:T(4,128)S(1)} %copy-done.2, s32[4]{0:T(128)S(1)} %copy-done.4, bf16[32,128]{1,0:T(8,128)(2,1)S(1)} %broadcast_in_dim.7.q_ref, bf16[2,4,128]{2,1,0:T(4,128)(2,1)S(1)} %copy-done.3, bf16[2,2048,128]{2,1,0:T(8,128)(2,1)S(1)} %bitcast.44), custom_call_target="tpu_custom_call" | custom-call | tf_op jit(solution)/shard_map/own_attention/pallas_call | solution.py:60
  35.1 7.6 %all-to-all-done.1.parts_ref = bf16[16,40,128]{2,1,0:T(8,128)(2,1)S(1)} async-done(((bf16[16,40,128]{2,1,0:T(8,128)(2,1)}), bf16[16,40,128]{2,1,0:T(8,128)(2,1)S(1)}, u32[]{:S(2)}, u32[]{:S(2)}) %all-to-all-start.1) | async-done | bytes 163872 | tf_op jit(solution)/shard_map/all_to_all | solution.py:193
  42.7 1.4 %join_attention.1 = bf16[32,4,1024]{2,1,0:T(4,128)(2,1)} custom-call(s32[1]{0:T(128)} %bitcast.place_ref, bf16[16,40,128]{2,1,0:T(8,128)(2,1)S(1)} %all-to-all-done.1.parts_ref, f32[32,128]{1,0:T(8,128)S(1)} %get-tuple-element.19.acc_ref, f32[32,128]{1,0:T(8,128)S(1)} %get-tuple-element.20.top_ref, f32[32,128]{1,0:T(8,128)S(1)} %get-tuple-element.21.total_ref), custom_call_target="tpu_custom_call" | custom-call | tf_op jit(solution)/shard_map/join_attention/pallas_call | solution.py:128
  44.1 3.9 %all-to-all-start.2 = ((bf16[32,4,1024]{2,1,0:T(4,128)(2,1)}), bf16[32,4,1024]{2,1,0:T(4,128)(2,1)S(1)}, u32[]{:S(2)}, u32[]{:S(2)}) async-start(bf16[32,4,1024]{2,1,0:T(4,128)(2,1)} %join_attention.1), calls=%async_computation.2 | async-start | bytes 524288 | tf_op jit(solution)/shard_map/all_to_all | solution.py:193
  48.1 1.9 %collective-permute-start.1 = (bf16[128,1792]{1,0:T(8,128)(2,1)S(1)}, bf16[128,1792]{1,0:T(8,128)(2,1)S(1)}, u32[]{:S(2)}, u32[]{:S(2)}) collective-permute-start(bf16[128,1792]{1,0:T(8,128)(2,1)S(1)} %get-tuple-element.29.w0_ref), channel_id=1, source_target_pairs={{0,8},{8,0},{1,9},{9,1},{2,10},{10,2},{3,11},{11,3},{4,12},{12,4},... | collective-permute-start | bytes 1376264 | tf_op jit(solution)/shard_map/ppermute | solution.py:185
  50.0 3.6 %collective-permute-start.2 = (bf16[128,1792]{1,0:T(8,128)(2,1)S(1)}, bf16[128,1792]{1,0:T(8,128)(2,1)S(1)}, u32[]{:S(2)}, u32[]{:S(2)}) collective-permute-start(bf16[128,1792]{1,0:T(8,128)(2,1)S(1)} %get-tuple-element.28), channel_id=1, source_target_pairs={{0,16},{16,0},{1,17},{17,1},{2,18},{18,2},{3,19},{19,3},{4,20},{20... | collective-permute-start | bytes 1376264 | tf_op jit(solution)/shard_map/ppermute | solution.py:189
  53.6 7.3 %all-to-all-done.2 = bf16[32,4,1024]{2,1,0:T(4,128)(2,1)S(1)} async-done(((bf16[32,4,1024]{2,1,0:T(4,128)(2,1)}), bf16[32,4,1024]{2,1,0:T(4,128)(2,1)S(1)}, u32[]{:S(2)}, u32[]{:S(2)}) %all-to-all-start.2) | async-done | bytes 262176 | tf_op jit(solution)/shard_map/all_to_all | solution.py:193
  61.0 0.2 project.1
  61.3 12.9 %all-gather = bf16[256,256]{1,0:T(8,128)(2,1)S(1)} all-gather(bf16[128,256]{1,0:T(8,128)(2,1)S(1)} %project.1), channel_id=2, replica_groups=mesh['y'=8,'zq'=2,'p'=2,'c'=2,'zh'=2,'x'=4] {'zh'}, dimensions={0}, use_global_device_ids=true | all-gather | bytes 196608 | tf_op jit(solution)/shard_map/all_gather | solution.py:215
  74.2 0.7 add_shares.1
  74.9 5.0 %all-to-all-start.3 = ((bf16[4,128,256]{2,1,0:T(8,128)(2,1)}), bf16[4,128,256]{2,1,0:T(8,128)(2,1)S(1)}, u32[]{:S(2)}, u32[]{:S(2)}) async-start(bf16[4,128,256]{2,1,0:T(8,128)(2,1)} %add_shares.1), calls=%async_computation.3 | async-start | bytes 524288 | tf_op jit(solution)/shard_map/all_to_all | solution.py:193
  79.9 1.9 %collective-permute-start.3 = (bf16[32,4,128]{2,1,0:T(4,128)(2,1)S(1)}, bf16[32,4,128]{2,1,0:T(4,128)(2,1)S(1)}, u32[]{:S(2)}, u32[]{:S(2)}) collective-permute-start(bf16[32,4,128]{2,1,0:T(4,128)(2,1)S(1)} %get-tuple-element.33), channel_id=1, source_target_pairs={{0,8},{8,0},{1,9},{9,1},{2,10},{10,2},{3,11},{11,3},{4,12},{12,4},... | collective-permute-start | bytes 98312 | tf_op jit(solution)/shard_map/ppermute | solution.py:185
  81.9 2.4 %collective-permute-start.5 = (bf16[128,1792]{1,0:T(8,128)(2,1)S(1)}, bf16[128,1792]{1,0:T(8,128)(2,1)S(1)}, u32[]{:S(2)}, u32[]{:S(2)}) collective-permute-start(bf16[128,1792]{1,0:T(8,128)(2,1)S(1)} %collective-permute-done.2.w2_ref), channel_id=1, source_target_pairs={{0,8},{8,0},{1,9},{9,1},{2,10},{10,2},{3,11},{11,3},{4,12},{12,4},... | collective-permute-start | bytes 1376264 | tf_op jit(solution)/shard_map/ppermute | solution.py:185
  84.4 0.7 all-to-all-done.3
  85.2 4.9 %all_gather.16.both_ref = bf16[2,128,256]{2,1,0:T(8,128)(2,1)S(1)} all-gather(bf16[1,128,256]{2,1,0:T(8,128)(2,1)S(1)} %fusion), channel_id=1, replica_groups=mesh['y'=8,'zq'=2,'p'=2,'c'=2,'zh'=2,'x'=4] {'p'}, dimensions={0}, use_global_device_ids=true | all-gather | bytes 196608 | tf_op jit(solution)/shard_map/all_gather | solution.py:224
  90.1 1.2 %gate_up.1 = bf16[32,8,896]{2,1,0:T(8,128)(2,1)} custom-call(s32[1]{0:T(128)} %bitcast.11.side_ref, bf16[128,256]{1,0:T(8,128)(2,1)S(1)} %add_convert_fusion.x_ref, bf16[2,128,256]{2,1,0:T(8,128)(2,1)S(1)} %all_gather.16.both_ref, bf16[128,1792]{1,0:T(8,128)(2,1)S(1)} %get-tuple-element.29.w0_ref, bf16[128,1792]{1,0:T(8,128)(2,1)S(1)} %collective-permute-done.1.w1_ref, ...), custom_call_target="tpu_custom_call" | custom-call | tf_op jit(solution)/shard_map/gate_up/pallas_call | solution.py:174
  91.4 8.4 %all-to-all-start.4 = ((bf16[32,8,896]{2,1,0:T(8,128)(2,1)}), bf16[32,8,896]{2,1,0:T(8,128)(2,1)S(1)}, u32[]{:S(2)}, u32[]{:S(2)}) async-start(bf16[32,8,896]{2,1,0:T(8,128)(2,1)} %gate_up.1), calls=%async_computation.4 | async-start | bytes 917504 | tf_op jit(solution)/shard_map/all_to_all | solution.py:193
  99.7 1.9 %collective-permute-start.4 = (bf16[128,128]{1,0:T(8,128)(2,1)S(1)}, bf16[128,128]{1,0:T(8,128)(2,1)S(1)}, u32[]{:S(2)}, u32[]{:S(2)}) collective-permute-start(bf16[128,128]{1,0:T(8,128)(2,1)S(1)} %slice.37), channel_id=1, source_target_pairs={{0,8},{8,0},{1,9},{9,1},{2,10},{10,2},{3,11},{11,3},{4,12},{12,4},... | collective-permute-start | bytes 98312 | tf_op jit(solution)/shard_map/ppermute | solution.py:185
  101.7 1.2 %collective-permute-done.4 = bf16[128,128]{1,0:T(8,128)(2,1)S(1)} collective-permute-done((bf16[128,128]{1,0:T(8,128)(2,1)S(1)}, bf16[128,128]{1,0:T(8,128)(2,1)S(1)}, u32[]{:S(2)}, u32[]{:S(2)}) %collective-permute-start.4) | collective-permute-done | bytes 32800 | tf_op jit(solution)/shard_map/ppermute | solution.py:185
  102.9 0.7 copy.17
  103.6 11.9 %all-to-all-done.4 = bf16[32,8,896]{2,1,0:T(8,128)(2,1)S(1)} async-done(((bf16[32,8,896]{2,1,0:T(8,128)(2,1)}), bf16[32,8,896]{2,1,0:T(8,128)(2,1)S(1)}, u32[]{:S(2)}, u32[]{:S(2)}) %all-to-all-start.4) | async-done | bytes 458784 | tf_op jit(solution)/shard_map/all_to_all | solution.py:193
  115.5 0.1 convert_reduce_fusion
  115.6 0.6 fusion.5
  (33 shorter events, 0.5 us)
Async XLA Ops:
  0.6 32.6 %copy-start = (bf16[2,32,64,128]{3,2,1,0:T(8,128)(2,1)S(1)}, bf16[2,32,64,128]{3,2,1,0:T(8,128)(2,1)}, u32[]{:S(2)}) copy-start(bf16[2,32,64,128]{3,2,1,0:T(8,128)(2,1)} %param.12) | copy-start | bytes 3145732
  2.1 21.3 %all-to-all-start = ((bf16[16,32,128]{2,1,0:T(8,128)(2,1)}), bf16[16,32,128]{2,1,0:T(8,128)(2,1)S(1)}, u32[]{:S(2)}, u32[]{:S(2)}) async-start(bf16[16,32,128]{2,1,0:T(8,128)(2,1)} %broadcast_in_dim.8), calls=%async_computation | async-start | bytes 262144 | tf_op jit(solution)/shard_map/all_to_all | solution.py:193
  25.1 6.1 %copy-start.1 = (bf16[1024,128]{1,0:T(8,128)(2,1)S(1)}, bf16[1024,128]{1,0:T(8,128)(2,1)}, u32[]{:S(2)}) copy-start(bf16[1024,128]{1,0:T(8,128)(2,1)} %w0_ref.1) | copy-start | bytes 786436
  25.1 17.6 %all-to-all-start.1 = ((bf16[16,40,128]{2,1,0:T(8,128)(2,1)}), bf16[16,40,128]{2,1,0:T(8,128)(2,1)S(1)}, u32[]{:S(2)}, u32[]{:S(2)}) async-start(bf16[16,40,128]{2,1,0:T(8,128)(2,1)} %manifest_attention.1), calls=%async_computation.1 | async-start | bytes 327680 | tf_op jit(solution)/shard_map/all_to_all | solution.py:193
  31.2 3.9 %collective-permute-start = (bf16[1024,128]{1,0:T(8,128)(2,1)S(1)}, bf16[1024,128]{1,0:T(8,128)(2,1)S(1)}, u32[]{:S(2)}, u32[]{:S(2)}) collective-permute-start(bf16[1024,128]{1,0:T(8,128)(2,1)S(1)} %copy-done.1), channel_id=1, source_target_pairs={{0,8},{8,0},{1,9},{9,1},{2,10},{10,2},{3,11},{11,3},{4,12},{12,4},... | collective-permute-start | bytes 786440 | tf_op jit(solution)/shard_map/ppermute | solution.py:185
  33.2 0.7 copy-start.3
  33.2 0.7 copy-start.2
  33.2 0.7 copy-start.4
  42.7 5.3 %copy-start.5 = (bf16[128,1792]{1,0:T(8,128)(2,1)S(1)}, bf16[128,1792]{1,0:T(8,128)(2,1)}, u32[]{:S(2)}) copy-start(bf16[128,1792]{1,0:T(8,128)(2,1)} %param.19) | copy-start | bytes 1376260
  42.7 5.3 %copy-start.6 = (bf16[128,1792]{1,0:T(8,128)(2,1)S(1)}, bf16[128,1792]{1,0:T(8,128)(2,1)}, u32[]{:S(2)}) copy-start(bf16[128,1792]{1,0:T(8,128)(2,1)} %param.18) | copy-start | bytes 1376260
  44.1 16.8 %all-to-all-start.2 = ((bf16[32,4,1024]{2,1,0:T(4,128)(2,1)}), bf16[32,4,1024]{2,1,0:T(4,128)(2,1)S(1)}, u32[]{:S(2)}, u32[]{:S(2)}) async-start(bf16[32,4,1024]{2,1,0:T(4,128)(2,1)} %join_attention.1), calls=%async_computation.2 | async-start | bytes 524288 | tf_op jit(solution)/shard_map/all_to_all | solution.py:193
  48.1 12.9 %collective-permute-start.1 = (bf16[128,1792]{1,0:T(8,128)(2,1)S(1)}, bf16[128,1792]{1,0:T(8,128)(2,1)S(1)}, u32[]{:S(2)}, u32[]{:S(2)}) collective-permute-start(bf16[128,1792]{1,0:T(8,128)(2,1)S(1)} %get-tuple-element.29.w0_ref), channel_id=1, source_target_pairs={{0,8},{8,0},{1,9},{9,1},{2,10},{10,2},{3,11},{11,3},{4,12},{12,4},... | collective-permute-start | bytes 1376264 | tf_op jit(solution)/shard_map/ppermute | solution.py:185
  50.0 24.2 %collective-permute-start.2 = (bf16[128,1792]{1,0:T(8,128)(2,1)S(1)}, bf16[128,1792]{1,0:T(8,128)(2,1)S(1)}, u32[]{:S(2)}, u32[]{:S(2)}) collective-permute-start(bf16[128,1792]{1,0:T(8,128)(2,1)S(1)} %get-tuple-element.28), channel_id=1, source_target_pairs={{0,16},{16,0},{1,17},{17,1},{2,18},{18,2},{3,19},{19,3},{4,20},{20... | collective-permute-start | bytes 1376264 | tf_op jit(solution)/shard_map/ppermute | solution.py:189
  74.9 5.0 %copy-start.7 = (bf16[256,128]{1,0:T(8,128)(2,1)S(1)}, bf16[256,128]{1,0:T(8,128)(2,1)}, u32[]{:S(2)}) copy-start(bf16[256,128]{1,0:T(8,128)(2,1)} %param.16) | copy-start | bytes 196612
  74.9 10.2 %all-to-all-start.3 = ((bf16[4,128,256]{2,1,0:T(8,128)(2,1)}), bf16[4,128,256]{2,1,0:T(8,128)(2,1)S(1)}, u32[]{:S(2)}, u32[]{:S(2)}) async-start(bf16[4,128,256]{2,1,0:T(8,128)(2,1)} %add_shares.1), calls=%async_computation.3 | async-start | bytes 524288 | tf_op jit(solution)/shard_map/all_to_all | solution.py:193
  79.9 4.3 %collective-permute-start.3 = (bf16[32,4,128]{2,1,0:T(4,128)(2,1)S(1)}, bf16[32,4,128]{2,1,0:T(4,128)(2,1)S(1)}, u32[]{:S(2)}, u32[]{:S(2)}) collective-permute-start(bf16[32,4,128]{2,1,0:T(4,128)(2,1)S(1)} %get-tuple-element.33), channel_id=1, source_target_pairs={{0,8},{8,0},{1,9},{9,1},{2,10},{10,2},{3,11},{11,3},{4,12},{12,4},... | collective-permute-start | bytes 98312 | tf_op jit(solution)/shard_map/ppermute | solution.py:185
  81.9 8.3 %collective-permute-start.5 = (bf16[128,1792]{1,0:T(8,128)(2,1)S(1)}, bf16[128,1792]{1,0:T(8,128)(2,1)S(1)}, u32[]{:S(2)}, u32[]{:S(2)}) collective-permute-start(bf16[128,1792]{1,0:T(8,128)(2,1)S(1)} %collective-permute-done.2.w2_ref), channel_id=1, source_target_pairs={{0,8},{8,0},{1,9},{9,1},{2,10},{10,2},{3,11},{11,3},{4,12},{12,4},... | collective-permute-start | bytes 1376264 | tf_op jit(solution)/shard_map/ppermute | solution.py:185
  91.4 24.1 %all-to-all-start.4 = ((bf16[32,8,896]{2,1,0:T(8,128)(2,1)}), bf16[32,8,896]{2,1,0:T(8,128)(2,1)S(1)}, u32[]{:S(2)}, u32[]{:S(2)}) async-start(bf16[32,8,896]{2,1,0:T(8,128)(2,1)} %gate_up.1), calls=%async_computation.4 | async-start | bytes 917504 | tf_op jit(solution)/shard_map/all_to_all | solution.py:193
  99.7 3.1 %collective-permute-start.4 = (bf16[128,128]{1,0:T(8,128)(2,1)S(1)}, bf16[128,128]{1,0:T(8,128)(2,1)S(1)}, u32[]{:S(2)}, u32[]{:S(2)}) collective-permute-start(bf16[128,128]{1,0:T(8,128)(2,1)S(1)} %slice.37), channel_id=1, source_target_pairs={{0,8},{8,0},{1,9},{9,1},{2,10},{10,2},{3,11},{11,3},{4,12},{12,4},... | collective-permute-start | bytes 98312 | tf_op jit(solution)/shard_map/ppermute | solution.py:185

commit v12 on v11

--- a/solution.py
+++ b/solution.py
@@ -203,17 +203,19 @@
     kv = lax.all_gather(man_kv.reshape(1, 2, 2 * PAGE, HD), ("p", "c"), axis=0, tiled=True)
     parts = exchange(man_part(q_all, kv), SPARSE)
     own = own_part(pages, own_len, q, new_kv, own_kv.reshape(2, POOL * PAGE, HD))
-    parts, own, w_out_c = tie((parts, own, swap(w_out)))
+    side = lax.axis_index("p")
+    w_keep = jnp.where(side == 0, w_gate, w_up)
+    w_send = jnp.where(side == 0, w_up, w_gate)
+    w_pair = [pair(w_send[: HD // 2]), pair(w_send[HD // 2 :])]
+    parts, own, w_out_c, w_pair[0] = tie((parts, own, swap(w_out), w_pair[0]))
+    w_pair = jnp.concatenate(w_pair, axis=0)
     place = (lax.axis_index(SPARSE) % 4).astype(jnp.int32).reshape(1)
     attn = exchange(join_part(place, parts, *own), PLANE).reshape(rows, GROUP * HD)
-    side = lax.axis_index("p")
-    w_keep = jnp.where(side == 0, w_gate, w_up)
-    w_pair = pair(jnp.where(side == 0, w_up, w_gate))
-    attn, w_keep_c = tie((attn, swap(w_keep)))
+    attn, w_keep_c, w_pair = tie((attn, swap(w_keep), w_pair))
 
     share = dense(project_kernel, "project", (rows, 2 * HD), attn, w_out, w_out_c)
     shares = lax.all_gather(share, "zh", axis=0)
-    shares, resid, w_pair = tie((shares, resid, w_pair))
+    shares, resid = tie((shares, resid))
     heads = exchange(dense(add_kernel, "add_shares", (4, rows, 2 * HD), shares), "x")
     res = resid.reshape(CHIPS, 2, ROWS, HD)
     mine = jnp.where(core == 0, res[:, 0], res[:, 1])

time: 117 us -> 120 us (1.026)
  starting transfers between devices: 47.8 us -> 58.5 us
  waiting for transfers between devices: 32.1 us -> 27.5 us
  blocking collectives: 25.1 us -> 21.1 us
  other arithmetic: 0.97 us -> 2.18 us
    all_to_all x5, waiting for transfers between devices: 30.9 us -> 14.2 us  [exchange(): return lax.all_to_all(x, axes, 0, 0, tiled=True)]
    ppermute x1 -> x2, waiting for transfers between devices: 0.01 us -> 12.1 us  [pair(): return lax.ppermute(x, 'p', [(0, 1), (1, 0)])]
    all_to_all x5, starting transfers between devices: 34.1 us -> 41 us  [exchange(): return lax.all_to_all(x, axes, 0, 0, tiled=True)]
    all_gather x1, blocking collectives: 12.9 us -> 9.15 us  [on_device(): shares = lax.all_gather(share, 'zh', axis=0)]
    ppermute x1 -> x2, starting transfers between devices: 3.59 us -> 7.35 us  [pair(): return lax.ppermute(x, 'p', [(0, 1), (1, 0)])]
  transfers between devices with their start and end apart: 11 -> 12, of which waited for: 6 -> 8; matrix products, arithmetic and copies ran while one was open for 1% -> 2% of each run, Pallas kernels for 1% -> 2%
where the time goes in v12:
time: 120 us
  starting transfers between devices  58.5 us (49%)
  waiting for transfers between devices  27.5 us (23%)
  blocking collectives  21.1 us (18%)
  Pallas kernels  6.44 us (5%)
  local copies, waits for them, and re-layouts  2.94 us (2%)
  other arithmetic  2.18 us (2%)
    all_to_all x5, starting transfers between devices, exchange(): return lax.all_to_all(x, axes, 0, 0, tiled=True)  41 us
    all_to_all x5, waiting for transfers between devices, exchange(): return lax.all_to_all(x, axes, 0, 0, tiled=True)  14.2 us
    ppermute x2, waiting for transfers between devices, pair(): return lax.ppermute(x, 'p', [(0, 1), (1, 0)])  12.1 us
    ppermute x5, starting transfers between devices, swap(): return lax.ppermute(x, 'c', [(0, 1), (1, 0)])  10.1 us
    all_gather x1, blocking collectives, on_device(): shares = lax.all_gather(share, 'zh', axis=0)  9.15 us
    ppermute x2, starting transfers between devices, pair(): return lax.ppermute(x, 'p', [(0, 1), (1, 0)])  7.35 us
    all_gather x1, blocking collectives, on_device(): lax.all_gather(man_kv.reshape(1, 2, 2 * PAGE, HD), ('p', 'c'), axis=0, ti...  6.99 us
    all_gather x1, blocking collectives, on_device(): pairs = lax.all_gather(out2, 'p', axis=0)  4.94 us
  transfers between devices with their start and end apart: 12, of which 8 were waited for; matrix products, arithmetic and copies ran while one was open for 2% of the time, Pallas kernels for 2%

profile of v12, /device:TPU:2, one launch (start us, length us, event | category | flops | bytes accessed | tf_op | source)
XLA Modules:
  0.0 119.6 jit_solution(12102823947082021712)
XLA Ops:
  0.6 0.8 broadcast_in_dim.7.q_ref
  1.4 0.7 broadcast_in_dim.8
  2.1 10.8 %all-to-all-start = ((bf16[16,32,128]{2,1,0:T(8,128)(2,1)}), bf16[16,32,128]{2,1,0:T(8,128)(2,1)S(1)}, u32[]{:S(2)}, u32[]{:S(2)}) async-start(bf16[16,32,128]{2,1,0:T(8,128)(2,1)} %broadcast_in_dim.8), calls=%async_computation | async-start | bytes 262144 | tf_op jit(solution)/shard_map/all_to_all | solution.py:193
  12.9 1.9 %collective-permute-start = (bf16[1024,128]{1,0:T(8,128)(2,1)S(1)}, bf16[1024,128]{1,0:T(8,128)(2,1)S(1)}, u32[]{:S(2)}, u32[]{:S(2)}) collective-permute-start(bf16[1024,128]{1,0:T(8,128)(2,1)S(1)} %copy-done.1), channel_id=1, source_target_pairs={{0,8},{8,0},{1,9},{9,1},{2,10},{10,2},{3,11},{11,3},{4,12},{12,4},... | collective-permute-start | bytes 786440 | tf_op jit(solution)/shard_map/ppermute | solution.py:185
  14.8 1.3 %broadcast_select_fusion = (bf16[128,1792]{1,0:T(8,128)(2,1)S(1)}, bf16[128,1792]{1,0:T(8,128)(2,1)S(1)}) fusion(bf16[128,1792]{1,0:T(8,128)(2,1)} %param.18, bf16[128,1792]{1,0:T(8,128)(2,1)} %param.19, pred[]{:T(512)S(6)} %eq.16), kind=kLoop, calls=%fused_computation.3 | loop fusion | flops 458752 | bytes 1835009 | tf_op jit(solution)/shard_map/jit(_where)/select_n | solution.py:207
  16.1 7.0 %all_gather.13.kv_ref = bf16[4,2,128,128]{3,2,1,0:T(8,128)(2,1)S(1)} all-gather(bf16[1,2,128,128]{3,2,1,0:T(8,128)(2,1)S(1)} %bitcast.50), channel_id=1, replica_groups=mesh['y'=8,'zq'=2,'p'=2,'c'=2,'zh'=2,'x'=4] {'p','c'}, dimensions={0}, use_global_device_ids=true | all-gather | bytes 327680 | tf_op jit(solution)/shard_map/all_gather | solution.py:203
  23.4 1.6 %manifest_attention.1 = bf16[16,40,128]{2,1,0:T(8,128)(2,1)} custom-call(bf16[512,128]{1,0:T(8,128)(2,1)S(1)} %bitcast.45, bf16[4,2,128,128]{3,2,1,0:T(8,128)(2,1)S(1)} %all_gather.13.kv_ref), custom_call_target="tpu_custom_call" | custom-call | tf_op jit(solution)/shard_map/manifest_attention/pallas_call | solution.py:91
  25.0 8.5 %all-to-all-start.1 = ((bf16[16,40,128]{2,1,0:T(8,128)(2,1)}), bf16[16,40,128]{2,1,0:T(8,128)(2,1)S(1)}, u32[]{:S(2)}, u32[]{:S(2)}) async-start(bf16[16,40,128]{2,1,0:T(8,128)(2,1)} %manifest_attention.1), calls=%async_computation.1 | async-start | bytes 327680 | tf_op jit(solution)/shard_map/all_to_all | solution.py:193
  33.6 3.7 %collective-permute-start.1 = (bf16[64,1792]{1,0:T(8,128)(2,1)S(1)}, bf16[64,1792]{1,0:T(8,128)(2,1)S(1)}, u32[]{:S(2)}, u32[]{:S(2)}) collective-permute-start(bf16[64,1792]{1,0:T(8,128)(2,1)S(1)} %get-tuple-element.33), channel_id=1, source_target_pairs={{0,16},{16,0},{1,17},{17,1},{2,18},{18,2},{3,19},{19,3},{4,20},{20... | collective-permute-start | bytes 688136 | tf_op jit(solution)/shard_map/ppermute | solution.py:189
  37.3 0.6 copy-done.3
  38.0 1.2 own_attention.1
  39.2 5.4 %collective-permute-done.1 = bf16[64,1792]{1,0:T(8,128)(2,1)S(1)} collective-permute-done((bf16[64,1792]{1,0:T(8,128)(2,1)S(1)}, bf16[64,1792]{1,0:T(8,128)(2,1)S(1)}, u32[]{:S(2)}, u32[]{:S(2)}) %collective-permute-start.1) | collective-permute-done | bytes 229408 | tf_op jit(solution)/shard_map/ppermute | solution.py:189
  45.1 1.4 %join_attention.1 = bf16[32,4,1024]{2,1,0:T(4,128)(2,1)} custom-call(s32[1]{0:T(128)} %bitcast.place_ref, bf16[16,40,128]{2,1,0:T(8,128)(2,1)S(1)} %all-to-all-done.1.parts_ref, f32[32,128]{1,0:T(8,128)S(1)} %get-tuple-element.20.acc_ref, f32[32,128]{1,0:T(8,128)S(1)} %get-tuple-element.21.top_ref, f32[32,128]{1,0:T(8,128)S(1)} %get-tuple-element.22.total_ref), custom_call_target="tpu_custom_call" | custom-call | tf_op jit(solution)/shard_map/join_attention/pallas_call | solution.py:128
  46.5 8.7 %all-to-all-start.2 = ((bf16[32,4,1024]{2,1,0:T(4,128)(2,1)}), bf16[32,4,1024]{2,1,0:T(4,128)(2,1)S(1)}, u32[]{:S(2)}, u32[]{:S(2)}) async-start(bf16[32,4,1024]{2,1,0:T(4,128)(2,1)} %join_attention.1), calls=%async_computation.2 | async-start | bytes 524288 | tf_op jit(solution)/shard_map/all_to_all | solution.py:193
  55.3 3.7 %collective-permute-start.3 = (bf16[64,1792]{1,0:T(8,128)(2,1)S(1)}, bf16[64,1792]{1,0:T(8,128)(2,1)S(1)}, u32[]{:S(2)}, u32[]{:S(2)}) collective-permute-start(bf16[64,1792]{1,0:T(8,128)(2,1)S(1)} %get-tuple-element.32), channel_id=1, source_target_pairs={{0,16},{16,0},{1,17},{17,1},{2,18},{18,2},{3,19},{19,3},{4,20},{20... | collective-permute-start | bytes 688136 | tf_op jit(solution)/shard_map/ppermute | solution.py:189
  59.0 1.9 %collective-permute-start.2 = (bf16[128,1792]{1,0:T(8,128)(2,1)S(1)}, bf16[128,1792]{1,0:T(8,128)(2,1)S(1)}, u32[]{:S(2)}, u32[]{:S(2)}) collective-permute-start(bf16[128,1792]{1,0:T(8,128)(2,1)S(1)} %get-tuple-element.30.w0_ref), channel_id=1, source_target_pairs={{0,8},{8,0},{1,9},{9,1},{2,10},{10,2},{3,11},{11,3},{4,12},{12,4},... | collective-permute-start | bytes 1376264 | tf_op jit(solution)/shard_map/ppermute | solution.py:185
  60.9 6.7 %collective-permute-done.3 = bf16[64,1792]{1,0:T(8,128)(2,1)S(1)} collective-permute-done((bf16[64,1792]{1,0:T(8,128)(2,1)S(1)}, bf16[64,1792]{1,0:T(8,128)(2,1)S(1)}, u32[]{:S(2)}, u32[]{:S(2)}) %collective-permute-start.3) | collective-permute-done | bytes 229408 | tf_op jit(solution)/shard_map/ppermute | solution.py:189
  67.6 0.8 all-to-all-done.2
  68.8 9.2 %all-gather = bf16[256,256]{1,0:T(8,128)(2,1)S(1)} all-gather(bf16[128,256]{1,0:T(8,128)(2,1)S(1)} %project.1), channel_id=2, replica_groups=mesh['y'=8,'zq'=2,'p'=2,'c'=2,'zh'=2,'x'=4] {'zh'}, dimensions={0}, use_global_device_ids=true | all-gather | bytes 196608 | tf_op jit(solution)/shard_map/all_gather | solution.py:217
  77.9 0.7 add_shares.1
  78.7 5.0 %all-to-all-start.3 = ((bf16[4,128,256]{2,1,0:T(8,128)(2,1)}), bf16[4,128,256]{2,1,0:T(8,128)(2,1)S(1)}, u32[]{:S(2)}, u32[]{:S(2)}) async-start(bf16[4,128,256]{2,1,0:T(8,128)(2,1)} %add_shares.1), calls=%async_computation.3 | async-start | bytes 524288 | tf_op jit(solution)/shard_map/all_to_all | solution.py:193
  83.7 1.9 %collective-permute-start.4 = (bf16[32,4,128]{2,1,0:T(4,128)(2,1)S(1)}, bf16[32,4,128]{2,1,0:T(4,128)(2,1)S(1)}, u32[]{:S(2)}, u32[]{:S(2)}) collective-permute-start(bf16[32,4,128]{2,1,0:T(4,128)(2,1)S(1)} %get-tuple-element.37), channel_id=1, source_target_pairs={{0,8},{8,0},{1,9},{9,1},{2,10},{10,2},{3,11},{11,3},{4,12},{12,4},... | collective-permute-start | bytes 98312 | tf_op jit(solution)/shard_map/ppermute | solution.py:185
  85.6 2.4 %collective-permute-start.6 = (bf16[128,1792]{1,0:T(8,128)(2,1)S(1)}, bf16[128,1792]{1,0:T(8,128)(2,1)S(1)}, u32[]{:S(2)}, u32[]{:S(2)}) collective-permute-start(bf16[128,1792]{1,0:T(8,128)(2,1)S(1)} %pad_maximum_fusion.w2_ref), channel_id=1, source_target_pairs={{0,8},{8,0},{1,9},{9,1},{2,10},{10,2},{3,11},{11,3},{4,12},{12,4},... | collective-permute-start | bytes 1376264 | tf_op jit(solution)/shard_map/ppermute | solution.py:185
  88.2 0.7 all-to-all-done.3
  88.9 4.9 %all_gather.16.both_ref = bf16[2,128,256]{2,1,0:T(8,128)(2,1)S(1)} all-gather(bf16[1,128,256]{2,1,0:T(8,128)(2,1)S(1)} %fusion), channel_id=1, replica_groups=mesh['y'=8,'zq'=2,'p'=2,'c'=2,'zh'=2,'x'=4] {'p'}, dimensions={0}, use_global_device_ids=true | all-gather | bytes 196608 | tf_op jit(solution)/shard_map/all_gather | solution.py:226
  93.9 1.2 %gate_up.1 = bf16[32,8,896]{2,1,0:T(8,128)(2,1)} custom-call(s32[1]{0:T(128)} %bitcast.11.side_ref, bf16[128,256]{1,0:T(8,128)(2,1)S(1)} %add_convert_fusion.x_ref, bf16[2,128,256]{2,1,0:T(8,128)(2,1)S(1)} %all_gather.16.both_ref, bf16[128,1792]{1,0:T(8,128)(2,1)S(1)} %get-tuple-element.30.w0_ref, bf16[128,1792]{1,0:T(8,128)(2,1)S(1)} %collective-permute-done.2.w1_ref, ...), custom_call_target="tpu_custom_call" | custom-call | tf_op jit(solution)/shard_map/gate_up/pallas_call | solution.py:174
  95.1 8.0 %all-to-all-start.4 = ((bf16[32,8,896]{2,1,0:T(8,128)(2,1)}), bf16[32,8,896]{2,1,0:T(8,128)(2,1)S(1)}, u32[]{:S(2)}, u32[]{:S(2)}) async-start(bf16[32,8,896]{2,1,0:T(8,128)(2,1)} %gate_up.1), calls=%async_computation.4 | async-start | bytes 917504 | tf_op jit(solution)/shard_map/all_to_all | solution.py:193
  103.1 1.9 %collective-permute-start.5 = (bf16[128,128]{1,0:T(8,128)(2,1)S(1)}, bf16[128,128]{1,0:T(8,128)(2,1)S(1)}, u32[]{:S(2)}, u32[]{:S(2)}) collective-permute-start(bf16[128,128]{1,0:T(8,128)(2,1)S(1)} %slice.47), channel_id=1, source_target_pairs={{0,8},{8,0},{1,9},{9,1},{2,10},{10,2},{3,11},{11,3},{4,12},{12,4},... | collective-permute-start | bytes 98312 | tf_op jit(solution)/shard_map/ppermute | solution.py:185
  105.1 1.2 collective-permute-done.5
  106.3 0.7 copy.17
  106.9 11.9 %all-to-all-done.4 = bf16[32,8,896]{2,1,0:T(8,128)(2,1)S(1)} async-done(((bf16[32,8,896]{2,1,0:T(8,128)(2,1)}), bf16[32,8,896]{2,1,0:T(8,128)(2,1)S(1)}, u32[]{:S(2)}, u32[]{:S(2)}) %all-to-all-start.4) | async-done | bytes 458784 | tf_op jit(solution)/shard_map/all_to_all | solution.py:193
  118.9 0.6 fusion.5
  (35 shorter events, 1.6 us)
Async XLA Ops:
  0.6 12.3 %copy-start.1 = (bf16[1024,128]{1,0:T(8,128)(2,1)S(1)}, bf16[1024,128]{1,0:T(8,128)(2,1)}, u32[]{:S(2)}) copy-start(bf16[1024,128]{1,0:T(8,128)(2,1)} %w0_ref.1) | copy-start | bytes 786436
  2.1 21.3 %all-to-all-start = ((bf16[16,32,128]{2,1,0:T(8,128)(2,1)}), bf16[16,32,128]{2,1,0:T(8,128)(2,1)S(1)}, u32[]{:S(2)}, u32[]{:S(2)}) async-start(bf16[16,32,128]{2,1,0:T(8,128)(2,1)} %broadcast_in_dim.8), calls=%async_computation | async-start | bytes 262144 | tf_op jit(solution)/shard_map/all_to_all | solution.py:193
  12.9 31.7 %collective-permute-start = (bf16[1024,128]{1,0:T(8,128)(2,1)S(1)}, bf16[1024,128]{1,0:T(8,128)(2,1)S(1)}, u32[]{:S(2)}, u32[]{:S(2)}) collective-permute-start(bf16[1024,128]{1,0:T(8,128)(2,1)S(1)} %copy-done.1), channel_id=1, source_target_pairs={{0,8},{8,0},{1,9},{9,1},{2,10},{10,2},{3,11},{11,3},{4,12},{12,4},... | collective-permute-start | bytes 786440 | tf_op jit(solution)/shard_map/ppermute | solution.py:185
  14.8 1.3 %copy-start.5 = (bf16[2,2,64,128]{3,2,1,0:T(8,128)(2,1)S(1)}, bf16[2,2,64,128]{3,2,1,0:T(8,128)(2,1)}, u32[]{:S(2)}) copy-start(bf16[2,2,64,128]{3,2,1,0:T(8,128)(2,1)} %param.13) | copy-start | bytes 196612
  16.1 21.2 %copy-start = (bf16[2,32,64,128]{3,2,1,0:T(8,128)(2,1)S(1)}, bf16[2,32,64,128]{3,2,1,0:T(8,128)(2,1)}, u32[]{:S(2)}) copy-start(bf16[2,32,64,128]{3,2,1,0:T(8,128)(2,1)} %param.12) | copy-start | bytes 3145732
  25.0 20.1 %all-to-all-start.1 = ((bf16[16,40,128]{2,1,0:T(8,128)(2,1)}), bf16[16,40,128]{2,1,0:T(8,128)(2,1)S(1)}, u32[]{:S(2)}, u32[]{:S(2)}) async-start(bf16[16,40,128]{2,1,0:T(8,128)(2,1)} %manifest_attention.1), calls=%async_computation.1 | async-start | bytes 327680 | tf_op jit(solution)/shard_map/all_to_all | solution.py:193
  33.6 11.0 %collective-permute-start.1 = (bf16[64,1792]{1,0:T(8,128)(2,1)S(1)}, bf16[64,1792]{1,0:T(8,128)(2,1)S(1)}, u32[]{:S(2)}, u32[]{:S(2)}) collective-permute-start(bf16[64,1792]{1,0:T(8,128)(2,1)S(1)} %get-tuple-element.33), channel_id=1, source_target_pairs={{0,16},{16,0},{1,17},{17,1},{2,18},{18,2},{3,19},{19,3},{4,20},{20... | collective-permute-start | bytes 688136 | tf_op jit(solution)/shard_map/ppermute | solution.py:189
  37.3 0.7 copy-start.3
  37.3 0.7 copy-start.2
  37.3 0.7 copy-start.4
  46.5 21.9 %all-to-all-start.2 = ((bf16[32,4,1024]{2,1,0:T(4,128)(2,1)}), bf16[32,4,1024]{2,1,0:T(4,128)(2,1)S(1)}, u32[]{:S(2)}, u32[]{:S(2)}) async-start(bf16[32,4,1024]{2,1,0:T(4,128)(2,1)} %join_attention.1), calls=%async_computation.2 | async-start | bytes 524288 | tf_op jit(solution)/shard_map/all_to_all | solution.py:193
  55.3 12.3 %collective-permute-start.3 = (bf16[64,1792]{1,0:T(8,128)(2,1)S(1)}, bf16[64,1792]{1,0:T(8,128)(2,1)S(1)}, u32[]{:S(2)}, u32[]{:S(2)}) collective-permute-start(bf16[64,1792]{1,0:T(8,128)(2,1)S(1)} %get-tuple-element.32), channel_id=1, source_target_pairs={{0,16},{16,0},{1,17},{17,1},{2,18},{18,2},{3,19},{19,3},{4,20},{20... | collective-permute-start | bytes 688136 | tf_op jit(solution)/shard_map/ppermute | solution.py:189
  59.0 9.5 %collective-permute-start.2 = (bf16[128,1792]{1,0:T(8,128)(2,1)S(1)}, bf16[128,1792]{1,0:T(8,128)(2,1)S(1)}, u32[]{:S(2)}, u32[]{:S(2)}) collective-permute-start(bf16[128,1792]{1,0:T(8,128)(2,1)S(1)} %get-tuple-element.30.w0_ref), channel_id=1, source_target_pairs={{0,8},{8,0},{1,9},{9,1},{2,10},{10,2},{3,11},{11,3},{4,12},{12,4},... | collective-permute-start | bytes 1376264 | tf_op jit(solution)/shard_map/ppermute | solution.py:185
  78.7 5.0 %copy-start.6 = (bf16[256,128]{1,0:T(8,128)(2,1)S(1)}, bf16[256,128]{1,0:T(8,128)(2,1)}, u32[]{:S(2)}) copy-start(bf16[256,128]{1,0:T(8,128)(2,1)} %param.16) | copy-start | bytes 196612
  78.7 10.2 %all-to-all-start.3 = ((bf16[4,128,256]{2,1,0:T(8,128)(2,1)}), bf16[4,128,256]{2,1,0:T(8,128)(2,1)S(1)}, u32[]{:S(2)}, u32[]{:S(2)}) async-start(bf16[4,128,256]{2,1,0:T(8,128)(2,1)} %add_shares.1), calls=%async_computation.3 | async-start | bytes 524288 | tf_op jit(solution)/shard_map/all_to_all | solution.py:193
  83.7 4.3 %collective-permute-start.4 = (bf16[32,4,128]{2,1,0:T(4,128)(2,1)S(1)}, bf16[32,4,128]{2,1,0:T(4,128)(2,1)S(1)}, u32[]{:S(2)}, u32[]{:S(2)}) collective-permute-start(bf16[32,4,128]{2,1,0:T(4,128)(2,1)S(1)} %get-tuple-element.37), channel_id=1, source_target_pairs={{0,8},{8,0},{1,9},{9,1},{2,10},{10,2},{3,11},{11,3},{4,12},{12,4},... | collective-permute-start | bytes 98312 | tf_op jit(solution)/shard_map/ppermute | solution.py:185
  85.6 8.3 %collective-permute-start.6 = (bf16[128,1792]{1,0:T(8,128)(2,1)S(1)}, bf16[128,1792]{1,0:T(8,128)(2,1)S(1)}, u32[]{:S(2)}, u32[]{:S(2)}) collective-permute-start(bf16[128,1792]{1,0:T(8,128)(2,1)S(1)} %pad_maximum_fusion.w2_ref), channel_id=1, source_target_pairs={{0,8},{8,0},{1,9},{9,1},{2,10},{10,2},{3,11},{11,3},{4,12},{12,4},... | collective-permute-start | bytes 1376264 | tf_op jit(solution)/shard_map/ppermute | solution.py:185
  95.1 23.7 %all-to-all-start.4 = ((bf16[32,8,896]{2,1,0:T(8,128)(2,1)}), bf16[32,8,896]{2,1,0:T(8,128)(2,1)S(1)}, u32[]{:S(2)}, u32[]{:S(2)}) async-start(bf16[32,8,896]{2,1,0:T(8,128)(2,1)} %gate_up.1), calls=%async_computation.4 | async-start | bytes 917504 | tf_op jit(solution)/shard_map/all_to_all | solution.py:193
  103.1 3.1 %collective-permute-start.5 = (bf16[128,128]{1,0:T(8,128)(2,1)S(1)}, bf16[128,128]{1,0:T(8,128)(2,1)S(1)}, u32[]{:S(2)}, u32[]{:S(2)}) collective-permute-start(bf16[128,128]{1,0:T(8,128)(2,1)S(1)} %slice.47), channel_id=1, source_target_pairs={{0,8},{8,0},{1,9},{9,1},{2,10},{10,2},{3,11},{11,3},{4,12},{12,4},... | collective-permute-start | bytes 98312 | tf_op jit(solution)/shard_map/ppermute | solution.py:185

commit v13 on v10

--- a/solution.py
+++ b/solution.py
@@ -16,10 +16,10 @@
 PEERS = 16
 STATS = 8
 SCALE = HD**-0.5
-PLANE = ("y", "zq", "p")
+PLANE = ("y", "p", "zq")
 SPARSE = ("y", "zq")
 HEAD = ("zh", "x")
-REQ = ("y", "zq", "p", "c")
+REQ = ("y", "p", "zq", "c")
 BF = jnp.bfloat16
 F32 = jnp.float32
 
@@ -206,7 +206,7 @@
     out2 = (res + heads.astype(F32).sum(0)).astype(BF)
     both = dense(mlp_kernel, "gate_up", (CHIPS, 2 * ROWS, width), out2, w_gate, w_gate_c, w_up, w_up_c)
     joined = exchange(both, PLANE).astype(F32).sum(0)
-    odd = lax.axis_index("p") == 1
+    odd = lax.axis_index("zq") == 1
     gate = jnp.where(odd, joined[ROWS:], joined[:ROWS])
     up = jnp.where(odd, joined[:ROWS], joined[ROWS:])
     hidden = (jax.nn.silu(gate) * up).astype(BF)
@@ -220,7 +220,7 @@
 
 
 def solution(mesh):
-    fine = Mesh(mesh.devices.reshape(8, 2, 2, 2, 2, 4), ("y", "zq", "p", "c", "zh", "x"))
+    fine = Mesh(mesh.devices.reshape(8, 2, 2, 2, 2, 4), ("y", "p", "zq", "c", "zh", "x"))
     in_specs = (
         P(REQ, HEAD),
         P(None, REQ, HEAD),

time: 113 us -> 113 us (level)
  the two profiles are of different devices: /device:TPU:2 before, /device:TPU:4 now
where the time goes in v13:
time: 113 us; the launch traced here: 112 us
  waiting for transfers between devices  42.1 us (37%)
  starting transfers between devices  40.2 us (36%)
  blocking collectives  18.8 us (17%)
  Pallas kernels  6.55 us (6%)
  local copies, waits for them, and re-layouts  2.28 us (2%)
    all_to_all x5, waiting for transfers between devices, exchange(): return lax.all_to_all(x, axes, 0, 0, tiled=True)  39.6 us
    all_to_all x5, starting transfers between devices, exchange(): return lax.all_to_all(x, axes, 0, 0, tiled=True)  30.1 us
    ppermute x5, starting transfers between devices, swap(): return lax.ppermute(x, 'c', [(0, 1), (1, 0)])  10.1 us
    all_gather x1, blocking collectives, on_device(): shares = lax.all_gather(share, 'zh', axis=0)  9.91 us
    all_gather x1, blocking collectives, on_device(): lax.all_gather(man_kv.reshape(1, 2, 2 * PAGE, HD), ('p', 'c'), axis=0, ti...  8.91 us
    ppermute x5, waiting for transfers between devices, swap(): return lax.ppermute(x, 'c', [(0, 1), (1, 0)])  2.51 us
    pallas_call x3, Pallas kernels, dense(): pl.pallas_call(kernel, out_shape=jax.ShapeDtypeStruct(out_shape, BF), in_...  2.31 us
  transfers between devices with their start and end apart: 10, of which 8 were waited for; matrix products, arithmetic and copies ran while one was open for 1% of the time, Pallas kernels for 1%

profile of v13, /device:TPU:4, one launch (start us, length us, event | category | flops | bytes accessed | tf_op | source)
XLA Modules:
  0.0 111.8 jit_solution(14590951409107366853)
XLA Ops:
  0.7 0.8 broadcast_in_dim.7.q_ref
  1.5 0.7 broadcast_in_dim.8
  2.2 9.0 %all-to-all-start = ((bf16[16,32,128]{2,1,0:T(8,128)(2,1)}), bf16[16,32,128]{2,1,0:T(8,128)(2,1)S(1)}, u32[]{:S(2)}, u32[]{:S(2)}) async-start(bf16[16,32,128]{2,1,0:T(8,128)(2,1)} %broadcast_in_dim.8), calls=%async_computation | async-start | bytes 262144 | tf_op jit(solution)/shard_map/all_to_all | solution.py:180
  11.2 8.9 %all_gather.9.kv_ref = bf16[4,2,128,128]{3,2,1,0:T(8,128)(2,1)S(1)} all-gather(bf16[1,2,128,128]{3,2,1,0:T(8,128)(2,1)} %bitcast.30), channel_id=1, replica_groups=mesh['y'=8,'p'=2,'zq'=2,'c'=2,'zh'=2,'x'=4] {'p','c'}, dimensions={0}, use_global_device_ids=true | all-gather | bytes 327680 | tf_op jit(solution)/shard_map/all_gather | solution.py:190
  20.1 0.7 all-to-all-done
  20.8 1.6 %manifest_attention.1 = bf16[16,40,128]{2,1,0:T(8,128)(2,1)} custom-call(bf16[512,128]{1,0:T(8,128)(2,1)S(1)} %bitcast.26, bf16[4,2,128,128]{3,2,1,0:T(8,128)(2,1)S(1)} %all_gather.9.kv_ref), custom_call_target="tpu_custom_call" | custom-call | tf_op jit(solution)/shard_map/manifest_attention/pallas_call | solution.py:91
  22.4 7.7 %all-to-all-start.1 = ((bf16[16,40,128]{2,1,0:T(8,128)(2,1)}), bf16[16,40,128]{2,1,0:T(8,128)(2,1)S(1)}, u32[]{:S(2)}, u32[]{:S(2)}) async-start(bf16[16,40,128]{2,1,0:T(8,128)(2,1)} %manifest_attention.1), calls=%async_computation.1 | async-start | bytes 327680 | tf_op jit(solution)/shard_map/all_to_all | solution.py:180
  30.2 2.0 %collective-permute-start = (bf16[1024,128]{1,0:T(8,128)(2,1)S(1)}, bf16[1024,128]{1,0:T(8,128)(2,1)S(1)}, u32[]{:S(2)}, u32[]{:S(2)}) collective-permute-start(bf16[1024,128]{1,0:T(8,128)(2,1)S(1)} %copy-done.3), channel_id=1, source_target_pairs={{0,8},{8,0},{1,9},{9,1},{2,10},{10,2},{3,11},{11,3},{4,12},{12,4},... | collective-permute-start | bytes 786440 | tf_op jit(solution)/shard_map/ppermute | solution.py:176
  32.3 1.2 %own_attention.1 = (f32[32,128]{1,0:T(8,128)S(1)}, f32[32,128]{1,0:T(8,128)S(1)}, f32[32,128]{1,0:T(8,128)S(1)}) custom-call(s32[4,8]{1,0:T(4,128)S(1)} %copy-done.4, s32[4]{0:T(128)S(1)} %copy-done.6, bf16[32,128]{1,0:T(8,128)(2,1)S(1)} %broadcast_in_dim.7.q_ref, bf16[2,4,128]{2,1,0:T(4,128)(2,1)S(1)} %copy-done.5, bf16[2,2048,128]{2,1,0:T(8,128)(2,1)S(1)} %bitcast.25), custom_call_target="tpu_custom_call" | custom-call | tf_op jit(solution)/shard_map/own_attention/pallas_call | solution.py:60
  33.5 0.2 collective-permute-done.w1_ref
  33.6 7.2 %all-to-all-done.1.parts_ref = bf16[16,40,128]{2,1,0:T(8,128)(2,1)S(1)} async-done(((bf16[16,40,128]{2,1,0:T(8,128)(2,1)}), bf16[16,40,128]{2,1,0:T(8,128)(2,1)S(1)}, u32[]{:S(2)}, u32[]{:S(2)}) %all-to-all-start.1) | async-done | bytes 163872 | tf_op jit(solution)/shard_map/all_to_all | solution.py:180
  40.9 1.4 %join_attention.1 = bf16[32,4,1024]{2,1,0:T(4,128)(2,1)} custom-call(s32[1]{0:T(128)} %bitcast.place_ref, bf16[16,40,128]{2,1,0:T(8,128)(2,1)S(1)} %all-to-all-done.1.parts_ref, f32[32,128]{1,0:T(8,128)S(1)} %get-tuple-element.19.acc_ref, f32[32,128]{1,0:T(8,128)S(1)} %get-tuple-element.20.top_ref, f32[32,128]{1,0:T(8,128)S(1)} %get-tuple-element.21.total_ref), custom_call_target="tpu_custom_call" | custom-call | tf_op jit(solution)/shard_map/join_attention/pallas_call | solution.py:128
  42.2 4.6 %all-to-all-start.2 = ((bf16[32,4,1024]{2,1,0:T(4,128)(2,1)}), bf16[32,4,1024]{2,1,0:T(4,128)(2,1)S(1)}, u32[]{:S(2)}, u32[]{:S(2)}) async-start(bf16[32,4,1024]{2,1,0:T(4,128)(2,1)} %join_attention.1), calls=%async_computation.2 | async-start | bytes 524288 | tf_op jit(solution)/shard_map/all_to_all | solution.py:180
  46.9 1.9 %collective-permute-start.1 = (bf16[128,1792]{1,0:T(8,128)(2,1)S(1)}, bf16[128,1792]{1,0:T(8,128)(2,1)S(1)}, u32[]{:S(2)}, u32[]{:S(2)}) collective-permute-start(bf16[128,1792]{1,0:T(8,128)(2,1)S(1)} %copy-done.1), channel_id=1, source_target_pairs={{0,8},{8,0},{1,9},{9,1},{2,10},{10,2},{3,11},{11,3},{4,12},{12,4},... | collective-permute-start | bytes 1376264 | tf_op jit(solution)/shard_map/ppermute | solution.py:176
  48.8 2.4 %collective-permute-start.2 = (bf16[128,1792]{1,0:T(8,128)(2,1)S(1)}, bf16[128,1792]{1,0:T(8,128)(2,1)S(1)}, u32[]{:S(2)}, u32[]{:S(2)}) collective-permute-start(bf16[128,1792]{1,0:T(8,128)(2,1)S(1)} %copy-done.2), channel_id=1, source_target_pairs={{0,8},{8,0},{1,9},{9,1},{2,10},{10,2},{3,11},{11,3},{4,12},{12,4},... | collective-permute-start | bytes 1376264 | tf_op jit(solution)/shard_map/ppermute | solution.py:176
  51.2 8.6 %all-to-all-done.2 = bf16[32,4,1024]{2,1,0:T(4,128)(2,1)S(1)} async-done(((bf16[32,4,1024]{2,1,0:T(4,128)(2,1)}), bf16[32,4,1024]{2,1,0:T(4,128)(2,1)S(1)}, u32[]{:S(2)}, u32[]{:S(2)}) %all-to-all-start.2) | async-done | bytes 262176 | tf_op jit(solution)/shard_map/all_to_all | solution.py:180
  59.9 0.1 reshape.84.x_ref
  60.0 0.2 project.1
  60.2 9.9 %all-gather = bf16[256,256]{1,0:T(8,128)(2,1)S(1)} all-gather(bf16[128,256]{1,0:T(8,128)(2,1)S(1)} %project.1), channel_id=2, replica_groups=mesh['y'=8,'p'=2,'zq'=2,'c'=2,'zh'=2,'x'=4] {'zh'}, dimensions={0}, use_global_device_ids=true | all-gather | bytes 196608 | tf_op jit(solution)/shard_map/all_gather | solution.py:199
  70.1 0.7 add_shares.1
  70.9 4.8 %all-to-all-start.3 = ((bf16[4,128,256]{2,1,0:T(8,128)(2,1)}), bf16[4,128,256]{2,1,0:T(8,128)(2,1)S(1)}, u32[]{:S(2)}, u32[]{:S(2)}) async-start(bf16[4,128,256]{2,1,0:T(8,128)(2,1)} %add_shares.1), calls=%async_computation.3 | async-start | bytes 524288 | tf_op jit(solution)/shard_map/all_to_all | solution.py:180
  75.7 1.9 %collective-permute-start.3 = (bf16[32,4,128]{2,1,0:T(4,128)(2,1)S(1)}, bf16[32,4,128]{2,1,0:T(4,128)(2,1)S(1)}, u32[]{:S(2)}, u32[]{:S(2)}) collective-permute-start(bf16[32,4,128]{2,1,0:T(4,128)(2,1)S(1)} %get-tuple-element.31), channel_id=1, source_target_pairs={{0,8},{8,0},{1,9},{9,1},{2,10},{10,2},{3,11},{11,3},{4,12},{12,4},... | collective-permute-start | bytes 98312 | tf_op jit(solution)/shard_map/ppermute | solution.py:176
  77.6 1.2 %collective-permute-done.3 = bf16[32,4,128]{2,1,0:T(4,128)(2,1)S(1)} collective-permute-done((bf16[32,4,128]{2,1,0:T(4,128)(2,1)S(1)}, bf16[32,4,128]{2,1,0:T(4,128)(2,1)S(1)}, u32[]{:S(2)}, u32[]{:S(2)}) %collective-permute-start.3) | collective-permute-done | bytes 32800 | tf_op jit(solution)/shard_map/ppermute | solution.py:176
  78.9 0.5 all-to-all-done.3
  79.4 1.4 %gate_up.1 = bf16[32,8,1792]{2,1,0:T(8,128)(2,1)} custom-call(bf16[128,256]{1,0:T(8,128)(2,1)S(1)} %add_convert_fusion.x_ref, bf16[128,1792]{1,0:T(8,128)(2,1)S(1)} %copy-done.1, bf16[128,1792]{1,0:T(8,128)(2,1)S(1)} %collective-permute-done.1.g1_ref, bf16[128,1792]{1,0:T(8,128)(2,1)S(1)} %copy-done.2, bf16[128,1792]{1,0:T(8,128)(2,1)S(1)} %collective-permute-done.2.u1_ref), custom_call_target="tpu_custom_call" | custom-call | tf_op jit(solution)/shard_map/gate_up/pallas_call | solution.py:165
  80.8 3.9 %all-to-all-start.4 = ((bf16[32,8,1792]{2,1,0:T(8,128)(2,1)}), bf16[32,8,1792]{2,1,0:T(8,128)(2,1)S(1)}, u32[]{:S(2)}, u32[]{:S(2)}) async-start(bf16[32,8,1792]{2,1,0:T(8,128)(2,1)} %gate_up.1), calls=%async_computation.4 | async-start | bytes 1835008 | tf_op jit(solution)/shard_map/all_to_all | solution.py:180
  84.7 1.9 %collective-permute-start.4 = (bf16[128,128]{1,0:T(8,128)(2,1)S(1)}, bf16[128,128]{1,0:T(8,128)(2,1)S(1)}, u32[]{:S(2)}, u32[]{:S(2)}) collective-permute-start(bf16[128,128]{1,0:T(8,128)(2,1)S(1)} %slice.31), channel_id=1, source_target_pairs={{0,8},{8,0},{1,9},{9,1},{2,10},{10,2},{3,11},{11,3},{4,12},{12,4},... | collective-permute-start | bytes 98312 | tf_op jit(solution)/shard_map/ppermute | solution.py:176
  86.7 1.2 %collective-permute-done.4 = bf16[128,128]{1,0:T(8,128)(2,1)S(1)} collective-permute-done((bf16[128,128]{1,0:T(8,128)(2,1)S(1)}, bf16[128,128]{1,0:T(8,128)(2,1)S(1)}, u32[]{:S(2)}, u32[]{:S(2)}) %collective-permute-start.4) | collective-permute-done | bytes 32800 | tf_op jit(solution)/shard_map/ppermute | solution.py:176
  87.9 0.7 copy.17
  88.5 22.5 %all-to-all-done.4 = bf16[32,8,1792]{2,1,0:T(8,128)(2,1)S(1)} async-done(((bf16[32,8,1792]{2,1,0:T(8,128)(2,1)}), bf16[32,8,1792]{2,1,0:T(8,128)(2,1)S(1)}, u32[]{:S(2)}, u32[]{:S(2)}) %all-to-all-start.4) | async-done | bytes 917536 | tf_op jit(solution)/shard_map/all_to_all | solution.py:180
  111.0 0.1 convert_reduce_fusion
  111.2 0.6 fusion.1
  (26 shorter events, 0.3 us)
Async XLA Ops:
  0.6 29.6 %copy-start.3 = (bf16[1024,128]{1,0:T(8,128)(2,1)S(1)}, bf16[1024,128]{1,0:T(8,128)(2,1)}, u32[]{:S(2)}) copy-start(bf16[1024,128]{1,0:T(8,128)(2,1)} %w0_ref.1) | copy-start | bytes 786436
  0.6 31.6 %copy-start.6 = (s32[4]{0:T(128)S(1)}, s32[4]{0:T(128)}, u32[]{:S(2)}) copy-start(s32[4]{0:T(128)} %len_ref.1) | copy-start | bytes 52
  0.7 31.6 %copy-start.4 = (s32[4,8]{1,0:T(4,128)S(1)}, s32[4,8]{1,0:T(4,128)}, u32[]{:S(2)}) copy-start(s32[4,8]{1,0:T(4,128)} %pages_ref.1) | copy-start | bytes 388
  0.7 31.6 %copy-start = (bf16[2,32,64,128]{3,2,1,0:T(8,128)(2,1)S(1)}, bf16[2,32,64,128]{3,2,1,0:T(8,128)(2,1)}, u32[]{:S(2)}) copy-start(bf16[2,32,64,128]{3,2,1,0:T(8,128)(2,1)} %param.12) | copy-start | bytes 3145732
  0.7 31.6 %copy-start.5 = (bf16[2,4,128]{2,1,0:T(4,128)(2,1)S(1)}, bf16[2,4,128]{2,1,0:T(4,128)(2,1)}, u32[]{:S(2)}) copy-start(bf16[2,4,128]{2,1,0:T(4,128)(2,1)} %new_ref.1) | copy-start | bytes 6148
  2.2 18.6 %all-to-all-start = ((bf16[16,32,128]{2,1,0:T(8,128)(2,1)}), bf16[16,32,128]{2,1,0:T(8,128)(2,1)S(1)}, u32[]{:S(2)}, u32[]{:S(2)}) async-start(bf16[16,32,128]{2,1,0:T(8,128)(2,1)} %broadcast_in_dim.8), calls=%async_computation | async-start | bytes 262144 | tf_op jit(solution)/shard_map/all_to_all | solution.py:180
  22.4 18.4 %all-to-all-start.1 = ((bf16[16,40,128]{2,1,0:T(8,128)(2,1)}), bf16[16,40,128]{2,1,0:T(8,128)(2,1)S(1)}, u32[]{:S(2)}, u32[]{:S(2)}) async-start(bf16[16,40,128]{2,1,0:T(8,128)(2,1)} %manifest_attention.1), calls=%async_computation.1 | async-start | bytes 327680 | tf_op jit(solution)/shard_map/all_to_all | solution.py:180
  30.2 3.4 %collective-permute-start = (bf16[1024,128]{1,0:T(8,128)(2,1)S(1)}, bf16[1024,128]{1,0:T(8,128)(2,1)S(1)}, u32[]{:S(2)}, u32[]{:S(2)}) collective-permute-start(bf16[1024,128]{1,0:T(8,128)(2,1)S(1)} %copy-done.3), channel_id=1, source_target_pairs={{0,8},{8,0},{1,9},{9,1},{2,10},{10,2},{3,11},{11,3},{4,12},{12,4},... | collective-permute-start | bytes 786440 | tf_op jit(solution)/shard_map/ppermute | solution.py:176
  32.2 14.7 %copy-start.1 = (bf16[128,1792]{1,0:T(8,128)(2,1)S(1)}, bf16[128,1792]{1,0:T(8,128)(2,1)}, u32[]{:S(2)}) copy-start(bf16[128,1792]{1,0:T(8,128)(2,1)} %g0_ref.1) | copy-start | bytes 1376260
  32.2 16.6 %copy-start.2 = (bf16[128,1792]{1,0:T(8,128)(2,1)S(1)}, bf16[128,1792]{1,0:T(8,128)(2,1)}, u32[]{:S(2)}) copy-start(bf16[128,1792]{1,0:T(8,128)(2,1)} %u0_ref.1) | copy-start | bytes 1376260
  42.2 17.6 %all-to-all-start.2 = ((bf16[32,4,1024]{2,1,0:T(4,128)(2,1)}), bf16[32,4,1024]{2,1,0:T(4,128)(2,1)S(1)}, u32[]{:S(2)}, u32[]{:S(2)}) async-start(bf16[32,4,1024]{2,1,0:T(4,128)(2,1)} %join_attention.1), calls=%async_computation.2 | async-start | bytes 524288 | tf_op jit(solution)/shard_map/all_to_all | solution.py:180
  46.9 13.1 %collective-permute-start.1 = (bf16[128,1792]{1,0:T(8,128)(2,1)S(1)}, bf16[128,1792]{1,0:T(8,128)(2,1)S(1)}, u32[]{:S(2)}, u32[]{:S(2)}) collective-permute-start(bf16[128,1792]{1,0:T(8,128)(2,1)S(1)} %copy-done.1), channel_id=1, source_target_pairs={{0,8},{8,0},{1,9},{9,1},{2,10},{10,2},{3,11},{11,3},{4,12},{12,4},... | collective-permute-start | bytes 1376264 | tf_op jit(solution)/shard_map/ppermute | solution.py:176
  48.8 11.2 %collective-permute-start.2 = (bf16[128,1792]{1,0:T(8,128)(2,1)S(1)}, bf16[128,1792]{1,0:T(8,128)(2,1)S(1)}, u32[]{:S(2)}, u32[]{:S(2)}) collective-permute-start(bf16[128,1792]{1,0:T(8,128)(2,1)S(1)} %copy-done.2), channel_id=1, source_target_pairs={{0,8},{8,0},{1,9},{9,1},{2,10},{10,2},{3,11},{11,3},{4,12},{12,4},... | collective-permute-start | bytes 1376264 | tf_op jit(solution)/shard_map/ppermute | solution.py:176
  60.0 15.7 %copy-start.7 = (bf16[256,128]{1,0:T(8,128)(2,1)S(1)}, bf16[256,128]{1,0:T(8,128)(2,1)}, u32[]{:S(2)}) copy-start(bf16[256,128]{1,0:T(8,128)(2,1)} %param.16) | copy-start | bytes 196612
  70.9 8.5 %all-to-all-start.3 = ((bf16[4,128,256]{2,1,0:T(8,128)(2,1)}), bf16[4,128,256]{2,1,0:T(8,128)(2,1)S(1)}, u32[]{:S(2)}, u32[]{:S(2)}) async-start(bf16[4,128,256]{2,1,0:T(8,128)(2,1)} %add_shares.1), calls=%async_computation.3 | async-start | bytes 524288 | tf_op jit(solution)/shard_map/all_to_all | solution.py:180
  75.7 3.1 %collective-permute-start.3 = (bf16[32,4,128]{2,1,0:T(4,128)(2,1)S(1)}, bf16[32,4,128]{2,1,0:T(4,128)(2,1)S(1)}, u32[]{:S(2)}, u32[]{:S(2)}) collective-permute-start(bf16[32,4,128]{2,1,0:T(4,128)(2,1)S(1)} %get-tuple-element.31), channel_id=1, source_target_pairs={{0,8},{8,0},{1,9},{9,1},{2,10},{10,2},{3,11},{11,3},{4,12},{12,4},... | collective-permute-start | bytes 98312 | tf_op jit(solution)/shard_map/ppermute | solution.py:176
  80.8 30.3 %all-to-all-start.4 = ((bf16[32,8,1792]{2,1,0:T(8,128)(2,1)}), bf16[32,8,1792]{2,1,0:T(8,128)(2,1)S(1)}, u32[]{:S(2)}, u32[]{:S(2)}) async-start(bf16[32,8,1792]{2,1,0:T(8,128)(2,1)} %gate_up.1), calls=%async_computation.4 | async-start | bytes 1835008 | tf_op jit(solution)/shard_map/all_to_all | solution.py:180
  84.7 3.1 %collective-permute-start.4 = (bf16[128,128]{1,0:T(8,128)(2,1)S(1)}, bf16[128,128]{1,0:T(8,128)(2,1)S(1)}, u32[]{:S(2)}, u32[]{:S(2)}) collective-permute-start(bf16[128,128]{1,0:T(8,128)(2,1)S(1)} %slice.31), channel_id=1, source_target_pairs={{0,8},{8,0},{1,9},{9,1},{2,10},{10,2},{3,11},{11,3},{4,12},{12,4},... | collective-permute-start | bytes 98312 | tf_op jit(solution)/shard_map/ppermute | solution.py:176

commit v14 on v13

--- a/solution.py
+++ b/solution.py
@@ -186,7 +186,7 @@
     width = w_gate.shape[1]
     rows = CHIPS * ROWS
     q = queries.reshape(QROWS, HD)
-    q_all = exchange(jnp.broadcast_to(q[None], (PEERS, QROWS, HD)), SPARSE).reshape(PEERS * QROWS, HD)
+    q_all = exchange(jnp.broadcast_to(queries[None], (PEERS, *queries.shape)), SPARSE).reshape(PEERS * QROWS, HD)
     kv = lax.all_gather(man_kv.reshape(1, 2, 2 * PAGE, HD), ("p", "c"), axis=0, tiled=True)
     parts = exchange(man_part(q_all, kv), SPARSE)
     own = own_part(pages, own_len, q, new_kv, own_kv.reshape(2, POOL * PAGE, HD))

time: 113 us -> 113 us (level)
  the two profiles are of different devices: /device:TPU:4 before, /device:TPU:2 now
where the time goes in v14:
time: 113 us; the launch traced here: 112 us
  waiting for transfers between devices  41.8 us (37%)
  starting transfers between devices  40.3 us (36%)
  blocking collectives  18.8 us (17%)
  Pallas kernels  6.53 us (6%)
  local copies, waits for them, and re-layouts  2.35 us (2%)
    all_to_all x5, waiting for transfers between devices, exchange(): return lax.all_to_all(x, axes, 0, 0, tiled=True)  39.4 us
    all_to_all x5, starting transfers between devices, exchange(): return lax.all_to_all(x, axes, 0, 0, tiled=True)  30.1 us
    ppermute x5, starting transfers between devices, swap(): return lax.ppermute(x, 'c', [(0, 1), (1, 0)])  10.1 us
    all_gather x1, blocking collectives, on_device(): shares = lax.all_gather(share, 'zh', axis=0)  9.91 us
    all_gather x1, blocking collectives, on_device(): lax.all_gather(man_kv.reshape(1, 2, 2 * PAGE, HD), ('p', 'c'), axis=0, ti...  8.91 us
    ppermute x5, waiting for transfers between devices, swap(): return lax.ppermute(x, 'c', [(0, 1), (1, 0)])  2.48 us
    pallas_call x3, Pallas kernels, dense(): pl.pallas_call(kernel, out_shape=jax.ShapeDtypeStruct(out_shape, BF), in_...  2.3 us
  transfers between devices with their start and end apart: 10, of which 8 were waited for; matrix products, arithmetic and copies ran while one was open for 1% of the time, Pallas kernels for 1%

profile of v14, /device:TPU:2, one launch (start us, length us, event | category | flops | bytes accessed | tf_op | source)
XLA Modules:
  0.0 111.7 jit_solution(9852589887876702859)
XLA Ops:
  0.7 1.5 %broadcast_in_dim.2 = bf16[16,4,1024]{2,1,0:T(4,128)(2,1)} broadcast(bf16[4,1024]{1,0:T(4,128)(2,1)} %param.10), dimensions={1,2} | broadcast | bytes 139264 | tf_op jit(solution)/shard_map/broadcast_in_dim | solution.py:189
  2.2 9.0 %all-to-all-start = ((bf16[16,4,1024]{2,1,0:T(4,128)(2,1)}), bf16[16,4,1024]{2,1,0:T(4,128)(2,1)S(1)}, u32[]{:S(2)}, u32[]{:S(2)}) async-start(bf16[16,4,1024]{2,1,0:T(4,128)(2,1)} %broadcast_in_dim.2), calls=%async_computation | async-start | bytes 262144 | tf_op jit(solution)/shard_map/all_to_all | solution.py:180
  11.2 8.9 %all_gather.9.kv_ref = bf16[4,2,128,128]{3,2,1,0:T(8,128)(2,1)S(1)} all-gather(bf16[1,2,128,128]{3,2,1,0:T(8,128)(2,1)} %bitcast.28), channel_id=1, replica_groups=mesh['y'=8,'p'=2,'zq'=2,'c'=2,'zh'=2,'x'=4] {'p','c'}, dimensions={0}, use_global_device_ids=true | all-gather | bytes 327680 | tf_op jit(solution)/shard_map/all_gather | solution.py:190
  20.1 0.7 all-to-all-done
  20.8 0.1 reshape.83.q_ref
  20.9 1.6 %manifest_attention.1 = bf16[16,40,128]{2,1,0:T(8,128)(2,1)} custom-call(bf16[512,128]{1,0:T(8,128)(2,1)S(1)} %reshape.83.q_ref, bf16[4,2,128,128]{3,2,1,0:T(8,128)(2,1)S(1)} %all_gather.9.kv_ref), custom_call_target="tpu_custom_call" | custom-call | tf_op jit(solution)/shard_map/manifest_attention/pallas_call | solution.py:91
  22.5 7.7 %all-to-all-start.1 = ((bf16[16,40,128]{2,1,0:T(8,128)(2,1)}), bf16[16,40,128]{2,1,0:T(8,128)(2,1)S(1)}, u32[]{:S(2)}, u32[]{:S(2)}) async-start(bf16[16,40,128]{2,1,0:T(8,128)(2,1)} %manifest_attention.1), calls=%async_computation.1 | async-start | bytes 327680 | tf_op jit(solution)/shard_map/all_to_all | solution.py:180
  30.3 2.0 %collective-permute-start = (bf16[1024,128]{1,0:T(8,128)(2,1)S(1)}, bf16[1024,128]{1,0:T(8,128)(2,1)S(1)}, u32[]{:S(2)}, u32[]{:S(2)}) collective-permute-start(bf16[1024,128]{1,0:T(8,128)(2,1)S(1)} %copy-done.3), channel_id=1, source_target_pairs={{0,8},{8,0},{1,9},{9,1},{2,10},{10,2},{3,11},{11,3},{4,12},{12,4},... | collective-permute-start | bytes 786440 | tf_op jit(solution)/shard_map/ppermute | solution.py:176
  32.4 1.2 %own_attention.1 = (f32[32,128]{1,0:T(8,128)S(1)}, f32[32,128]{1,0:T(8,128)S(1)}, f32[32,128]{1,0:T(8,128)S(1)}) custom-call(s32[4,8]{1,0:T(4,128)S(1)} %copy-done.4, s32[4]{0:T(128)S(1)} %copy-done.6, bf16[32,128]{1,0:T(8,128)(2,1)S(1)} %reshape.85.q_ref, bf16[2,4,128]{2,1,0:T(4,128)(2,1)S(1)} %copy-done.5, bf16[2,2048,128]{2,1,0:T(8,128)(2,1)S(1)} %bitcast.24), custom_call_target="tpu_custom_call" | custom-call | tf_op jit(solution)/shard_map/own_attention/pallas_call | solution.py:60
  33.6 0.1 collective-permute-done.w1_ref
  33.7 7.2 %all-to-all-done.1.parts_ref = bf16[16,40,128]{2,1,0:T(8,128)(2,1)S(1)} async-done(((bf16[16,40,128]{2,1,0:T(8,128)(2,1)}), bf16[16,40,128]{2,1,0:T(8,128)(2,1)S(1)}, u32[]{:S(2)}, u32[]{:S(2)}) %all-to-all-start.1) | async-done | bytes 163872 | tf_op jit(solution)/shard_map/all_to_all | solution.py:180
  40.9 1.4 %join_attention.1 = bf16[32,4,1024]{2,1,0:T(4,128)(2,1)} custom-call(s32[1]{0:T(128)} %bitcast.place_ref, bf16[16,40,128]{2,1,0:T(8,128)(2,1)S(1)} %all-to-all-done.1.parts_ref, f32[32,128]{1,0:T(8,128)S(1)} %get-tuple-element.19.acc_ref, f32[32,128]{1,0:T(8,128)S(1)} %get-tuple-element.20.top_ref, f32[32,128]{1,0:T(8,128)S(1)} %get-tuple-element.21.total_ref), custom_call_target="tpu_custom_call" | custom-call | tf_op jit(solution)/shard_map/join_attention/pallas_call | solution.py:128
  42.3 4.6 %all-to-all-start.2 = ((bf16[32,4,1024]{2,1,0:T(4,128)(2,1)}), bf16[32,4,1024]{2,1,0:T(4,128)(2,1)S(1)}, u32[]{:S(2)}, u32[]{:S(2)}) async-start(bf16[32,4,1024]{2,1,0:T(4,128)(2,1)} %join_attention.1), calls=%async_computation.2 | async-start | bytes 524288 | tf_op jit(solution)/shard_map/all_to_all | solution.py:180
  46.9 1.9 %collective-permute-start.1 = (bf16[128,1792]{1,0:T(8,128)(2,1)S(1)}, bf16[128,1792]{1,0:T(8,128)(2,1)S(1)}, u32[]{:S(2)}, u32[]{:S(2)}) collective-permute-start(bf16[128,1792]{1,0:T(8,128)(2,1)S(1)} %copy-done.1), channel_id=1, source_target_pairs={{0,8},{8,0},{1,9},{9,1},{2,10},{10,2},{3,11},{11,3},{4,12},{12,4},... | collective-permute-start | bytes 1376264 | tf_op jit(solution)/shard_map/ppermute | solution.py:176
  48.9 2.4 %collective-permute-start.2 = (bf16[128,1792]{1,0:T(8,128)(2,1)S(1)}, bf16[128,1792]{1,0:T(8,128)(2,1)S(1)}, u32[]{:S(2)}, u32[]{:S(2)}) collective-permute-start(bf16[128,1792]{1,0:T(8,128)(2,1)S(1)} %copy-done.2), channel_id=1, source_target_pairs={{0,8},{8,0},{1,9},{9,1},{2,10},{10,2},{3,11},{11,3},{4,12},{12,4},... | collective-permute-start | bytes 1376264 | tf_op jit(solution)/shard_map/ppermute | solution.py:176
  51.3 8.7 %all-to-all-done.2 = bf16[32,4,1024]{2,1,0:T(4,128)(2,1)S(1)} async-done(((bf16[32,4,1024]{2,1,0:T(4,128)(2,1)}), bf16[32,4,1024]{2,1,0:T(4,128)(2,1)S(1)}, u32[]{:S(2)}, u32[]{:S(2)}) %all-to-all-start.2) | async-done | bytes 262176 | tf_op jit(solution)/shard_map/all_to_all | solution.py:180
  60.0 0.1 reshape.87.x_ref
  60.1 0.2 project.1
  60.3 9.9 %all-gather = bf16[256,256]{1,0:T(8,128)(2,1)S(1)} all-gather(bf16[128,256]{1,0:T(8,128)(2,1)S(1)} %project.1), channel_id=2, replica_groups=mesh['y'=8,'p'=2,'zq'=2,'c'=2,'zh'=2,'x'=4] {'zh'}, dimensions={0}, use_global_device_ids=true | all-gather | bytes 196608 | tf_op jit(solution)/shard_map/all_gather | solution.py:199
  70.2 0.7 add_shares.1
  70.9 4.8 %all-to-all-start.3 = ((bf16[4,128,256]{2,1,0:T(8,128)(2,1)}), bf16[4,128,256]{2,1,0:T(8,128)(2,1)S(1)}, u32[]{:S(2)}, u32[]{:S(2)}) async-start(bf16[4,128,256]{2,1,0:T(8,128)(2,1)} %add_shares.1), calls=%async_computation.3 | async-start | bytes 524288 | tf_op jit(solution)/shard_map/all_to_all | solution.py:180
  75.8 1.9 %collective-permute-start.3 = (bf16[32,4,128]{2,1,0:T(4,128)(2,1)S(1)}, bf16[32,4,128]{2,1,0:T(4,128)(2,1)S(1)}, u32[]{:S(2)}, u32[]{:S(2)}) collective-permute-start(bf16[32,4,128]{2,1,0:T(4,128)(2,1)S(1)} %get-tuple-element.31), channel_id=1, source_target_pairs={{0,8},{8,0},{1,9},{9,1},{2,10},{10,2},{3,11},{11,3},{4,12},{12,4},... | collective-permute-start | bytes 98312 | tf_op jit(solution)/shard_map/ppermute | solution.py:176
  77.7 1.2 %collective-permute-done.3 = bf16[32,4,128]{2,1,0:T(4,128)(2,1)S(1)} collective-permute-done((bf16[32,4,128]{2,1,0:T(4,128)(2,1)S(1)}, bf16[32,4,128]{2,1,0:T(4,128)(2,1)S(1)}, u32[]{:S(2)}, u32[]{:S(2)}) %collective-permute-start.3) | collective-permute-done | bytes 32800 | tf_op jit(solution)/shard_map/ppermute | solution.py:176
  79.0 2.0 %all-to-all-done.3 = bf16[4,128,256]{2,1,0:T(8,128)(2,1)S(1)} async-done(((bf16[4,128,256]{2,1,0:T(8,128)(2,1)}), bf16[4,128,256]{2,1,0:T(8,128)(2,1)S(1)}, u32[]{:S(2)}, u32[]{:S(2)}) %all-to-all-start.3) | async-done | bytes 262176 | tf_op jit(solution)/shard_map/all_to_all | solution.py:180
  81.0 1.3 %gate_up.1 = bf16[32,8,1792]{2,1,0:T(8,128)(2,1)} custom-call(bf16[128,256]{1,0:T(8,128)(2,1)S(1)} %add_convert_fusion.x_ref, bf16[128,1792]{1,0:T(8,128)(2,1)S(1)} %copy-done.1, bf16[128,1792]{1,0:T(8,128)(2,1)S(1)} %collective-permute-done.1.g1_ref, bf16[128,1792]{1,0:T(8,128)(2,1)S(1)} %copy-done.2, bf16[128,1792]{1,0:T(8,128)(2,1)S(1)} %collective-permute-done.2.u1_ref), custom_call_target="tpu_custom_call" | custom-call | tf_op jit(solution)/shard_map/gate_up/pallas_call | solution.py:165
  82.4 3.9 %all-to-all-start.4 = ((bf16[32,8,1792]{2,1,0:T(8,128)(2,1)}), bf16[32,8,1792]{2,1,0:T(8,128)(2,1)S(1)}, u32[]{:S(2)}, u32[]{:S(2)}) async-start(bf16[32,8,1792]{2,1,0:T(8,128)(2,1)} %gate_up.1), calls=%async_computation.4 | async-start | bytes 1835008 | tf_op jit(solution)/shard_map/all_to_all | solution.py:180
  86.3 1.9 %collective-permute-start.4 = (bf16[128,128]{1,0:T(8,128)(2,1)S(1)}, bf16[128,128]{1,0:T(8,128)(2,1)S(1)}, u32[]{:S(2)}, u32[]{:S(2)}) collective-permute-start(bf16[128,128]{1,0:T(8,128)(2,1)S(1)} %slice.31), channel_id=1, source_target_pairs={{0,8},{8,0},{1,9},{9,1},{2,10},{10,2},{3,11},{11,3},{4,12},{12,4},... | collective-permute-start | bytes 98312 | tf_op jit(solution)/shard_map/ppermute | solution.py:176
  88.3 1.2 %collective-permute-done.4 = bf16[128,128]{1,0:T(8,128)(2,1)S(1)} collective-permute-done((bf16[128,128]{1,0:T(8,128)(2,1)S(1)}, bf16[128,128]{1,0:T(8,128)(2,1)S(1)}, u32[]{:S(2)}, u32[]{:S(2)}) %collective-permute-start.4) | collective-permute-done | bytes 32800 | tf_op jit(solution)/shard_map/ppermute | solution.py:176
  89.5 0.7 copy.17
  90.1 20.8 %all-to-all-done.4 = bf16[32,8,1792]{2,1,0:T(8,128)(2,1)S(1)} async-done(((bf16[32,8,1792]{2,1,0:T(8,128)(2,1)}), bf16[32,8,1792]{2,1,0:T(8,128)(2,1)S(1)}, u32[]{:S(2)}, u32[]{:S(2)}) %all-to-all-start.4) | async-done | bytes 917536 | tf_op jit(solution)/shard_map/all_to_all | solution.py:180
  110.9 0.1 convert_reduce_fusion
  111.1 0.6 fusion.1
  (29 shorter events, 0.3 us)
Async XLA Ops:
  0.6 31.7 %copy-start.8 = (bf16[4,1024]{1,0:T(4,128)(2,1)S(1)}, bf16[4,1024]{1,0:T(4,128)(2,1)}, u32[]{:S(2)}) copy-start(bf16[4,1024]{1,0:T(4,128)(2,1)} %param.10) | copy-start | bytes 24580
  0.6 29.6 %copy-start.3 = (bf16[1024,128]{1,0:T(8,128)(2,1)S(1)}, bf16[1024,128]{1,0:T(8,128)(2,1)}, u32[]{:S(2)}) copy-start(bf16[1024,128]{1,0:T(8,128)(2,1)} %w0_ref.1) | copy-start | bytes 786436
  0.7 31.7 %copy-start.6 = (s32[4]{0:T(128)S(1)}, s32[4]{0:T(128)}, u32[]{:S(2)}) copy-start(s32[4]{0:T(128)} %len_ref.1) | copy-start | bytes 52
  0.7 31.7 %copy-start.4 = (s32[4,8]{1,0:T(4,128)S(1)}, s32[4,8]{1,0:T(4,128)}, u32[]{:S(2)}) copy-start(s32[4,8]{1,0:T(4,128)} %pages_ref.1) | copy-start | bytes 388
  0.7 31.7 %copy-start = (bf16[2,32,64,128]{3,2,1,0:T(8,128)(2,1)S(1)}, bf16[2,32,64,128]{3,2,1,0:T(8,128)(2,1)}, u32[]{:S(2)}) copy-start(bf16[2,32,64,128]{3,2,1,0:T(8,128)(2,1)} %param.12) | copy-start | bytes 3145732
  0.7 31.7 %copy-start.5 = (bf16[2,4,128]{2,1,0:T(4,128)(2,1)S(1)}, bf16[2,4,128]{2,1,0:T(4,128)(2,1)}, u32[]{:S(2)}) copy-start(bf16[2,4,128]{2,1,0:T(4,128)(2,1)} %new_ref.1) | copy-start | bytes 6148
  2.2 18.6 %all-to-all-start = ((bf16[16,4,1024]{2,1,0:T(4,128)(2,1)}), bf16[16,4,1024]{2,1,0:T(4,128)(2,1)S(1)}, u32[]{:S(2)}, u32[]{:S(2)}) async-start(bf16[16,4,1024]{2,1,0:T(4,128)(2,1)} %broadcast_in_dim.2), calls=%async_computation | async-start | bytes 262144 | tf_op jit(solution)/shard_map/all_to_all | solution.py:180
  22.5 18.4 %all-to-all-start.1 = ((bf16[16,40,128]{2,1,0:T(8,128)(2,1)}), bf16[16,40,128]{2,1,0:T(8,128)(2,1)S(1)}, u32[]{:S(2)}, u32[]{:S(2)}) async-start(bf16[16,40,128]{2,1,0:T(8,128)(2,1)} %manifest_attention.1), calls=%async_computation.1 | async-start | bytes 327680 | tf_op jit(solution)/shard_map/all_to_all | solution.py:180
  30.3 3.4 %collective-permute-start = (bf16[1024,128]{1,0:T(8,128)(2,1)S(1)}, bf16[1024,128]{1,0:T(8,128)(2,1)S(1)}, u32[]{:S(2)}, u32[]{:S(2)}) collective-permute-start(bf16[1024,128]{1,0:T(8,128)(2,1)S(1)} %copy-done.3), channel_id=1, source_target_pairs={{0,8},{8,0},{1,9},{9,1},{2,10},{10,2},{3,11},{11,3},{4,12},{12,4},... | collective-permute-start | bytes 786440 | tf_op jit(solution)/shard_map/ppermute | solution.py:176
  32.3 14.7 %copy-start.1 = (bf16[128,1792]{1,0:T(8,128)(2,1)S(1)}, bf16[128,1792]{1,0:T(8,128)(2,1)}, u32[]{:S(2)}) copy-start(bf16[128,1792]{1,0:T(8,128)(2,1)} %g0_ref.1) | copy-start | bytes 1376260
  32.3 16.6 %copy-start.2 = (bf16[128,1792]{1,0:T(8,128)(2,1)S(1)}, bf16[128,1792]{1,0:T(8,128)(2,1)}, u32[]{:S(2)}) copy-start(bf16[128,1792]{1,0:T(8,128)(2,1)} %u0_ref.1) | copy-start | bytes 1376260
  42.3 17.6 %all-to-all-start.2 = ((bf16[32,4,1024]{2,1,0:T(4,128)(2,1)}), bf16[32,4,1024]{2,1,0:T(4,128)(2,1)S(1)}, u32[]{:S(2)}, u32[]{:S(2)}) async-start(bf16[32,4,1024]{2,1,0:T(4,128)(2,1)} %join_attention.1), calls=%async_computation.2 | async-start | bytes 524288 | tf_op jit(solution)/shard_map/all_to_all | solution.py:180
  46.9 13.1 %collective-permute-start.1 = (bf16[128,1792]{1,0:T(8,128)(2,1)S(1)}, bf16[128,1792]{1,0:T(8,128)(2,1)S(1)}, u32[]{:S(2)}, u32[]{:S(2)}) collective-permute-start(bf16[128,1792]{1,0:T(8,128)(2,1)S(1)} %copy-done.1), channel_id=1, source_target_pairs={{0,8},{8,0},{1,9},{9,1},{2,10},{10,2},{3,11},{11,3},{4,12},{12,4},... | collective-permute-start | bytes 1376264 | tf_op jit(solution)/shard_map/ppermute | solution.py:176
  48.9 11.2 %collective-permute-start.2 = (bf16[128,1792]{1,0:T(8,128)(2,1)S(1)}, bf16[128,1792]{1,0:T(8,128)(2,1)S(1)}, u32[]{:S(2)}, u32[]{:S(2)}) collective-permute-start(bf16[128,1792]{1,0:T(8,128)(2,1)S(1)} %copy-done.2), channel_id=1, source_target_pairs={{0,8},{8,0},{1,9},{9,1},{2,10},{10,2},{3,11},{11,3},{4,12},{12,4},... | collective-permute-start | bytes 1376264 | tf_op jit(solution)/shard_map/ppermute | solution.py:176
  60.0 15.7 %copy-start.7 = (bf16[256,128]{1,0:T(8,128)(2,1)S(1)}, bf16[256,128]{1,0:T(8,128)(2,1)}, u32[]{:S(2)}) copy-start(bf16[256,128]{1,0:T(8,128)(2,1)} %param.16) | copy-start | bytes 196612
  70.9 10.0 %all-to-all-start.3 = ((bf16[4,128,256]{2,1,0:T(8,128)(2,1)}), bf16[4,128,256]{2,1,0:T(8,128)(2,1)S(1)}, u32[]{:S(2)}, u32[]{:S(2)}) async-start(bf16[4,128,256]{2,1,0:T(8,128)(2,1)} %add_shares.1), calls=%async_computation.3 | async-start | bytes 524288 | tf_op jit(solution)/shard_map/all_to_all | solution.py:180
  75.8 3.1 %collective-permute-start.3 = (bf16[32,4,128]{2,1,0:T(4,128)(2,1)S(1)}, bf16[32,4,128]{2,1,0:T(4,128)(2,1)S(1)}, u32[]{:S(2)}, u32[]{:S(2)}) collective-permute-start(bf16[32,4,128]{2,1,0:T(4,128)(2,1)S(1)} %get-tuple-element.31), channel_id=1, source_target_pairs={{0,8},{8,0},{1,9},{9,1},{2,10},{10,2},{3,11},{11,3},{4,12},{12,4},... | collective-permute-start | bytes 98312 | tf_op jit(solution)/shard_map/ppermute | solution.py:176
  82.4 28.6 %all-to-all-start.4 = ((bf16[32,8,1792]{2,1,0:T(8,128)(2,1)}), bf16[32,8,1792]{2,1,0:T(8,128)(2,1)S(1)}, u32[]{:S(2)}, u32[]{:S(2)}) async-start(bf16[32,8,1792]{2,1,0:T(8,128)(2,1)} %gate_up.1), calls=%async_computation.4 | async-start | bytes 1835008 | tf_op jit(solution)/shard_map/all_to_all | solution.py:180
  86.3 3.1 %collective-permute-start.4 = (bf16[128,128]{1,0:T(8,128)(2,1)S(1)}, bf16[128,128]{1,0:T(8,128)(2,1)S(1)}, u32[]{:S(2)}, u32[]{:S(2)}) collective-permute-start(bf16[128,128]{1,0:T(8,128)(2,1)S(1)} %slice.31), channel_id=1, source_target_pairs={{0,8},{8,0},{1,9},{9,1},{2,10},{10,2},{3,11},{11,3},{4,12},{12,4},... | collective-permute-start | bytes 98312 | tf_op jit(solution)/shard_map/ppermute | solution.py:176

commit v15 on v13

--- a/solution.py
+++ b/solution.py
@@ -187,7 +187,7 @@
     rows = CHIPS * ROWS
     q = queries.reshape(QROWS, HD)
     q_all = exchange(jnp.broadcast_to(q[None], (PEERS, QROWS, HD)), SPARSE).reshape(PEERS * QROWS, HD)
-    kv = lax.all_gather(man_kv.reshape(1, 2, 2 * PAGE, HD), ("p", "c"), axis=0, tiled=True)
+    kv = lax.all_gather(man_kv.reshape(1, 2, 2 * PAGE, HD), ("c", "p"), axis=0, tiled=True)
     parts = exchange(man_part(q_all, kv), SPARSE)
     own = own_part(pages, own_len, q, new_kv, own_kv.reshape(2, POOL * PAGE, HD))
     parts, own, w_out_c = tie((parts, own, swap(w_out)))

time: 113 us -> 120 us (1.062)
  blocking collectives: 18.8 us -> 25.2 us
  starting transfers between devices: 40.2 us -> 42.3 us
  waiting for transfers between devices: 42.1 us -> 40.8 us
    all_gather x1, blocking collectives: 8.91 us -> 15.5 us  [on_device(): lax.all_gather(man_kv.reshape(1, 2, 2 * PAGE, HD), ('c', 'p'), axis=0, ti...]
    all_to_all x5, starting transfers between devices: 30.1 us -> 32.2 us  [exchange(): return lax.all_to_all(x, axes, 0, 0, tiled=True)]
    all_to_all x5, waiting for transfers between devices: 39.6 us -> 38.2 us  [exchange(): return lax.all_to_all(x, axes, 0, 0, tiled=True)]
  transfers between devices with their start and end apart: 10 -> 10, of which waited for: 8 -> 7; matrix products, arithmetic and copies ran while one was open for 1% -> 1% of each run, Pallas kernels for 1% -> 1%
where the time goes in v15:
time: 120 us; the launch traced here: 119 us
  starting transfers between devices  42.3 us (35%)
  waiting for transfers between devices  40.8 us (34%)
  blocking collectives  25.2 us (21%)
  Pallas kernels  6.54 us (5%)
  local copies, waits for them, and re-layouts  2.28 us (2%)
    all_to_all x5, waiting for transfers between devices, exchange(): return lax.all_to_all(x, axes, 0, 0, tiled=True)  38.2 us
    all_to_all x5, starting transfers between devices, exchange(): return lax.all_to_all(x, axes, 0, 0, tiled=True)  32.2 us
    all_gather x1, blocking collectives, on_device(): lax.all_gather(man_kv.reshape(1, 2, 2 * PAGE, HD), ('c', 'p'), axis=0, ti...  15.5 us
    ppermute x5, starting transfers between devices, swap(): return lax.ppermute(x, 'c', [(0, 1), (1, 0)])  10.1 us
    all_gather x1, blocking collectives, on_device(): shares = lax.all_gather(share, 'zh', axis=0)  9.73 us
    ppermute x5, waiting for transfers between devices, swap(): return lax.ppermute(x, 'c', [(0, 1), (1, 0)])  2.56 us
  transfers between devices with their start and end apart: 10, of which 7 were waited for; matrix products, arithmetic and copies ran while one was open for 1% of the time, Pallas kernels for 1%

profile of v15, /device:TPU:4, one launch (start us, length us, event | category | flops | bytes accessed | tf_op | source)
XLA Modules:
  0.0 118.9 jit_solution(15654044405227003672)
XLA Ops:
  0.7 0.8 broadcast_in_dim.7.q_ref
  1.5 0.7 broadcast_in_dim.8
  2.2 9.0 %all-to-all-start = ((bf16[16,32,128]{2,1,0:T(8,128)(2,1)}), bf16[16,32,128]{2,1,0:T(8,128)(2,1)S(1)}, u32[]{:S(2)}, u32[]{:S(2)}) async-start(bf16[16,32,128]{2,1,0:T(8,128)(2,1)} %broadcast_in_dim.8), calls=%async_computation | async-start | bytes 262144 | tf_op jit(solution)/shard_map/all_to_all | solution.py:180
  11.2 15.5 %all_gather.9.kv_ref = bf16[4,2,128,128]{3,2,1,0:T(8,128)(2,1)S(1)} all-gather(bf16[1,2,128,128]{3,2,1,0:T(8,128)(2,1)} %bitcast.30), channel_id=1, replica_groups=mesh['y'=8,'p'=2,'zq'=2,'c'=2,'zh'=2,'x'=4] {'c','p'}, dimensions={0}, use_global_device_ids=true | all-gather | bytes 327680 | tf_op jit(solution)/shard_map/all_gather | solution.py:190
  26.6 1.6 %manifest_attention.1 = bf16[16,40,128]{2,1,0:T(8,128)(2,1)} custom-call(bf16[512,128]{1,0:T(8,128)(2,1)S(1)} %bitcast.26, bf16[4,2,128,128]{3,2,1,0:T(8,128)(2,1)S(1)} %all_gather.9.kv_ref), custom_call_target="tpu_custom_call" | custom-call | tf_op jit(solution)/shard_map/manifest_attention/pallas_call | solution.py:91
  28.3 8.9 %all-to-all-start.1 = ((bf16[16,40,128]{2,1,0:T(8,128)(2,1)}), bf16[16,40,128]{2,1,0:T(8,128)(2,1)S(1)}, u32[]{:S(2)}, u32[]{:S(2)}) async-start(bf16[16,40,128]{2,1,0:T(8,128)(2,1)} %manifest_attention.1), calls=%async_computation.1 | async-start | bytes 327680 | tf_op jit(solution)/shard_map/all_to_all | solution.py:180
  37.2 1.9 %collective-permute-start = (bf16[1024,128]{1,0:T(8,128)(2,1)S(1)}, bf16[1024,128]{1,0:T(8,128)(2,1)S(1)}, u32[]{:S(2)}, u32[]{:S(2)}) collective-permute-start(bf16[1024,128]{1,0:T(8,128)(2,1)S(1)} %copy-done.3), channel_id=1, source_target_pairs={{0,8},{8,0},{1,9},{9,1},{2,10},{10,2},{3,11},{11,3},{4,12},{12,4},... | collective-permute-start | bytes 786440 | tf_op jit(solution)/shard_map/ppermute | solution.py:176
  39.2 0.0 copy-start.1
  39.2 1.2 %own_attention.1 = (f32[32,128]{1,0:T(8,128)S(1)}, f32[32,128]{1,0:T(8,128)S(1)}, f32[32,128]{1,0:T(8,128)S(1)}) custom-call(s32[4,8]{1,0:T(4,128)S(1)} %copy-done.4, s32[4]{0:T(128)S(1)} %copy-done.6, bf16[32,128]{1,0:T(8,128)(2,1)S(1)} %broadcast_in_dim.7.q_ref, bf16[2,4,128]{2,1,0:T(4,128)(2,1)S(1)} %copy-done.5, bf16[2,2048,128]{2,1,0:T(8,128)(2,1)S(1)} %bitcast.25), custom_call_target="tpu_custom_call" | custom-call | tf_op jit(solution)/shard_map/own_attention/pallas_call | solution.py:60
  40.4 0.2 collective-permute-done.w1_ref
  40.7 6.7 %all-to-all-done.1.parts_ref = bf16[16,40,128]{2,1,0:T(8,128)(2,1)S(1)} async-done(((bf16[16,40,128]{2,1,0:T(8,128)(2,1)}), bf16[16,40,128]{2,1,0:T(8,128)(2,1)S(1)}, u32[]{:S(2)}, u32[]{:S(2)}) %all-to-all-start.1) | async-done | bytes 163872 | tf_op jit(solution)/shard_map/all_to_all | solution.py:180
  47.3 1.4 %join_attention.1 = bf16[32,4,1024]{2,1,0:T(4,128)(2,1)} custom-call(s32[1]{0:T(128)} %bitcast.place_ref, bf16[16,40,128]{2,1,0:T(8,128)(2,1)S(1)} %all-to-all-done.1.parts_ref, f32[32,128]{1,0:T(8,128)S(1)} %get-tuple-element.19.acc_ref, f32[32,128]{1,0:T(8,128)S(1)} %get-tuple-element.20.top_ref, f32[32,128]{1,0:T(8,128)S(1)} %get-tuple-element.21.total_ref), custom_call_target="tpu_custom_call" | custom-call | tf_op jit(solution)/shard_map/join_attention/pallas_call | solution.py:128
  48.7 5.5 %all-to-all-start.2 = ((bf16[32,4,1024]{2,1,0:T(4,128)(2,1)}), bf16[32,4,1024]{2,1,0:T(4,128)(2,1)S(1)}, u32[]{:S(2)}, u32[]{:S(2)}) async-start(bf16[32,4,1024]{2,1,0:T(4,128)(2,1)} %join_attention.1), calls=%async_computation.2 | async-start | bytes 524288 | tf_op jit(solution)/shard_map/all_to_all | solution.py:180
  54.3 1.9 %collective-permute-start.1 = (bf16[128,1792]{1,0:T(8,128)(2,1)S(1)}, bf16[128,1792]{1,0:T(8,128)(2,1)S(1)}, u32[]{:S(2)}, u32[]{:S(2)}) collective-permute-start(bf16[128,1792]{1,0:T(8,128)(2,1)S(1)} %copy-done.1), channel_id=1, source_target_pairs={{0,8},{8,0},{1,9},{9,1},{2,10},{10,2},{3,11},{11,3},{4,12},{12,4},... | collective-permute-start | bytes 1376264 | tf_op jit(solution)/shard_map/ppermute | solution.py:176
  56.2 2.4 %collective-permute-start.2 = (bf16[128,1792]{1,0:T(8,128)(2,1)S(1)}, bf16[128,1792]{1,0:T(8,128)(2,1)S(1)}, u32[]{:S(2)}, u32[]{:S(2)}) collective-permute-start(bf16[128,1792]{1,0:T(8,128)(2,1)S(1)} %copy-done.2), channel_id=1, source_target_pairs={{0,8},{8,0},{1,9},{9,1},{2,10},{10,2},{3,11},{11,3},{4,12},{12,4},... | collective-permute-start | bytes 1376264 | tf_op jit(solution)/shard_map/ppermute | solution.py:176
  58.6 8.6 %all-to-all-done.2 = bf16[32,4,1024]{2,1,0:T(4,128)(2,1)S(1)} async-done(((bf16[32,4,1024]{2,1,0:T(4,128)(2,1)}), bf16[32,4,1024]{2,1,0:T(4,128)(2,1)S(1)}, u32[]{:S(2)}, u32[]{:S(2)}) %all-to-all-start.2) | async-done | bytes 262176 | tf_op jit(solution)/shard_map/all_to_all | solution.py:180
  67.2 0.1 reshape.84.x_ref
  67.3 0.2 project.1
  67.5 9.7 %all-gather = bf16[256,256]{1,0:T(8,128)(2,1)S(1)} all-gather(bf16[128,256]{1,0:T(8,128)(2,1)S(1)} %project.1), channel_id=2, replica_groups=mesh['y'=8,'p'=2,'zq'=2,'c'=2,'zh'=2,'x'=4] {'zh'}, dimensions={0}, use_global_device_ids=true | all-gather | bytes 196608 | tf_op jit(solution)/shard_map/all_gather | solution.py:199
  77.3 0.7 add_shares.1
  78.0 4.8 %all-to-all-start.3 = ((bf16[4,128,256]{2,1,0:T(8,128)(2,1)}), bf16[4,128,256]{2,1,0:T(8,128)(2,1)S(1)}, u32[]{:S(2)}, u32[]{:S(2)}) async-start(bf16[4,128,256]{2,1,0:T(8,128)(2,1)} %add_shares.1), calls=%async_computation.3 | async-start | bytes 524288 | tf_op jit(solution)/shard_map/all_to_all | solution.py:180
  82.8 1.9 %collective-permute-start.3 = (bf16[32,4,128]{2,1,0:T(4,128)(2,1)S(1)}, bf16[32,4,128]{2,1,0:T(4,128)(2,1)S(1)}, u32[]{:S(2)}, u32[]{:S(2)}) collective-permute-start(bf16[32,4,128]{2,1,0:T(4,128)(2,1)S(1)} %get-tuple-element.31), channel_id=1, source_target_pairs={{0,8},{8,0},{1,9},{9,1},{2,10},{10,2},{3,11},{11,3},{4,12},{12,4},... | collective-permute-start | bytes 98312 | tf_op jit(solution)/shard_map/ppermute | solution.py:176
  84.7 1.2 collective-permute-done.3
  86.0 0.5 all-to-all-done.3
  86.6 1.4 %gate_up.1 = bf16[32,8,1792]{2,1,0:T(8,128)(2,1)} custom-call(bf16[128,256]{1,0:T(8,128)(2,1)S(1)} %add_convert_fusion.x_ref, bf16[128,1792]{1,0:T(8,128)(2,1)S(1)} %copy-done.1, bf16[128,1792]{1,0:T(8,128)(2,1)S(1)} %collective-permute-done.1.g1_ref, bf16[128,1792]{1,0:T(8,128)(2,1)S(1)} %copy-done.2, bf16[128,1792]{1,0:T(8,128)(2,1)S(1)} %collective-permute-done.2.u1_ref), custom_call_target="tpu_custom_call" | custom-call | tf_op jit(solution)/shard_map/gate_up/pallas_call | solution.py:165
  87.9 3.9 %all-to-all-start.4 = ((bf16[32,8,1792]{2,1,0:T(8,128)(2,1)}), bf16[32,8,1792]{2,1,0:T(8,128)(2,1)S(1)}, u32[]{:S(2)}, u32[]{:S(2)}) async-start(bf16[32,8,1792]{2,1,0:T(8,128)(2,1)} %gate_up.1), calls=%async_computation.4 | async-start | bytes 1835008 | tf_op jit(solution)/shard_map/all_to_all | solution.py:180
  91.8 1.9 %collective-permute-start.4 = (bf16[128,128]{1,0:T(8,128)(2,1)S(1)}, bf16[128,128]{1,0:T(8,128)(2,1)S(1)}, u32[]{:S(2)}, u32[]{:S(2)}) collective-permute-start(bf16[128,128]{1,0:T(8,128)(2,1)S(1)} %slice.31), channel_id=1, source_target_pairs={{0,8},{8,0},{1,9},{9,1},{2,10},{10,2},{3,11},{11,3},{4,12},{12,4},... | collective-permute-start | bytes 98312 | tf_op jit(solution)/shard_map/ppermute | solution.py:176
  93.8 1.2 collective-permute-done.4
  95.0 0.7 copy.17
  95.7 22.5 %all-to-all-done.4 = bf16[32,8,1792]{2,1,0:T(8,128)(2,1)S(1)} async-done(((bf16[32,8,1792]{2,1,0:T(8,128)(2,1)}), bf16[32,8,1792]{2,1,0:T(8,128)(2,1)S(1)}, u32[]{:S(2)}, u32[]{:S(2)}) %all-to-all-start.4) | async-done | bytes 917536 | tf_op jit(solution)/shard_map/all_to_all | solution.py:180
  118.2 0.1 convert_reduce_fusion
  118.3 0.6 fusion.1
  (26 shorter events, 0.3 us)
Async XLA Ops:
  0.6 36.6 %copy-start.3 = (bf16[1024,128]{1,0:T(8,128)(2,1)S(1)}, bf16[1024,128]{1,0:T(8,128)(2,1)}, u32[]{:S(2)}) copy-start(bf16[1024,128]{1,0:T(8,128)(2,1)} %w0_ref.1) | copy-start | bytes 786436
  0.6 38.6 %copy-start.6 = (s32[4]{0:T(128)S(1)}, s32[4]{0:T(128)}, u32[]{:S(2)}) copy-start(s32[4]{0:T(128)} %len_ref.1) | copy-start | bytes 52
  0.7 38.6 %copy-start.4 = (s32[4,8]{1,0:T(4,128)S(1)}, s32[4,8]{1,0:T(4,128)}, u32[]{:S(2)}) copy-start(s32[4,8]{1,0:T(4,128)} %pages_ref.1) | copy-start | bytes 388
  0.7 38.6 %copy-start = (bf16[2,32,64,128]{3,2,1,0:T(8,128)(2,1)S(1)}, bf16[2,32,64,128]{3,2,1,0:T(8,128)(2,1)}, u32[]{:S(2)}) copy-start(bf16[2,32,64,128]{3,2,1,0:T(8,128)(2,1)} %param.12) | copy-start | bytes 3145732
  0.7 38.6 %copy-start.5 = (bf16[2,4,128]{2,1,0:T(4,128)(2,1)S(1)}, bf16[2,4,128]{2,1,0:T(4,128)(2,1)}, u32[]{:S(2)}) copy-start(bf16[2,4,128]{2,1,0:T(4,128)(2,1)} %new_ref.1) | copy-start | bytes 6148
  2.2 24.5 %all-to-all-start = ((bf16[16,32,128]{2,1,0:T(8,128)(2,1)}), bf16[16,32,128]{2,1,0:T(8,128)(2,1)S(1)}, u32[]{:S(2)}, u32[]{:S(2)}) async-start(bf16[16,32,128]{2,1,0:T(8,128)(2,1)} %broadcast_in_dim.8), calls=%async_computation | async-start | bytes 262144 | tf_op jit(solution)/shard_map/all_to_all | solution.py:180
  28.3 19.0 %all-to-all-start.1 = ((bf16[16,40,128]{2,1,0:T(8,128)(2,1)}), bf16[16,40,128]{2,1,0:T(8,128)(2,1)S(1)}, u32[]{:S(2)}, u32[]{:S(2)}) async-start(bf16[16,40,128]{2,1,0:T(8,128)(2,1)} %manifest_attention.1), calls=%async_computation.1 | async-start | bytes 327680 | tf_op jit(solution)/shard_map/all_to_all | solution.py:180
  37.2 3.4 %collective-permute-start = (bf16[1024,128]{1,0:T(8,128)(2,1)S(1)}, bf16[1024,128]{1,0:T(8,128)(2,1)S(1)}, u32[]{:S(2)}, u32[]{:S(2)}) collective-permute-start(bf16[1024,128]{1,0:T(8,128)(2,1)S(1)} %copy-done.3), channel_id=1, source_target_pairs={{0,8},{8,0},{1,9},{9,1},{2,10},{10,2},{3,11},{11,3},{4,12},{12,4},... | collective-permute-start | bytes 786440 | tf_op jit(solution)/shard_map/ppermute | solution.py:176
  39.2 15.1 %copy-start.1 = (bf16[128,1792]{1,0:T(8,128)(2,1)S(1)}, bf16[128,1792]{1,0:T(8,128)(2,1)}, u32[]{:S(2)}) copy-start(bf16[128,1792]{1,0:T(8,128)(2,1)} %g0_ref.1) | copy-start | bytes 1376260
  39.2 17.0 %copy-start.2 = (bf16[128,1792]{1,0:T(8,128)(2,1)S(1)}, bf16[128,1792]{1,0:T(8,128)(2,1)}, u32[]{:S(2)}) copy-start(bf16[128,1792]{1,0:T(8,128)(2,1)} %u0_ref.1) | copy-start | bytes 1376260
  48.7 18.5 %all-to-all-start.2 = ((bf16[32,4,1024]{2,1,0:T(4,128)(2,1)}), bf16[32,4,1024]{2,1,0:T(4,128)(2,1)S(1)}, u32[]{:S(2)}, u32[]{:S(2)}) async-start(bf16[32,4,1024]{2,1,0:T(4,128)(2,1)} %join_attention.1), calls=%async_computation.2 | async-start | bytes 524288 | tf_op jit(solution)/shard_map/all_to_all | solution.py:180
  54.3 13.0 %collective-permute-start.1 = (bf16[128,1792]{1,0:T(8,128)(2,1)S(1)}, bf16[128,1792]{1,0:T(8,128)(2,1)S(1)}, u32[]{:S(2)}, u32[]{:S(2)}) collective-permute-start(bf16[128,1792]{1,0:T(8,128)(2,1)S(1)} %copy-done.1), channel_id=1, source_target_pairs={{0,8},{8,0},{1,9},{9,1},{2,10},{10,2},{3,11},{11,3},{4,12},{12,4},... | collective-permute-start | bytes 1376264 | tf_op jit(solution)/shard_map/ppermute | solution.py:176
  56.2 11.1 %collective-permute-start.2 = (bf16[128,1792]{1,0:T(8,128)(2,1)S(1)}, bf16[128,1792]{1,0:T(8,128)(2,1)S(1)}, u32[]{:S(2)}, u32[]{:S(2)}) collective-permute-start(bf16[128,1792]{1,0:T(8,128)(2,1)S(1)} %copy-done.2), channel_id=1, source_target_pairs={{0,8},{8,0},{1,9},{9,1},{2,10},{10,2},{3,11},{11,3},{4,12},{12,4},... | collective-permute-start | bytes 1376264 | tf_op jit(solution)/shard_map/ppermute | solution.py:176
  67.3 15.5 %copy-start.7 = (bf16[256,128]{1,0:T(8,128)(2,1)S(1)}, bf16[256,128]{1,0:T(8,128)(2,1)}, u32[]{:S(2)}) copy-start(bf16[256,128]{1,0:T(8,128)(2,1)} %param.16) | copy-start | bytes 196612
  78.0 8.5 %all-to-all-start.3 = ((bf16[4,128,256]{2,1,0:T(8,128)(2,1)}), bf16[4,128,256]{2,1,0:T(8,128)(2,1)S(1)}, u32[]{:S(2)}, u32[]{:S(2)}) async-start(bf16[4,128,256]{2,1,0:T(8,128)(2,1)} %add_shares.1), calls=%async_computation.3 | async-start | bytes 524288 | tf_op jit(solution)/shard_map/all_to_all | solution.py:180
  82.8 3.1 %collective-permute-start.3 = (bf16[32,4,128]{2,1,0:T(4,128)(2,1)S(1)}, bf16[32,4,128]{2,1,0:T(4,128)(2,1)S(1)}, u32[]{:S(2)}, u32[]{:S(2)}) collective-permute-start(bf16[32,4,128]{2,1,0:T(4,128)(2,1)S(1)} %get-tuple-element.31), channel_id=1, source_target_pairs={{0,8},{8,0},{1,9},{9,1},{2,10},{10,2},{3,11},{11,3},{4,12},{12,4},... | collective-permute-start | bytes 98312 | tf_op jit(solution)/shard_map/ppermute | solution.py:176
  87.9 30.3 %all-to-all-start.4 = ((bf16[32,8,1792]{2,1,0:T(8,128)(2,1)}), bf16[32,8,1792]{2,1,0:T(8,128)(2,1)S(1)}, u32[]{:S(2)}, u32[]{:S(2)}) async-start(bf16[32,8,1792]{2,1,0:T(8,128)(2,1)} %gate_up.1), calls=%async_computation.4 | async-start | bytes 1835008 | tf_op jit(solution)/shard_map/all_to_all | solution.py:180
  91.8 3.1 %collective-permute-start.4 = (bf16[128,128]{1,0:T(8,128)(2,1)S(1)}, bf16[128,128]{1,0:T(8,128)(2,1)S(1)}, u32[]{:S(2)}, u32[]{:S(2)}) collective-permute-start(bf16[128,128]{1,0:T(8,128)(2,1)S(1)} %slice.31), channel_id=1, source_target_pairs={{0,8},{8,0},{1,9},{9,1},{2,10},{10,2},{3,11},{11,3},{4,12},{12,4},... | collective-permute-start | bytes 98312 | tf_op jit(solution)/shard_map/ppermute | solution.py:176
